TPU v7x, 128 devices: a whole 4x4x4 slice. The times are simulated.
128 devices in a mesh: aa: 32 (over y, x, core), ba: 4 (over z).
Axes of the slice: x: 4, y: 4, z: 4, core: 2. Of those that a mesh axis runs over, the one named last changes fastest.
Arguments:
- table_a: bfloat16 [131072, 768], P('aa'), may hold values from -6 to 6
- table_b: bfloat16 [65536, 768], P(('ba', 'aa')), may hold values from -6 to 6
- pair_a: int32 [32, 4, 32], P('aa', 'ba'), may hold values from 0 to 7, as said below
- pair_b: int32 [32, 4, 32], P('aa', 'ba'), may hold values from 0 to 31, as said below
- pair_count: int32 [32, 4], P('aa', 'ba'), may hold values from 4 to 32, as said below
Outputs:
- log_u: float32 [131072], P('aa')
- log_v: float32 [65536], P(('ba', 'aa'))
Inputs may be any that keep to these rules, and one draw needn't show every extreme that they name: `pair_a`: each entry names one of the 8 A blocks of its owner. `pair_b`: each entry names one of the 32 blocks of its B slab; within one list no two slots name the same A block and B block together. `pair_count`: some list is full in every draw.
All inputs are finite; a program needn't handle non-finite values.
Results may differ from a plain program's by a relative error of at most 0.0003.
Values may be sent and summed in bfloat16 or wider, within the bound.
No kernel may reach another device: no remote copies, remote signals or barrier semaphores. Data moves between devices by JAX's collectives and lax.ppermute only.
A program may use at most 128 MiB of HBM per device.

v0:
```python
import math

import jax
import jax.numpy as jnp
from jax import lax
from jax.sharding import PartitionSpec as P

TILE = 512
ABLK = 8
ITERS = 3


def on_device(table_a, table_b, pair_a, pair_b, pair_count):
    width = table_a.shape[1]
    scale = 2.5 / math.sqrt(width)
    slot_total = pair_a.shape[2]
    blocks_a = table_a.reshape(ABLK, TILE, width)
    slots_a = pair_a[0, 0]
    slots_b = pair_b[0, 0]
    count = pair_count[0, 0]
    owners = lax.axis_size("aa")
    empty = jnp.zeros((slot_total, TILE, TILE), jnp.bfloat16)
    slab = lax.all_gather(table_b, "aa", axis=0, tiled=True)
    rows = slab.shape[0]

    def one_slot(slot, held):
        first = slots_b[slot] * TILE
        alive = (slot < count) & (first >= 0) & (first < 0 + rows)

        def build(inner):
            offset = jnp.clip(first - 0, 0, rows - TILE)
            block_b = lax.dynamic_slice_in_dim(slab, offset, TILE, 0)
            block_a = lax.dynamic_index_in_dim(blocks_a, slots_a[slot], 0, keepdims=False)
            score = lax.dot_general(
                block_a, block_b, (((1,), (1,)), ((), ())), preferred_element_type=jnp.float32
            )
            return lax.dynamic_update_index_in_dim(
                inner, jnp.exp(score * scale).astype(jnp.bfloat16), slot, 0
            )

        return lax.cond(alive, build, lambda inner: inner, held)

    store = lax.fori_loop(0, slot_total, one_slot, empty)
    match_a = slots_a[:, None] == jnp.arange(ABLK, dtype=jnp.int32)[None, :]
    match_b = slots_b[:, None] == jnp.arange(owners, dtype=jnp.int32)[None, :]
    v_slab = jnp.ones((owners, TILE), jnp.float32)
    v_mine = jnp.ones((1, TILE), jnp.float32)
    u_rows = jnp.ones((ABLK, TILE), jnp.float32)
    for step in range(ITERS):
        v_slots = v_slab.astype(jnp.bfloat16)[slots_b]
        row_terms = jnp.einsum("sij,sj->si", store, v_slots, preferred_element_type=jnp.float32)
        kernel_a = jnp.sum(jnp.where(match_a[:, :, None], row_terms[:, None, :], 0.0), axis=0)
        kernel_a = lax.psum(kernel_a, "ba")
        u_rows = 1.0 / (1.0 + kernel_a)
        u_slots = u_rows.astype(jnp.bfloat16)[slots_a]
        col_terms = jnp.einsum("sij,si->sj", store, u_slots, preferred_element_type=jnp.float32)
        kernel_b = jnp.sum(jnp.where(match_b[:, :, None], col_terms[:, None, :], 0.0), axis=0)
        totals = lax.psum(kernel_b, "aa")
        v_slab = 1.0 / (1.0 + totals)
        v_mine = lax.dynamic_slice_in_dim(v_slab, lax.axis_index("aa"), 1, 0)
    return (jnp.log(u_rows).reshape(-1), jnp.log(v_mine).reshape(-1))


def solution(mesh):
    in_specs = (
        P("aa", None),
        P(("ba", "aa"), None),
        P("aa", "ba", None),
        P("aa", "ba", None),
        P("aa", "ba"),
    )
    out_specs = (P("aa"), P(("ba", "aa")))
    return jax.shard_map(
        on_device, mesh=mesh, in_specs=in_specs, out_specs=out_specs, check_vma=False
    )
```

profile of v0, /device:TPU:0, one launch (start us, length us, event | category | flops | bytes accessed | tf_op | source)
XLA Modules:
  0.0 735.4 jit_solution(4747070453101454134)
XLA Ops:
  7.2 0.7 all-gather.2.cloned.1.call-update
  8.0 0.7 fusion.23
  9.3 0.7 fusion.24
  9.9 0.7 iota_compare_fusion.1
  10.7 0.7 iota_compare_fusion
  11.4 93.4 %all-gather.2.cloned.1.call-done = bf16[16384,768]{1,0:T(8,128)(2,1)} async-done(((bf16[512,768]{1,0:T(8,128)(2,1)}), bf16[16384,768]{1,0:T(8,128)(2,1)}) %all-gather.2.cloned.1.call-update) | async-done | bytes 25165840 | tf_op jit(solution)/shard_map/all_gather | solution.py:23
  104.8 5.9 broadcast_in_dim.104
  110.6 94.7 %while.16 = (s32[]{:T(128)}, bf16[32,512,512]{2,1,0:T(8,128)(2,1)}, s32[]{:T(128)}, s32[32]{0:T(128)S(1)}, s32[32]{0:T(128)S(1)}, /*index=5*/bf16[8,512,768]{2,1...) while((s32[]{:T(128)}, bf16[32,512,512]{2,1,0:T(8,128)(2,1)}, ...), condition=%wide.region_3.4_spmd, body=%wide.region_0.3_spmd.sunk | while | flops 403177472 | bytes 2097495 | solution.py:43
  112.5 5.6 conditional.2
  112.5 0.6 dynamic_slice.15
  115.2 2.9 fusion.3
  120.0 5.6 conditional.2
  120.0 0.6 dynamic_slice.15
  122.7 2.9 fusion.3
  127.4 5.5 conditional.2
  127.5 0.6 dynamic_slice.15
  130.1 2.8 fusion.3
  134.8 5.5 conditional.2
  134.8 0.6 dynamic_slice.15
  137.5 2.8 fusion.3
  142.2 5.5 conditional.2
  142.2 0.6 dynamic_slice.15
  144.9 2.8 fusion.3
  149.6 5.5 conditional.2
  149.6 0.6 dynamic_slice.15
  152.3 2.8 fusion.3
  205.4 8.1 %fusion.18 = f32[32,1,512]{2,1,0:T(1,128)S(1)} fusion(bf16[32,512,512]{2,1,0:T(8,128)(2,1)} %get-tuple-element.152, bf16[32,512,1]{1,0,2:T(8,128)(2,1)S(1)} %bitcast.57), kind=kOutput, calls=%fused_computation.37 | convolution fusion | flops 16777216 | bytes 16875520 | tf_op jit(solution)/shard_map/sij,sj->si/dot_general | solution.py:51
  213.6 97.7 %psum.42 = f32[8,512]{1,0:T(8,128)S(1)} all-reduce(f32[8,512]{1,0:T(8,128)S(1)} %select_reduce_fusion.5), channel_id=1, replica_groups=mesh['aa'=32,'ba'=4] {'ba'}, use_global_device_ids=true, to_apply=%region_5.6 | all-reduce | flops 4096 | bytes 32768 | tf_op jit(solution)/shard_map/psum | solution.py:53
  311.3 0.6 gather_fusion.1
  311.9 7.0 fusion.16
  318.9 0.8 select_reduce_fusion.2
  319.9 152.6 %all-reduce.4.cloned.1.call-done = f32[32,512]{1,0:T(8,128)} async-done(((f32[32,512]{1,0:T(8,128)}), f32[32,512]{1,0:T(8,128)}) %all-reduce.4.cloned.1.call-update) | async-done | bytes 65552 | tf_op jit(solution)/shard_map/psum | solution.py:58
  472.5 0.9 divide_convert_fusion.1
  473.3 0.6 gather_fusion.2
  474.0 8.1 %fusion.14 = f32[32,1,512]{2,1,0:T(1,128)S(1)} fusion(bf16[32,512,512]{2,1,0:T(8,128)(2,1)} %get-tuple-element.152, bf16[32,512,1]{1,0,2:T(8,128)(2,1)S(1)} %bitcast.61), kind=kOutput, calls=%fused_computation.31 | convolution fusion | flops 16777216 | bytes 16875520 | tf_op jit(solution)/shard_map/sij,sj->si/dot_general | solution.py:51
  482.2 17.2 %psum.44 = f32[8,512]{1,0:T(8,128)S(1)} all-reduce(f32[8,512]{1,0:T(8,128)S(1)} %select_reduce_fusion.4), channel_id=1, replica_groups=mesh['aa'=32,'ba'=4] {'ba'}, use_global_device_ids=true, to_apply=%region_9.10 | all-reduce | flops 4096 | bytes 32768 | tf_op jit(solution)/shard_map/psum | solution.py:53
  499.4 0.6 gather_fusion.3
  500.0 7.0 fusion.12
  507.1 0.8 select_reduce_fusion.1
  508.0 92.0 %all-reduce.6.cloned.1.call-done = f32[32,512]{1,0:T(8,128)} async-done(((f32[32,512]{1,0:T(8,128)}), f32[32,512]{1,0:T(8,128)}) %all-reduce.6.cloned.1.call-update) | async-done | bytes 65552 | tf_op jit(solution)/shard_map/psum | solution.py:58
  600.0 0.9 divide_convert_fusion
  601.5 8.1 %fusion.10 = f32[32,1,512]{2,1,0:T(1,128)S(1)} fusion(bf16[32,512,512]{2,1,0:T(8,128)(2,1)} %get-tuple-element.152, bf16[32,512,1]{1,0,2:T(8,128)(2,1)S(1)} %bitcast.59), kind=kOutput, calls=%fused_computation.25 | convolution fusion | flops 16777216 | bytes 16875520 | tf_op jit(solution)/shard_map/sij,sj->si/dot_general | solution.py:51
  609.7 17.2 %psum.46 = f32[8,512]{1,0:T(8,128)S(1)} all-reduce(f32[8,512]{1,0:T(8,128)S(1)} %select_reduce_fusion.3), channel_id=1, replica_groups=mesh['aa'=32,'ba'=4] {'ba'}, use_global_device_ids=true, to_apply=%region_13.14 | all-reduce | flops 4096 | bytes 32768 | tf_op jit(solution)/shard_map/psum | solution.py:53
  626.9 0.6 gather_fusion.5
  627.6 7.0 fusion.8
  634.6 0.8 select_reduce_fusion
  636.1 91.5 %all-reduce.8.cloned.1.call-done = f32[32,512]{1,0:T(8,128)} async-done(((f32[32,512]{1,0:T(8,128)}), f32[32,512]{1,0:T(8,128)}) %all-reduce.8.cloned.1.call-update) | async-done | bytes 65552 | tf_op jit(solution)/shard_map/psum | solution.py:58
  727.5 1.3 fusion.22
  (87 shorter events, 21.6 us)
Async XLA Ops:
  7.2 103.5 %copy-start = (s32[1,1,32]{2,1,0:T(1,128)S(1)}, s32[1,1,32]{2,1,0:T(1,128)}, u32[]{:S(2)}) copy-start(s32[1,1,32]{2,1,0:T(1,128)} %param.12) | copy-start | bytes 388
  7.2 103.5 %copy-start.1 = (s32[1,1,32]{2,1,0:T(1,128)S(1)}, s32[1,1,32]{2,1,0:T(1,128)}, u32[]{:S(2)}) copy-start(s32[1,1,32]{2,1,0:T(1,128)} %param.11) | copy-start | bytes 388
  7.2 97.6 %all-gather.2.cloned.1.call-start = ((), (), s32[]{:S(2)}) async-start(), calls=%async_computation | async-start | bytes 25952256 | tf_op jit(solution)/shard_map/all_gather | solution.py:23
  7.9 464.6 %all-reduce.4.cloned.1.call-start = ((), (), s32[]{:S(2)}) async-start(), calls=%async_computation.1 | async-start | bytes 131072 | tf_op jit(solution)/shard_map/psum | solution.py:58
  319.8 280.2 %all-reduce.6.cloned.1.call-start = ((), (), s32[]{:S(2)}) async-start(), calls=%async_computation.2 | async-start | bytes 131072 | tf_op jit(solution)/shard_map/psum | solution.py:58
  507.9 219.6 %all-reduce.8.cloned.1.call-start = ((), (), s32[]{:S(2)}) async-start(), calls=%async_computation.3 | async-start | bytes 131072 | tf_op jit(solution)/shard_map/psum | solution.py:58
Sparse Core Ops, SparseCore 0:
  10.3 94.4 all-gather.1
  319.9 152.5 all-reduce.3
  508.0 91.9 all-reduce.5
  635.6 91.9 all-reduce.7
where the time goes:
time: 739 us; the launch traced here: 735 us
  waiting for transfers between devices  430 us (58%)
  blocking collectives  132 us (18%)
  matrix products  62.2 us (8%)
  loops' own time  55.1 us (7%)
  local copies, waits for them, and re-layouts  32.9 us (4%)
  between operations  13.9 us (2%)
  other arithmetic  8.73 us (1%)
    psum x3, waiting for transfers between devices, on_device(): totals = lax.psum(kernel_b, 'aa')  336 us
    psum x3, blocking collectives, on_device(): kernel_a = lax.psum(kernel_a, 'ba')  132 us
    all_gather x1, waiting for transfers between devices, on_device(): slab = lax.all_gather(table_b, 'aa', axis=0, tiled=True)  93.4 us
    another operation x1, loops' own time, on_device(): store = lax.fori_loop(0, slot_total, one_slot, empty)  42.5 us
    dot_general x3, matrix products, on_device(): jnp.einsum('sij,sj->si', store, v_slots, preferred_element_type=jnp.float32)  24.2 us
    dot_general x3, matrix products, on_device(): jnp.einsum('sij,si->sj', store, u_slots, preferred_element_type=jnp.float32)  21 us
    dynamic_slice x32, local copies, waits for them, and re-layouts, one_slot(): first = slots_b[slot] * TILE  18.7 us
    dot_general x6, matrix products, build(): lax.dot_general(block_a, block_b, (((1,), (1,)), ((), ())), preferred_ele...  17 us
  transfers between devices with their start and end apart: 4, of which 4 were waited for; matrix products, arithmetic and copies ran while one was open for 1% of the time, Pallas kernels for 0%

commit v1 on v0

v1 whole, which is shorter than its diff:
```python
import math

import jax
import jax.numpy as jnp
from jax import lax
from jax.experimental import pallas as pl
from jax.experimental.pallas import tpu as pltpu
from jax.sharding import PartitionSpec as P

TILE = 512
ABLK = 8
ITERS = 3
NY, NX, NC, NZ = 4, 4, 2, 4
NCHIP = NY * NX
SLOTS = 32
CAP = NC * SLOTS
F32 = jnp.float32
BF16 = jnp.bfloat16
VM = pl.BlockSpec(memory_space=pltpu.VMEM)
SM = pl.BlockSpec(memory_space=pltpu.SMEM)
ANY = pl.BlockSpec(memory_space=pl.ANY)


def plan_pairs(lists, pairs, total, tally):
    core = lists[0, 2 * SLOTS + 1]
    for k in range(NCHIP + 1):
        tally[k] = 0

    def scan(body):
        for which in range(NC):
            live = lists[which, 2 * SLOTS]

            def step(s, carry, which=which):
                b = lists[which, SLOTS + s]

                @pl.when((b % NC) == core)
                def _():
                    body(which * ABLK + lists[which, s], b // NC)

                return carry

            lax.fori_loop(0, jnp.minimum(live, SLOTS), step, 0)

    def count(a, b):
        tally[b + 1] = tally[b + 1] + 1

    scan(count)
    for k in range(NCHIP):
        tally[k + 1] = tally[k + 1] + tally[k]

    total[0] = tally[NCHIP]

    def place(a, b):
        spot = tally[b]
        pairs[0, spot] = a
        pairs[1, spot] = b
        tally[b] = spot + 1

    scan(place)


def build_kernel(scale, lists, a_mine, a_other, b_all, store, out, pairs, total, abuf, bbuf, kv, tally, sems):
    plan_pairs(lists, pairs, total, tally)
    core = lists[0, 2 * SLOTS + 1]
    number = total[0]
    kv[...] = jnp.zeros_like(kv)

    def fetch(t, slot):
        a = pairs[0, t]
        row = pl.multiple_of((a % ABLK) * TILE, TILE)

        @pl.when(a // ABLK == core)
        def _():
            pltpu.make_async_copy(a_mine.at[pl.ds(row, TILE)], abuf.at[slot], sems.at[0, slot]).start()

        @pl.when(a // ABLK != core)
        def _():
            pltpu.make_async_copy(a_other.at[pl.ds(row, TILE)], abuf.at[slot], sems.at[0, slot]).start()

        brow = pl.multiple_of(pairs[1, t] * TILE, TILE)
        pltpu.make_async_copy(b_all.at[pl.ds(brow, TILE)], bbuf.at[slot], sems.at[1, slot]).start()

    @pl.when(number > 0)
    def _():
        fetch(0, 0)

    def step(t, carry):
        slot = t % 2

        @pl.when(t + 1 < number)
        def _():
            fetch(t + 1, 1 - slot)

        pltpu.make_async_copy(a_mine.at[pl.ds(0, TILE)], abuf.at[slot], sems.at[0, slot]).wait()
        pltpu.make_async_copy(b_all.at[pl.ds(0, TILE)], bbuf.at[slot], sems.at[1, slot]).wait()
        a = pairs[0, t]
        ones = jnp.ones((16, TILE), BF16)
        rows = 256
        for r in range(0, TILE, rows):
            score = lax.dot_general(
                abuf[slot, pl.ds(r, rows), :], bbuf[slot], (((1,), (1,)), ((), ())), preferred_element_type=F32
            )
            tile = jnp.exp(score * scale).astype(BF16)
            store[t, pl.ds(r, rows), :] = tile
            part = lax.dot_general(ones, tile, (((1,), (1,)), ((), ())), preferred_element_type=F32)
            kv[pl.ds(a, 1), pl.ds(r, rows)] += part[0:1]
        return carry

    lax.fori_loop(0, number, step, 0)
    spread(out, kv[...])


def spread(out, value):
    for k in range(out.shape[0]):
        out[k] = value


def pass_kernel(over_rows, pairs, total, parts, store, out, sums, weight):
    weight[...] = (1.0 / (1.0 + jnp.sum(parts[...], axis=0))).astype(BF16).astype(F32)
    sums[...] = jnp.zeros_like(sums)

    def step(t, carry):
        a = pairs[0, t]
        b = pairs[1, t]
        source, target = (b, a) if over_rows else (a, b)
        row = jnp.broadcast_to(weight[pl.ds(source, 1), :], (16, TILE)).astype(BF16)
        dims = (((1,), (1,)), ((), ())) if over_rows else (((1,), (0,)), ((), ()))
        part = lax.dot_general(row, store[t], dims, preferred_element_type=F32)
        sums[pl.ds(target, 1), :] += part[0:1]
        return carry

    lax.fori_loop(0, total[0], step, 0)
    spread(out, sums[...])


def params(mib=16):
    return pltpu.CompilerParams(vmem_limit_bytes=mib << 20)


def on_device(table_a, table_b, pair_a, pair_b, pair_count):
    scale = 2.5 / math.sqrt(table_a.shape[1])
    width = table_a.shape[1]
    core = lax.axis_index("core")
    swap = [(0, 1), (1, 0)]
    b_all = lax.all_gather(table_b, ("y", "x"), axis=0, tiled=True)
    a_other = lax.ppermute(table_a, "core", swap)
    own = jnp.concatenate(
        [pair_a.reshape(1, -1), pair_b.reshape(1, -1), pair_count.reshape(1, 1), jnp.full((1, 63), core, jnp.int32)],
        axis=1,
    )
    other = lax.ppermute(own, "core", swap)
    first = jnp.where(core == 0, own, other)
    second = jnp.where(core == 0, other, own)
    mark = jnp.arange(128)[None] > 2 * SLOTS
    lists = jnp.where(mark, core, jnp.concatenate([first, second], axis=0)).astype(jnp.int32)

    store, kv, pairs, total = pl.pallas_call(
        lambda *refs: build_kernel(scale, *refs),
        out_shape=(
            pltpu.VMEM((CAP, TILE, TILE), BF16),
            jax.ShapeDtypeStruct((NC * NZ, NC * ABLK, TILE), F32),
            jax.ShapeDtypeStruct((2, CAP), jnp.int32),
            jax.ShapeDtypeStruct((1,), jnp.int32),
        ),
        in_specs=[SM, ANY, ANY, ANY],
        out_specs=(VM, VM, SM, SM),
        scratch_shapes=[
            pltpu.VMEM((2, TILE, width), BF16),
            pltpu.VMEM((2, TILE, width), BF16),
            pltpu.VMEM((NC * ABLK, TILE), F32),
            pltpu.SMEM((NCHIP + 1,), jnp.int32),
            pltpu.SemaphoreType.DMA((2, 2)),
        ],
        compiler_params=params(),
        name="build",
    )(lists, table_a, a_other, b_all)

    def half(over_rows, parts, copies, name):
        return pl.pallas_call(
            lambda *refs: pass_kernel(over_rows, *refs),
            out_shape=jax.ShapeDtypeStruct((copies, NCHIP, TILE), F32),
            in_specs=[SM, SM, VM, VM],
            out_specs=VM,
            scratch_shapes=[pltpu.VMEM((NCHIP, TILE), F32), pltpu.VMEM((NCHIP, TILE), F32)],
            compiler_params=params(),
            name=name,
        )(pairs, total, parts, store)

    for step in range(ITERS):
        if step:
            kv = half(True, ktu_parts, NC * NZ, "rows")
        kv_parts = lax.all_to_all(kv, ("core", "z"), 0, 0, tiled=True)
        ktu = half(False, kv_parts, NCHIP, "columns")
        ktu_parts = lax.all_to_all(ktu, ("y", "x"), 0, 0, tiled=True)
    mine = lax.axis_index("y") * NX + lax.axis_index("x")
    u_sum = lax.dynamic_slice_in_dim(kv_parts, core * ABLK, ABLK, 1)
    v_sum = lax.dynamic_slice_in_dim(ktu_parts, mine, 1, 1)

    def final(parts):
        return jnp.log(1.0 / (1.0 + jnp.sum(parts, axis=0))).reshape(-1)

    return final(u_sum), final(v_sum)


def solution(mesh):
    fine = jax.sharding.Mesh(mesh.devices.reshape(NY, NX, NC, NZ), ("y", "x", "core", "z"))
    a_axes = ("y", "x", "core")
    b_axes = ("z", "y", "x", "core")
    in_specs = (P(a_axes, None), P(b_axes, None), P(a_axes, "z", None), P(a_axes, "z", None), P(a_axes, "z"))
    out_specs = (P(a_axes), P(b_axes))
    return jax.shard_map(on_device, mesh=fine, in_specs=in_specs, out_specs=out_specs, check_vma=False)
```

time: 739 us -> 300 us (0.41)
  waiting for transfers between devices: 430 us -> 105 us
  matrix products: 62.2 us -> 0 us
  loops' own time: 55.1 us -> 0 us
  Pallas kernels: 0 us -> 45 us
  blocking collectives: 132 us -> 97.6 us
  local copies, waits for them, and re-layouts: 32.9 us -> 22.2 us
    psum x3 -> x0, waiting for transfers between devices: 336 us -> none  [on_device(): totals = lax.psum(kernel_b, 'aa')]
    psum x3 -> x0, blocking collectives: 132 us -> none  [on_device(): kernel_a = lax.psum(kernel_a, 'ba')]
    all_to_all x0 -> x5, blocking collectives: none -> 97.6 us  [the longest x3 51.4 us: on_device(): kv_parts = lax.all_to_all(kv, ('core', 'z'), 0, 0, tiled=True)]
    dot_general x12 -> x0, matrix products: 62.2 us -> none  [the longest x3 24.2 us: on_device(): jnp.einsum('sij,sj->si', store, v_slots, preferred_element_type=jnp.float32)]
    another operation x33 -> x0, loops' own time: 55.1 us -> none  [the longest x1 42.5 us: on_device(): store = lax.fori_loop(0, slot_total, one_slot, empty)]
    pallas_call x0 -> x6, Pallas kernels: none -> 45 us  [the longest x5 23.3 us: half(): pl.pallas_call(lambda *refs: pass_kernel(over_rows, *refs), out_shape=jax...]
    dynamic_slice x38 -> x0, local copies, waits for them, and re-layouts: 22.6 us -> none  [the longest x32 18.7 us: one_slot(): first = slots_b[slot] * TILE]
    unnamed x5, local copies, waits for them, and re-layouts: 0.62 us -> 22.2 us
  transfers between devices with their start and end apart: 4 -> 4, of which waited for: 4 -> 3; matrix products, arithmetic and copies ran while one was open for 1% -> 1% of each run, Pallas kernels for 0% -> 0%
where the time goes in v1:
time: 300 us; the launch traced here: 294 us
  waiting for transfers between devices  105 us (35%)
  blocking collectives  97.6 us (33%)
  Pallas kernels  45 us (15%)
  local copies, waits for them, and re-layouts  22.2 us (7%)
  between operations  14.8 us (5%)
  starting transfers between devices  7.17 us (2%)
    all_gather x1, waiting for transfers between devices, on_device(): b_all = lax.all_gather(table_b, ('y', 'x'), axis=0, tiled=True)  83.6 us
    all_to_all x3, blocking collectives, on_device(): kv_parts = lax.all_to_all(kv, ('core', 'z'), 0, 0, tiled=True)  51.4 us
    all_to_all x2, blocking collectives, on_device(): ktu_parts = lax.all_to_all(ktu, ('y', 'x'), 0, 0, tiled=True)  46.2 us
    pallas_call x5, Pallas kernels, half(): pl.pallas_call(lambda *refs: pass_kernel(over_rows, *refs), out_shape=jax...  23.3 us
    unnamed x5, local copies, waits for them, and re-layouts  22.2 us
    pallas_call x1, Pallas kernels, on_device(): pl.pallas_call(lambda *refs: build_kernel(scale, *refs), out_shape=(pltpu...  21.7 us
    all_to_all x1, waiting for transfers between devices, on_device(): ktu_parts = lax.all_to_all(ktu, ('y', 'x'), 0, 0, tiled=True)  12.4 us
    ppermute x1, waiting for transfers between devices, on_device(): other = lax.ppermute(own, 'core', swap)  8.17 us
  transfers between devices with their start and end apart: 4, of which 3 were waited for; matrix products, arithmetic and copies ran while one was open for 1% of the time, Pallas kernels for 0%

profile of v1, /device:TPU:0, one launch (start us, length us, event | category | flops | bytes accessed | tf_op | source)
XLA Modules:
  0.0 293.9 jit_solution(13418669896349666596)
XLA Ops:
  7.2 0.0 all-gather.2.cloned.1.call-start
  7.2 0.7 all-gather.2.cloned.1.call-update
  7.9 0.1 collective-permute-start.1
  8.7 0.8 bitcast_add_fusion
  9.4 0.5 collective-permute-start
  9.9 8.2 %collective-permute-done = s32[1,128]{1,0:T(1,128)S(1)} collective-permute-done((s32[1,128]{1,0:T(1,128)S(1)}, s32[1,128]{1,0:T(1,128)S(1)}, u32[]{:S(2)}, u32[]{:S(2)}) %collective-permute-start) | collective-permute-done | bytes 544 | tf_op jit(solution)/shard_map/ppermute | solution.py:151
  18.1 0.7 broadcast_select_fusion.1
  18.9 0.0 collective-permute-done.1.refs_2_
  18.9 83.6 %all-gather.2.cloned.1.call-done.refs_3_ = bf16[8192,768]{1,0:T(8,128)(2,1)} async-done(((bf16[512,768]{1,0:T(8,128)(2,1)}), bf16[8192,768]{1,0:T(8,128)(2,1)}) %all-gather.2.cloned.1.call-update) | async-done | bytes 12582928 | tf_op jit(solution)/shard_map/all_gather | solution.py:145
  102.5 21.7 %build.1 = (bf16[64,512,512]{2,1,0:T(8,128)(2,1)S(1)}, f32[8,16,512]{2,1,0:T(8,128)S(1)}, s32[2,64]{1,0:T(2,128)S(1)}, s32[1]{0:T(128)}) custom-call(s32[2,128]{1,0:T(2,128)S(1)} %add_select_fusion.refs_0_, bf16[4096,768]{1,0:T(8,128)(2,1)} %refs_1_.1, bf16[4096,768]{1,0:T(8,128)(2,1)} %collective-permute-done.1.refs_2_, ...), custom_call_target="tpu_custom_call" | custom-call | tf_op jit(solution)/shard_map/build/pallas_call | solution.py:157
  124.2 0.0 copy-start
  124.3 11.1 %copy-done = bf16[64,512,512]{2,1,0:T(8,128)(2,1)} copy-done((bf16[64,512,512]{2,1,0:T(8,128)(2,1)}, bf16[64,512,512]{2,1,0:T(8,128)(2,1)S(1)}, u32[]{:S(2)}) %copy-start) | copy-done | bytes 33554456
  135.3 27.6 %all_to_all.30.refs_2_ = f32[8,16,512]{2,1,0:T(8,128)S(1)} all-to-all(f32[8,16,512]{2,1,0:T(8,128)S(1)} %get-tuple-element.8), channel_id=1, replica_groups=mesh['y'=4,'x'=4,'core'=2,'z'=4] {'core','z'}, dimensions={0} | all-to-all | bytes 524288 | tf_op jit(solution)/shard_map/all_to_all | solution.py:192
  162.9 0.0 copy-start.1
  162.9 10.5 %copy-done.1 = bf16[64,512,512]{2,1,0:T(8,128)(2,1)S(1)} copy-done((bf16[64,512,512]{2,1,0:T(8,128)(2,1)S(1)}, bf16[64,512,512]{2,1,0:T(8,128)(2,1)}, u32[]{:S(2)}) %copy-start.1) | copy-done | bytes 33554456
  173.4 4.1 %columns.3 = f32[16,16,512]{2,1,0:T(8,128)S(1)} custom-call(s32[2,64]{1,0:T(2,128)S(1)} %get-tuple-element.6.refs_0_, s32[1]{0:T(128)} %get-tuple-element.7.refs_1_, f32[8,16,512]{2,1,0:T(8,128)S(1)} %all_to_all.30.refs_2_, bf16[64,512,512]{2,1,0:T(8,128)(2,1)S(1)} %copy-done.1), custom_call_target="tpu_custom_call" | custom-call | tf_op jit(solution)/shard_map/columns/pallas_call | solution.py:179
  177.5 26.8 %all_to_all.31.refs_2_ = f32[16,16,512]{2,1,0:T(8,128)S(1)} all-to-all(f32[16,16,512]{2,1,0:T(8,128)S(1)} %columns.3), channel_id=1, replica_groups=mesh['y'=4,'x'=4,'core'=2,'z'=4] {'y','x'}, dimensions={0} | all-to-all | bytes 1048576 | tf_op jit(solution)/shard_map/all_to_all | solution.py:194
  204.3 5.1 %rows.2 = f32[8,16,512]{2,1,0:T(8,128)S(1)} custom-call(s32[2,64]{1,0:T(2,128)S(1)} %get-tuple-element.6.refs_0_, s32[1]{0:T(128)} %get-tuple-element.7.refs_1_, f32[16,16,512]{2,1,0:T(8,128)S(1)} %all_to_all.31.refs_2_, bf16[64,512,512]{2,1,0:T(8,128)(2,1)S(1)} %copy-done.1), custom_call_target="tpu_custom_call" | custom-call | tf_op jit(solution)/shard_map/rows/pallas_call | solution.py:179
  209.4 11.9 %all_to_all.32.refs_2_ = f32[8,16,512]{2,1,0:T(8,128)S(1)} all-to-all(f32[8,16,512]{2,1,0:T(8,128)S(1)} %rows.2), channel_id=1, replica_groups=mesh['y'=4,'x'=4,'core'=2,'z'=4] {'core','z'}, dimensions={0} | all-to-all | bytes 524288 | tf_op jit(solution)/shard_map/all_to_all | solution.py:192
  221.4 4.1 %columns.4 = f32[16,16,512]{2,1,0:T(8,128)S(1)} custom-call(s32[2,64]{1,0:T(2,128)S(1)} %get-tuple-element.6.refs_0_, s32[1]{0:T(128)} %get-tuple-element.7.refs_1_, f32[8,16,512]{2,1,0:T(8,128)S(1)} %all_to_all.32.refs_2_, bf16[64,512,512]{2,1,0:T(8,128)(2,1)S(1)} %copy-done.1), custom_call_target="tpu_custom_call" | custom-call | tf_op jit(solution)/shard_map/columns/pallas_call | solution.py:179
  225.5 19.4 %all_to_all.33.refs_2_ = f32[16,16,512]{2,1,0:T(8,128)S(1)} all-to-all(f32[16,16,512]{2,1,0:T(8,128)S(1)} %columns.4), channel_id=1, replica_groups=mesh['y'=4,'x'=4,'core'=2,'z'=4] {'y','x'}, dimensions={0} | all-to-all | bytes 1048576 | tf_op jit(solution)/shard_map/all_to_all | solution.py:194
  244.9 5.1 %rows.3 = f32[8,16,512]{2,1,0:T(8,128)S(1)} custom-call(s32[2,64]{1,0:T(2,128)S(1)} %get-tuple-element.6.refs_0_, s32[1]{0:T(128)} %get-tuple-element.7.refs_1_, f32[16,16,512]{2,1,0:T(8,128)S(1)} %all_to_all.33.refs_2_, bf16[64,512,512]{2,1,0:T(8,128)(2,1)S(1)} %copy-done.1), custom_call_target="tpu_custom_call" | custom-call | tf_op jit(solution)/shard_map/rows/pallas_call | solution.py:179
  250.0 11.9 %all_to_all.34.refs_2_ = f32[8,16,512]{2,1,0:T(8,128)S(1)} all-to-all(f32[8,16,512]{2,1,0:T(8,128)S(1)} %rows.3), channel_id=1, replica_groups=mesh['y'=4,'x'=4,'core'=2,'z'=4] {'core','z'}, dimensions={0} | all-to-all | bytes 524288 | tf_op jit(solution)/shard_map/all_to_all | solution.py:192
  261.9 4.9 %columns.5 = f32[16,16,512]{2,1,0:T(8,128)} custom-call(s32[2,64]{1,0:T(2,128)S(1)} %get-tuple-element.6.refs_0_, s32[1]{0:T(128)} %get-tuple-element.7.refs_1_, f32[8,16,512]{2,1,0:T(8,128)S(1)} %all_to_all.34.refs_2_, bf16[64,512,512]{2,1,0:T(8,128)(2,1)S(1)} %copy-done.1), custom_call_target="tpu_custom_call" | custom-call | tf_op jit(solution)/shard_map/columns/pallas_call | solution.py:179
  266.8 6.5 %all-to-all-start.5 = ((f32[16,16,512]{2,1,0:T(8,128)}), f32[16,16,512]{2,1,0:T(8,128)S(1)}, u32[]{:S(2)}, u32[]{:S(2)}) async-start(f32[16,16,512]{2,1,0:T(8,128)} %columns.5), calls=%async_computation.5 | async-start | bytes 1048576 | tf_op jit(solution)/shard_map/all_to_all | solution.py:194
  273.4 0.6 copy.7
  274.0 12.4 %all-to-all-done.5 = f32[16,16,512]{2,1,0:T(8,128)S(1)} async-done(((f32[16,16,512]{2,1,0:T(8,128)}), f32[16,16,512]{2,1,0:T(8,128)S(1)}, u32[]{:S(2)}, u32[]{:S(2)}) %all-to-all-start.5) | async-done | bytes 524320 | tf_op jit(solution)/shard_map/all_to_all | solution.py:194
  286.4 0.1 dynamic-slice_reduce_fusion.1
  286.5 0.6 divide_log_fusion
  (5 shorter events, 0.0 us)
Async XLA Ops:
  7.2 95.3 %all-gather.2.cloned.1.call-start = ((), (), s32[]{:S(2)}) async-start(), calls=%async_computation.6 | async-start | bytes 13369344 | tf_op jit(solution)/shard_map/all_gather | solution.py:145
  7.9 11.0 %collective-permute-start.1 = (bf16[4096,768]{1,0:T(8,128)(2,1)}, bf16[4096,768]{1,0:T(8,128)(2,1)}, u32[]{:S(2)}, u32[]{:S(2)}) collective-permute-start(bf16[4096,768]{1,0:T(8,128)(2,1)} %refs_1_.1), channel_id=1, source_target_pairs={{0,4},{4,0},{1,5},{5,1},{2,6},{6,2},{3,7},{7,3},{8,12},{12,8},{9,1... | collective-permute-start | bytes 18874376 | tf_op jit(solution)/shard_map/ppermute | solution.py:146
  9.4 8.7 %collective-permute-start = (s32[1,128]{1,0:T(1,128)S(1)}, s32[1,128]{1,0:T(1,128)S(1)}, u32[]{:S(2)}, u32[]{:S(2)}) collective-permute-start(s32[1,128]{1,0:T(1,128)S(1)} %bitcast_add_fusion), channel_id=1, source_target_pairs={{0,4},{4,0},{1,5},{5,1},{2,6},{6,2},{3,7},{7,3},{8,12},{12,8},{9,1... | collective-permute-start | bytes 1544 | tf_op jit(solution)/shard_map/ppermute | solution.py:151
  124.2 11.1 %copy-start = (bf16[64,512,512]{2,1,0:T(8,128)(2,1)}, bf16[64,512,512]{2,1,0:T(8,128)(2,1)S(1)}, u32[]{:S(2)}) copy-start(bf16[64,512,512]{2,1,0:T(8,128)(2,1)S(1)} %get-tuple-element.9.refs_3_) | copy-start | bytes 100663296
  162.9 10.5 %copy-start.1 = (bf16[64,512,512]{2,1,0:T(8,128)(2,1)S(1)}, bf16[64,512,512]{2,1,0:T(8,128)(2,1)}, u32[]{:S(2)}) copy-start(bf16[64,512,512]{2,1,0:T(8,128)(2,1)} %copy-done) | copy-start | bytes 100663296
  266.8 19.6 %all-to-all-start.5 = ((f32[16,16,512]{2,1,0:T(8,128)}), f32[16,16,512]{2,1,0:T(8,128)S(1)}, u32[]{:S(2)}, u32[]{:S(2)}) async-start(f32[16,16,512]{2,1,0:T(8,128)} %columns.5), calls=%async_computation.5 | async-start | bytes 1048576 | tf_op jit(solution)/shard_map/all_to_all | solution.py:194
Sparse Core Ops, SparseCore 0:
  10.1 92.3 all-gather.1

commit v2 on v1

v2 whole, which is shorter than its diff:
```python
import math

import jax
import jax.numpy as jnp
from jax import lax
from jax.experimental import pallas as pl
from jax.experimental.pallas import tpu as pltpu
from jax.sharding import PartitionSpec as P

TILE = 512
ABLK = 8
ITERS = 3
NY, NX, NC, NZ = 4, 4, 2, 4
NCHIP = NY * NX
SLOTS = 32
CAP = NC * SLOTS
F32 = jnp.float32
BF16 = jnp.bfloat16
VM = pl.BlockSpec(memory_space=pltpu.VMEM)
SM = pl.BlockSpec(memory_space=pltpu.SMEM)
HB = pl.BlockSpec(memory_space=pltpu.HBM)


ORDER = (
    ((0, 0),),
    ((3, 0), (1, 0), (0, 3), (0, 1)),
    ((2, 0), (3, 3), (1, 3), (3, 1), (1, 1), (0, 2)),
    ((2, 3), (2, 1), (3, 2), (1, 2), (2, 2)),
)


def plan_kernel(lists, place, table, pairs, bounds, tally):
    core, my_y, my_x = place[0], place[1], place[2]
    for k in range(NCHIP + 1):
        tally[k] = 0

    def scan(body):
        for which in range(NC):
            live = lists[which, 2 * SLOTS]

            def step(s, carry, which=which):
                b = lists[which, SLOTS + s]

                @pl.when((b % NC) == core)
                def _():
                    chip = b // NC
                    dy = (chip // NX - my_y + NY) % NY
                    dx = (chip % NX - my_x + NX) % NX
                    code = jnp.where(core == 0, dx * NY + dy, dy * NX + dx)
                    body(which * ABLK + lists[which, s], chip, table[code])

                return carry

            lax.fori_loop(0, jnp.minimum(live, SLOTS), step, 0)

    def count(a, chip, rank):
        tally[rank + 1] = tally[rank + 1] + 1

    scan(count)
    for k in range(NCHIP):
        tally[k + 1] = tally[k + 1] + tally[k]
    for k in range(NCHIP + 1):
        bounds[k] = tally[k]

    def put(a, chip, rank):
        spot = tally[rank]
        pairs[0, spot] = a
        pairs[1, spot] = chip
        pairs[2, spot] = rank
        tally[rank] = spot + 1

    scan(put)


def alloc_kernel(pairs, bounds, place, store):
    pass


def build_kernel(scale, first, blocks, last, pairs, bounds, place, a_mine, a_other, *refs):
    b_refs, (_, kv_in, store, out), (kv, abuf, bbuf, sems) = refs[:blocks], refs[blocks : blocks + 4], refs[blocks + 4 :]
    core = place[0]
    low, high = bounds[first], bounds[first + blocks]
    kv[...] = kv_in[...]

    def fetch(t, slot):
        a = pairs[0, t]
        row = pl.multiple_of((a % ABLK) * TILE, TILE)

        @pl.when(a // ABLK == core)
        def _():
            pltpu.make_async_copy(a_mine.at[pl.ds(row, TILE)], abuf.at[slot], sems.at[0, slot]).start()

        @pl.when(a // ABLK != core)
        def _():
            pltpu.make_async_copy(a_other.at[pl.ds(row, TILE)], abuf.at[slot], sems.at[0, slot]).start()

        for k in range(blocks):

            @pl.when(pairs[2, t] == first + k)
            def _():
                pltpu.make_async_copy(b_refs[k], bbuf.at[slot], sems.at[1, slot]).start()

    @pl.when(high > low)
    def _():
        fetch(low, 0)

    def step(t, carry):
        slot = (t - low) % 2

        @pl.when(t + 1 < high)
        def _():
            fetch(t + 1, 1 - slot)

        pltpu.make_async_copy(a_mine.at[pl.ds(0, TILE)], abuf.at[slot], sems.at[0, slot]).wait()
        pltpu.make_async_copy(b_refs[0], bbuf.at[slot], sems.at[1, slot]).wait()
        a = pairs[0, t]
        ones = jnp.ones((16, TILE), BF16)
        rows = 256
        for r in range(0, TILE, rows):
            score = lax.dot_general(
                abuf[slot, pl.ds(r, rows), :], bbuf[slot], (((1,), (1,)), ((), ())), preferred_element_type=F32
            )
            tile = jnp.exp(score * scale).astype(BF16)
            store[t, pl.ds(r, rows), :] = tile
            part = lax.dot_general(ones, tile, (((1,), (1,)), ((), ())), preferred_element_type=F32)
            kv[pl.ds(a, 1), pl.ds(r, rows)] += part[0:1]
        return carry

    lax.fori_loop(low, high, step, 0)
    if last:
        spread(out, kv[...])
    else:
        out[...] = kv[...]


def spread(out, value):
    for k in range(out.shape[0]):
        out[k] = value


def pass_kernel(over_rows, pairs, bounds, place, parts, store, out, _, sums, weight):
    weight[...] = (1.0 / (1.0 + jnp.sum(parts[...], axis=0))).astype(BF16).astype(F32)
    sums[...] = jnp.zeros_like(sums)

    def step(t, carry):
        a = pairs[0, t]
        b = pairs[1, t]
        source, target = (b, a) if over_rows else (a, b)
        row = jnp.broadcast_to(weight[pl.ds(source, 1), :], (16, TILE)).astype(BF16)
        dims = (((1,), (1,)), ((), ())) if over_rows else (((1,), (0,)), ((), ()))
        part = lax.dot_general(row, store[t], dims, preferred_element_type=F32)
        sums[pl.ds(target, 1), :] += part[0:1]
        return carry

    lax.fori_loop(0, bounds[NCHIP], step, 0)
    spread(out, sums[...])


def params(mib=16):
    return pltpu.CompilerParams(vmem_limit_bytes=mib << 20)


def moves(first, shift):
    pairs = []
    for y in range(NY):
        for x in range(NX):
            for c in range(NC):
                dy, dx = (0, shift) if (c == 0) == first else (shift, 0)
                there = ((y + dy) % NY * NX + (x + dx) % NX) * NC + c
                pairs.append(((y * NX + x) * NC + c, there))
    return pairs


def gather_groups(own):
    def go(block, first, shift):
        moved = lax.ppermute(block, ("y", "x", "core"), moves(first, shift))
        return pltpu.with_memory_space_constraint(moved, pltpu.HBM)

    left, right = go(own, True, 1), go(own, True, -1)
    down, up = go(own, False, 1), go(own, False, -1)
    left_down, left_up = go(left, False, 1), go(left, False, -1)
    right_down, right_up = go(right, False, 1), go(right, False, -1)
    first_two, second_two = go(left, True, 1), go(down, False, 1)
    two_down, two_up = go(first_two, False, 1), go(first_two, False, -1)
    left_two, right_two, both_two = go(left_up, False, -1), go(right_down, False, 1), go(two_up, False, -1)
    return (
        (own,),
        (left, right, down, up),
        (first_two, left_down, right_down, left_up, right_up, second_two),
        (two_down, two_up, left_two, right_two, both_two),
    )


def on_device(table_a, table_b, pair_a, pair_b, pair_count):
    width = table_a.shape[1]
    scale = 2.5 / math.sqrt(width)
    core = lax.axis_index("core")
    swap = [(0, 1), (1, 0)]
    own = jnp.concatenate(
        [pair_a.reshape(1, -1), pair_b.reshape(1, -1), pair_count.reshape(1, 1), jnp.zeros((1, 63), jnp.int32)], axis=1
    )
    other = lax.ppermute(own, "core", swap)
    a_other = lax.ppermute(table_a, "core", swap)
    lists = jnp.where(core == 0, jnp.concatenate([own, other]), jnp.concatenate([other, own]))
    place = jnp.stack([core, lax.axis_index("y"), lax.axis_index("x")]).astype(jnp.int32)
    table = [0] * NCHIP
    for rank, (f, s) in enumerate(sum(ORDER, ())):
        table[f * NY + s] = rank
    groups = gather_groups(table_b)

    pairs, bounds = pl.pallas_call(
        plan_kernel,
        out_shape=(jax.ShapeDtypeStruct((3, CAP), jnp.int32), jax.ShapeDtypeStruct((NCHIP + 1,), jnp.int32)),
        in_specs=[SM, SM, SM],
        out_specs=(SM, SM),
        scratch_shapes=[pltpu.SMEM((NCHIP + 1,), jnp.int32)],
        compiler_params=params(1),
        name="plan",
    )(lists, place, jnp.array(table, jnp.int32))

    store = pl.pallas_call(
        alloc_kernel,
        out_shape=pltpu.VMEM((CAP, TILE, TILE), BF16),
        in_specs=[SM, SM, SM],
        out_specs=VM,
        compiler_params=params(),
        name="alloc",
    )(pairs, bounds, place)
    kv = jnp.zeros((NC * ABLK, TILE), F32)
    first = 0
    for group in groups:
        blocks = len(group)
        last = first + blocks == NCHIP
        shape = (NC * NZ, NC * ABLK, TILE) if last else (NC * ABLK, TILE)
        share = 2 * blocks
        store, kv = pl.pallas_call(
            lambda *refs, first=first, blocks=blocks, last=last: build_kernel(scale, first, blocks, last, *refs),
            out_shape=(pltpu.VMEM((CAP, TILE, TILE), BF16), jax.ShapeDtypeStruct(shape, F32)),
            in_specs=[SM, SM, SM] + [HB] * (2 + blocks) + [VM, VM],
            out_specs=(VM, VM),
            scratch_shapes=[
                pltpu.VMEM((NC * ABLK, TILE), F32),
                pltpu.VMEM((2, TILE, width), BF16),
                pltpu.VMEM((2, TILE, width), BF16),
                pltpu.SemaphoreType.DMA((2, 2)),
            ],
            input_output_aliases={5 + blocks: 0},
            cost_estimate=pl.CostEstimate(
                flops=share * 2 * TILE * TILE * width,
                transcendentals=share * TILE * TILE,
                bytes_accessed=share * 2 * TILE * width * 2,
            ),
            compiler_params=params(),
            name="build",
        )(pairs, bounds, place, table_a, a_other, *group, store, kv)
        first += blocks
    def half(over_rows, parts, copies, name, store):
        return pl.pallas_call(
            lambda *refs: pass_kernel(over_rows, *refs),
            out_shape=(jax.ShapeDtypeStruct((copies, NCHIP, TILE), F32), pltpu.VMEM((CAP, TILE, TILE), BF16)),
            in_specs=[SM, SM, SM, VM, VM],
            out_specs=(VM, VM),
            input_output_aliases={4: 1},
            scratch_shapes=[pltpu.VMEM((NCHIP, TILE), F32), pltpu.VMEM((NCHIP, TILE), F32)],
            compiler_params=params(),
            name=name,
        )(pairs, bounds, place, parts, store)

    for step in range(ITERS):
        if step:
            kv, store = half(True, ktu_parts, NC * NZ, "rows", store)
        kv_parts = lax.all_to_all(kv, ("core", "z"), 0, 0, tiled=True)
        ktu, store = half(False, kv_parts, NCHIP, "columns", store)
        ktu_parts = lax.all_to_all(ktu, ("y", "x"), 0, 0, tiled=True)
    mine = lax.axis_index("y") * NX + lax.axis_index("x")
    u_sum = lax.dynamic_slice_in_dim(kv_parts, core * ABLK, ABLK, 1)
    v_sum = lax.dynamic_slice_in_dim(ktu_parts, mine, 1, 1)

    def final(parts):
        return jnp.log(1.0 / (1.0 + jnp.sum(parts, axis=0))).reshape(-1)

    return final(u_sum), final(v_sum)


def solution(mesh):
    fine = jax.sharding.Mesh(mesh.devices.reshape(NY, NX, NC, NZ), ("y", "x", "core", "z"))
    a_axes = ("y", "x", "core")
    b_axes = ("z", "y", "x", "core")
    in_specs = (P(a_axes, None), P(b_axes, None), P(a_axes, "z", None), P(a_axes, "z", None), P(a_axes, "z"))
    out_specs = (P(a_axes), P(b_axes))
    return jax.shard_map(on_device, mesh=fine, in_specs=in_specs, out_specs=out_specs, check_vma=False)
```

time: 300 us -> 224 us (0.75); the launches traced: 294 us -> 224 us
  waiting for transfers between devices: 105 us -> 42 us
  starting transfers between devices: 7.17 us -> 40.3 us
  local copies, waits for them, and re-layouts: 22.2 us -> 3.06 us
  between operations: 14.8 us -> 1.58 us
  blocking collectives: 97.6 us -> 92.6 us
  Pallas kernels: 45 us -> 41.8 us
    all_gather x1 -> x0, waiting for transfers between devices: 83.6 us -> none  [on_device(): b_all = lax.all_gather(table_b, ('y', 'x'), axis=0, tiled=True)]
    ppermute x0 -> x15, starting transfers between devices: none -> 29.7 us  [go(): moved = lax.ppermute(block, ('y', 'x', 'core'), moves(first, shift))]
    ppermute x0 -> x15, waiting for transfers between devices: none -> 27.6 us  [go(): moved = lax.ppermute(block, ('y', 'x', 'core'), moves(first, shift))]
    unnamed x5 -> x27, local copies, waits for them, and re-layouts: 22.2 us -> 3.06 us
    all_to_all x3, blocking collectives: 51.4 us -> 37.6 us  [on_device(): kv_parts = lax.all_to_all(kv, ('core', 'z'), 0, 0, tiled=True)]
    all_to_all x2, blocking collectives: 46.2 us -> 55 us  [on_device(): ktu_parts = lax.all_to_all(ktu, ('y', 'x'), 0, 0, tiled=True)]
    ppermute x1, waiting for transfers between devices: 8.17 us -> 3.69 us  [on_device(): other = lax.ppermute(own, 'core', swap)]
    all_to_all x1, starting transfers between devices: 6.53 us -> 10.5 us  [on_device(): ktu_parts = lax.all_to_all(ktu, ('y', 'x'), 0, 0, tiled=True)]
  transfers between devices with their start and end apart: 4 -> 18, of which waited for: 3 -> 6; matrix products, arithmetic and copies ran while one was open for 1% -> 1% of each run, Pallas kernels for 0% -> 10%
where the time goes in v2:
time: 224 us
  blocking collectives  92.6 us (41%)
  waiting for transfers between devices  42 us (19%)
  Pallas kernels  41.8 us (19%)
  starting transfers between devices  40.3 us (18%)
  local copies, waits for them, and re-layouts  3.06 us (1%)
  other arithmetic  2.33 us (1%)
    all_to_all x2, blocking collectives, on_device(): ktu_parts = lax.all_to_all(ktu, ('y', 'x'), 0, 0, tiled=True)  55 us
    all_to_all x3, blocking collectives, on_device(): kv_parts = lax.all_to_all(kv, ('core', 'z'), 0, 0, tiled=True)  37.6 us
    ppermute x15, starting transfers between devices, go(): moved = lax.ppermute(block, ('y', 'x', 'core'), moves(first, shift))  29.7 us
    ppermute x15, waiting for transfers between devices, go(): moved = lax.ppermute(block, ('y', 'x', 'core'), moves(first, shift))  27.6 us
    pallas_call x4, Pallas kernels, on_device(): pl.pallas_call(lambda *refs, first=first, blocks=blocks, last=last: build...  21.4 us
    pallas_call x5, Pallas kernels, half(): pl.pallas_call(lambda *refs: pass_kernel(over_rows, *refs), out_shape=(ja...  17 us
    all_to_all x1, waiting for transfers between devices, on_device(): ktu_parts = lax.all_to_all(ktu, ('y', 'x'), 0, 0, tiled=True)  10.8 us
    all_to_all x1, starting transfers between devices, on_device(): ktu_parts = lax.all_to_all(ktu, ('y', 'x'), 0, 0, tiled=True)  10.5 us
  transfers between devices with their start and end apart: 18, of which 6 were waited for; matrix products, arithmetic and copies ran while one was open for 1% of the time, Pallas kernels for 10%

profile of v2, /device:TPU:0, one launch (start us, length us, event | category | flops | bytes accessed | tf_op | source)
XLA Modules:
  0.0 223.6 jit_solution(14049139803506023049)
XLA Ops:
  0.6 0.1 collective-permute-start.1
  0.7 1.6 collective-permute-start.2
  2.4 1.7 collective-permute-start.8
  4.0 1.7 collective-permute-start.14
  6.4 0.8 pad_add_fusion
  7.1 3.7 %collective-permute-done = s32[1,128]{1,0:T(1,128)S(1)} collective-permute-done((s32[1,128]{1,0:T(1,128)S(1)}, s32[1,128]{1,0:T(1,128)S(1)}, u32[]{:S(2)}, u32[]{:S(2)}) %collective-permute-start) | collective-permute-done | bytes 544 | tf_op jit(solution)/shard_map/ppermute | solution.py:202
  10.8 3.1 %collective-permute-start.16 = (bf16[512,768]{1,0:T(8,128)(2,1)}, bf16[512,768]{1,0:T(8,128)(2,1)S(1)}, u32[]{:S(2)}, u32[]{:S(2)}) collective-permute-start(bf16[512,768]{1,0:T(8,128)(2,1)} %refs_5_.1), channel_id=1, source_target_pairs={{0,96},{4,28},{8,104},{12,4},{16,112},{20,12},{24,120},{28,20},{32... | collective-permute-start | bytes 2359304 | tf_op jit(solution)/shard_map/ppermute | solution.py:176
  13.9 6.4 %collective-permute-done.2.refs_5_ = bf16[512,768]{1,0:T(8,128)(2,1)S(1)} collective-permute-done((bf16[512,768]{1,0:T(8,128)(2,1)}, bf16[512,768]{1,0:T(8,128)(2,1)S(1)}, u32[]{:S(2)}, u32[]{:S(2)}) %collective-permute-start.2) | collective-permute-done | bytes 786464 | tf_op jit(solution)/shard_map/ppermute | solution.py:176
  20.3 0.4 collective-permute-start.3
  20.8 4.4 %collective-permute-start.6 = (bf16[512,768]{1,0:T(8,128)(2,1)S(1)}, bf16[512,768]{1,0:T(8,128)(2,1)S(1)}, u32[]{:S(2)}, u32[]{:S(2)}) collective-permute-start(bf16[512,768]{1,0:T(8,128)(2,1)S(1)} %collective-permute-done.2.refs_5_), channel_id=1, source_target_pairs={{0,96},{4,28},{8,104},{12,4},{16,112},{20,12},{24,120},{28,20},{32... | collective-permute-start | bytes 2359304 | tf_op jit(solution)/shard_map/ppermute | solution.py:176
  25.2 0.6 collective-permute-start.9
  25.7 15.1 %collective-permute-done.3.refs_5_ = bf16[512,768]{1,0:T(8,128)(2,1)} collective-permute-done((bf16[512,768]{1,0:T(8,128)(2,1)S(1)}, bf16[512,768]{1,0:T(8,128)(2,1)}, u32[]{:S(2)}, u32[]{:S(2)}) %collective-permute-start.3) | collective-permute-done | bytes 786464 | tf_op jit(solution)/shard_map/ppermute | solution.py:176
  40.8 5.7 %collective-permute-start.13 = (bf16[512,768]{1,0:T(8,128)(2,1)S(1)}, bf16[512,768]{1,0:T(8,128)(2,1)}, u32[]{:S(2)}, u32[]{:S(2)}) collective-permute-start(bf16[512,768]{1,0:T(8,128)(2,1)S(1)} %collective-permute-done.8.refs_6_), channel_id=1, source_target_pairs={{0,96},{4,28},{8,104},{12,4},{16,112},{20,12},{24,120},{28,20},{32... | collective-permute-start | bytes 2359304 | tf_op jit(solution)/shard_map/ppermute | solution.py:176
  46.5 0.8 collective-permute-start.5
  47.3 0.1 copy-done.5
  47.4 1.2 collective-permute-start.15
  48.7 0.8 add_select_fusion.lists
  49.5 0.7 copy-done.1
  50.2 2.9 %plan.1 = (s32[3,64]{1,0:T(4,128)S(1)}, s32[17]{0:T(128)S(1)}) custom-call(s32[2,128]{1,0:T(2,128)S(1)} %add_select_fusion.lists, s32[3]{0:T(128)S(1)} %pad_add_fusion.1.place.refs_2_, s32[16]{0:T(128)S(1)} %copy-done.1), custom_call_target="tpu_custom_call" | custom-call | tf_op jit(solution)/shard_map/plan/pallas_call | solution.py:211
  53.0 0.6 alloc.1.refs_6_
  53.6 1.1 collective-permute-start.4
  54.7 1.3 collective-permute-done.13.refs_9_
  56.0 3.8 %collective-permute-start.7 = (bf16[512,768]{1,0:T(8,128)(2,1)S(1)}, bf16[512,768]{1,0:T(8,128)(2,1)S(1)}, u32[]{:S(2)}, u32[]{:S(2)}) collective-permute-start(bf16[512,768]{1,0:T(8,128)(2,1)S(1)} %copy-done.6), channel_id=1, source_target_pairs={{0,96},{4,28},{8,104},{12,4},{16,112},{20,12},{24,120},{28,20},{32... | collective-permute-start | bytes 2359304 | tf_op jit(solution)/shard_map/ppermute | solution.py:176
  59.8 4.7 %collective-permute-done.5.refs_6_ = bf16[512,768]{1,0:T(8,128)(2,1)} collective-permute-done((bf16[512,768]{1,0:T(8,128)(2,1)}, bf16[512,768]{1,0:T(8,128)(2,1)}, u32[]{:S(2)}, u32[]{:S(2)}) %collective-permute-start.5) | collective-permute-done | bytes 786464 | tf_op jit(solution)/shard_map/ppermute | solution.py:176
  64.5 1.1 collective-permute-start.10
  65.7 2.6 %collective-permute-start.11 = (bf16[512,768]{1,0:T(8,128)(2,1)}, bf16[512,768]{1,0:T(8,128)(2,1)S(1)}, u32[]{:S(2)}, u32[]{:S(2)}) collective-permute-start(bf16[512,768]{1,0:T(8,128)(2,1)} %collective-permute-done.5.refs_6_), channel_id=1, source_target_pairs={{0,96},{4,28},{8,104},{12,4},{16,112},{20,12},{24,120},{28,20},{32... | collective-permute-start | bytes 2359304 | tf_op jit(solution)/shard_map/ppermute | solution.py:176
  68.3 2.8 %build.4 = (bf16[64,512,512]{2,1,0:T(8,128)(2,1)S(1)}, f32[16,512]{1,0:T(8,128)S(1)}) custom-call(s32[3,64]{1,0:T(4,128)S(1)} %get-tuple-element.21.pairs.refs_0_, s32[17]{0:T(128)S(1)} %get-tuple-element.22.bounds.refs_1_, s32[3]{0:T(128)S(1)} %pad_add_fusion.1.place.refs_2_, bf16[4096,768]{1,0:T(8,128)(2,1)} %refs_3_.7, ...), custom_call_target="tpu_custom_call", output_to_operand_aliasing={{0}: (6, {})} | custom-call | flops 805306368 | bytes 3145728 | tf_op jit(solution)/shard_map/build/pallas_call | solution.py:236
  71.1 7.8 %build.5 = (bf16[64,512,512]{2,1,0:T(8,128)(2,1)S(1)}, f32[16,512]{1,0:T(8,128)S(1)}) custom-call(s32[3,64]{1,0:T(4,128)S(1)} %get-tuple-element.21.pairs.refs_0_, s32[17]{0:T(128)S(1)} %get-tuple-element.22.bounds.refs_1_, s32[3]{0:T(128)S(1)} %pad_add_fusion.1.place.refs_2_, bf16[4096,768]{1,0:T(8,128)(2,1)} %refs_3_.7, ...), custom_call_target="tpu_custom_call", output_to_operand_aliasing={{0}: (9, {})} | custom-call | flops 3221225472 | bytes 12582912 | tf_op jit(solution)/shard_map/build/pallas_call | solution.py:236
  78.9 7.8 %build.6 = (bf16[64,512,512]{2,1,0:T(8,128)(2,1)S(1)}, f32[16,512]{1,0:T(8,128)S(1)}) custom-call(s32[3,64]{1,0:T(4,128)S(1)} %get-tuple-element.21.pairs.refs_0_, s32[17]{0:T(128)S(1)} %get-tuple-element.22.bounds.refs_1_, s32[3]{0:T(128)S(1)} %pad_add_fusion.1.place.refs_2_, bf16[4096,768]{1,0:T(8,128)(2,1)} %refs_3_.7, ...), custom_call_target="tpu_custom_call", output_to_operand_aliasing={{0}: (11, {})} | custom-call | flops 4831838208 | bytes 18874368 | tf_op jit(solution)/shard_map/build/pallas_call | solution.py:236
  86.8 0.8 copy-done.9
  87.6 0.3 copy-done.10
  87.8 0.3 copy-done.11
  88.2 0.2 copy-done.12
  88.4 3.0 %build.7 = (bf16[64,512,512]{2,1,0:T(8,128)(2,1)S(1)}, f32[8,16,512]{2,1,0:T(8,128)S(1)}) custom-call(s32[3,64]{1,0:T(4,128)S(1)} %get-tuple-element.21.pairs.refs_0_, s32[17]{0:T(128)S(1)} %get-tuple-element.22.bounds.refs_1_, s32[3]{0:T(128)S(1)} %pad_add_fusion.1.place.refs_2_, bf16[4096,768]{1,0:T(8,128)(2,1)} %refs_3_.7, ...), custom_call_target="tpu_custom_call", output_to_operand_aliasing={{0}: (10, {})} | custom-call | flops 4026531840 | bytes 15728640 | tf_op jit(solution)/shard_map/build/pallas_call | solution.py:236
  91.5 17.6 %all_to_all.30.refs_3_ = f32[8,16,512]{2,1,0:T(8,128)S(1)} all-to-all(f32[8,16,512]{2,1,0:T(8,128)S(1)} %get-tuple-element.29), channel_id=1, replica_groups=mesh['y'=4,'x'=4,'core'=2,'z'=4] {'core','z'}, dimensions={0} | all-to-all | bytes 524288 | tf_op jit(solution)/shard_map/all_to_all | solution.py:272
  109.1 2.9 %columns.3 = (f32[16,16,512]{2,1,0:T(8,128)S(1)}, bf16[64,512,512]{2,1,0:T(8,128)(2,1)S(1)}) custom-call(s32[3,64]{1,0:T(4,128)S(1)} %get-tuple-element.21.pairs.refs_0_, s32[17]{0:T(128)S(1)} %get-tuple-element.22.bounds.refs_1_, s32[3]{0:T(128)S(1)} %pad_add_fusion.1.place.refs_2_, ...), custom_call_target="tpu_custom_call", output_to_operand_aliasing={{1}: (4, {})} | custom-call | tf_op jit(solution)/shard_map/columns/pallas_call | solution.py:258
  112.0 33.2 %all_to_all.31.refs_3_ = f32[16,16,512]{2,1,0:T(8,128)S(1)} all-to-all(f32[16,16,512]{2,1,0:T(8,128)S(1)} %get-tuple-element.31), channel_id=1, replica_groups=mesh['y'=4,'x'=4,'core'=2,'z'=4] {'y','x'}, dimensions={0} | all-to-all | bytes 1048576 | tf_op jit(solution)/shard_map/all_to_all | solution.py:274
  145.2 3.7 %rows.2 = (f32[8,16,512]{2,1,0:T(8,128)S(1)}, bf16[64,512,512]{2,1,0:T(8,128)(2,1)S(1)}) custom-call(s32[3,64]{1,0:T(4,128)S(1)} %get-tuple-element.21.pairs.refs_0_, s32[17]{0:T(128)S(1)} %get-tuple-element.22.bounds.refs_1_, s32[3]{0:T(128)S(1)} %pad_add_fusion.1.place.refs_2_, ...), custom_call_target="tpu_custom_call", output_to_operand_aliasing={{1}: (4, {})} | custom-call | tf_op jit(solution)/shard_map/rows/pallas_call | solution.py:258
  149.0 10.0 %all_to_all.32.refs_3_ = f32[8,16,512]{2,1,0:T(8,128)S(1)} all-to-all(f32[8,16,512]{2,1,0:T(8,128)S(1)} %get-tuple-element.33), channel_id=1, replica_groups=mesh['y'=4,'x'=4,'core'=2,'z'=4] {'core','z'}, dimensions={0} | all-to-all | bytes 524288 | tf_op jit(solution)/shard_map/all_to_all | solution.py:272
  158.9 2.9 %columns.4 = (f32[16,16,512]{2,1,0:T(8,128)S(1)}, bf16[64,512,512]{2,1,0:T(8,128)(2,1)S(1)}) custom-call(s32[3,64]{1,0:T(4,128)S(1)} %get-tuple-element.21.pairs.refs_0_, s32[17]{0:T(128)S(1)} %get-tuple-element.22.bounds.refs_1_, s32[3]{0:T(128)S(1)} %pad_add_fusion.1.place.refs_2_, ...), custom_call_target="tpu_custom_call", output_to_operand_aliasing={{1}: (4, {})} | custom-call | tf_op jit(solution)/shard_map/columns/pallas_call | solution.py:258
  161.9 21.7 %all_to_all.33.refs_3_ = f32[16,16,512]{2,1,0:T(8,128)S(1)} all-to-all(f32[16,16,512]{2,1,0:T(8,128)S(1)} %get-tuple-element.35), channel_id=1, replica_groups=mesh['y'=4,'x'=4,'core'=2,'z'=4] {'y','x'}, dimensions={0} | all-to-all | bytes 1048576 | tf_op jit(solution)/shard_map/all_to_all | solution.py:274
  183.6 3.7 %rows.3 = (f32[8,16,512]{2,1,0:T(8,128)S(1)}, bf16[64,512,512]{2,1,0:T(8,128)(2,1)S(1)}) custom-call(s32[3,64]{1,0:T(4,128)S(1)} %get-tuple-element.21.pairs.refs_0_, s32[17]{0:T(128)S(1)} %get-tuple-element.22.bounds.refs_1_, s32[3]{0:T(128)S(1)} %pad_add_fusion.1.place.refs_2_, ...), custom_call_target="tpu_custom_call", output_to_operand_aliasing={{1}: (4, {})} | custom-call | tf_op jit(solution)/shard_map/rows/pallas_call | solution.py:258
  187.3 10.0 %all_to_all.34.refs_3_ = f32[8,16,512]{2,1,0:T(8,128)S(1)} all-to-all(f32[8,16,512]{2,1,0:T(8,128)S(1)} %get-tuple-element.37), channel_id=1, replica_groups=mesh['y'=4,'x'=4,'core'=2,'z'=4] {'core','z'}, dimensions={0} | all-to-all | bytes 524288 | tf_op jit(solution)/shard_map/all_to_all | solution.py:272
  197.3 3.7 %columns.5 = (f32[16,16,512]{2,1,0:T(8,128)}, bf16[64,512,512]{2,1,0:T(8,128)(2,1)S(1)}) custom-call(s32[3,64]{1,0:T(4,128)S(1)} %get-tuple-element.21.pairs.refs_0_, s32[17]{0:T(128)S(1)} %get-tuple-element.22.bounds.refs_1_, s32[3]{0:T(128)S(1)} %pad_add_fusion.1.place.refs_2_, ...), custom_call_target="tpu_custom_call", output_to_operand_aliasing={{1}: (4, {})} | custom-call | tf_op jit(solution)/shard_map/columns/pallas_call | solution.py:258
  201.0 10.5 %all-to-all-start.5 = ((f32[16,16,512]{2,1,0:T(8,128)}), f32[16,16,512]{2,1,0:T(8,128)S(1)}, u32[]{:S(2)}, u32[]{:S(2)}) async-start(f32[16,16,512]{2,1,0:T(8,128)} %get-tuple-element.39), calls=%async_computation.5 | async-start | bytes 1048576 | tf_op jit(solution)/shard_map/all_to_all | solution.py:274
  211.6 0.6 copy.17
  212.2 10.8 %all-to-all-done.5 = f32[16,16,512]{2,1,0:T(8,128)S(1)} async-done(((f32[16,16,512]{2,1,0:T(8,128)}), f32[16,16,512]{2,1,0:T(8,128)S(1)}, u32[]{:S(2)}, u32[]{:S(2)}) %all-to-all-start.5) | async-done | bytes 524320 | tf_op jit(solution)/shard_map/all_to_all | solution.py:274
  223.0 0.6 divide_log_fusion
  (40 shorter events, 0.3 us)
Async XLA Ops:
  0.6 67.6 %copy-start = (bf16[512,768]{1,0:T(8,128)(2,1)S(1)}, bf16[512,768]{1,0:T(8,128)(2,1)}, u32[]{:S(2)}) copy-start(bf16[512,768]{1,0:T(8,128)(2,1)} %refs_5_.1) | copy-start | bytes 2359300
  0.6 65.0 %collective-permute-start.1 = (bf16[4096,768]{1,0:T(8,128)(2,1)}, bf16[4096,768]{1,0:T(8,128)(2,1)}, u32[]{:S(2)}, u32[]{:S(2)}) collective-permute-start(bf16[4096,768]{1,0:T(8,128)(2,1)} %refs_3_.7), channel_id=1, source_target_pairs={{0,4},{4,0},{1,5},{5,1},{2,6},{6,2},{3,7},{7,3},{8,12},{12,8},{9,1... | collective-permute-start | bytes 18874376 | tf_op jit(solution)/shard_map/ppermute | solution.py:203
  0.7 19.6 %collective-permute-start.2 = (bf16[512,768]{1,0:T(8,128)(2,1)}, bf16[512,768]{1,0:T(8,128)(2,1)S(1)}, u32[]{:S(2)}, u32[]{:S(2)}) collective-permute-start(bf16[512,768]{1,0:T(8,128)(2,1)} %refs_5_.1), channel_id=1, source_target_pairs={{0,8},{4,36},{8,16},{12,44},{16,24},{20,52},{24,0},{28,60},{32,40}... | collective-permute-start | bytes 2359304 | tf_op jit(solution)/shard_map/ppermute | solution.py:176
  2.4 18.4 %collective-permute-start.8 = (bf16[512,768]{1,0:T(8,128)(2,1)}, bf16[512,768]{1,0:T(8,128)(2,1)S(1)}, u32[]{:S(2)}, u32[]{:S(2)}) collective-permute-start(bf16[512,768]{1,0:T(8,128)(2,1)} %refs_5_.1), channel_id=1, source_target_pairs={{0,24},{4,100},{8,0},{12,108},{16,8},{20,116},{24,16},{28,124},{32... | collective-permute-start | bytes 2359304 | tf_op jit(solution)/shard_map/ppermute | solution.py:176
  4.0 21.1 %collective-permute-start.14 = (bf16[512,768]{1,0:T(8,128)(2,1)}, bf16[512,768]{1,0:T(8,128)(2,1)S(1)}, u32[]{:S(2)}, u32[]{:S(2)}) collective-permute-start(bf16[512,768]{1,0:T(8,128)(2,1)} %refs_5_.1), channel_id=1, source_target_pairs={{0,32},{4,12},{8,40},{12,20},{16,48},{20,28},{24,56},{28,4},{32,64... | collective-permute-start | bytes 2359304 | tf_op jit(solution)/shard_map/ppermute | solution.py:176
  7.1 3.7 %collective-permute-start = (s32[1,128]{1,0:T(1,128)S(1)}, s32[1,128]{1,0:T(1,128)S(1)}, u32[]{:S(2)}, u32[]{:S(2)}) collective-permute-start(s32[1,128]{1,0:T(1,128)S(1)} %pad_add_fusion), channel_id=1, source_target_pairs={{0,4},{4,0},{1,5},{5,1},{2,6},{6,2},{3,7},{7,3},{8,12},{12,8},{9,1... | collective-permute-start | bytes 1544 | tf_op jit(solution)/shard_map/ppermute | solution.py:202
  10.8 14.3 %collective-permute-start.16 = (bf16[512,768]{1,0:T(8,128)(2,1)}, bf16[512,768]{1,0:T(8,128)(2,1)S(1)}, u32[]{:S(2)}, u32[]{:S(2)}) collective-permute-start(bf16[512,768]{1,0:T(8,128)(2,1)} %refs_5_.1), channel_id=1, source_target_pairs={{0,96},{4,28},{8,104},{12,4},{16,112},{20,12},{24,120},{28,20},{32... | collective-permute-start | bytes 2359304 | tf_op jit(solution)/shard_map/ppermute | solution.py:176
  20.3 50.7 %copy-start.2 = (bf16[512,768]{1,0:T(8,128)(2,1)}, bf16[512,768]{1,0:T(8,128)(2,1)S(1)}, u32[]{:S(2)}) copy-start(bf16[512,768]{1,0:T(8,128)(2,1)S(1)} %collective-permute-done.2.refs_5_) | copy-start | bytes 2359300
  20.3 20.5 %collective-permute-start.3 = (bf16[512,768]{1,0:T(8,128)(2,1)S(1)}, bf16[512,768]{1,0:T(8,128)(2,1)}, u32[]{:S(2)}, u32[]{:S(2)}) collective-permute-start(bf16[512,768]{1,0:T(8,128)(2,1)S(1)} %collective-permute-done.2.refs_5_), channel_id=1, source_target_pairs={{0,8},{4,36},{8,16},{12,44},{16,24},{20,52},{24,0},{28,60},{32,40}... | collective-permute-start | bytes 2359304 | tf_op jit(solution)/shard_map/ppermute | solution.py:176
  20.8 50.3 %copy-start.3 = (bf16[512,768]{1,0:T(8,128)(2,1)}, bf16[512,768]{1,0:T(8,128)(2,1)S(1)}, u32[]{:S(2)}) copy-start(bf16[512,768]{1,0:T(8,128)(2,1)S(1)} %collective-permute-done.8.refs_6_) | copy-start | bytes 2359300
  20.8 25.8 %collective-permute-start.6 = (bf16[512,768]{1,0:T(8,128)(2,1)S(1)}, bf16[512,768]{1,0:T(8,128)(2,1)S(1)}, u32[]{:S(2)}, u32[]{:S(2)}) collective-permute-start(bf16[512,768]{1,0:T(8,128)(2,1)S(1)} %collective-permute-done.2.refs_5_), channel_id=1, source_target_pairs={{0,96},{4,28},{8,104},{12,4},{16,112},{20,12},{24,120},{28,20},{32... | collective-permute-start | bytes 2359304 | tf_op jit(solution)/shard_map/ppermute | solution.py:176
  25.1 45.9 %copy-start.4 = (bf16[512,768]{1,0:T(8,128)(2,1)}, bf16[512,768]{1,0:T(8,128)(2,1)S(1)}, u32[]{:S(2)}) copy-start(bf16[512,768]{1,0:T(8,128)(2,1)S(1)} %collective-permute-done.14.refs_7_) | copy-start | bytes 2359300
  25.1 22.2 %collective-permute-start.12 = (bf16[512,768]{1,0:T(8,128)(2,1)S(1)}, bf16[512,768]{1,0:T(8,128)(2,1)S(1)}, u32[]{:S(2)}, u32[]{:S(2)}) collective-permute-start(bf16[512,768]{1,0:T(8,128)(2,1)S(1)} %collective-permute-done.2.refs_5_), channel_id=1, source_target_pairs={{0,32},{4,12},{8,40},{12,20},{16,48},{20,28},{24,56},{28,4},{32,64... | collective-permute-start | bytes 2359304 | tf_op jit(solution)/shard_map/ppermute | solution.py:176
  25.1 23.5 %copy-start.7 = (bf16[512,768]{1,0:T(8,128)(2,1)}, bf16[512,768]{1,0:T(8,128)(2,1)S(1)}, u32[]{:S(2)}) copy-start(bf16[512,768]{1,0:T(8,128)(2,1)S(1)} %collective-permute-done.16.refs_8_) | copy-start | bytes 2359300
  25.2 28.5 %collective-permute-start.9 = (bf16[512,768]{1,0:T(8,128)(2,1)S(1)}, bf16[512,768]{1,0:T(8,128)(2,1)}, u32[]{:S(2)}, u32[]{:S(2)}) collective-permute-start(bf16[512,768]{1,0:T(8,128)(2,1)S(1)} %collective-permute-done.8.refs_6_), channel_id=1, source_target_pairs={{0,32},{4,12},{8,40},{12,20},{16,48},{20,28},{24,56},{28,4},{32,64... | collective-permute-start | bytes 2359304 | tf_op jit(solution)/shard_map/ppermute | solution.py:176
  40.8 15.2 %collective-permute-start.13 = (bf16[512,768]{1,0:T(8,128)(2,1)S(1)}, bf16[512,768]{1,0:T(8,128)(2,1)}, u32[]{:S(2)}, u32[]{:S(2)}) collective-permute-start(bf16[512,768]{1,0:T(8,128)(2,1)S(1)} %collective-permute-done.8.refs_6_), channel_id=1, source_target_pairs={{0,96},{4,28},{8,104},{12,4},{16,112},{20,12},{24,120},{28,20},{32... | collective-permute-start | bytes 2359304 | tf_op jit(solution)/shard_map/ppermute | solution.py:176
  46.5 0.9 copy-start.5
  46.5 18.0 %collective-permute-start.5 = (bf16[512,768]{1,0:T(8,128)(2,1)}, bf16[512,768]{1,0:T(8,128)(2,1)}, u32[]{:S(2)}, u32[]{:S(2)}) collective-permute-start(bf16[512,768]{1,0:T(8,128)(2,1)} %collective-permute-done.3.refs_5_), channel_id=1, source_target_pairs={{0,96},{4,28},{8,104},{12,4},{16,112},{20,12},{24,120},{28,20},{32... | collective-permute-start | bytes 2359304 | tf_op jit(solution)/shard_map/ppermute | solution.py:176
  47.4 1.2 copy-start.8
  47.4 31.5 %collective-permute-start.15 = (bf16[512,768]{1,0:T(8,128)(2,1)S(1)}, bf16[512,768]{1,0:T(8,128)(2,1)}, u32[]{:S(2)}, u32[]{:S(2)}) collective-permute-start(bf16[512,768]{1,0:T(8,128)(2,1)S(1)} %collective-permute-done.14.refs_7_), channel_id=1, source_target_pairs={{0,32},{4,12},{8,40},{12,20},{16,48},{20,28},{24,56},{28,4},{32,64... | collective-permute-start | bytes 2359304 | tf_op jit(solution)/shard_map/ppermute | solution.py:176
  49.5 0.7 copy-start.1
  50.2 5.9 %copy-start.6 = (bf16[512,768]{1,0:T(8,128)(2,1)S(1)}, bf16[512,768]{1,0:T(8,128)(2,1)}, u32[]{:S(2)}) copy-start(bf16[512,768]{1,0:T(8,128)(2,1)} %copy-done.5) | copy-start | bytes 2359300
  53.6 33.1 %collective-permute-start.4 = (bf16[512,768]{1,0:T(8,128)(2,1)}, bf16[512,768]{1,0:T(8,128)(2,1)S(1)}, u32[]{:S(2)}, u32[]{:S(2)}) collective-permute-start(bf16[512,768]{1,0:T(8,128)(2,1)} %collective-permute-done.3.refs_5_), channel_id=1, source_target_pairs={{0,32},{4,12},{8,40},{12,20},{16,48},{20,28},{24,56},{28,4},{32,64... | collective-permute-start | bytes 2359304 | tf_op jit(solution)/shard_map/ppermute | solution.py:176
  56.0 30.7 %collective-permute-start.7 = (bf16[512,768]{1,0:T(8,128)(2,1)S(1)}, bf16[512,768]{1,0:T(8,128)(2,1)S(1)}, u32[]{:S(2)}, u32[]{:S(2)}) collective-permute-start(bf16[512,768]{1,0:T(8,128)(2,1)S(1)} %copy-done.6), channel_id=1, source_target_pairs={{0,96},{4,28},{8,104},{12,4},{16,112},{20,12},{24,120},{28,20},{32... | collective-permute-start | bytes 2359304 | tf_op jit(solution)/shard_map/ppermute | solution.py:176
  64.5 22.2 %collective-permute-start.10 = (bf16[512,768]{1,0:T(8,128)(2,1)}, bf16[512,768]{1,0:T(8,128)(2,1)S(1)}, u32[]{:S(2)}, u32[]{:S(2)}) collective-permute-start(bf16[512,768]{1,0:T(8,128)(2,1)} %collective-permute-done.9.refs_7_), channel_id=1, source_target_pairs={{0,32},{4,12},{8,40},{12,20},{16,48},{20,28},{24,56},{28,4},{32,64... | collective-permute-start | bytes 2359304 | tf_op jit(solution)/shard_map/ppermute | solution.py:176
  65.7 21.1 %collective-permute-start.11 = (bf16[512,768]{1,0:T(8,128)(2,1)}, bf16[512,768]{1,0:T(8,128)(2,1)S(1)}, u32[]{:S(2)}, u32[]{:S(2)}) collective-permute-start(bf16[512,768]{1,0:T(8,128)(2,1)} %collective-permute-done.5.refs_6_), channel_id=1, source_target_pairs={{0,96},{4,28},{8,104},{12,4},{16,112},{20,12},{24,120},{28,20},{32... | collective-permute-start | bytes 2359304 | tf_op jit(solution)/shard_map/ppermute | solution.py:176
  86.7 0.9 copy-start.9
  86.7 1.1 copy-start.10
  86.7 1.4 copy-start.11
  86.7 1.7 copy-start.12
  201.0 21.9 %all-to-all-start.5 = ((f32[16,16,512]{2,1,0:T(8,128)}), f32[16,16,512]{2,1,0:T(8,128)S(1)}, u32[]{:S(2)}, u32[]{:S(2)}) async-start(f32[16,16,512]{2,1,0:T(8,128)} %get-tuple-element.39), calls=%async_computation.5 | async-start | bytes 1048576 | tf_op jit(solution)/shard_map/all_to_all | solution.py:274

commit v3 on v2

v3 whole, which is shorter than its diff:
```python
import math

import jax
import jax.numpy as jnp
from jax import lax
from jax.experimental import pallas as pl
from jax.experimental.pallas import tpu as pltpu
from jax.sharding import PartitionSpec as P

TILE = 512
ABLK = 8
ITERS = 3
BUILD_STEP = 2
BUFFERS = 4
ROW_STEP = 4
COLUMN_STEP = 8
NY, NX, NC, NZ = 4, 4, 2, 4
NCHIP = NY * NX
SLOTS = 32
CAP = NC * SLOTS
F32 = jnp.float32
BF16 = jnp.bfloat16
VM = pl.BlockSpec(memory_space=pltpu.VMEM)
SM = pl.BlockSpec(memory_space=pltpu.SMEM)
ANY = pl.BlockSpec(memory_space=pl.ANY)
HB = pl.BlockSpec(memory_space=pltpu.HBM)


ORDER = (
    ((0, 0),),
    ((3, 0), (1, 0), (0, 3), (0, 1)),
    ((2, 0), (3, 3), (1, 3), (3, 1), (1, 1)),
    ((0, 2), (2, 3), (2, 1), (3, 2), (1, 2)),
    ((2, 2),),
)


def plan_kernel(lists, place, table, pairs, bounds, tally):
    core, my_y, my_x = place[0], place[1], place[2]
    for k in range(NCHIP + 1):
        tally[k] = 0

    def scan(body):
        for which in range(NC):
            live = lists[which, 2 * SLOTS]

            def step(s, carry, which=which):
                b = lists[which, SLOTS + s]

                @pl.when((b % NC) == core)
                def _():
                    chip = b // NC
                    dy = (chip // NX - my_y + NY) % NY
                    dx = (chip % NX - my_x + NX) % NX
                    code = jnp.where(core == 0, dx * NY + dy, dy * NX + dx)
                    body(which * ABLK + lists[which, s], chip, table[code])

                return carry

            lax.fori_loop(0, jnp.minimum(live, SLOTS), step, 0)

    def count(a, chip, rank):
        tally[rank + 1] = tally[rank + 1] + 1

    scan(count)
    for k in range(NCHIP):
        tally[k + 1] = tally[k + 1] + tally[k]
    for k in range(NCHIP + 1):
        bounds[k] = tally[k]

    def put(a, chip, rank):
        spot = tally[rank]
        pairs[0, spot] = a
        pairs[1, spot] = chip
        pairs[2, spot] = rank
        tally[rank] = spot + 1

    scan(put)


def room_kernel(pairs, bounds, place, store):
    pass


def build_kernel(scale, first, blocks, last, pairs, bounds, place, a_mine, a_other, *refs):
    b_refs, (_, kv_in, store, out), scratch = refs[:blocks], refs[blocks : blocks + 4], refs[blocks + 4 :]
    kv, abuf, bbuf, a_sems, b_sems = scratch
    core = place[0]
    low, high = bounds[first], bounds[first + blocks]
    ahead = BUFFERS - BUILD_STEP

    def fetch(t):
        @pl.when(t < high)
        def _():
            a = pairs[0, t]
            slot = (t - low) % BUFFERS
            row = pl.multiple_of((a % ABLK) * TILE, TILE)

            @pl.when(a // ABLK == core)
            def _():
                pltpu.make_async_copy(a_mine.at[pl.ds(row, TILE)], abuf.at[slot], a_sems.at[slot]).start()

            @pl.when(a // ABLK != core)
            def _():
                pltpu.make_async_copy(a_other.at[pl.ds(row, TILE)], abuf.at[slot], a_sems.at[slot]).start()

    loads = [pltpu.make_async_copy(b_refs[k], bbuf.at[k], b_sems.at[k]) for k in range(blocks)]
    for load in loads:
        load.start()
    for k in range(ahead):
        fetch(low + k)
    kv[...] = kv_in[...]
    ones = jnp.ones((16, TILE), BF16)
    for load in loads:
        load.wait()

    def step(c, carry):
        base = low + c * BUILD_STEP
        for k in range(BUILD_STEP):
            fetch(base + ahead + k)
        for k in range(BUILD_STEP):

            @pl.when(base + k < high)
            def _(k=k):
                slot = (base + k - low) % BUFFERS
                pltpu.make_async_copy(a_mine.at[pl.ds(0, TILE)], abuf.at[slot], a_sems.at[slot]).wait()

        sums = []
        for k in range(BUILD_STEP):
            t = jnp.minimum(base + k, high - 1)
            block_a, block_b = abuf[(t - low) % BUFFERS], bbuf[pairs[2, t] - first]
            score = lax.dot_general(block_a, block_b, (((1,), (1,)), ((), ())), preferred_element_type=F32)
            tile = jnp.exp(score * scale).astype(BF16)
            store[t] = tile
            part = lax.dot_general(ones, tile, (((1,), (1,)), ((), ())), preferred_element_type=F32)
            sums.append((pairs[0, t], jnp.where(base + k < high, part[0:1], 0.0)))
        for a, part in sums:
            kv[pl.ds(a, 1), :] += part
        return carry

    lax.fori_loop(0, (high - low + BUILD_STEP - 1) // BUILD_STEP, step, 0)
    if last:
        spread(out, kv[...])
    else:
        out[...] = kv[...]


def spread(out, value):
    for k in range(out.shape[0]):
        out[k] = value


def pass_kernel(over_rows, last, pairs, bounds, place, parts, store, out, *refs):
    sums, weight = refs[-2:]
    scaling = 1.0 / (1.0 + jnp.sum(parts[...], axis=0))
    weight[...] = scaling.astype(BF16).astype(F32)
    if last:
        refs[0][...] = jnp.log(jnp.where(place[0] == 0, scaling[:ABLK], scaling[ABLK:]))
    sums[...] = jnp.zeros_like(sums)
    number = bounds[NCHIP]
    size = ROW_STEP if over_rows else COLUMN_STEP
    dims = (((1,), (1,)), ((), ())) if over_rows else (((1,), (0,)), ((), ()))

    def step(c, carry):
        found = []
        for k in range(size):
            t = c * size + k
            safe = jnp.minimum(t, number - 1)
            a = pairs[0, safe]
            b = pairs[1, safe]
            source, target = (b, a) if over_rows else (a, b)
            row = jnp.where(t < number, weight[pl.ds(source, 1), :], 0.0)
            row = jnp.broadcast_to(row, (16, TILE)).astype(BF16)
            found.append((target, lax.dot_general(row, store[safe], dims, preferred_element_type=F32)))
        for target, part in found:
            sums[pl.ds(target, 1), :] += part[0:1]
        return carry

    lax.fori_loop(0, (number + size - 1) // size, step, 0)
    if last:
        out[...] = sums[...]
    else:
        spread(out, sums[...])


def params(mib=16):
    return pltpu.CompilerParams(vmem_limit_bytes=mib << 20)


def moves(first, shift):
    pairs = []
    for y in range(NY):
        for x in range(NX):
            for c in range(NC):
                dy, dx = (0, shift) if (c == 0) == first else (shift, 0)
                there = ((y + dy) % NY * NX + (x + dx) % NX) * NC + c
                pairs.append(((y * NX + x) * NC + c, there))
    return pairs


def go(block, first, shift):
    return lax.ppermute(block, ("y", "x", "core"), moves(first, shift))


def on_device(table_a, table_b, pair_a, pair_b, pair_count):
    width = table_a.shape[1]
    scale = 2.5 / math.sqrt(width)
    core = lax.axis_index("core")
    swap = [(0, 1), (1, 0)]
    own = jnp.concatenate(
        [pair_a.reshape(1, -1), pair_b.reshape(1, -1), pair_count.reshape(1, 1), jnp.zeros((1, 63), jnp.int32)], axis=1
    )
    other = lax.ppermute(own, "core", swap)
    a_other = lax.ppermute(table_a, "core", swap)
    lists = jnp.where(core == 0, jnp.concatenate([own, other]), jnp.concatenate([other, own]))
    place = jnp.stack([core, lax.axis_index("y"), lax.axis_index("x")]).astype(jnp.int32)
    table = [0] * NCHIP
    for rank, (f, s) in enumerate(sum(ORDER, ())):
        table[f * NY + s] = rank
    left, right = go(table_b, True, 1), go(table_b, True, -1)
    down, up = go(table_b, False, 1), go(table_b, False, -1)

    pairs, bounds = pl.pallas_call(
        plan_kernel,
        out_shape=(jax.ShapeDtypeStruct((3, CAP), jnp.int32), jax.ShapeDtypeStruct((NCHIP + 1,), jnp.int32)),
        in_specs=[SM, SM, SM],
        out_specs=(SM, SM),
        scratch_shapes=[pltpu.SMEM((NCHIP + 1,), jnp.int32)],
        compiler_params=params(1),
        name="plan",
    )(lists, place, jnp.array(table, jnp.int32))

    store = pl.pallas_call(
        room_kernel,
        out_shape=pltpu.VMEM((CAP, TILE, TILE), BF16),
        in_specs=[SM, SM, SM],
        out_specs=VM,
        compiler_params=params(),
        name="room",
    )(pairs, bounds, place)

    def build(first, group, store, kv):
        blocks = len(group)
        last = first + blocks == NCHIP
        shape = (NC * NZ, NC * ABLK, TILE) if last else (NC * ABLK, TILE)
        share = 2 * blocks
        return pl.pallas_call(
            lambda *refs: build_kernel(scale, first, blocks, last, *refs),
            out_shape=(pltpu.VMEM((CAP, TILE, TILE), BF16), jax.ShapeDtypeStruct(shape, F32)),
            in_specs=[SM, SM, SM, HB, HB] + [ANY] * blocks + [VM, VM],
            out_specs=(VM, VM),
            scratch_shapes=[
                pltpu.VMEM((NC * ABLK, TILE), F32),
                pltpu.VMEM((BUFFERS, TILE, width), BF16),
                pltpu.VMEM((blocks, TILE, width), BF16),
                pltpu.SemaphoreType.DMA((BUFFERS,)),
                pltpu.SemaphoreType.DMA((blocks,)),
            ],
            input_output_aliases={5 + blocks: 0},
            cost_estimate=pl.CostEstimate(
                flops=share * 2 * TILE * TILE * width,
                transcendentals=share * TILE * TILE,
                bytes_accessed=share * 2 * TILE * width * 2,
            ),
            compiler_params=params(),
            name="build",
        )(pairs, bounds, place, table_a, a_other, *group, store, kv)

    kv = jnp.zeros((NC * ABLK, TILE), F32)
    store, kv = build(0, (table_b,), store, kv)
    left, right, down, up, kv = lax.optimization_barrier((left, right, down, up, kv))
    near = (left, right, down, up)
    first_two = go(right, True, -1)
    left_down, right_down = go(left, False, 1), go(right, False, 1)
    left_up, right_up = go(left, False, -1), go(right, False, -1)
    store, kv = build(1, near, store, kv)
    middle = (first_two, left_down, right_down, left_up, right_up)
    *middle, down, kv = lax.optimization_barrier((*middle, down, kv))
    first_two, left_down, right_down, left_up, right_up = middle
    two_up, two_down = go(first_two, False, -1), go(first_two, False, 1)
    left_two, right_two, second_two = go(left_up, False, -1), go(right_down, False, 1), go(down, False, 1)
    store, kv = build(5, middle, store, kv)
    two_up, kv = lax.optimization_barrier((two_up, kv))
    both_two = go(two_up, False, -1)
    store, kv = build(10, (second_two, two_down, two_up, left_two, right_two), store, kv)
    store, kv = build(15, (both_two,), store, kv)

    def half(over_rows, parts, copies, store):
        last = copies == 0
        sums = jax.ShapeDtypeStruct((NCHIP, TILE) if last else (copies, NCHIP, TILE), F32)
        logs = jax.ShapeDtypeStruct((ABLK, TILE), F32)
        return pl.pallas_call(
            lambda *refs: pass_kernel(over_rows, last, *refs),
            out_shape=(sums, logs if last else pltpu.VMEM((CAP, TILE, TILE), BF16)),
            in_specs=[SM, SM, SM, VM, VM],
            out_specs=(VM, VM),
            scratch_shapes=[pltpu.VMEM((NCHIP, TILE), F32), pltpu.VMEM((NCHIP, TILE), F32)],
            input_output_aliases={} if last else {4: 1},
            compiler_params=params(),
            name="rows" if over_rows else "columns",
        )(pairs, bounds, place, parts, store)

    for step in range(ITERS):
        if step:
            kv, store = half(True, ktu_parts, NC * NZ, store)
        kv_parts = lax.all_to_all(kv, ("core", "z"), 0, 0, tiled=True)
        if step < ITERS - 1:
            ktu, store = half(False, kv_parts, NCHIP, store)
            ktu_parts = lax.all_to_all(ktu, ("y", "x"), 0, 0, tiled=True)
    ktu, log_u = half(False, kv_parts, 0, store)
    mine = lax.all_to_all(ktu, ("y", "x"), 0, 0, tiled=True)
    log_v = jnp.log(1.0 / (1.0 + jnp.sum(mine, axis=0)))
    return log_u.reshape(-1), log_v


def solution(mesh):
    fine = jax.sharding.Mesh(mesh.devices.reshape(NY, NX, NC, NZ), ("y", "x", "core", "z"))
    a_axes = ("y", "x", "core")
    b_axes = ("z", "y", "x", "core")
    in_specs = (P(a_axes, None), P(b_axes, None), P(a_axes, "z", None), P(a_axes, "z", None), P(a_axes, "z"))
    out_specs = (P(a_axes), P(b_axes))
    return jax.shard_map(on_device, mesh=fine, in_specs=in_specs, out_specs=out_specs, check_vma=False)
```

time: 224 us -> 196 us (0.88)
  blocking collectives: 92.6 us -> 65.4 us
  starting transfers between devices: 40.3 us -> 31.8 us
  waiting for transfers between devices: 42 us -> 45.6 us
  Pallas kernels: 41.8 us -> 45.3 us
    all_to_all x2, blocking collectives: 55 us -> 32 us  [on_device(): ktu_parts = lax.all_to_all(ktu, ('y', 'x'), 0, 0, tiled=True)]
    ppermute x15, waiting for transfers between devices: 27.6 us -> 34.8 us  [go(): return lax.ppermute(block, ('y', 'x', 'core'), moves(first, shift))]
    all_to_all x1, starting transfers between devices: 10.5 us -> 3.93 us  [on_device(): mine = lax.all_to_all(ktu, ('y', 'x'), 0, 0, tiled=True)]
    all_to_all x3, blocking collectives: 37.6 us -> 33.4 us  [on_device(): kv_parts = lax.all_to_all(kv, ('core', 'z'), 0, 0, tiled=True)]
    all_to_all x1, waiting for transfers between devices: 10.8 us -> 6.99 us  [on_device(): mine = lax.all_to_all(ktu, ('y', 'x'), 0, 0, tiled=True)]
    pallas_call x10 -> x11, Pallas kernels: 38.9 us -> 41.6 us  [the longest x5 25.2 us: build(): pl.pallas_call(lambda *refs: build_kernel(scale, first, blocks, last, *re...]
    ppermute x15, starting transfers between devices: 29.7 us -> 27.3 us  [go(): return lax.ppermute(block, ('y', 'x', 'core'), moves(first, shift))]
  transfers between devices with their start and end apart: 18 -> 18, of which waited for: 6 -> 9; matrix products, arithmetic and copies ran while one was open for 1% -> 1% of each run, Pallas kernels for 10% -> 13%
where the time goes in v3:
time: 196 us; the launch traced here: 194 us
  blocking collectives  65.4 us (33%)
  waiting for transfers between devices  45.6 us (23%)
  Pallas kernels  45.3 us (23%)
  starting transfers between devices  31.8 us (16%)
  other arithmetic  2.28 us (1%)
    ppermute x15, waiting for transfers between devices, go(): return lax.ppermute(block, ('y', 'x', 'core'), moves(first, shift))  34.8 us
    all_to_all x3, blocking collectives, on_device(): kv_parts = lax.all_to_all(kv, ('core', 'z'), 0, 0, tiled=True)  33.4 us
    all_to_all x2, blocking collectives, on_device(): ktu_parts = lax.all_to_all(ktu, ('y', 'x'), 0, 0, tiled=True)  32 us
    ppermute x15, starting transfers between devices, go(): return lax.ppermute(block, ('y', 'x', 'core'), moves(first, shift))  27.3 us
    pallas_call x5, Pallas kernels, build(): pl.pallas_call(lambda *refs: build_kernel(scale, first, blocks, last, *re...  25.2 us
    pallas_call x5, Pallas kernels, half(): pl.pallas_call(lambda *refs: pass_kernel(over_rows, last, *refs), out_sha...  15.8 us
    all_to_all x1, waiting for transfers between devices, on_device(): mine = lax.all_to_all(ktu, ('y', 'x'), 0, 0, tiled=True)  6.99 us
    all_to_all x1, starting transfers between devices, on_device(): mine = lax.all_to_all(ktu, ('y', 'x'), 0, 0, tiled=True)  3.93 us
  transfers between devices with their start and end apart: 18, of which 9 were waited for; matrix products, arithmetic and copies ran while one was open for 1% of the time, Pallas kernels for 13%

profile of v3, /device:TPU:0, one launch (start us, length us, event | category | flops | bytes accessed | tf_op | source)
XLA Modules:
  0.0 193.7 jit_solution(5468891608187236092)
XLA Ops:
  0.6 0.0 copy-start
  0.6 0.1 collective-permute-start.1
  1.4 0.8 pad_add_fusion
  2.2 0.5 collective-permute-start
  2.7 1.7 collective-permute-start.4
  4.3 2.8 %collective-permute-start.3 = (bf16[512,768]{1,0:T(8,128)(2,1)}, bf16[512,768]{1,0:T(8,128)(2,1)S(1)}, u32[]{:S(2)}, u32[]{:S(2)}) collective-permute-start(bf16[512,768]{1,0:T(8,128)(2,1)} %refs_5_.1), channel_id=1, source_target_pairs={{0,24},{4,100},{8,0},{12,108},{16,8},{20,116},{24,16},{28,124},{32... | collective-permute-start | bytes 2359304 | tf_op jit(solution)/shard_map/ppermute | solution.py:202
  7.1 3.7 %collective-permute-done = s32[1,128]{1,0:T(1,128)S(1)} collective-permute-done((s32[1,128]{1,0:T(1,128)S(1)}, s32[1,128]{1,0:T(1,128)S(1)}, u32[]{:S(2)}, u32[]{:S(2)}) %collective-permute-start) | collective-permute-done | bytes 544 | tf_op jit(solution)/shard_map/ppermute | solution.py:213
  10.8 3.1 %collective-permute-start.5 = (bf16[512,768]{1,0:T(8,128)(2,1)}, bf16[512,768]{1,0:T(8,128)(2,1)}, u32[]{:S(2)}, u32[]{:S(2)}) collective-permute-start(bf16[512,768]{1,0:T(8,128)(2,1)} %refs_5_.1), channel_id=1, source_target_pairs={{0,96},{4,28},{8,104},{12,4},{16,112},{20,12},{24,120},{28,20},{32... | collective-permute-start | bytes 2359304 | tf_op jit(solution)/shard_map/ppermute | solution.py:202
  13.9 0.1 pad_add_fusion.1.place.refs_2_
  14.0 0.8 add_select_fusion.lists
  14.8 0.7 copy-done.1
  15.5 3.7 %plan.1 = (s32[3,64]{1,0:T(4,128)S(1)}, s32[17]{0:T(128)S(1)}) custom-call(s32[2,128]{1,0:T(2,128)S(1)} %add_select_fusion.lists, s32[3]{0:T(128)S(1)} %pad_add_fusion.1.place.refs_2_, s32[16]{0:T(128)S(1)} %copy-done.1), custom_call_target="tpu_custom_call" | custom-call | tf_op jit(solution)/shard_map/plan/pallas_call | solution.py:223
  19.2 0.6 room.1.refs_6_
  19.8 3.3 %build.5 = (bf16[64,512,512]{2,1,0:T(8,128)(2,1)S(1)}, f32[16,512]{1,0:T(8,128)S(1)}) custom-call(s32[3,64]{1,0:T(4,128)S(1)} %get-tuple-element.38.pairs.refs_0_, s32[17]{0:T(128)S(1)} %get-tuple-element.39.bounds.refs_1_, s32[3]{0:T(128)S(1)} %pad_add_fusion.1.place.refs_2_, bf16[4096,768]{1,0:T(8,128)(2,1)} %refs_3_.9, ...), custom_call_target="tpu_custom_call", output_to_operand_aliasing={{0}: (6, {})} | custom-call | flops 805306368 | bytes 3145728 | tf_op jit(solution)/shard_map/build/pallas_call | solution.py:247
  23.0 0.0 collective-permute-done.4.refs_7_
  23.1 0.6 collective-permute-done.2.refs_5_
  23.6 0.7 collective-permute-done.5.refs_8_
  24.3 3.7 %collective-permute-start.9 = (bf16[512,768]{1,0:T(8,128)(2,1)S(1)}, bf16[512,768]{1,0:T(8,128)(2,1)S(1)}, u32[]{:S(2)}, u32[]{:S(2)}) collective-permute-start(bf16[512,768]{1,0:T(8,128)(2,1)S(1)} %collective-permute-done.2.refs_5_), channel_id=1, source_target_pairs={{0,96},{4,28},{8,104},{12,4},{16,112},{20,12},{24,120},{28,20},{32... | collective-permute-start | bytes 2359304 | tf_op jit(solution)/shard_map/ppermute | solution.py:202
  28.0 3.2 %collective-permute-start.10 = (bf16[512,768]{1,0:T(8,128)(2,1)S(1)}, bf16[512,768]{1,0:T(8,128)(2,1)S(1)}, u32[]{:S(2)}, u32[]{:S(2)}) collective-permute-start(bf16[512,768]{1,0:T(8,128)(2,1)S(1)} %collective-permute-done.3.refs_6_), channel_id=1, source_target_pairs={{0,96},{4,28},{8,104},{12,4},{16,112},{20,12},{24,120},{28,20},{32... | collective-permute-start | bytes 2359304 | tf_op jit(solution)/shard_map/ppermute | solution.py:202
  31.3 2.2 %collective-permute-start.6 = (bf16[512,768]{1,0:T(8,128)(2,1)S(1)}, bf16[512,768]{1,0:T(8,128)(2,1)S(1)}, u32[]{:S(2)}, u32[]{:S(2)}) collective-permute-start(bf16[512,768]{1,0:T(8,128)(2,1)S(1)} %collective-permute-done.3.refs_6_), channel_id=1, source_target_pairs={{0,24},{4,100},{8,0},{12,108},{16,8},{20,116},{24,16},{28,124},{32... | collective-permute-start | bytes 2359304 | tf_op jit(solution)/shard_map/ppermute | solution.py:202
  33.5 5.3 %build.6 = (bf16[64,512,512]{2,1,0:T(8,128)(2,1)S(1)}, f32[16,512]{1,0:T(8,128)S(1)}) custom-call(s32[3,64]{1,0:T(4,128)S(1)} %get-tuple-element.38.pairs.refs_0_, s32[17]{0:T(128)S(1)} %get-tuple-element.39.bounds.refs_1_, s32[3]{0:T(128)S(1)} %pad_add_fusion.1.place.refs_2_, bf16[4096,768]{1,0:T(8,128)(2,1)} %refs_3_.9, ...), custom_call_target="tpu_custom_call", output_to_operand_aliasing={{0}: (9, {})} | custom-call | flops 3221225472 | bytes 12582912 | tf_op jit(solution)/shard_map/build/pallas_call | solution.py:247
  38.7 3.2 %collective-permute-done.9.refs_8_ = bf16[512,768]{1,0:T(8,128)(2,1)S(1)} collective-permute-done((bf16[512,768]{1,0:T(8,128)(2,1)S(1)}, bf16[512,768]{1,0:T(8,128)(2,1)S(1)}, u32[]{:S(2)}, u32[]{:S(2)}) %collective-permute-start.9) | collective-permute-done | bytes 786464 | tf_op jit(solution)/shard_map/ppermute | solution.py:202
  42.0 12.4 %collective-permute-done.10.refs_9_ = bf16[512,768]{1,0:T(8,128)(2,1)S(1)} collective-permute-done((bf16[512,768]{1,0:T(8,128)(2,1)S(1)}, bf16[512,768]{1,0:T(8,128)(2,1)S(1)}, u32[]{:S(2)}, u32[]{:S(2)}) %collective-permute-start.10) | collective-permute-done | bytes 786464 | tf_op jit(solution)/shard_map/ppermute | solution.py:202
  54.4 3.7 %collective-permute-start.11 = (bf16[512,768]{1,0:T(8,128)(2,1)S(1)}, bf16[512,768]{1,0:T(8,128)(2,1)S(1)}, u32[]{:S(2)}, u32[]{:S(2)}) collective-permute-start(bf16[512,768]{1,0:T(8,128)(2,1)S(1)} %collective-permute-done.6.refs_5_), channel_id=1, source_target_pairs={{0,96},{4,28},{8,104},{12,4},{16,112},{20,12},{24,120},{28,20},{32... | collective-permute-start | bytes 2359304 | tf_op jit(solution)/shard_map/ppermute | solution.py:202
  58.1 1.5 collective-permute-start.16
  59.6 1.8 collective-permute-start.15
  61.4 5.2 %build.7 = (bf16[64,512,512]{2,1,0:T(8,128)(2,1)S(1)}, f32[16,512]{1,0:T(8,128)S(1)}) custom-call(s32[3,64]{1,0:T(4,128)S(1)} %get-tuple-element.38.pairs.refs_0_, s32[17]{0:T(128)S(1)} %get-tuple-element.39.bounds.refs_1_, s32[3]{0:T(128)S(1)} %pad_add_fusion.1.place.refs_2_, bf16[4096,768]{1,0:T(8,128)(2,1)} %refs_3_.9, ...), custom_call_target="tpu_custom_call", output_to_operand_aliasing={{0}: (10, {})} | custom-call | flops 4026531840 | bytes 15728640 | tf_op jit(solution)/shard_map/build/pallas_call | solution.py:247
  66.5 1.1 collective-permute-done.11.refs_7_
  67.6 3.7 %collective-permute-start.12 = (bf16[512,768]{1,0:T(8,128)(2,1)S(1)}, bf16[512,768]{1,0:T(8,128)(2,1)S(1)}, u32[]{:S(2)}, u32[]{:S(2)}) collective-permute-start(bf16[512,768]{1,0:T(8,128)(2,1)S(1)} %collective-permute-done.11.refs_7_), channel_id=1, source_target_pairs={{0,96},{4,28},{8,104},{12,4},{16,112},{20,12},{24,120},{28,20},{32... | collective-permute-start | bytes 2359304 | tf_op jit(solution)/shard_map/ppermute | solution.py:202
  71.3 8.4 %collective-permute-done.13.refs_5_ = bf16[512,768]{1,0:T(8,128)(2,1)S(1)} collective-permute-done((bf16[512,768]{1,0:T(8,128)(2,1)S(1)}, bf16[512,768]{1,0:T(8,128)(2,1)S(1)}, u32[]{:S(2)}, u32[]{:S(2)}) %collective-permute-start.13) | collective-permute-done | bytes 786464 | tf_op jit(solution)/shard_map/ppermute | solution.py:202
  79.7 8.4 %collective-permute-done.16.refs_9_ = bf16[512,768]{1,0:T(8,128)(2,1)S(1)} collective-permute-done((bf16[512,768]{1,0:T(8,128)(2,1)S(1)}, bf16[512,768]{1,0:T(8,128)(2,1)S(1)}, u32[]{:S(2)}, u32[]{:S(2)}) %collective-permute-start.16) | collective-permute-done | bytes 786464 | tf_op jit(solution)/shard_map/ppermute | solution.py:202
  88.1 8.0 %build.8 = (bf16[64,512,512]{2,1,0:T(8,128)(2,1)S(1)}, f32[16,512]{1,0:T(8,128)S(1)}) custom-call(s32[3,64]{1,0:T(4,128)S(1)} %get-tuple-element.38.pairs.refs_0_, s32[17]{0:T(128)S(1)} %get-tuple-element.39.bounds.refs_1_, s32[3]{0:T(128)S(1)} %pad_add_fusion.1.place.refs_2_, bf16[4096,768]{1,0:T(8,128)(2,1)} %refs_3_.9, ...), custom_call_target="tpu_custom_call", output_to_operand_aliasing={{0}: (10, {})} | custom-call | flops 4026531840 | bytes 15728640 | tf_op jit(solution)/shard_map/build/pallas_call | solution.py:247
  96.2 3.5 %build.9 = (bf16[64,512,512]{2,1,0:T(8,128)(2,1)S(1)}, f32[8,16,512]{2,1,0:T(8,128)S(1)}) custom-call(s32[3,64]{1,0:T(4,128)S(1)} %get-tuple-element.38.pairs.refs_0_, s32[17]{0:T(128)S(1)} %get-tuple-element.39.bounds.refs_1_, s32[3]{0:T(128)S(1)} %pad_add_fusion.1.place.refs_2_, bf16[4096,768]{1,0:T(8,128)(2,1)} %refs_3_.9, ...), custom_call_target="tpu_custom_call", output_to_operand_aliasing={{0}: (6, {})} | custom-call | flops 805306368 | bytes 3145728 | tf_op jit(solution)/shard_map/build/pallas_call | solution.py:247
  99.7 13.0 %all_to_all.34.refs_3_ = f32[8,16,512]{2,1,0:T(8,128)S(1)} all-to-all(f32[8,16,512]{2,1,0:T(8,128)S(1)} %get-tuple-element.62), channel_id=1, replica_groups=mesh['y'=4,'x'=4,'core'=2,'z'=4] {'core','z'}, dimensions={0} | all-to-all | bytes 524288 | tf_op jit(solution)/shard_map/all_to_all | solution.py:306
  112.7 2.6 %columns.3 = (f32[16,16,512]{2,1,0:T(8,128)S(1)}, bf16[64,512,512]{2,1,0:T(8,128)(2,1)S(1)}) custom-call(s32[3,64]{1,0:T(4,128)S(1)} %get-tuple-element.38.pairs.refs_0_, s32[17]{0:T(128)S(1)} %get-tuple-element.39.bounds.refs_1_, s32[3]{0:T(128)S(1)} %pad_add_fusion.1.place.refs_2_, ...), custom_call_target="tpu_custom_call", output_to_operand_aliasing={{1}: (4, {})} | custom-call | tf_op jit(solution)/shard_map/columns/pallas_call | solution.py:292
  115.4 16.1 %all_to_all.35.refs_3_ = f32[16,16,512]{2,1,0:T(8,128)S(1)} all-to-all(f32[16,16,512]{2,1,0:T(8,128)S(1)} %get-tuple-element.64), channel_id=1, replica_groups=mesh['y'=4,'x'=4,'core'=2,'z'=4] {'y','x'}, dimensions={0} | all-to-all | bytes 1048576 | tf_op jit(solution)/shard_map/all_to_all | solution.py:309
  131.5 4.0 %rows.2 = (f32[8,16,512]{2,1,0:T(8,128)S(1)}, bf16[64,512,512]{2,1,0:T(8,128)(2,1)S(1)}) custom-call(s32[3,64]{1,0:T(4,128)S(1)} %get-tuple-element.38.pairs.refs_0_, s32[17]{0:T(128)S(1)} %get-tuple-element.39.bounds.refs_1_, s32[3]{0:T(128)S(1)} %pad_add_fusion.1.place.refs_2_, ...), custom_call_target="tpu_custom_call", output_to_operand_aliasing={{1}: (4, {})} | custom-call | tf_op jit(solution)/shard_map/rows/pallas_call | solution.py:292
  135.5 9.9 %all_to_all.36.refs_3_ = f32[8,16,512]{2,1,0:T(8,128)S(1)} all-to-all(f32[8,16,512]{2,1,0:T(8,128)S(1)} %get-tuple-element.66), channel_id=1, replica_groups=mesh['y'=4,'x'=4,'core'=2,'z'=4] {'core','z'}, dimensions={0} | all-to-all | bytes 524288 | tf_op jit(solution)/shard_map/all_to_all | solution.py:306
  145.4 2.6 %columns.4 = (f32[16,16,512]{2,1,0:T(8,128)S(1)}, bf16[64,512,512]{2,1,0:T(8,128)(2,1)S(1)}) custom-call(s32[3,64]{1,0:T(4,128)S(1)} %get-tuple-element.38.pairs.refs_0_, s32[17]{0:T(128)S(1)} %get-tuple-element.39.bounds.refs_1_, s32[3]{0:T(128)S(1)} %pad_add_fusion.1.place.refs_2_, ...), custom_call_target="tpu_custom_call", output_to_operand_aliasing={{1}: (4, {})} | custom-call | tf_op jit(solution)/shard_map/columns/pallas_call | solution.py:292
  148.0 15.8 %all_to_all.37.refs_3_ = f32[16,16,512]{2,1,0:T(8,128)S(1)} all-to-all(f32[16,16,512]{2,1,0:T(8,128)S(1)} %get-tuple-element.68), channel_id=1, replica_groups=mesh['y'=4,'x'=4,'core'=2,'z'=4] {'y','x'}, dimensions={0} | all-to-all | bytes 1048576 | tf_op jit(solution)/shard_map/all_to_all | solution.py:309
  163.9 4.0 %rows.3 = (f32[8,16,512]{2,1,0:T(8,128)S(1)}, bf16[64,512,512]{2,1,0:T(8,128)(2,1)S(1)}) custom-call(s32[3,64]{1,0:T(4,128)S(1)} %get-tuple-element.38.pairs.refs_0_, s32[17]{0:T(128)S(1)} %get-tuple-element.39.bounds.refs_1_, s32[3]{0:T(128)S(1)} %pad_add_fusion.1.place.refs_2_, ...), custom_call_target="tpu_custom_call", output_to_operand_aliasing={{1}: (4, {})} | custom-call | tf_op jit(solution)/shard_map/rows/pallas_call | solution.py:292
  167.8 10.5 %all_to_all.38.refs_3_ = f32[8,16,512]{2,1,0:T(8,128)S(1)} all-to-all(f32[8,16,512]{2,1,0:T(8,128)S(1)} %get-tuple-element.70), channel_id=1, replica_groups=mesh['y'=4,'x'=4,'core'=2,'z'=4] {'core','z'}, dimensions={0} | all-to-all | bytes 524288 | tf_op jit(solution)/shard_map/all_to_all | solution.py:306
  178.3 2.6 %columns.5 = (f32[16,512]{1,0:T(8,128)S(1)}, f32[8,512]{1,0:T(8,128)S(1)}) custom-call(s32[3,64]{1,0:T(4,128)S(1)} %get-tuple-element.38.pairs.refs_0_, s32[17]{0:T(128)S(1)} %get-tuple-element.39.bounds.refs_1_, s32[3]{0:T(128)S(1)} %pad_add_fusion.1.place.refs_2_, f32[8,16,512]{2,1,0:T(8,128)S(1)} %all_to_all.38.refs_3_, ...), custom_call_target="tpu_custom_call" | custom-call | tf_op jit(solution)/shard_map/columns/pallas_call | solution.py:292
  180.9 0.7 copy.17
  181.5 3.9 %all-to-all-start.5 = ((f32[16,1,512]{2,1,0:T(1,128)}), f32[16,1,512]{2,1,0:T(1,128)S(1)}, u32[]{:S(2)}, u32[]{:S(2)}) async-start(f32[16,1,512]{2,1,0:T(1,128)} %copy.17), calls=%async_computation.5 | async-start | bytes 65536 | tf_op jit(solution)/shard_map/all_to_all | solution.py:311
  185.5 0.6 copy.18
  186.1 7.0 %all-to-all-done.5 = f32[16,1,512]{2,1,0:T(1,128)S(1)} async-done(((f32[16,1,512]{2,1,0:T(1,128)}), f32[16,1,512]{2,1,0:T(1,128)S(1)}, u32[]{:S(2)}, u32[]{:S(2)}) %all-to-all-start.5) | async-done | bytes 32800 | tf_op jit(solution)/shard_map/all_to_all | solution.py:311
  193.1 0.6 divide_log_fusion
  (18 shorter events, 0.1 us)
Async XLA Ops:
  0.6 19.1 %copy-start = (bf16[512,768]{1,0:T(8,128)(2,1)S(1)}, bf16[512,768]{1,0:T(8,128)(2,1)}, u32[]{:S(2)}) copy-start(bf16[512,768]{1,0:T(8,128)(2,1)} %refs_5_.1) | copy-start | bytes 2359300
  0.6 19.1 %collective-permute-start.1 = (bf16[4096,768]{1,0:T(8,128)(2,1)}, bf16[4096,768]{1,0:T(8,128)(2,1)}, u32[]{:S(2)}, u32[]{:S(2)}) collective-permute-start(bf16[4096,768]{1,0:T(8,128)(2,1)} %refs_3_.9), channel_id=1, source_target_pairs={{0,4},{4,0},{1,5},{5,1},{2,6},{6,2},{3,7},{7,3},{8,12},{12,8},{9,1... | collective-permute-start | bytes 18874376 | tf_op jit(solution)/shard_map/ppermute | solution.py:214
  2.2 8.6 %collective-permute-start = (s32[1,128]{1,0:T(1,128)S(1)}, s32[1,128]{1,0:T(1,128)S(1)}, u32[]{:S(2)}, u32[]{:S(2)}) collective-permute-start(s32[1,128]{1,0:T(1,128)S(1)} %pad_add_fusion), channel_id=1, source_target_pairs={{0,4},{4,0},{1,5},{5,1},{2,6},{6,2},{3,7},{7,3},{8,12},{12,8},{9,1... | collective-permute-start | bytes 1544 | tf_op jit(solution)/shard_map/ppermute | solution.py:213
  2.7 20.4 %collective-permute-start.4 = (bf16[512,768]{1,0:T(8,128)(2,1)}, bf16[512,768]{1,0:T(8,128)(2,1)S(1)}, u32[]{:S(2)}, u32[]{:S(2)}) collective-permute-start(bf16[512,768]{1,0:T(8,128)(2,1)} %refs_5_.1), channel_id=1, source_target_pairs={{0,32},{4,12},{8,40},{12,20},{16,48},{20,28},{24,56},{28,4},{32,64... | collective-permute-start | bytes 2359304 | tf_op jit(solution)/shard_map/ppermute | solution.py:202
  4.3 18.7 %collective-permute-start.3 = (bf16[512,768]{1,0:T(8,128)(2,1)}, bf16[512,768]{1,0:T(8,128)(2,1)S(1)}, u32[]{:S(2)}, u32[]{:S(2)}) collective-permute-start(bf16[512,768]{1,0:T(8,128)(2,1)} %refs_5_.1), channel_id=1, source_target_pairs={{0,24},{4,100},{8,0},{12,108},{16,8},{20,116},{24,16},{28,124},{32... | collective-permute-start | bytes 2359304 | tf_op jit(solution)/shard_map/ppermute | solution.py:202
  7.1 16.5 %collective-permute-start.2 = (bf16[512,768]{1,0:T(8,128)(2,1)}, bf16[512,768]{1,0:T(8,128)(2,1)S(1)}, u32[]{:S(2)}, u32[]{:S(2)}) collective-permute-start(bf16[512,768]{1,0:T(8,128)(2,1)} %refs_5_.1), channel_id=1, source_target_pairs={{0,8},{4,36},{8,16},{12,44},{16,24},{20,52},{24,0},{28,60},{32,40}... | collective-permute-start | bytes 2359304 | tf_op jit(solution)/shard_map/ppermute | solution.py:202
  10.8 13.5 %collective-permute-start.5 = (bf16[512,768]{1,0:T(8,128)(2,1)}, bf16[512,768]{1,0:T(8,128)(2,1)}, u32[]{:S(2)}, u32[]{:S(2)}) collective-permute-start(bf16[512,768]{1,0:T(8,128)(2,1)} %refs_5_.1), channel_id=1, source_target_pairs={{0,96},{4,28},{8,104},{12,4},{16,112},{20,12},{24,120},{28,20},{32... | collective-permute-start | bytes 2359304 | tf_op jit(solution)/shard_map/ppermute | solution.py:202
  14.8 0.7 copy-start.1
  24.3 17.6 %collective-permute-start.9 = (bf16[512,768]{1,0:T(8,128)(2,1)S(1)}, bf16[512,768]{1,0:T(8,128)(2,1)S(1)}, u32[]{:S(2)}, u32[]{:S(2)}) collective-permute-start(bf16[512,768]{1,0:T(8,128)(2,1)S(1)} %collective-permute-done.2.refs_5_), channel_id=1, source_target_pairs={{0,96},{4,28},{8,104},{12,4},{16,112},{20,12},{24,120},{28,20},{32... | collective-permute-start | bytes 2359304 | tf_op jit(solution)/shard_map/ppermute | solution.py:202
  28.0 14.0 %collective-permute-start.7 = (bf16[512,768]{1,0:T(8,128)(2,1)S(1)}, bf16[512,768]{1,0:T(8,128)(2,1)S(1)}, u32[]{:S(2)}, u32[]{:S(2)}) collective-permute-start(bf16[512,768]{1,0:T(8,128)(2,1)S(1)} %collective-permute-done.2.refs_5_), channel_id=1, source_target_pairs={{0,32},{4,12},{8,40},{12,20},{16,48},{20,28},{24,56},{28,4},{32,64... | collective-permute-start | bytes 2359304 | tf_op jit(solution)/shard_map/ppermute | solution.py:202
  28.0 26.4 %collective-permute-start.10 = (bf16[512,768]{1,0:T(8,128)(2,1)S(1)}, bf16[512,768]{1,0:T(8,128)(2,1)S(1)}, u32[]{:S(2)}, u32[]{:S(2)}) collective-permute-start(bf16[512,768]{1,0:T(8,128)(2,1)S(1)} %collective-permute-done.3.refs_6_), channel_id=1, source_target_pairs={{0,96},{4,28},{8,104},{12,4},{16,112},{20,12},{24,120},{28,20},{32... | collective-permute-start | bytes 2359304 | tf_op jit(solution)/shard_map/ppermute | solution.py:202
  31.3 23.1 %collective-permute-start.8 = (bf16[512,768]{1,0:T(8,128)(2,1)S(1)}, bf16[512,768]{1,0:T(8,128)(2,1)S(1)}, u32[]{:S(2)}, u32[]{:S(2)}) collective-permute-start(bf16[512,768]{1,0:T(8,128)(2,1)S(1)} %collective-permute-done.3.refs_6_), channel_id=1, source_target_pairs={{0,32},{4,12},{8,40},{12,20},{16,48},{20,28},{24,56},{28,4},{32,64... | collective-permute-start | bytes 2359304 | tf_op jit(solution)/shard_map/ppermute | solution.py:202
  31.3 23.1 %collective-permute-start.6 = (bf16[512,768]{1,0:T(8,128)(2,1)S(1)}, bf16[512,768]{1,0:T(8,128)(2,1)S(1)}, u32[]{:S(2)}, u32[]{:S(2)}) collective-permute-start(bf16[512,768]{1,0:T(8,128)(2,1)S(1)} %collective-permute-done.3.refs_6_), channel_id=1, source_target_pairs={{0,24},{4,100},{8,0},{12,108},{16,8},{20,116},{24,16},{28,124},{32... | collective-permute-start | bytes 2359304 | tf_op jit(solution)/shard_map/ppermute | solution.py:202
  54.4 13.2 %collective-permute-start.11 = (bf16[512,768]{1,0:T(8,128)(2,1)S(1)}, bf16[512,768]{1,0:T(8,128)(2,1)S(1)}, u32[]{:S(2)}, u32[]{:S(2)}) collective-permute-start(bf16[512,768]{1,0:T(8,128)(2,1)S(1)} %collective-permute-done.6.refs_5_), channel_id=1, source_target_pairs={{0,96},{4,28},{8,104},{12,4},{16,112},{20,12},{24,120},{28,20},{32... | collective-permute-start | bytes 2359304 | tf_op jit(solution)/shard_map/ppermute | solution.py:202
  58.1 30.1 %collective-permute-start.14 = (bf16[512,768]{1,0:T(8,128)(2,1)S(1)}, bf16[512,768]{1,0:T(8,128)(2,1)S(1)}, u32[]{:S(2)}, u32[]{:S(2)}) collective-permute-start(bf16[512,768]{1,0:T(8,128)(2,1)S(1)} %collective-permute-done.6.refs_5_), channel_id=1, source_target_pairs={{0,32},{4,12},{8,40},{12,20},{16,48},{20,28},{24,56},{28,4},{32,64... | collective-permute-start | bytes 2359304 | tf_op jit(solution)/shard_map/ppermute | solution.py:202
  58.1 21.6 %collective-permute-start.13 = (bf16[512,768]{1,0:T(8,128)(2,1)S(1)}, bf16[512,768]{1,0:T(8,128)(2,1)S(1)}, u32[]{:S(2)}, u32[]{:S(2)}) collective-permute-start(bf16[512,768]{1,0:T(8,128)(2,1)S(1)} %collective-permute-done.4.refs_7_), channel_id=1, source_target_pairs={{0,32},{4,12},{8,40},{12,20},{16,48},{20,28},{24,56},{28,4},{32,64... | collective-permute-start | bytes 2359304 | tf_op jit(solution)/shard_map/ppermute | solution.py:202
  58.1 30.0 %collective-permute-start.16 = (bf16[512,768]{1,0:T(8,128)(2,1)S(1)}, bf16[512,768]{1,0:T(8,128)(2,1)S(1)}, u32[]{:S(2)}, u32[]{:S(2)}) collective-permute-start(bf16[512,768]{1,0:T(8,128)(2,1)S(1)} %collective-permute-done.8.refs_7_), channel_id=1, source_target_pairs={{0,32},{4,12},{8,40},{12,20},{16,48},{20,28},{24,56},{28,4},{32,64... | collective-permute-start | bytes 2359304 | tf_op jit(solution)/shard_map/ppermute | solution.py:202
  59.6 28.6 %collective-permute-start.15 = (bf16[512,768]{1,0:T(8,128)(2,1)S(1)}, bf16[512,768]{1,0:T(8,128)(2,1)S(1)}, u32[]{:S(2)}, u32[]{:S(2)}) collective-permute-start(bf16[512,768]{1,0:T(8,128)(2,1)S(1)} %collective-permute-done.9.refs_8_), channel_id=1, source_target_pairs={{0,96},{4,28},{8,104},{12,4},{16,112},{20,12},{24,120},{28,20},{32... | collective-permute-start | bytes 2359304 | tf_op jit(solution)/shard_map/ppermute | solution.py:202
  67.6 28.6 %collective-permute-start.12 = (bf16[512,768]{1,0:T(8,128)(2,1)S(1)}, bf16[512,768]{1,0:T(8,128)(2,1)S(1)}, u32[]{:S(2)}, u32[]{:S(2)}) collective-permute-start(bf16[512,768]{1,0:T(8,128)(2,1)S(1)} %collective-permute-done.11.refs_7_), channel_id=1, source_target_pairs={{0,96},{4,28},{8,104},{12,4},{16,112},{20,12},{24,120},{28,20},{32... | collective-permute-start | bytes 2359304 | tf_op jit(solution)/shard_map/ppermute | solution.py:202
  181.5 11.5 %all-to-all-start.5 = ((f32[16,1,512]{2,1,0:T(1,128)}), f32[16,1,512]{2,1,0:T(1,128)S(1)}, u32[]{:S(2)}, u32[]{:S(2)}) async-start(f32[16,1,512]{2,1,0:T(1,128)} %copy.17), calls=%async_computation.5 | async-start | bytes 65536 | tf_op jit(solution)/shard_map/all_to_all | solution.py:311

commit v4 on v3

--- a/solution.py
+++ b/solution.py
@@ -10,6 +10,7 @@
 TILE = 512
 ABLK = 8
 ITERS = 3
+LANES = 128
 BUILD_STEP = 2
 BUFFERS = 4
 ROW_STEP = 4
@@ -155,7 +156,10 @@
     scaling = 1.0 / (1.0 + jnp.sum(parts[...], axis=0))
     weight[...] = scaling.astype(BF16).astype(F32)
     if last:
-        refs[0][...] = jnp.log(jnp.where(place[0] == 0, scaling[:ABLK], scaling[ABLK:]))
+        logs = jnp.log(jnp.where(place[0] == 0, scaling[:ABLK], scaling[ABLK:]))
+        for k in range(ABLK):
+            for q in range(TILE // LANES):
+                refs[0][pl.ds(k * (TILE // LANES) + q, 1), :] = logs[k : k + 1, q * LANES : (q + 1) * LANES]
     sums[...] = jnp.zeros_like(sums)
     number = bounds[NCHIP]
     size = ROW_STEP if over_rows else COLUMN_STEP
@@ -178,7 +182,8 @@
 
     lax.fori_loop(0, (number + size - 1) // size, step, 0)
     if last:
-        out[...] = sums[...]
+        for q in range(TILE // LANES):
+            out[:, q, :] = sums[:, q * LANES : (q + 1) * LANES]
     else:
         spread(out, sums[...])
 
@@ -210,8 +215,9 @@
     own = jnp.concatenate(
         [pair_a.reshape(1, -1), pair_b.reshape(1, -1), pair_count.reshape(1, 1), jnp.zeros((1, 63), jnp.int32)], axis=1
     )
+    a_other = lax.ppermute(table_a, "core", swap)
+    own, a_other = lax.optimization_barrier((own, a_other))
     other = lax.ppermute(own, "core", swap)
-    a_other = lax.ppermute(table_a, "core", swap)
     lists = jnp.where(core == 0, jnp.concatenate([own, other]), jnp.concatenate([other, own]))
     place = jnp.stack([core, lax.axis_index("y"), lax.axis_index("x")]).astype(jnp.int32)
     table = [0] * NCHIP
@@ -268,18 +274,14 @@
 
     kv = jnp.zeros((NC * ABLK, TILE), F32)
     store, kv = build(0, (table_b,), store, kv)
-    left, right, down, up, kv = lax.optimization_barrier((left, right, down, up, kv))
-    near = (left, right, down, up)
     first_two = go(right, True, -1)
     left_down, right_down = go(left, False, 1), go(right, False, 1)
     left_up, right_up = go(left, False, -1), go(right, False, -1)
-    store, kv = build(1, near, store, kv)
-    middle = (first_two, left_down, right_down, left_up, right_up)
-    *middle, down, kv = lax.optimization_barrier((*middle, down, kv))
-    first_two, left_down, right_down, left_up, right_up = middle
-    two_up, two_down = go(first_two, False, -1), go(first_two, False, 1)
-    left_two, right_two, second_two = go(left_up, False, -1), go(right_down, False, 1), go(down, False, 1)
-    store, kv = build(5, middle, store, kv)
+    store, kv = build(1, (left, right, down, up), store, kv)
+    first_two, down, kv = lax.optimization_barrier((first_two, down, kv))
+    two_up, two_down, second_two = go(first_two, False, -1), go(first_two, False, 1), go(down, False, 1)
+    left_two, right_two = go(left_up, False, -1), go(right_down, False, 1)
+    store, kv = build(5, (first_two, left_down, right_down, left_up, right_up), store, kv)
     two_up, kv = lax.optimization_barrier((two_up, kv))
     both_two = go(two_up, False, -1)
     store, kv = build(10, (second_two, two_down, two_up, left_two, right_two), store, kv)
@@ -287,8 +289,8 @@
 
     def half(over_rows, parts, copies, store):
         last = copies == 0
-        sums = jax.ShapeDtypeStruct((NCHIP, TILE) if last else (copies, NCHIP, TILE), F32)
-        logs = jax.ShapeDtypeStruct((ABLK, TILE), F32)
+        sums = jax.ShapeDtypeStruct((NCHIP, TILE // LANES, LANES) if last else (copies, NCHIP, TILE), F32)
+        logs = jax.ShapeDtypeStruct((ABLK * TILE // LANES, LANES), F32)
         return pl.pallas_call(
             lambda *refs: pass_kernel(over_rows, last, *refs),
             out_shape=(sums, logs if last else pltpu.VMEM((CAP, TILE, TILE), BF16)),
@@ -310,7 +312,7 @@
     ktu, log_u = half(False, kv_parts, 0, store)
     mine = lax.all_to_all(ktu, ("y", "x"), 0, 0, tiled=True)
     log_v = jnp.log(1.0 / (1.0 + jnp.sum(mine, axis=0)))
-    return log_u.reshape(-1), log_v
+    return log_u.reshape(-1), log_v.reshape(-1)
 
 
 def solution(mesh):

time: 196 us -> 190 us (0.969); the launches traced: 194 us -> 190 us
  blocking collectives: 65.4 us -> 86.1 us
  waiting for transfers between devices: 45.6 us -> 26.6 us
  Pallas kernels: 45.3 us -> 39.1 us
  starting transfers between devices: 31.8 us -> 35.1 us
    all_to_all x0 -> x1, blocking collectives: none -> 14.3 us  [on_device(): mine = lax.all_to_all(ktu, ('y', 'x'), 0, 0, tiled=True)]
    ppermute x15, waiting for transfers between devices: 34.8 us -> 25.5 us  [go(): return lax.ppermute(block, ('y', 'x', 'core'), moves(first, shift))]
    ppermute x15, starting transfers between devices: 27.3 us -> 35 us  [go(): return lax.ppermute(block, ('y', 'x', 'core'), moves(first, shift))]
    all_to_all x1 -> x0, waiting for transfers between devices: 6.99 us -> none  [on_device(): mine = lax.all_to_all(ktu, ('y', 'x'), 0, 0, tiled=True)]
    all_to_all x3, blocking collectives: 33.4 us -> 38 us  [on_device(): kv_parts = lax.all_to_all(kv, ('core', 'z'), 0, 0, tiled=True)]
    all_to_all x1 -> x0, starting transfers between devices: 3.93 us -> none  [on_device(): mine = lax.all_to_all(ktu, ('y', 'x'), 0, 0, tiled=True)]
    pallas_call x5, Pallas kernels: 25.2 us -> 22.5 us  [build(): pl.pallas_call(lambda *refs: build_kernel(scale, first, blocks, last, *re...]
    ppermute x1, waiting for transfers between devices: 3.74 us -> 1.03 us  [on_device(): other = lax.ppermute(own, 'core', swap)]
  transfers between devices with their start and end apart: 18 -> 17, of which waited for: 9 -> 4; matrix products, arithmetic and copies ran while one was open for 1% -> 0% of each run, Pallas kernels for 13% -> 12%
where the time goes in v4:
time: 190 us
  blocking collectives  86.1 us (45%)
  Pallas kernels  39.1 us (21%)
  starting transfers between devices  35.1 us (18%)
  waiting for transfers between devices  26.6 us (14%)
    all_to_all x3, blocking collectives, on_device(): kv_parts = lax.all_to_all(kv, ('core', 'z'), 0, 0, tiled=True)  38 us
    ppermute x15, starting transfers between devices, go(): return lax.ppermute(block, ('y', 'x', 'core'), moves(first, shift))  35 us
    all_to_all x2, blocking collectives, on_device(): ktu_parts = lax.all_to_all(ktu, ('y', 'x'), 0, 0, tiled=True)  33.8 us
    ppermute x15, waiting for transfers between devices, go(): return lax.ppermute(block, ('y', 'x', 'core'), moves(first, shift))  25.5 us
    pallas_call x5, Pallas kernels, build(): pl.pallas_call(lambda *refs: build_kernel(scale, first, blocks, last, *re...  22.5 us
    all_to_all x1, blocking collectives, on_device(): mine = lax.all_to_all(ktu, ('y', 'x'), 0, 0, tiled=True)  14.3 us
    pallas_call x5, Pallas kernels, half(): pl.pallas_call(lambda *refs: pass_kernel(over_rows, last, *refs), out_sha...  13.1 us
  transfers between devices with their start and end apart: 17, of which 4 were waited for; matrix products, arithmetic and copies ran while one was open for 0% of the time, Pallas kernels for 12%

profile of v4, /device:TPU:0, one launch (start us, length us, event | category | flops | bytes accessed | tf_op | source)
XLA Modules:
  0.0 190.5 jit_solution(15222849008166556849)
XLA Ops:
  0.6 0.1 collective-permute-start
  0.7 2.9 %collective-permute-start.2 = (bf16[512,768]{1,0:T(8,128)(2,1)}, bf16[512,768]{1,0:T(8,128)(2,1)}, u32[]{:S(2)}, u32[]{:S(2)}) collective-permute-start(bf16[512,768]{1,0:T(8,128)(2,1)} %refs_5_.1), channel_id=1, source_target_pairs={{0,24},{4,100},{8,0},{12,108},{16,8},{20,116},{24,16},{28,124},{32... | collective-permute-start | bytes 2359304 | tf_op jit(solution)/shard_map/ppermute | solution.py:207
  3.6 1.6 collective-permute-start.4
  5.2 1.7 collective-permute-start.6
  6.9 12.5 %collective-permute-done.2.refs_6_ = bf16[512,768]{1,0:T(8,128)(2,1)} collective-permute-done((bf16[512,768]{1,0:T(8,128)(2,1)}, bf16[512,768]{1,0:T(8,128)(2,1)}, u32[]{:S(2)}, u32[]{:S(2)}) %collective-permute-start.2) | collective-permute-done | bytes 786464 | tf_op jit(solution)/shard_map/ppermute | solution.py:207
  19.4 3.7 %collective-permute-start.3 = (bf16[512,768]{1,0:T(8,128)(2,1)}, bf16[512,768]{1,0:T(8,128)(2,1)S(1)}, u32[]{:S(2)}, u32[]{:S(2)}) collective-permute-start(bf16[512,768]{1,0:T(8,128)(2,1)} %collective-permute-done.2.refs_6_), channel_id=1, source_target_pairs={{0,24},{4,100},{8,0},{12,108},{16,8},{20,116},{24,16},{28,124},{32... | collective-permute-start | bytes 2359304 | tf_op jit(solution)/shard_map/ppermute | solution.py:207
  23.8 0.8 bitcast_add_fusion
  24.5 0.0 collective-permute-start.1
  24.6 0.1 pad_add_fusion.place.refs_2_
  24.6 1.0 collective-permute-done.1
  25.7 2.9 %collective-permute-start.9 = (bf16[512,768]{1,0:T(8,128)(2,1)}, bf16[512,768]{1,0:T(8,128)(2,1)S(1)}, u32[]{:S(2)}, u32[]{:S(2)}) collective-permute-start(bf16[512,768]{1,0:T(8,128)(2,1)} %collective-permute-done.2.refs_6_), channel_id=1, source_target_pairs={{0,32},{4,12},{8,40},{12,20},{16,48},{20,28},{24,56},{28,4},{32,64... | collective-permute-start | bytes 2359304 | tf_op jit(solution)/shard_map/ppermute | solution.py:207
  28.6 0.7 copy-done.1
  29.3 2.9 %plan.1 = (s32[3,64]{1,0:T(4,128)S(1)}, s32[17]{0:T(128)S(1)}) custom-call(s32[2,128]{1,0:T(2,128)S(1)} %add_select_fusion.lists, s32[3]{0:T(128)S(1)} %pad_add_fusion.place.refs_2_, s32[16]{0:T(128)S(1)} %copy-done.1), custom_call_target="tpu_custom_call" | custom-call | tf_op jit(solution)/shard_map/plan/pallas_call | solution.py:229
  32.2 0.6 room.1.refs_6_
  32.8 2.3 %collective-permute-start.11 = (bf16[512,768]{1,0:T(8,128)(2,1)}, bf16[512,768]{1,0:T(8,128)(2,1)S(1)}, u32[]{:S(2)}, u32[]{:S(2)}) collective-permute-start(bf16[512,768]{1,0:T(8,128)(2,1)} %collective-permute-done.2.refs_6_), channel_id=1, source_target_pairs={{0,96},{4,28},{8,104},{12,4},{16,112},{20,12},{24,120},{28,20},{32... | collective-permute-start | bytes 2359304 | tf_op jit(solution)/shard_map/ppermute | solution.py:207
  35.1 0.2 collective-permute-start.10
  35.3 0.0 collective-permute-done.6.refs_8_
  35.3 1.8 collective-permute-start.8
  37.1 3.2 %build.5 = (bf16[64,512,512]{2,1,0:T(8,128)(2,1)S(1)}, f32[16,512]{1,0:T(8,128)S(1)}) custom-call(s32[3,64]{1,0:T(4,128)S(1)} %get-tuple-element.32.pairs.refs_0_, s32[17]{0:T(128)S(1)} %get-tuple-element.33.bounds.refs_1_, s32[3]{0:T(128)S(1)} %pad_add_fusion.place.refs_2_, bf16[4096,768]{1,0:T(8,128)(2,1)} %refs_3_.9, ...), custom_call_target="tpu_custom_call", output_to_operand_aliasing={{0}: (6, {})} | custom-call | flops 805306368 | bytes 3145728 | tf_op jit(solution)/shard_map/build/pallas_call | solution.py:253
  40.4 4.0 %build.6 = (bf16[64,512,512]{2,1,0:T(8,128)(2,1)S(1)}, f32[16,512]{1,0:T(8,128)S(1)}) custom-call(s32[3,64]{1,0:T(4,128)S(1)} %get-tuple-element.32.pairs.refs_0_, s32[17]{0:T(128)S(1)} %get-tuple-element.33.bounds.refs_1_, s32[3]{0:T(128)S(1)} %pad_add_fusion.place.refs_2_, bf16[4096,768]{1,0:T(8,128)(2,1)} %refs_3_.9, ...), custom_call_target="tpu_custom_call", output_to_operand_aliasing={{0}: (9, {})} | custom-call | flops 3221225472 | bytes 12582912 | tf_op jit(solution)/shard_map/build/pallas_call | solution.py:253
  44.4 0.0 collective-permute-done.3.refs_5_
  44.4 6.0 %collective-permute-start.7 = (bf16[512,768]{1,0:T(8,128)(2,1)S(1)}, bf16[512,768]{1,0:T(8,128)(2,1)S(1)}, u32[]{:S(2)}, u32[]{:S(2)}) collective-permute-start(bf16[512,768]{1,0:T(8,128)(2,1)S(1)} %collective-permute-done.3.refs_5_), channel_id=1, source_target_pairs={{0,96},{4,28},{8,104},{12,4},{16,112},{20,12},{24,120},{28,20},{32... | collective-permute-start | bytes 2359304 | tf_op jit(solution)/shard_map/ppermute | solution.py:207
  50.4 0.0 collective-permute-done.9.refs_7_
  50.4 0.0 collective-permute-start.16
  50.4 3.7 %collective-permute-done.10.refs_8_ = bf16[512,768]{1,0:T(8,128)(2,1)S(1)} collective-permute-done((bf16[512,768]{1,0:T(8,128)(2,1)S(1)}, bf16[512,768]{1,0:T(8,128)(2,1)S(1)}, u32[]{:S(2)}, u32[]{:S(2)}) %collective-permute-start.10) | collective-permute-done | bytes 786464 | tf_op jit(solution)/shard_map/ppermute | solution.py:207
  54.1 2.8 %collective-permute-start.15 = (bf16[512,768]{1,0:T(8,128)(2,1)S(1)}, bf16[512,768]{1,0:T(8,128)(2,1)S(1)}, u32[]{:S(2)}, u32[]{:S(2)}) collective-permute-start(bf16[512,768]{1,0:T(8,128)(2,1)S(1)} %collective-permute-done.10.refs_8_), channel_id=1, source_target_pairs={{0,96},{4,28},{8,104},{12,4},{16,112},{20,12},{24,120},{28,20},{32... | collective-permute-start | bytes 2359304 | tf_op jit(solution)/shard_map/ppermute | solution.py:207
  56.9 0.0 collective-permute-start.14
  56.9 0.0 collective-permute-done.8.refs_6_
  56.9 1.2 collective-permute-start.13
  58.2 5.2 %build.7 = (bf16[64,512,512]{2,1,0:T(8,128)(2,1)S(1)}, f32[16,512]{1,0:T(8,128)S(1)}) custom-call(s32[3,64]{1,0:T(4,128)S(1)} %get-tuple-element.32.pairs.refs_0_, s32[17]{0:T(128)S(1)} %get-tuple-element.33.bounds.refs_1_, s32[3]{0:T(128)S(1)} %pad_add_fusion.place.refs_2_, bf16[4096,768]{1,0:T(8,128)(2,1)} %refs_3_.9, ...), custom_call_target="tpu_custom_call", output_to_operand_aliasing={{0}: (10, {})} | custom-call | flops 4026531840 | bytes 15728640 | tf_op jit(solution)/shard_map/build/pallas_call | solution.py:253
  63.3 0.0 collective-permute-done.7.refs_7_
  63.4 7.9 %collective-permute-start.12 = (bf16[512,768]{1,0:T(8,128)(2,1)S(1)}, bf16[512,768]{1,0:T(8,128)(2,1)S(1)}, u32[]{:S(2)}, u32[]{:S(2)}) collective-permute-start(bf16[512,768]{1,0:T(8,128)(2,1)S(1)} %collective-permute-done.7.refs_7_), channel_id=1, source_target_pairs={{0,96},{4,28},{8,104},{12,4},{16,112},{20,12},{24,120},{28,20},{32... | collective-permute-start | bytes 2359304 | tf_op jit(solution)/shard_map/ppermute | solution.py:207
  71.2 0.0 collective-permute-done.16.refs_9_
  71.2 9.3 %collective-permute-done.13.refs_5_ = bf16[512,768]{1,0:T(8,128)(2,1)S(1)} collective-permute-done((bf16[512,768]{1,0:T(8,128)(2,1)S(1)}, bf16[512,768]{1,0:T(8,128)(2,1)S(1)}, u32[]{:S(2)}, u32[]{:S(2)}) %collective-permute-start.13) | collective-permute-done | bytes 786464 | tf_op jit(solution)/shard_map/ppermute | solution.py:207
  80.5 6.6 %build.8 = (bf16[64,512,512]{2,1,0:T(8,128)(2,1)S(1)}, f32[16,512]{1,0:T(8,128)S(1)}) custom-call(s32[3,64]{1,0:T(4,128)S(1)} %get-tuple-element.32.pairs.refs_0_, s32[17]{0:T(128)S(1)} %get-tuple-element.33.bounds.refs_1_, s32[3]{0:T(128)S(1)} %pad_add_fusion.place.refs_2_, bf16[4096,768]{1,0:T(8,128)(2,1)} %refs_3_.9, ...), custom_call_target="tpu_custom_call", output_to_operand_aliasing={{0}: (10, {})} | custom-call | flops 4026531840 | bytes 15728640 | tf_op jit(solution)/shard_map/build/pallas_call | solution.py:253
  87.1 3.5 %build.9 = (bf16[64,512,512]{2,1,0:T(8,128)(2,1)S(1)}, f32[8,16,512]{2,1,0:T(8,128)S(1)}) custom-call(s32[3,64]{1,0:T(4,128)S(1)} %get-tuple-element.32.pairs.refs_0_, s32[17]{0:T(128)S(1)} %get-tuple-element.33.bounds.refs_1_, s32[3]{0:T(128)S(1)} %pad_add_fusion.place.refs_2_, bf16[4096,768]{1,0:T(8,128)(2,1)} %refs_3_.9, ...), custom_call_target="tpu_custom_call", output_to_operand_aliasing={{0}: (6, {})} | custom-call | flops 805306368 | bytes 3145728 | tf_op jit(solution)/shard_map/build/pallas_call | solution.py:253
  90.6 16.4 %all_to_all.30.refs_3_ = f32[8,16,512]{2,1,0:T(8,128)S(1)} all-to-all(f32[8,16,512]{2,1,0:T(8,128)S(1)} %get-tuple-element.48), channel_id=1, replica_groups=mesh['y'=4,'x'=4,'core'=2,'z'=4] {'core','z'}, dimensions={0} | all-to-all | bytes 524288 | tf_op jit(solution)/shard_map/all_to_all | solution.py:308
  106.9 2.0 %columns.3 = (f32[16,16,512]{2,1,0:T(8,128)S(1)}, bf16[64,512,512]{2,1,0:T(8,128)(2,1)S(1)}) custom-call(s32[3,64]{1,0:T(4,128)S(1)} %get-tuple-element.32.pairs.refs_0_, s32[17]{0:T(128)S(1)} %get-tuple-element.33.bounds.refs_1_, s32[3]{0:T(128)S(1)} %pad_add_fusion.place.refs_2_, ...), custom_call_target="tpu_custom_call", output_to_operand_aliasing={{1}: (4, {})} | custom-call | tf_op jit(solution)/shard_map/columns/pallas_call | solution.py:294
  108.9 16.5 %all_to_all.31.refs_3_ = f32[16,16,512]{2,1,0:T(8,128)S(1)} all-to-all(f32[16,16,512]{2,1,0:T(8,128)S(1)} %get-tuple-element.50), channel_id=1, replica_groups=mesh['y'=4,'x'=4,'core'=2,'z'=4] {'y','x'}, dimensions={0} | all-to-all | bytes 1048576 | tf_op jit(solution)/shard_map/all_to_all | solution.py:311
  125.4 3.3 %rows.2 = (f32[8,16,512]{2,1,0:T(8,128)S(1)}, bf16[64,512,512]{2,1,0:T(8,128)(2,1)S(1)}) custom-call(s32[3,64]{1,0:T(4,128)S(1)} %get-tuple-element.32.pairs.refs_0_, s32[17]{0:T(128)S(1)} %get-tuple-element.33.bounds.refs_1_, s32[3]{0:T(128)S(1)} %pad_add_fusion.place.refs_2_, ...), custom_call_target="tpu_custom_call", output_to_operand_aliasing={{1}: (4, {})} | custom-call | tf_op jit(solution)/shard_map/rows/pallas_call | solution.py:294
  128.7 10.8 %all_to_all.32.refs_3_ = f32[8,16,512]{2,1,0:T(8,128)S(1)} all-to-all(f32[8,16,512]{2,1,0:T(8,128)S(1)} %get-tuple-element.52), channel_id=1, replica_groups=mesh['y'=4,'x'=4,'core'=2,'z'=4] {'core','z'}, dimensions={0} | all-to-all | bytes 524288 | tf_op jit(solution)/shard_map/all_to_all | solution.py:308
  139.6 2.0 %columns.4 = (f32[16,16,512]{2,1,0:T(8,128)S(1)}, bf16[64,512,512]{2,1,0:T(8,128)(2,1)S(1)}) custom-call(s32[3,64]{1,0:T(4,128)S(1)} %get-tuple-element.32.pairs.refs_0_, s32[17]{0:T(128)S(1)} %get-tuple-element.33.bounds.refs_1_, s32[3]{0:T(128)S(1)} %pad_add_fusion.place.refs_2_, ...), custom_call_target="tpu_custom_call", output_to_operand_aliasing={{1}: (4, {})} | custom-call | tf_op jit(solution)/shard_map/columns/pallas_call | solution.py:294
  141.6 17.3 %all_to_all.33.refs_3_ = f32[16,16,512]{2,1,0:T(8,128)S(1)} all-to-all(f32[16,16,512]{2,1,0:T(8,128)S(1)} %get-tuple-element.54), channel_id=1, replica_groups=mesh['y'=4,'x'=4,'core'=2,'z'=4] {'y','x'}, dimensions={0} | all-to-all | bytes 1048576 | tf_op jit(solution)/shard_map/all_to_all | solution.py:311
  158.8 3.3 %rows.3 = (f32[8,16,512]{2,1,0:T(8,128)S(1)}, bf16[64,512,512]{2,1,0:T(8,128)(2,1)S(1)}) custom-call(s32[3,64]{1,0:T(4,128)S(1)} %get-tuple-element.32.pairs.refs_0_, s32[17]{0:T(128)S(1)} %get-tuple-element.33.bounds.refs_1_, s32[3]{0:T(128)S(1)} %pad_add_fusion.place.refs_2_, ...), custom_call_target="tpu_custom_call", output_to_operand_aliasing={{1}: (4, {})} | custom-call | tf_op jit(solution)/shard_map/rows/pallas_call | solution.py:294
  162.1 10.8 %all_to_all.34.refs_3_ = f32[8,16,512]{2,1,0:T(8,128)S(1)} all-to-all(f32[8,16,512]{2,1,0:T(8,128)S(1)} %get-tuple-element.56), channel_id=1, replica_groups=mesh['y'=4,'x'=4,'core'=2,'z'=4] {'core','z'}, dimensions={0} | all-to-all | bytes 524288 | tf_op jit(solution)/shard_map/all_to_all | solution.py:308
  173.0 2.5 %columns.5 = (f32[16,4,128]{2,1,0:T(4,128)S(1)}, f32[32,128]{1,0:T(8,128)}) custom-call(s32[3,64]{1,0:T(4,128)S(1)} %get-tuple-element.32.pairs.refs_0_, s32[17]{0:T(128)S(1)} %get-tuple-element.33.bounds.refs_1_, s32[3]{0:T(128)S(1)} %pad_add_fusion.place.refs_2_, f32[8,16,512]{2,1,0:T(8,128)S(1)} %all_to_all.34.refs_3_, ...), custom_call_target="tpu_custom_call" | custom-call | tf_op jit(solution)/shard_map/columns/pallas_call | solution.py:294
  175.5 14.3 %all_to_all.35 = f32[16,4,128]{2,1,0:T(4,128)S(1)} all-to-all(f32[16,4,128]{2,1,0:T(4,128)S(1)} %get-tuple-element.59), channel_id=1, replica_groups=mesh['y'=4,'x'=4,'core'=2,'z'=4] {'y','x'}, dimensions={0} | all-to-all | bytes 65536 | tf_op jit(solution)/shard_map/all_to_all | solution.py:313
  189.9 0.6 log_bitcast_fusion
  (15 shorter events, 0.1 us)
Async XLA Ops:
  0.6 36.5 %copy-start = (bf16[512,768]{1,0:T(8,128)(2,1)S(1)}, bf16[512,768]{1,0:T(8,128)(2,1)}, u32[]{:S(2)}) copy-start(bf16[512,768]{1,0:T(8,128)(2,1)} %refs_5_.1) | copy-start | bytes 2359300
  0.6 23.9 %collective-permute-start = (bf16[4096,768]{1,0:T(8,128)(2,1)}, bf16[4096,768]{1,0:T(8,128)(2,1)}, u32[]{:S(2)}, u32[]{:S(2)}) collective-permute-start(bf16[4096,768]{1,0:T(8,128)(2,1)} %refs_3_.9), channel_id=1, source_target_pairs={{0,4},{4,0},{1,5},{5,1},{2,6},{6,2},{3,7},{7,3},{8,12},{12,8},{9,1... | collective-permute-start | bytes 18874376 | tf_op jit(solution)/shard_map/ppermute | solution.py:218
  0.7 18.7 %collective-permute-start.2 = (bf16[512,768]{1,0:T(8,128)(2,1)}, bf16[512,768]{1,0:T(8,128)(2,1)}, u32[]{:S(2)}, u32[]{:S(2)}) collective-permute-start(bf16[512,768]{1,0:T(8,128)(2,1)} %refs_5_.1), channel_id=1, source_target_pairs={{0,24},{4,100},{8,0},{12,108},{16,8},{20,116},{24,16},{28,124},{32... | collective-permute-start | bytes 2359304 | tf_op jit(solution)/shard_map/ppermute | solution.py:207
  3.6 29.1 %collective-permute-start.5 = (bf16[512,768]{1,0:T(8,128)(2,1)}, bf16[512,768]{1,0:T(8,128)(2,1)S(1)}, u32[]{:S(2)}, u32[]{:S(2)}) collective-permute-start(bf16[512,768]{1,0:T(8,128)(2,1)} %refs_5_.1), channel_id=1, source_target_pairs={{0,8},{4,36},{8,16},{12,44},{16,24},{20,52},{24,0},{28,60},{32,40}... | collective-permute-start | bytes 2359304 | tf_op jit(solution)/shard_map/ppermute | solution.py:207
  3.6 31.4 %collective-permute-start.4 = (bf16[512,768]{1,0:T(8,128)(2,1)}, bf16[512,768]{1,0:T(8,128)(2,1)S(1)}, u32[]{:S(2)}, u32[]{:S(2)}) collective-permute-start(bf16[512,768]{1,0:T(8,128)(2,1)} %refs_5_.1), channel_id=1, source_target_pairs={{0,32},{4,12},{8,40},{12,20},{16,48},{20,28},{24,56},{28,4},{32,64... | collective-permute-start | bytes 2359304 | tf_op jit(solution)/shard_map/ppermute | solution.py:207
  5.2 30.1 %collective-permute-start.6 = (bf16[512,768]{1,0:T(8,128)(2,1)}, bf16[512,768]{1,0:T(8,128)(2,1)}, u32[]{:S(2)}, u32[]{:S(2)}) collective-permute-start(bf16[512,768]{1,0:T(8,128)(2,1)} %refs_5_.1), channel_id=1, source_target_pairs={{0,96},{4,28},{8,104},{12,4},{16,112},{20,12},{24,120},{28,20},{32... | collective-permute-start | bytes 2359304 | tf_op jit(solution)/shard_map/ppermute | solution.py:207
  19.4 25.0 %collective-permute-start.3 = (bf16[512,768]{1,0:T(8,128)(2,1)}, bf16[512,768]{1,0:T(8,128)(2,1)S(1)}, u32[]{:S(2)}, u32[]{:S(2)}) collective-permute-start(bf16[512,768]{1,0:T(8,128)(2,1)} %collective-permute-done.2.refs_6_), channel_id=1, source_target_pairs={{0,24},{4,100},{8,0},{12,108},{16,8},{20,116},{24,16},{28,124},{32... | collective-permute-start | bytes 2359304 | tf_op jit(solution)/shard_map/ppermute | solution.py:207
  24.5 1.1 collective-permute-start.1
  25.7 24.7 %collective-permute-start.9 = (bf16[512,768]{1,0:T(8,128)(2,1)}, bf16[512,768]{1,0:T(8,128)(2,1)S(1)}, u32[]{:S(2)}, u32[]{:S(2)}) collective-permute-start(bf16[512,768]{1,0:T(8,128)(2,1)} %collective-permute-done.2.refs_6_), channel_id=1, source_target_pairs={{0,32},{4,12},{8,40},{12,20},{16,48},{20,28},{24,56},{28,4},{32,64... | collective-permute-start | bytes 2359304 | tf_op jit(solution)/shard_map/ppermute | solution.py:207
  28.6 0.7 copy-start.1
  32.8 24.2 %collective-permute-start.11 = (bf16[512,768]{1,0:T(8,128)(2,1)}, bf16[512,768]{1,0:T(8,128)(2,1)S(1)}, u32[]{:S(2)}, u32[]{:S(2)}) collective-permute-start(bf16[512,768]{1,0:T(8,128)(2,1)} %collective-permute-done.2.refs_6_), channel_id=1, source_target_pairs={{0,96},{4,28},{8,104},{12,4},{16,112},{20,12},{24,120},{28,20},{32... | collective-permute-start | bytes 2359304 | tf_op jit(solution)/shard_map/ppermute | solution.py:207
  35.1 19.0 %collective-permute-start.10 = (bf16[512,768]{1,0:T(8,128)(2,1)S(1)}, bf16[512,768]{1,0:T(8,128)(2,1)S(1)}, u32[]{:S(2)}, u32[]{:S(2)}) collective-permute-start(bf16[512,768]{1,0:T(8,128)(2,1)S(1)} %collective-permute-done.5.refs_5_), channel_id=1, source_target_pairs={{0,96},{4,28},{8,104},{12,4},{16,112},{20,12},{24,120},{28,20},{32... | collective-permute-start | bytes 2359304 | tf_op jit(solution)/shard_map/ppermute | solution.py:207
  35.3 21.6 %collective-permute-start.8 = (bf16[512,768]{1,0:T(8,128)(2,1)S(1)}, bf16[512,768]{1,0:T(8,128)(2,1)S(1)}, u32[]{:S(2)}, u32[]{:S(2)}) collective-permute-start(bf16[512,768]{1,0:T(8,128)(2,1)S(1)} %collective-permute-done.5.refs_5_), channel_id=1, source_target_pairs={{0,32},{4,12},{8,40},{12,20},{16,48},{20,28},{24,56},{28,4},{32,64... | collective-permute-start | bytes 2359304 | tf_op jit(solution)/shard_map/ppermute | solution.py:207
  44.4 18.9 %collective-permute-start.7 = (bf16[512,768]{1,0:T(8,128)(2,1)S(1)}, bf16[512,768]{1,0:T(8,128)(2,1)S(1)}, u32[]{:S(2)}, u32[]{:S(2)}) collective-permute-start(bf16[512,768]{1,0:T(8,128)(2,1)S(1)} %collective-permute-done.3.refs_5_), channel_id=1, source_target_pairs={{0,96},{4,28},{8,104},{12,4},{16,112},{20,12},{24,120},{28,20},{32... | collective-permute-start | bytes 2359304 | tf_op jit(solution)/shard_map/ppermute | solution.py:207
  50.4 20.8 %collective-permute-start.16 = (bf16[512,768]{1,0:T(8,128)(2,1)S(1)}, bf16[512,768]{1,0:T(8,128)(2,1)S(1)}, u32[]{:S(2)}, u32[]{:S(2)}) collective-permute-start(bf16[512,768]{1,0:T(8,128)(2,1)S(1)} %collective-permute-done.9.refs_7_), channel_id=1, source_target_pairs={{0,32},{4,12},{8,40},{12,20},{16,48},{20,28},{24,56},{28,4},{32,64... | collective-permute-start | bytes 2359304 | tf_op jit(solution)/shard_map/ppermute | solution.py:207
  54.1 17.1 %collective-permute-start.15 = (bf16[512,768]{1,0:T(8,128)(2,1)S(1)}, bf16[512,768]{1,0:T(8,128)(2,1)S(1)}, u32[]{:S(2)}, u32[]{:S(2)}) collective-permute-start(bf16[512,768]{1,0:T(8,128)(2,1)S(1)} %collective-permute-done.10.refs_8_), channel_id=1, source_target_pairs={{0,96},{4,28},{8,104},{12,4},{16,112},{20,12},{24,120},{28,20},{32... | collective-permute-start | bytes 2359304 | tf_op jit(solution)/shard_map/ppermute | solution.py:207
  56.9 23.5 %collective-permute-start.14 = (bf16[512,768]{1,0:T(8,128)(2,1)S(1)}, bf16[512,768]{1,0:T(8,128)(2,1)S(1)}, u32[]{:S(2)}, u32[]{:S(2)}) collective-permute-start(bf16[512,768]{1,0:T(8,128)(2,1)S(1)} %collective-permute-done.3.refs_5_), channel_id=1, source_target_pairs={{0,32},{4,12},{8,40},{12,20},{16,48},{20,28},{24,56},{28,4},{32,64... | collective-permute-start | bytes 2359304 | tf_op jit(solution)/shard_map/ppermute | solution.py:207
  56.9 23.5 %collective-permute-start.13 = (bf16[512,768]{1,0:T(8,128)(2,1)S(1)}, bf16[512,768]{1,0:T(8,128)(2,1)S(1)}, u32[]{:S(2)}, u32[]{:S(2)}) collective-permute-start(bf16[512,768]{1,0:T(8,128)(2,1)S(1)} %collective-permute-done.4.refs_7_), channel_id=1, source_target_pairs={{0,32},{4,12},{8,40},{12,20},{16,48},{20,28},{24,56},{28,4},{32,64... | collective-permute-start | bytes 2359304 | tf_op jit(solution)/shard_map/ppermute | solution.py:207
  63.4 23.7 %collective-permute-start.12 = (bf16[512,768]{1,0:T(8,128)(2,1)S(1)}, bf16[512,768]{1,0:T(8,128)(2,1)S(1)}, u32[]{:S(2)}, u32[]{:S(2)}) collective-permute-start(bf16[512,768]{1,0:T(8,128)(2,1)S(1)} %collective-permute-done.7.refs_7_), channel_id=1, source_target_pairs={{0,96},{4,28},{8,104},{12,4},{16,112},{20,12},{24,120},{28,20},{32... | collective-permute-start | bytes 2359304 | tf_op jit(solution)/shard_map/ppermute | solution.py:207

commit v5 on v4

--- a/solution.py
+++ b/solution.py
@@ -216,7 +216,6 @@
         [pair_a.reshape(1, -1), pair_b.reshape(1, -1), pair_count.reshape(1, 1), jnp.zeros((1, 63), jnp.int32)], axis=1
     )
     a_other = lax.ppermute(table_a, "core", swap)
-    own, a_other = lax.optimization_barrier((own, a_other))
     other = lax.ppermute(own, "core", swap)
     lists = jnp.where(core == 0, jnp.concatenate([own, other]), jnp.concatenate([other, own]))
     place = jnp.stack([core, lax.axis_index("y"), lax.axis_index("x")]).astype(jnp.int32)
@@ -274,6 +273,7 @@
 
     kv = jnp.zeros((NC * ABLK, TILE), F32)
     store, kv = build(0, (table_b,), store, kv)
+    left, right, bounds = lax.optimization_barrier((left, right, bounds))
     first_two = go(right, True, -1)
     left_down, right_down = go(left, False, 1), go(right, False, 1)
     left_up, right_up = go(left, False, -1), go(right, False, -1)

time: 190 us -> 182 us (0.958)
  starting transfers between devices: 35.1 us -> 25.7 us
  Pallas kernels: 39.1 us -> 46.1 us
  blocking collectives: 86.1 us -> 81.7 us
    ppermute x15, starting transfers between devices: 35 us -> 25.6 us  [go(): return lax.ppermute(block, ('y', 'x', 'core'), moves(first, shift))]
    all_to_all x3, blocking collectives: 38 us -> 32 us  [on_device(): kv_parts = lax.all_to_all(kv, ('core', 'z'), 0, 0, tiled=True)]
    ppermute x15, waiting for transfers between devices: 25.5 us -> 21.4 us  [go(): return lax.ppermute(block, ('y', 'x', 'core'), moves(first, shift))]
    all_to_all x2, blocking collectives: 33.8 us -> 37.1 us  [on_device(): ktu_parts = lax.all_to_all(ktu, ('y', 'x'), 0, 0, tiled=True)]
    pallas_call x5, Pallas kernels: 13.1 us -> 16.4 us  [half(): pl.pallas_call(lambda *refs: pass_kernel(over_rows, last, *refs), out_sha...]
    pallas_call x5, Pallas kernels: 22.5 us -> 25.4 us  [build(): pl.pallas_call(lambda *refs: build_kernel(scale, first, blocks, last, *re...]
    ppermute x1, waiting for transfers between devices: 1.03 us -> 3.62 us  [on_device(): other = lax.ppermute(own, 'core', swap)]
  transfers between devices with their start and end apart: 17 -> 17, of which waited for: 4 -> 5; matrix products, arithmetic and copies ran while one was open for 0% -> 1% of each run, Pallas kernels for 12% -> 14%
where the time goes in v5:
time: 182 us; the launch traced here: 183 us
  blocking collectives  81.7 us (45%)
  Pallas kernels  46.1 us (25%)
  starting transfers between devices  25.7 us (14%)
  waiting for transfers between devices  25 us (14%)
  other arithmetic  2.26 us (1%)
    all_to_all x2, blocking collectives, on_device(): ktu_parts = lax.all_to_all(ktu, ('y', 'x'), 0, 0, tiled=True)  37.1 us
    all_to_all x3, blocking collectives, on_device(): kv_parts = lax.all_to_all(kv, ('core', 'z'), 0, 0, tiled=True)  32 us
    ppermute x15, starting transfers between devices, go(): return lax.ppermute(block, ('y', 'x', 'core'), moves(first, shift))  25.6 us
    pallas_call x5, Pallas kernels, build(): pl.pallas_call(lambda *refs: build_kernel(scale, first, blocks, last, *re...  25.4 us
    ppermute x15, waiting for transfers between devices, go(): return lax.ppermute(block, ('y', 'x', 'core'), moves(first, shift))  21.4 us
    pallas_call x5, Pallas kernels, half(): pl.pallas_call(lambda *refs: pass_kernel(over_rows, last, *refs), out_sha...  16.4 us
    all_to_all x1, blocking collectives, on_device(): mine = lax.all_to_all(ktu, ('y', 'x'), 0, 0, tiled=True)  12.6 us
    pallas_call x1, Pallas kernels, on_device(): pl.pallas_call(plan_kernel, out_shape=(jax.ShapeDtypeStruct((3, CAP), jnp...  3.76 us
  transfers between devices with their start and end apart: 17, of which 5 were waited for; matrix products, arithmetic and copies ran while one was open for 1% of the time, Pallas kernels for 14%

profile of v5, /device:TPU:0, one launch (start us, length us, event | category | flops | bytes accessed | tf_op | source)
XLA Modules:
  0.0 183.0 jit_solution(6958470697227248590)
XLA Ops:
  0.6 0.0 copy-start
  0.6 0.1 collective-permute-start.3
  0.7 1.6 collective-permute-start.1
  2.4 1.7 collective-permute-start.2
  4.7 0.8 pad_add_fusion
  5.5 0.0 collective-permute-start
  5.5 1.7 collective-permute-start.5
  7.2 3.6 %collective-permute-done = s32[1,128]{1,0:T(1,128)S(1)} collective-permute-done((s32[1,128]{1,0:T(1,128)S(1)}, s32[1,128]{1,0:T(1,128)S(1)}, u32[]{:S(2)}, u32[]{:S(2)}) %collective-permute-start) | collective-permute-done | bytes 544 | tf_op jit(solution)/shard_map/ppermute | solution.py:219
  10.8 3.1 %collective-permute-start.6 = (bf16[512,768]{1,0:T(8,128)(2,1)}, bf16[512,768]{1,0:T(8,128)(2,1)}, u32[]{:S(2)}, u32[]{:S(2)}) collective-permute-start(bf16[512,768]{1,0:T(8,128)(2,1)} %refs_5_.1), channel_id=1, source_target_pairs={{0,96},{4,28},{8,104},{12,4},{16,112},{20,12},{24,120},{28,20},{32... | collective-permute-start | bytes 2359304 | tf_op jit(solution)/shard_map/ppermute | solution.py:207
  13.9 0.1 pad_add_fusion.1.place.refs_2_
  14.0 0.8 add_select_fusion.lists
  14.8 0.7 copy-done.1
  15.5 3.8 %plan.1 = (s32[3,64]{1,0:T(4,128)S(1)}, s32[17]{0:T(128)S(1)}) custom-call(s32[2,128]{1,0:T(2,128)S(1)} %add_select_fusion.lists, s32[3]{0:T(128)S(1)} %pad_add_fusion.1.place.refs_2_, s32[16]{0:T(128)S(1)} %copy-done.1), custom_call_target="tpu_custom_call" | custom-call | tf_op jit(solution)/shard_map/plan/pallas_call | solution.py:228
  19.3 0.0 collective-permute-done.1.refs_5_
  19.3 3.7 %collective-permute-start.4 = (bf16[512,768]{1,0:T(8,128)(2,1)S(1)}, bf16[512,768]{1,0:T(8,128)(2,1)S(1)}, u32[]{:S(2)}, u32[]{:S(2)}) collective-permute-start(bf16[512,768]{1,0:T(8,128)(2,1)S(1)} %collective-permute-done.2.refs_6_), channel_id=1, source_target_pairs={{0,24},{4,100},{8,0},{12,108},{16,8},{20,116},{24,16},{28,124},{32... | collective-permute-start | bytes 2359304 | tf_op jit(solution)/shard_map/ppermute | solution.py:207
  23.0 0.6 room.1.refs_6_
  23.5 0.1 collective-permute-start.9
  23.6 3.2 %collective-permute-start.11 = (bf16[512,768]{1,0:T(8,128)(2,1)S(1)}, bf16[512,768]{1,0:T(8,128)(2,1)S(1)}, u32[]{:S(2)}, u32[]{:S(2)}) collective-permute-start(bf16[512,768]{1,0:T(8,128)(2,1)S(1)} %collective-permute-done.2.refs_6_), channel_id=1, source_target_pairs={{0,96},{4,28},{8,104},{12,4},{16,112},{20,12},{24,120},{28,20},{32... | collective-permute-start | bytes 2359304 | tf_op jit(solution)/shard_map/ppermute | solution.py:207
  26.9 0.0 collective-permute-done.6.refs_8_
  26.9 1.9 %collective-permute-start.10 = (bf16[512,768]{1,0:T(8,128)(2,1)S(1)}, bf16[512,768]{1,0:T(8,128)(2,1)S(1)}, u32[]{:S(2)}, u32[]{:S(2)}) collective-permute-start(bf16[512,768]{1,0:T(8,128)(2,1)S(1)} %collective-permute-done.1.refs_5_), channel_id=1, source_target_pairs={{0,96},{4,28},{8,104},{12,4},{16,112},{20,12},{24,120},{28,20},{32... | collective-permute-start | bytes 2359304 | tf_op jit(solution)/shard_map/ppermute | solution.py:207
  28.8 0.1 collective-permute-start.8
  28.9 0.7 build.5
  29.6 6.7 %build.6 = (bf16[64,512,512]{2,1,0:T(8,128)(2,1)S(1)}, f32[16,512]{1,0:T(8,128)S(1)}) custom-call(s32[3,64]{1,0:T(4,128)S(1)} %get-tuple-element.32.pairs.refs_0_, s32[17]{0:T(128)S(1)} %get-tuple-element.34.bounds.refs_1_, s32[3]{0:T(128)S(1)} %pad_add_fusion.1.place.refs_2_, bf16[4096,768]{1,0:T(8,128)(2,1)} %refs_3_.9, ...), custom_call_target="tpu_custom_call", output_to_operand_aliasing={{0}: (9, {})} | custom-call | flops 3221225472 | bytes 12582912 | tf_op jit(solution)/shard_map/build/pallas_call | solution.py:252
  36.3 2.9 %collective-permute-done.4.refs_5_ = bf16[512,768]{1,0:T(8,128)(2,1)S(1)} collective-permute-done((bf16[512,768]{1,0:T(8,128)(2,1)S(1)}, bf16[512,768]{1,0:T(8,128)(2,1)S(1)}, u32[]{:S(2)}, u32[]{:S(2)}) %collective-permute-start.4) | collective-permute-done | bytes 786464 | tf_op jit(solution)/shard_map/ppermute | solution.py:207
  39.3 1.1 collective-permute-start.7
  40.4 1.7 collective-permute-start.16
  42.2 6.8 %collective-permute-done.10.refs_8_ = bf16[512,768]{1,0:T(8,128)(2,1)S(1)} collective-permute-done((bf16[512,768]{1,0:T(8,128)(2,1)S(1)}, bf16[512,768]{1,0:T(8,128)(2,1)S(1)}, u32[]{:S(2)}, u32[]{:S(2)}) %collective-permute-start.10) | collective-permute-done | bytes 786464 | tf_op jit(solution)/shard_map/ppermute | solution.py:207
  48.9 3.7 %collective-permute-start.15 = (bf16[512,768]{1,0:T(8,128)(2,1)S(1)}, bf16[512,768]{1,0:T(8,128)(2,1)S(1)}, u32[]{:S(2)}, u32[]{:S(2)}) collective-permute-start(bf16[512,768]{1,0:T(8,128)(2,1)S(1)} %collective-permute-done.10.refs_8_), channel_id=1, source_target_pairs={{0,96},{4,28},{8,104},{12,4},{16,112},{20,12},{24,120},{28,20},{32... | collective-permute-start | bytes 2359304 | tf_op jit(solution)/shard_map/ppermute | solution.py:207
  52.6 0.0 collective-permute-done.11.refs_9_
  52.6 0.1 collective-permute-start.13
  52.7 8.1 %build.7 = (bf16[64,512,512]{2,1,0:T(8,128)(2,1)S(1)}, f32[16,512]{1,0:T(8,128)S(1)}) custom-call(s32[3,64]{1,0:T(4,128)S(1)} %get-tuple-element.32.pairs.refs_0_, s32[17]{0:T(128)S(1)} %get-tuple-element.34.bounds.refs_1_, s32[3]{0:T(128)S(1)} %pad_add_fusion.1.place.refs_2_, bf16[4096,768]{1,0:T(8,128)(2,1)} %refs_3_.9, ...), custom_call_target="tpu_custom_call", output_to_operand_aliasing={{0}: (10, {})} | custom-call | flops 4026531840 | bytes 15728640 | tf_op jit(solution)/shard_map/build/pallas_call | solution.py:252
  60.8 1.8 collective-permute-start.12
  62.6 3.2 %collective-permute-done.15.refs_8_ = bf16[512,768]{1,0:T(8,128)(2,1)S(1)} collective-permute-done((bf16[512,768]{1,0:T(8,128)(2,1)S(1)}, bf16[512,768]{1,0:T(8,128)(2,1)S(1)}, u32[]{:S(2)}, u32[]{:S(2)}) %collective-permute-start.15) | collective-permute-done | bytes 786464 | tf_op jit(solution)/shard_map/ppermute | solution.py:207
  65.8 8.5 %collective-permute-done.13.refs_5_ = bf16[512,768]{1,0:T(8,128)(2,1)S(1)} collective-permute-done((bf16[512,768]{1,0:T(8,128)(2,1)S(1)}, bf16[512,768]{1,0:T(8,128)(2,1)S(1)}, u32[]{:S(2)}, u32[]{:S(2)}) %collective-permute-start.13) | collective-permute-done | bytes 786464 | tf_op jit(solution)/shard_map/ppermute | solution.py:207
  74.3 6.6 %build.8 = (bf16[64,512,512]{2,1,0:T(8,128)(2,1)S(1)}, f32[16,512]{1,0:T(8,128)S(1)}) custom-call(s32[3,64]{1,0:T(4,128)S(1)} %get-tuple-element.32.pairs.refs_0_, s32[17]{0:T(128)S(1)} %get-tuple-element.34.bounds.refs_1_, s32[3]{0:T(128)S(1)} %pad_add_fusion.1.place.refs_2_, bf16[4096,768]{1,0:T(8,128)(2,1)} %refs_3_.9, ...), custom_call_target="tpu_custom_call", output_to_operand_aliasing={{0}: (10, {})} | custom-call | flops 4026531840 | bytes 15728640 | tf_op jit(solution)/shard_map/build/pallas_call | solution.py:252
  80.9 3.3 %build.9 = (bf16[64,512,512]{2,1,0:T(8,128)(2,1)S(1)}, f32[8,16,512]{2,1,0:T(8,128)S(1)}) custom-call(s32[3,64]{1,0:T(4,128)S(1)} %get-tuple-element.32.pairs.refs_0_, s32[17]{0:T(128)S(1)} %get-tuple-element.34.bounds.refs_1_, s32[3]{0:T(128)S(1)} %pad_add_fusion.1.place.refs_2_, bf16[4096,768]{1,0:T(8,128)(2,1)} %refs_3_.9, ...), custom_call_target="tpu_custom_call", output_to_operand_aliasing={{0}: (6, {})} | custom-call | flops 805306368 | bytes 3145728 | tf_op jit(solution)/shard_map/build/pallas_call | solution.py:252
  84.1 12.4 %all_to_all.30.refs_3_ = f32[8,16,512]{2,1,0:T(8,128)S(1)} all-to-all(f32[8,16,512]{2,1,0:T(8,128)S(1)} %get-tuple-element.50), channel_id=1, replica_groups=mesh['y'=4,'x'=4,'core'=2,'z'=4] {'core','z'}, dimensions={0} | all-to-all | bytes 524288 | tf_op jit(solution)/shard_map/all_to_all | solution.py:308
  96.6 2.6 %columns.3 = (f32[16,16,512]{2,1,0:T(8,128)S(1)}, bf16[64,512,512]{2,1,0:T(8,128)(2,1)S(1)}) custom-call(s32[3,64]{1,0:T(4,128)S(1)} %get-tuple-element.32.pairs.refs_0_, s32[17]{0:T(128)S(1)} %get-tuple-element.34.bounds.refs_1_, s32[3]{0:T(128)S(1)} %pad_add_fusion.1.place.refs_2_, ...), custom_call_target="tpu_custom_call", output_to_operand_aliasing={{1}: (4, {})} | custom-call | tf_op jit(solution)/shard_map/columns/pallas_call | solution.py:294
  99.2 19.2 %all_to_all.31.refs_3_ = f32[16,16,512]{2,1,0:T(8,128)S(1)} all-to-all(f32[16,16,512]{2,1,0:T(8,128)S(1)} %get-tuple-element.52), channel_id=1, replica_groups=mesh['y'=4,'x'=4,'core'=2,'z'=4] {'y','x'}, dimensions={0} | all-to-all | bytes 1048576 | tf_op jit(solution)/shard_map/all_to_all | solution.py:311
  118.5 4.0 %rows.2 = (f32[8,16,512]{2,1,0:T(8,128)S(1)}, bf16[64,512,512]{2,1,0:T(8,128)(2,1)S(1)}) custom-call(s32[3,64]{1,0:T(4,128)S(1)} %get-tuple-element.32.pairs.refs_0_, s32[17]{0:T(128)S(1)} %get-tuple-element.34.bounds.refs_1_, s32[3]{0:T(128)S(1)} %pad_add_fusion.1.place.refs_2_, ...), custom_call_target="tpu_custom_call", output_to_operand_aliasing={{1}: (4, {})} | custom-call | tf_op jit(solution)/shard_map/rows/pallas_call | solution.py:294
  122.5 10.2 %all_to_all.32.refs_3_ = f32[8,16,512]{2,1,0:T(8,128)S(1)} all-to-all(f32[8,16,512]{2,1,0:T(8,128)S(1)} %get-tuple-element.54), channel_id=1, replica_groups=mesh['y'=4,'x'=4,'core'=2,'z'=4] {'core','z'}, dimensions={0} | all-to-all | bytes 524288 | tf_op jit(solution)/shard_map/all_to_all | solution.py:308
  132.7 2.6 %columns.4 = (f32[16,16,512]{2,1,0:T(8,128)S(1)}, bf16[64,512,512]{2,1,0:T(8,128)(2,1)S(1)}) custom-call(s32[3,64]{1,0:T(4,128)S(1)} %get-tuple-element.32.pairs.refs_0_, s32[17]{0:T(128)S(1)} %get-tuple-element.34.bounds.refs_1_, s32[3]{0:T(128)S(1)} %pad_add_fusion.1.place.refs_2_, ...), custom_call_target="tpu_custom_call", output_to_operand_aliasing={{1}: (4, {})} | custom-call | tf_op jit(solution)/shard_map/columns/pallas_call | solution.py:294
  135.3 17.9 %all_to_all.33.refs_3_ = f32[16,16,512]{2,1,0:T(8,128)S(1)} all-to-all(f32[16,16,512]{2,1,0:T(8,128)S(1)} %get-tuple-element.56), channel_id=1, replica_groups=mesh['y'=4,'x'=4,'core'=2,'z'=4] {'y','x'}, dimensions={0} | all-to-all | bytes 1048576 | tf_op jit(solution)/shard_map/all_to_all | solution.py:311
  153.2 4.0 %rows.3 = (f32[8,16,512]{2,1,0:T(8,128)S(1)}, bf16[64,512,512]{2,1,0:T(8,128)(2,1)S(1)}) custom-call(s32[3,64]{1,0:T(4,128)S(1)} %get-tuple-element.32.pairs.refs_0_, s32[17]{0:T(128)S(1)} %get-tuple-element.34.bounds.refs_1_, s32[3]{0:T(128)S(1)} %pad_add_fusion.1.place.refs_2_, ...), custom_call_target="tpu_custom_call", output_to_operand_aliasing={{1}: (4, {})} | custom-call | tf_op jit(solution)/shard_map/rows/pallas_call | solution.py:294
  157.2 9.3 %all_to_all.34.refs_3_ = f32[8,16,512]{2,1,0:T(8,128)S(1)} all-to-all(f32[8,16,512]{2,1,0:T(8,128)S(1)} %get-tuple-element.58), channel_id=1, replica_groups=mesh['y'=4,'x'=4,'core'=2,'z'=4] {'core','z'}, dimensions={0} | all-to-all | bytes 524288 | tf_op jit(solution)/shard_map/all_to_all | solution.py:308
  166.5 3.2 %columns.5 = (f32[16,4,128]{2,1,0:T(4,128)S(1)}, f32[32,128]{1,0:T(8,128)}) custom-call(s32[3,64]{1,0:T(4,128)S(1)} %get-tuple-element.32.pairs.refs_0_, s32[17]{0:T(128)S(1)} %get-tuple-element.34.bounds.refs_1_, s32[3]{0:T(128)S(1)} %pad_add_fusion.1.place.refs_2_, f32[8,16,512]{2,1,0:T(8,128)S(1)} %all_to_all.34.refs_3_, ...), custom_call_target="tpu_custom_call" | custom-call | tf_op jit(solution)/shard_map/columns/pallas_call | solution.py:294
  169.7 12.6 %all_to_all.35 = f32[16,4,128]{2,1,0:T(4,128)S(1)} all-to-all(f32[16,4,128]{2,1,0:T(4,128)S(1)} %get-tuple-element.61), channel_id=1, replica_groups=mesh['y'=4,'x'=4,'core'=2,'z'=4] {'y','x'}, dimensions={0} | all-to-all | bytes 65536 | tf_op jit(solution)/shard_map/all_to_all | solution.py:313
  182.4 0.6 log_bitcast_fusion
  (15 shorter events, 0.1 us)
Async XLA Ops:
  0.6 28.3 %copy-start = (bf16[512,768]{1,0:T(8,128)(2,1)S(1)}, bf16[512,768]{1,0:T(8,128)(2,1)}, u32[]{:S(2)}) copy-start(bf16[512,768]{1,0:T(8,128)(2,1)} %refs_5_.1) | copy-start | bytes 2359300
  0.6 28.1 %collective-permute-start.3 = (bf16[4096,768]{1,0:T(8,128)(2,1)}, bf16[4096,768]{1,0:T(8,128)(2,1)}, u32[]{:S(2)}, u32[]{:S(2)}) collective-permute-start(bf16[4096,768]{1,0:T(8,128)(2,1)} %refs_3_.9), channel_id=1, source_target_pairs={{0,4},{4,0},{1,5},{5,1},{2,6},{6,2},{3,7},{7,3},{8,12},{12,8},{9,1... | collective-permute-start | bytes 18874376 | tf_op jit(solution)/shard_map/ppermute | solution.py:218
  0.7 18.5 %collective-permute-start.1 = (bf16[512,768]{1,0:T(8,128)(2,1)}, bf16[512,768]{1,0:T(8,128)(2,1)S(1)}, u32[]{:S(2)}, u32[]{:S(2)}) collective-permute-start(bf16[512,768]{1,0:T(8,128)(2,1)} %refs_5_.1), channel_id=1, source_target_pairs={{0,8},{4,36},{8,16},{12,44},{16,24},{20,52},{24,0},{28,60},{32,40}... | collective-permute-start | bytes 2359304 | tf_op jit(solution)/shard_map/ppermute | solution.py:207
  2.4 16.9 %collective-permute-start.2 = (bf16[512,768]{1,0:T(8,128)(2,1)}, bf16[512,768]{1,0:T(8,128)(2,1)S(1)}, u32[]{:S(2)}, u32[]{:S(2)}) collective-permute-start(bf16[512,768]{1,0:T(8,128)(2,1)} %refs_5_.1), channel_id=1, source_target_pairs={{0,24},{4,100},{8,0},{12,108},{16,8},{20,116},{24,16},{28,124},{32... | collective-permute-start | bytes 2359304 | tf_op jit(solution)/shard_map/ppermute | solution.py:207
  5.5 5.4 %collective-permute-start = (s32[1,128]{1,0:T(1,128)S(1)}, s32[1,128]{1,0:T(1,128)S(1)}, u32[]{:S(2)}, u32[]{:S(2)}) collective-permute-start(s32[1,128]{1,0:T(1,128)S(1)} %pad_add_fusion), channel_id=1, source_target_pairs={{0,4},{4,0},{1,5},{5,1},{2,6},{6,2},{3,7},{7,3},{8,12},{12,8},{9,1... | collective-permute-start | bytes 1544 | tf_op jit(solution)/shard_map/ppermute | solution.py:219
  5.5 18.1 %collective-permute-start.5 = (bf16[512,768]{1,0:T(8,128)(2,1)}, bf16[512,768]{1,0:T(8,128)(2,1)S(1)}, u32[]{:S(2)}, u32[]{:S(2)}) collective-permute-start(bf16[512,768]{1,0:T(8,128)(2,1)} %refs_5_.1), channel_id=1, source_target_pairs={{0,32},{4,12},{8,40},{12,20},{16,48},{20,28},{24,56},{28,4},{32,64... | collective-permute-start | bytes 2359304 | tf_op jit(solution)/shard_map/ppermute | solution.py:207
  10.8 16.0 %collective-permute-start.6 = (bf16[512,768]{1,0:T(8,128)(2,1)}, bf16[512,768]{1,0:T(8,128)(2,1)}, u32[]{:S(2)}, u32[]{:S(2)}) collective-permute-start(bf16[512,768]{1,0:T(8,128)(2,1)} %refs_5_.1), channel_id=1, source_target_pairs={{0,96},{4,28},{8,104},{12,4},{16,112},{20,12},{24,120},{28,20},{32... | collective-permute-start | bytes 2359304 | tf_op jit(solution)/shard_map/ppermute | solution.py:207
  14.8 0.7 copy-start.1
  19.3 20.0 %collective-permute-start.4 = (bf16[512,768]{1,0:T(8,128)(2,1)S(1)}, bf16[512,768]{1,0:T(8,128)(2,1)S(1)}, u32[]{:S(2)}, u32[]{:S(2)}) collective-permute-start(bf16[512,768]{1,0:T(8,128)(2,1)S(1)} %collective-permute-done.2.refs_6_), channel_id=1, source_target_pairs={{0,24},{4,100},{8,0},{12,108},{16,8},{20,116},{24,16},{28,124},{32... | collective-permute-start | bytes 2359304 | tf_op jit(solution)/shard_map/ppermute | solution.py:207
  23.5 16.9 %collective-permute-start.9 = (bf16[512,768]{1,0:T(8,128)(2,1)S(1)}, bf16[512,768]{1,0:T(8,128)(2,1)S(1)}, u32[]{:S(2)}, u32[]{:S(2)}) collective-permute-start(bf16[512,768]{1,0:T(8,128)(2,1)S(1)} %collective-permute-done.2.refs_6_), channel_id=1, source_target_pairs={{0,32},{4,12},{8,40},{12,20},{16,48},{20,28},{24,56},{28,4},{32,64... | collective-permute-start | bytes 2359304 | tf_op jit(solution)/shard_map/ppermute | solution.py:207
  23.6 29.0 %collective-permute-start.11 = (bf16[512,768]{1,0:T(8,128)(2,1)S(1)}, bf16[512,768]{1,0:T(8,128)(2,1)S(1)}, u32[]{:S(2)}, u32[]{:S(2)}) collective-permute-start(bf16[512,768]{1,0:T(8,128)(2,1)S(1)} %collective-permute-done.2.refs_6_), channel_id=1, source_target_pairs={{0,96},{4,28},{8,104},{12,4},{16,112},{20,12},{24,120},{28,20},{32... | collective-permute-start | bytes 2359304 | tf_op jit(solution)/shard_map/ppermute | solution.py:207
  26.9 22.1 %collective-permute-start.10 = (bf16[512,768]{1,0:T(8,128)(2,1)S(1)}, bf16[512,768]{1,0:T(8,128)(2,1)S(1)}, u32[]{:S(2)}, u32[]{:S(2)}) collective-permute-start(bf16[512,768]{1,0:T(8,128)(2,1)S(1)} %collective-permute-done.1.refs_5_), channel_id=1, source_target_pairs={{0,96},{4,28},{8,104},{12,4},{16,112},{20,12},{24,120},{28,20},{32... | collective-permute-start | bytes 2359304 | tf_op jit(solution)/shard_map/ppermute | solution.py:207
  28.8 23.9 %collective-permute-start.8 = (bf16[512,768]{1,0:T(8,128)(2,1)S(1)}, bf16[512,768]{1,0:T(8,128)(2,1)S(1)}, u32[]{:S(2)}, u32[]{:S(2)}) collective-permute-start(bf16[512,768]{1,0:T(8,128)(2,1)S(1)} %collective-permute-done.1.refs_5_), channel_id=1, source_target_pairs={{0,32},{4,12},{8,40},{12,20},{16,48},{20,28},{24,56},{28,4},{32,64... | collective-permute-start | bytes 2359304 | tf_op jit(solution)/shard_map/ppermute | solution.py:207
  39.3 21.5 %collective-permute-start.7 = (bf16[512,768]{1,0:T(8,128)(2,1)S(1)}, bf16[512,768]{1,0:T(8,128)(2,1)S(1)}, u32[]{:S(2)}, u32[]{:S(2)}) collective-permute-start(bf16[512,768]{1,0:T(8,128)(2,1)S(1)} %collective-permute-done.4.refs_5_), channel_id=1, source_target_pairs={{0,96},{4,28},{8,104},{12,4},{16,112},{20,12},{24,120},{28,20},{32... | collective-permute-start | bytes 2359304 | tf_op jit(solution)/shard_map/ppermute | solution.py:207
  40.4 22.2 %collective-permute-start.16 = (bf16[512,768]{1,0:T(8,128)(2,1)S(1)}, bf16[512,768]{1,0:T(8,128)(2,1)S(1)}, u32[]{:S(2)}, u32[]{:S(2)}) collective-permute-start(bf16[512,768]{1,0:T(8,128)(2,1)S(1)} %collective-permute-done.9.refs_7_), channel_id=1, source_target_pairs={{0,32},{4,12},{8,40},{12,20},{16,48},{20,28},{24,56},{28,4},{32,64... | collective-permute-start | bytes 2359304 | tf_op jit(solution)/shard_map/ppermute | solution.py:207
  48.9 16.9 %collective-permute-start.15 = (bf16[512,768]{1,0:T(8,128)(2,1)S(1)}, bf16[512,768]{1,0:T(8,128)(2,1)S(1)}, u32[]{:S(2)}, u32[]{:S(2)}) collective-permute-start(bf16[512,768]{1,0:T(8,128)(2,1)S(1)} %collective-permute-done.10.refs_8_), channel_id=1, source_target_pairs={{0,96},{4,28},{8,104},{12,4},{16,112},{20,12},{24,120},{28,20},{32... | collective-permute-start | bytes 2359304 | tf_op jit(solution)/shard_map/ppermute | solution.py:207
  52.6 21.6 %collective-permute-start.14 = (bf16[512,768]{1,0:T(8,128)(2,1)S(1)}, bf16[512,768]{1,0:T(8,128)(2,1)S(1)}, u32[]{:S(2)}, u32[]{:S(2)}) collective-permute-start(bf16[512,768]{1,0:T(8,128)(2,1)S(1)} %collective-permute-done.4.refs_5_), channel_id=1, source_target_pairs={{0,32},{4,12},{8,40},{12,20},{16,48},{20,28},{24,56},{28,4},{32,64... | collective-permute-start | bytes 2359304 | tf_op jit(solution)/shard_map/ppermute | solution.py:207
  52.6 21.6 %collective-permute-start.13 = (bf16[512,768]{1,0:T(8,128)(2,1)S(1)}, bf16[512,768]{1,0:T(8,128)(2,1)S(1)}, u32[]{:S(2)}, u32[]{:S(2)}) collective-permute-start(bf16[512,768]{1,0:T(8,128)(2,1)S(1)} %collective-permute-done.5.refs_7_), channel_id=1, source_target_pairs={{0,32},{4,12},{8,40},{12,20},{16,48},{20,28},{24,56},{28,4},{32,64... | collective-permute-start | bytes 2359304 | tf_op jit(solution)/shard_map/ppermute | solution.py:207
  60.8 20.1 %collective-permute-start.12 = (bf16[512,768]{1,0:T(8,128)(2,1)S(1)}, bf16[512,768]{1,0:T(8,128)(2,1)S(1)}, u32[]{:S(2)}, u32[]{:S(2)}) collective-permute-start(bf16[512,768]{1,0:T(8,128)(2,1)S(1)} %collective-permute-done.7.refs_7_), channel_id=1, source_target_pairs={{0,96},{4,28},{8,104},{12,4},{16,112},{20,12},{24,120},{28,20},{32... | collective-permute-start | bytes 2359304 | tf_op jit(solution)/shard_map/ppermute | solution.py:207

commit v6 on v5

--- a/solution.py
+++ b/solution.py
@@ -28,11 +28,11 @@
 
 
 ORDER = (
-    ((0, 0),),
-    ((3, 0), (1, 0), (0, 3), (0, 1)),
-    ((2, 0), (3, 3), (1, 3), (3, 1), (1, 1)),
-    ((0, 2), (2, 3), (2, 1), (3, 2), (1, 2)),
-    ((2, 2),),
+    ((0, 0), (3, 0), (1, 0), (0, 3), (0, 1)),
+    ((2, 0), (1, 3)),
+    ((3, 1), (1, 1), (3, 3)),
+    ((2, 1), (1, 2), (3, 2)),
+    ((0, 2), (2, 3), (2, 2)),
 )
 
 
@@ -272,20 +272,23 @@
         )(pairs, bounds, place, table_a, a_other, *group, store, kv)
 
     kv = jnp.zeros((NC * ABLK, TILE), F32)
-    store, kv = build(0, (table_b,), store, kv)
     left, right, bounds = lax.optimization_barrier((left, right, bounds))
     first_two = go(right, True, -1)
     left_down, right_down = go(left, False, 1), go(right, False, 1)
     left_up, right_up = go(left, False, -1), go(right, False, -1)
-    store, kv = build(1, (left, right, down, up), store, kv)
-    first_two, down, kv = lax.optimization_barrier((first_two, down, kv))
+    store, kv = build(0, (table_b, left, right, down, up), store, kv)
+    first_two, right_down, down, kv = lax.optimization_barrier((first_two, right_down, down, kv))
     two_up, two_down, second_two = go(first_two, False, -1), go(first_two, False, 1), go(down, False, 1)
-    left_two, right_two = go(left_up, False, -1), go(right_down, False, 1)
-    store, kv = build(5, (first_two, left_down, right_down, left_up, right_up), store, kv)
+    right_two = go(right_down, False, 1)
+    store, kv = build(5, (first_two, right_down), store, kv)
+    left_up, right_up, left_down, kv = lax.optimization_barrier((left_up, right_up, left_down, kv))
+    left_two = go(left_up, False, -1)
+    store, kv = build(7, (left_up, right_up, left_down), store, kv)
     two_up, kv = lax.optimization_barrier((two_up, kv))
     both_two = go(two_up, False, -1)
-    store, kv = build(10, (second_two, two_down, two_up, left_two, right_two), store, kv)
-    store, kv = build(15, (both_two,), store, kv)
+    store, kv = build(10, (two_up, right_two, left_two), store, kv)
+    second_two, two_down, both_two, kv = lax.optimization_barrier((second_two, two_down, both_two, kv))
+    store, kv = build(13, (second_two, two_down, both_two), store, kv)
 
     def half(over_rows, parts, copies, store):
         last = copies == 0

time: 182 us -> 179 us (0.984)
  waiting for transfers between devices: 25 us -> 17.4 us
  Pallas kernels: 46.1 us -> 40.9 us
  starting transfers between devices: 25.7 us -> 30.3 us
  blocking collectives: 81.7 us -> 86.1 us
    ppermute x15, waiting for transfers between devices: 21.4 us -> 13.7 us  [go(): return lax.ppermute(block, ('y', 'x', 'core'), moves(first, shift))]
    ppermute x15, starting transfers between devices: 25.6 us -> 30.2 us  [go(): return lax.ppermute(block, ('y', 'x', 'core'), moves(first, shift))]
    pallas_call x5, Pallas kernels: 16.4 us -> 13.1 us  [half(): pl.pallas_call(lambda *refs: pass_kernel(over_rows, last, *refs), out_sha...]
    all_to_all x2, blocking collectives: 37.1 us -> 40.4 us  [on_device(): ktu_parts = lax.all_to_all(ktu, ('y', 'x'), 0, 0, tiled=True)]
  transfers between devices with their start and end apart: 17 -> 17, of which waited for: 5 -> 7; matrix products, arithmetic and copies ran while one was open for 1% -> 1% of each run, Pallas kernels for 14% -> 13%
where the time goes in v6:
time: 179 us
  blocking collectives  86.1 us (48%)
  Pallas kernels  40.9 us (23%)
  starting transfers between devices  30.3 us (17%)
  waiting for transfers between devices  17.4 us (10%)
  other arithmetic  2.26 us (1%)
    all_to_all x2, blocking collectives, on_device(): ktu_parts = lax.all_to_all(ktu, ('y', 'x'), 0, 0, tiled=True)  40.4 us
    all_to_all x3, blocking collectives, on_device(): kv_parts = lax.all_to_all(kv, ('core', 'z'), 0, 0, tiled=True)  33.5 us
    ppermute x15, starting transfers between devices, go(): return lax.ppermute(block, ('y', 'x', 'core'), moves(first, shift))  30.2 us
    pallas_call x5, Pallas kernels, build(): pl.pallas_call(lambda *refs: build_kernel(scale, first, blocks, last, *re...  23.8 us
    ppermute x15, waiting for transfers between devices, go(): return lax.ppermute(block, ('y', 'x', 'core'), moves(first, shift))  13.7 us
    pallas_call x5, Pallas kernels, half(): pl.pallas_call(lambda *refs: pass_kernel(over_rows, last, *refs), out_sha...  13.1 us
    all_to_all x1, blocking collectives, on_device(): mine = lax.all_to_all(ktu, ('y', 'x'), 0, 0, tiled=True)  12.1 us
    ppermute x1, waiting for transfers between devices, on_device(): other = lax.ppermute(own, 'core', swap)  3.62 us
  transfers between devices with their start and end apart: 17, of which 7 were waited for; matrix products, arithmetic and copies ran while one was open for 1% of the time, Pallas kernels for 13%

profile of v6, /device:TPU:0, one launch (start us, length us, event | category | flops | bytes accessed | tf_op | source)
XLA Modules:
  0.0 179.1 jit_solution(16793748304289962530)
XLA Ops:
  0.6 0.0 copy-start
  0.6 0.1 collective-permute-start.3
  0.7 1.6 collective-permute-start.1
  2.4 1.7 collective-permute-start.2
  4.7 0.8 pad_add_fusion
  5.5 0.0 collective-permute-start
  5.5 1.7 collective-permute-start.6
  7.2 3.6 %collective-permute-done = s32[1,128]{1,0:T(1,128)S(1)} collective-permute-done((s32[1,128]{1,0:T(1,128)S(1)}, s32[1,128]{1,0:T(1,128)S(1)}, u32[]{:S(2)}, u32[]{:S(2)}) %collective-permute-start) | collective-permute-done | bytes 544 | tf_op jit(solution)/shard_map/ppermute | solution.py:219
  10.8 3.1 %collective-permute-start.7 = (bf16[512,768]{1,0:T(8,128)(2,1)}, bf16[512,768]{1,0:T(8,128)(2,1)}, u32[]{:S(2)}, u32[]{:S(2)}) collective-permute-start(bf16[512,768]{1,0:T(8,128)(2,1)} %refs_5_.1), channel_id=1, source_target_pairs={{0,96},{4,28},{8,104},{12,4},{16,112},{20,12},{24,120},{28,20},{32... | collective-permute-start | bytes 2359304 | tf_op jit(solution)/shard_map/ppermute | solution.py:207
  13.9 0.1 pad_add_fusion.1.place.refs_2_
  14.0 0.8 add_select_fusion.lists
  14.8 0.7 copy-done.1
  15.5 3.5 %plan.1 = (s32[3,64]{1,0:T(4,128)S(1)}, s32[17]{0:T(128)S(1)}) custom-call(s32[2,128]{1,0:T(2,128)S(1)} %add_select_fusion.lists, s32[3]{0:T(128)S(1)} %pad_add_fusion.1.place.refs_2_, s32[16]{0:T(128)S(1)} %copy-done.1), custom_call_target="tpu_custom_call" | custom-call | tf_op jit(solution)/shard_map/plan/pallas_call | solution.py:228
  19.0 0.0 collective-permute-done.1.refs_6_
  19.0 0.0 collective-permute-done.2.refs_7_
  19.0 2.4 %collective-permute-start.4 = (bf16[512,768]{1,0:T(8,128)(2,1)S(1)}, bf16[512,768]{1,0:T(8,128)(2,1)S(1)}, u32[]{:S(2)}, u32[]{:S(2)}) collective-permute-start(bf16[512,768]{1,0:T(8,128)(2,1)S(1)} %collective-permute-done.2.refs_7_), channel_id=1, source_target_pairs={{0,24},{4,100},{8,0},{12,108},{16,8},{20,116},{24,16},{28,124},{32... | collective-permute-start | bytes 2359304 | tf_op jit(solution)/shard_map/ppermute | solution.py:207
  21.4 1.4 collective-permute-start.5
  22.8 0.6 room.1.refs_10_
  23.4 1.9 %collective-permute-start.12 = (bf16[512,768]{1,0:T(8,128)(2,1)S(1)}, bf16[512,768]{1,0:T(8,128)(2,1)S(1)}, u32[]{:S(2)}, u32[]{:S(2)}) collective-permute-start(bf16[512,768]{1,0:T(8,128)(2,1)S(1)} %collective-permute-done.2.refs_7_), channel_id=1, source_target_pairs={{0,96},{4,28},{8,104},{12,4},{16,112},{20,12},{24,120},{28,20},{32... | collective-permute-start | bytes 2359304 | tf_op jit(solution)/shard_map/ppermute | solution.py:207
  25.3 0.2 collective-permute-done.7.refs_9_
  25.5 3.7 %collective-permute-start.11 = (bf16[512,768]{1,0:T(8,128)(2,1)S(1)}, bf16[512,768]{1,0:T(8,128)(2,1)S(1)}, u32[]{:S(2)}, u32[]{:S(2)}) collective-permute-start(bf16[512,768]{1,0:T(8,128)(2,1)S(1)} %collective-permute-done.1.refs_6_), channel_id=1, source_target_pairs={{0,96},{4,28},{8,104},{12,4},{16,112},{20,12},{24,120},{28,20},{32... | collective-permute-start | bytes 2359304 | tf_op jit(solution)/shard_map/ppermute | solution.py:207
  29.2 6.8 %build.5 = (bf16[64,512,512]{2,1,0:T(8,128)(2,1)S(1)}, f32[16,512]{1,0:T(8,128)S(1)}) custom-call(s32[3,64]{1,0:T(4,128)S(1)} %get-tuple-element.41.pairs.refs_0_, s32[17]{0:T(128)S(1)} %get-tuple-element.43.bounds.refs_1_, s32[3]{0:T(128)S(1)} %pad_add_fusion.1.place.refs_2_, bf16[4096,768]{1,0:T(8,128)(2,1)} %refs_3_.9, ...), custom_call_target="tpu_custom_call", output_to_operand_aliasing={{0}: (10, {})} | custom-call | flops 4026531840 | bytes 15728640 | tf_op jit(solution)/shard_map/build/pallas_call | solution.py:252
  36.0 2.9 %collective-permute-done.4.refs_5_ = bf16[512,768]{1,0:T(8,128)(2,1)S(1)} collective-permute-done((bf16[512,768]{1,0:T(8,128)(2,1)S(1)}, bf16[512,768]{1,0:T(8,128)(2,1)S(1)}, u32[]{:S(2)}, u32[]{:S(2)}) %collective-permute-start.4) | collective-permute-done | bytes 786464 | tf_op jit(solution)/shard_map/ppermute | solution.py:207
  38.9 1.5 collective-permute-start.10
  40.4 0.5 collective-permute-start.15
  40.9 3.5 %build.6 = (bf16[64,512,512]{2,1,0:T(8,128)(2,1)S(1)}, f32[16,512]{1,0:T(8,128)S(1)}) custom-call(s32[3,64]{1,0:T(4,128)S(1)} %get-tuple-element.41.pairs.refs_0_, s32[17]{0:T(128)S(1)} %get-tuple-element.43.bounds.refs_1_, s32[3]{0:T(128)S(1)} %pad_add_fusion.1.place.refs_2_, bf16[4096,768]{1,0:T(8,128)(2,1)} %refs_3_.9, ...), custom_call_target="tpu_custom_call", output_to_operand_aliasing={{0}: (7, {})} | custom-call | flops 1610612736 | bytes 6291456 | tf_op jit(solution)/shard_map/build/pallas_call | solution.py:252
  44.5 3.3 %collective-permute-start.9 = (bf16[512,768]{1,0:T(8,128)(2,1)S(1)}, bf16[512,768]{1,0:T(8,128)(2,1)S(1)}, u32[]{:S(2)}, u32[]{:S(2)}) collective-permute-start(bf16[512,768]{1,0:T(8,128)(2,1)S(1)} %collective-permute-done.4.refs_5_), channel_id=1, source_target_pairs={{0,32},{4,12},{8,40},{12,20},{16,48},{20,28},{24,56},{28,4},{32,64... | collective-permute-start | bytes 2359304 | tf_op jit(solution)/shard_map/ppermute | solution.py:207
  47.8 1.2 collective-permute-done.11.refs_5_
  48.9 3.7 %collective-permute-start.16 = (bf16[512,768]{1,0:T(8,128)(2,1)S(1)}, bf16[512,768]{1,0:T(8,128)(2,1)S(1)}, u32[]{:S(2)}, u32[]{:S(2)}) collective-permute-start(bf16[512,768]{1,0:T(8,128)(2,1)S(1)} %collective-permute-done.11.refs_5_), channel_id=1, source_target_pairs={{0,96},{4,28},{8,104},{12,4},{16,112},{20,12},{24,120},{28,20},{32... | collective-permute-start | bytes 2359304 | tf_op jit(solution)/shard_map/ppermute | solution.py:207
  52.6 3.4 %build.7 = (bf16[64,512,512]{2,1,0:T(8,128)(2,1)S(1)}, f32[16,512]{1,0:T(8,128)S(1)}) custom-call(s32[3,64]{1,0:T(4,128)S(1)} %get-tuple-element.41.pairs.refs_0_, s32[17]{0:T(128)S(1)} %get-tuple-element.43.bounds.refs_1_, s32[3]{0:T(128)S(1)} %pad_add_fusion.1.place.refs_2_, bf16[4096,768]{1,0:T(8,128)(2,1)} %refs_3_.9, ...), custom_call_target="tpu_custom_call", output_to_operand_aliasing={{0}: (8, {})} | custom-call | flops 2415919104 | bytes 9437184 | tf_op jit(solution)/shard_map/build/pallas_call | solution.py:252
  56.0 1.3 collective-permute-done.10.refs_5_
  57.4 3.7 %collective-permute-start.14 = (bf16[512,768]{1,0:T(8,128)(2,1)S(1)}, bf16[512,768]{1,0:T(8,128)(2,1)S(1)}, u32[]{:S(2)}, u32[]{:S(2)}) collective-permute-start(bf16[512,768]{1,0:T(8,128)(2,1)S(1)} %collective-permute-done.10.refs_5_), channel_id=1, source_target_pairs={{0,96},{4,28},{8,104},{12,4},{16,112},{20,12},{24,120},{28,20},{32... | collective-permute-start | bytes 2359304 | tf_op jit(solution)/shard_map/ppermute | solution.py:207
  61.1 4.7 %collective-permute-done.16.refs_7_ = bf16[512,768]{1,0:T(8,128)(2,1)S(1)} collective-permute-done((bf16[512,768]{1,0:T(8,128)(2,1)S(1)}, bf16[512,768]{1,0:T(8,128)(2,1)S(1)}, u32[]{:S(2)}, u32[]{:S(2)}) %collective-permute-start.16) | collective-permute-done | bytes 786464 | tf_op jit(solution)/shard_map/ppermute | solution.py:207
  65.8 5.0 %build.8 = (bf16[64,512,512]{2,1,0:T(8,128)(2,1)S(1)}, f32[16,512]{1,0:T(8,128)S(1)}) custom-call(s32[3,64]{1,0:T(4,128)S(1)} %get-tuple-element.41.pairs.refs_0_, s32[17]{0:T(128)S(1)} %get-tuple-element.43.bounds.refs_1_, s32[3]{0:T(128)S(1)} %pad_add_fusion.1.place.refs_2_, bf16[4096,768]{1,0:T(8,128)(2,1)} %refs_3_.9, ...), custom_call_target="tpu_custom_call", output_to_operand_aliasing={{0}: (8, {})} | custom-call | flops 2415919104 | bytes 9437184 | tf_op jit(solution)/shard_map/build/pallas_call | solution.py:252
  70.9 3.4 %collective-permute-done.14.refs_7_ = bf16[512,768]{1,0:T(8,128)(2,1)S(1)} collective-permute-done((bf16[512,768]{1,0:T(8,128)(2,1)S(1)}, bf16[512,768]{1,0:T(8,128)(2,1)S(1)}, u32[]{:S(2)}, u32[]{:S(2)}) %collective-permute-start.14) | collective-permute-done | bytes 786464 | tf_op jit(solution)/shard_map/ppermute | solution.py:207
  74.2 5.0 %build.9 = (bf16[64,512,512]{2,1,0:T(8,128)(2,1)S(1)}, f32[8,16,512]{2,1,0:T(8,128)S(1)}) custom-call(s32[3,64]{1,0:T(4,128)S(1)} %get-tuple-element.41.pairs.refs_0_, s32[17]{0:T(128)S(1)} %get-tuple-element.43.bounds.refs_1_, s32[3]{0:T(128)S(1)} %pad_add_fusion.1.place.refs_2_, bf16[4096,768]{1,0:T(8,128)(2,1)} %refs_3_.9, ...), custom_call_target="tpu_custom_call", output_to_operand_aliasing={{0}: (8, {})} | custom-call | flops 2415919104 | bytes 9437184 | tf_op jit(solution)/shard_map/build/pallas_call | solution.py:252
  79.3 12.3 %all_to_all.30.refs_3_ = f32[8,16,512]{2,1,0:T(8,128)S(1)} all-to-all(f32[8,16,512]{2,1,0:T(8,128)S(1)} %get-tuple-element.68), channel_id=1, replica_groups=mesh['y'=4,'x'=4,'core'=2,'z'=4] {'core','z'}, dimensions={0} | all-to-all | bytes 524288 | tf_op jit(solution)/shard_map/all_to_all | solution.py:311
  91.5 2.0 %columns.3 = (f32[16,16,512]{2,1,0:T(8,128)S(1)}, bf16[64,512,512]{2,1,0:T(8,128)(2,1)S(1)}) custom-call(s32[3,64]{1,0:T(4,128)S(1)} %get-tuple-element.41.pairs.refs_0_, s32[17]{0:T(128)S(1)} %get-tuple-element.43.bounds.refs_1_, s32[3]{0:T(128)S(1)} %pad_add_fusion.1.place.refs_2_, ...), custom_call_target="tpu_custom_call", output_to_operand_aliasing={{1}: (4, {})} | custom-call | tf_op jit(solution)/shard_map/columns/pallas_call | solution.py:297
  93.5 24.0 %all_to_all.31.refs_3_ = f32[16,16,512]{2,1,0:T(8,128)S(1)} all-to-all(f32[16,16,512]{2,1,0:T(8,128)S(1)} %get-tuple-element.70), channel_id=1, replica_groups=mesh['y'=4,'x'=4,'core'=2,'z'=4] {'y','x'}, dimensions={0} | all-to-all | bytes 1048576 | tf_op jit(solution)/shard_map/all_to_all | solution.py:314
  117.6 3.3 %rows.2 = (f32[8,16,512]{2,1,0:T(8,128)S(1)}, bf16[64,512,512]{2,1,0:T(8,128)(2,1)S(1)}) custom-call(s32[3,64]{1,0:T(4,128)S(1)} %get-tuple-element.41.pairs.refs_0_, s32[17]{0:T(128)S(1)} %get-tuple-element.43.bounds.refs_1_, s32[3]{0:T(128)S(1)} %pad_add_fusion.1.place.refs_2_, ...), custom_call_target="tpu_custom_call", output_to_operand_aliasing={{1}: (4, {})} | custom-call | tf_op jit(solution)/shard_map/rows/pallas_call | solution.py:297
  120.9 11.1 %all_to_all.32.refs_3_ = f32[8,16,512]{2,1,0:T(8,128)S(1)} all-to-all(f32[8,16,512]{2,1,0:T(8,128)S(1)} %get-tuple-element.72), channel_id=1, replica_groups=mesh['y'=4,'x'=4,'core'=2,'z'=4] {'core','z'}, dimensions={0} | all-to-all | bytes 524288 | tf_op jit(solution)/shard_map/all_to_all | solution.py:311
  132.0 2.0 %columns.4 = (f32[16,16,512]{2,1,0:T(8,128)S(1)}, bf16[64,512,512]{2,1,0:T(8,128)(2,1)S(1)}) custom-call(s32[3,64]{1,0:T(4,128)S(1)} %get-tuple-element.41.pairs.refs_0_, s32[17]{0:T(128)S(1)} %get-tuple-element.43.bounds.refs_1_, s32[3]{0:T(128)S(1)} %pad_add_fusion.1.place.refs_2_, ...), custom_call_target="tpu_custom_call", output_to_operand_aliasing={{1}: (4, {})} | custom-call | tf_op jit(solution)/shard_map/columns/pallas_call | solution.py:297
  134.0 16.4 %all_to_all.33.refs_3_ = f32[16,16,512]{2,1,0:T(8,128)S(1)} all-to-all(f32[16,16,512]{2,1,0:T(8,128)S(1)} %get-tuple-element.74), channel_id=1, replica_groups=mesh['y'=4,'x'=4,'core'=2,'z'=4] {'y','x'}, dimensions={0} | all-to-all | bytes 1048576 | tf_op jit(solution)/shard_map/all_to_all | solution.py:314
  150.3 3.3 %rows.3 = (f32[8,16,512]{2,1,0:T(8,128)S(1)}, bf16[64,512,512]{2,1,0:T(8,128)(2,1)S(1)}) custom-call(s32[3,64]{1,0:T(4,128)S(1)} %get-tuple-element.41.pairs.refs_0_, s32[17]{0:T(128)S(1)} %get-tuple-element.43.bounds.refs_1_, s32[3]{0:T(128)S(1)} %pad_add_fusion.1.place.refs_2_, ...), custom_call_target="tpu_custom_call", output_to_operand_aliasing={{1}: (4, {})} | custom-call | tf_op jit(solution)/shard_map/rows/pallas_call | solution.py:297
  153.6 10.2 %all_to_all.34.refs_3_ = f32[8,16,512]{2,1,0:T(8,128)S(1)} all-to-all(f32[8,16,512]{2,1,0:T(8,128)S(1)} %get-tuple-element.76), channel_id=1, replica_groups=mesh['y'=4,'x'=4,'core'=2,'z'=4] {'core','z'}, dimensions={0} | all-to-all | bytes 524288 | tf_op jit(solution)/shard_map/all_to_all | solution.py:311
  163.8 2.5 %columns.5 = (f32[16,4,128]{2,1,0:T(4,128)S(1)}, f32[32,128]{1,0:T(8,128)}) custom-call(s32[3,64]{1,0:T(4,128)S(1)} %get-tuple-element.41.pairs.refs_0_, s32[17]{0:T(128)S(1)} %get-tuple-element.43.bounds.refs_1_, s32[3]{0:T(128)S(1)} %pad_add_fusion.1.place.refs_2_, f32[8,16,512]{2,1,0:T(8,128)S(1)} %all_to_all.34.refs_3_, ...), custom_call_target="tpu_custom_call" | custom-call | tf_op jit(solution)/shard_map/columns/pallas_call | solution.py:297
  166.4 12.1 %all_to_all.35 = f32[16,4,128]{2,1,0:T(4,128)S(1)} all-to-all(f32[16,4,128]{2,1,0:T(4,128)S(1)} %get-tuple-element.79), channel_id=1, replica_groups=mesh['y'=4,'x'=4,'core'=2,'z'=4] {'y','x'}, dimensions={0} | all-to-all | bytes 65536 | tf_op jit(solution)/shard_map/all_to_all | solution.py:316
  178.5 0.6 log_bitcast_fusion
  (15 shorter events, 0.1 us)
Async XLA Ops:
  0.6 28.6 %copy-start = (bf16[512,768]{1,0:T(8,128)(2,1)S(1)}, bf16[512,768]{1,0:T(8,128)(2,1)}, u32[]{:S(2)}) copy-start(bf16[512,768]{1,0:T(8,128)(2,1)} %refs_5_.1) | copy-start | bytes 2359300
  0.6 28.6 %collective-permute-start.3 = (bf16[4096,768]{1,0:T(8,128)(2,1)}, bf16[4096,768]{1,0:T(8,128)(2,1)}, u32[]{:S(2)}, u32[]{:S(2)}) collective-permute-start(bf16[4096,768]{1,0:T(8,128)(2,1)} %refs_3_.9), channel_id=1, source_target_pairs={{0,4},{4,0},{1,5},{5,1},{2,6},{6,2},{3,7},{7,3},{8,12},{12,8},{9,1... | collective-permute-start | bytes 18874376 | tf_op jit(solution)/shard_map/ppermute | solution.py:218
  0.7 18.2 %collective-permute-start.1 = (bf16[512,768]{1,0:T(8,128)(2,1)}, bf16[512,768]{1,0:T(8,128)(2,1)S(1)}, u32[]{:S(2)}, u32[]{:S(2)}) collective-permute-start(bf16[512,768]{1,0:T(8,128)(2,1)} %refs_5_.1), channel_id=1, source_target_pairs={{0,8},{4,36},{8,16},{12,44},{16,24},{20,52},{24,0},{28,60},{32,40}... | collective-permute-start | bytes 2359304 | tf_op jit(solution)/shard_map/ppermute | solution.py:207
  2.4 16.6 %collective-permute-start.2 = (bf16[512,768]{1,0:T(8,128)(2,1)}, bf16[512,768]{1,0:T(8,128)(2,1)S(1)}, u32[]{:S(2)}, u32[]{:S(2)}) collective-permute-start(bf16[512,768]{1,0:T(8,128)(2,1)} %refs_5_.1), channel_id=1, source_target_pairs={{0,24},{4,100},{8,0},{12,108},{16,8},{20,116},{24,16},{28,124},{32... | collective-permute-start | bytes 2359304 | tf_op jit(solution)/shard_map/ppermute | solution.py:207
  5.5 5.4 %collective-permute-start = (s32[1,128]{1,0:T(1,128)S(1)}, s32[1,128]{1,0:T(1,128)S(1)}, u32[]{:S(2)}, u32[]{:S(2)}) collective-permute-start(s32[1,128]{1,0:T(1,128)S(1)} %pad_add_fusion), channel_id=1, source_target_pairs={{0,4},{4,0},{1,5},{5,1},{2,6},{6,2},{3,7},{7,3},{8,12},{12,8},{9,1... | collective-permute-start | bytes 1544 | tf_op jit(solution)/shard_map/ppermute | solution.py:219
  5.5 17.9 %collective-permute-start.6 = (bf16[512,768]{1,0:T(8,128)(2,1)}, bf16[512,768]{1,0:T(8,128)(2,1)S(1)}, u32[]{:S(2)}, u32[]{:S(2)}) collective-permute-start(bf16[512,768]{1,0:T(8,128)(2,1)} %refs_5_.1), channel_id=1, source_target_pairs={{0,32},{4,12},{8,40},{12,20},{16,48},{20,28},{24,56},{28,4},{32,64... | collective-permute-start | bytes 2359304 | tf_op jit(solution)/shard_map/ppermute | solution.py:207
  10.8 14.7 %collective-permute-start.7 = (bf16[512,768]{1,0:T(8,128)(2,1)}, bf16[512,768]{1,0:T(8,128)(2,1)}, u32[]{:S(2)}, u32[]{:S(2)}) collective-permute-start(bf16[512,768]{1,0:T(8,128)(2,1)} %refs_5_.1), channel_id=1, source_target_pairs={{0,96},{4,28},{8,104},{12,4},{16,112},{20,12},{24,120},{28,20},{32... | collective-permute-start | bytes 2359304 | tf_op jit(solution)/shard_map/ppermute | solution.py:207
  14.8 0.7 copy-start.1
  19.0 19.9 %collective-permute-start.4 = (bf16[512,768]{1,0:T(8,128)(2,1)S(1)}, bf16[512,768]{1,0:T(8,128)(2,1)S(1)}, u32[]{:S(2)}, u32[]{:S(2)}) collective-permute-start(bf16[512,768]{1,0:T(8,128)(2,1)S(1)} %collective-permute-done.2.refs_7_), channel_id=1, source_target_pairs={{0,24},{4,100},{8,0},{12,108},{16,8},{20,116},{24,16},{28,124},{32... | collective-permute-start | bytes 2359304 | tf_op jit(solution)/shard_map/ppermute | solution.py:207
  21.4 17.5 %collective-permute-start.5 = (bf16[512,768]{1,0:T(8,128)(2,1)S(1)}, bf16[512,768]{1,0:T(8,128)(2,1)S(1)}, u32[]{:S(2)}, u32[]{:S(2)}) collective-permute-start(bf16[512,768]{1,0:T(8,128)(2,1)S(1)} %collective-permute-done.2.refs_7_), channel_id=1, source_target_pairs={{0,32},{4,12},{8,40},{12,20},{16,48},{20,28},{24,56},{28,4},{32,64... | collective-permute-start | bytes 2359304 | tf_op jit(solution)/shard_map/ppermute | solution.py:207
  23.4 21.1 %collective-permute-start.12 = (bf16[512,768]{1,0:T(8,128)(2,1)S(1)}, bf16[512,768]{1,0:T(8,128)(2,1)S(1)}, u32[]{:S(2)}, u32[]{:S(2)}) collective-permute-start(bf16[512,768]{1,0:T(8,128)(2,1)S(1)} %collective-permute-done.2.refs_7_), channel_id=1, source_target_pairs={{0,96},{4,28},{8,104},{12,4},{16,112},{20,12},{24,120},{28,20},{32... | collective-permute-start | bytes 2359304 | tf_op jit(solution)/shard_map/ppermute | solution.py:207
  25.5 23.4 %collective-permute-start.11 = (bf16[512,768]{1,0:T(8,128)(2,1)S(1)}, bf16[512,768]{1,0:T(8,128)(2,1)S(1)}, u32[]{:S(2)}, u32[]{:S(2)}) collective-permute-start(bf16[512,768]{1,0:T(8,128)(2,1)S(1)} %collective-permute-done.1.refs_6_), channel_id=1, source_target_pairs={{0,96},{4,28},{8,104},{12,4},{16,112},{20,12},{24,120},{28,20},{32... | collective-permute-start | bytes 2359304 | tf_op jit(solution)/shard_map/ppermute | solution.py:207
  29.2 19.7 %collective-permute-start.13 = (bf16[512,768]{1,0:T(8,128)(2,1)S(1)}, bf16[512,768]{1,0:T(8,128)(2,1)S(1)}, u32[]{:S(2)}, u32[]{:S(2)}) collective-permute-start(bf16[512,768]{1,0:T(8,128)(2,1)S(1)} %collective-permute-done.1.refs_6_), channel_id=1, source_target_pairs={{0,32},{4,12},{8,40},{12,20},{16,48},{20,28},{24,56},{28,4},{32,64... | collective-permute-start | bytes 2359304 | tf_op jit(solution)/shard_map/ppermute | solution.py:207
  38.9 18.5 %collective-permute-start.10 = (bf16[512,768]{1,0:T(8,128)(2,1)S(1)}, bf16[512,768]{1,0:T(8,128)(2,1)S(1)}, u32[]{:S(2)}, u32[]{:S(2)}) collective-permute-start(bf16[512,768]{1,0:T(8,128)(2,1)S(1)} %collective-permute-done.4.refs_5_), channel_id=1, source_target_pairs={{0,96},{4,28},{8,104},{12,4},{16,112},{20,12},{24,120},{28,20},{32... | collective-permute-start | bytes 2359304 | tf_op jit(solution)/shard_map/ppermute | solution.py:207
  40.4 25.4 %collective-permute-start.15 = (bf16[512,768]{1,0:T(8,128)(2,1)S(1)}, bf16[512,768]{1,0:T(8,128)(2,1)S(1)}, u32[]{:S(2)}, u32[]{:S(2)}) collective-permute-start(bf16[512,768]{1,0:T(8,128)(2,1)S(1)} %collective-permute-done.5.refs_6_), channel_id=1, source_target_pairs={{0,32},{4,12},{8,40},{12,20},{16,48},{20,28},{24,56},{28,4},{32,64... | collective-permute-start | bytes 2359304 | tf_op jit(solution)/shard_map/ppermute | solution.py:207
  44.5 26.4 %collective-permute-start.9 = (bf16[512,768]{1,0:T(8,128)(2,1)S(1)}, bf16[512,768]{1,0:T(8,128)(2,1)S(1)}, u32[]{:S(2)}, u32[]{:S(2)}) collective-permute-start(bf16[512,768]{1,0:T(8,128)(2,1)S(1)} %collective-permute-done.4.refs_5_), channel_id=1, source_target_pairs={{0,32},{4,12},{8,40},{12,20},{16,48},{20,28},{24,56},{28,4},{32,64... | collective-permute-start | bytes 2359304 | tf_op jit(solution)/shard_map/ppermute | solution.py:207
  48.9 16.8 %collective-permute-start.16 = (bf16[512,768]{1,0:T(8,128)(2,1)S(1)}, bf16[512,768]{1,0:T(8,128)(2,1)S(1)}, u32[]{:S(2)}, u32[]{:S(2)}) collective-permute-start(bf16[512,768]{1,0:T(8,128)(2,1)S(1)} %collective-permute-done.11.refs_5_), channel_id=1, source_target_pairs={{0,96},{4,28},{8,104},{12,4},{16,112},{20,12},{24,120},{28,20},{32... | collective-permute-start | bytes 2359304 | tf_op jit(solution)/shard_map/ppermute | solution.py:207
  52.6 18.2 %collective-permute-start.8 = (bf16[512,768]{1,0:T(8,128)(2,1)S(1)}, bf16[512,768]{1,0:T(8,128)(2,1)S(1)}, u32[]{:S(2)}, u32[]{:S(2)}) collective-permute-start(bf16[512,768]{1,0:T(8,128)(2,1)S(1)} %collective-permute-done.6.refs_8_), channel_id=1, source_target_pairs={{0,32},{4,12},{8,40},{12,20},{16,48},{20,28},{24,56},{28,4},{32,64... | collective-permute-start | bytes 2359304 | tf_op jit(solution)/shard_map/ppermute | solution.py:207
  57.4 16.9 %collective-permute-start.14 = (bf16[512,768]{1,0:T(8,128)(2,1)S(1)}, bf16[512,768]{1,0:T(8,128)(2,1)S(1)}, u32[]{:S(2)}, u32[]{:S(2)}) collective-permute-start(bf16[512,768]{1,0:T(8,128)(2,1)S(1)} %collective-permute-done.10.refs_5_), channel_id=1, source_target_pairs={{0,96},{4,28},{8,104},{12,4},{16,112},{20,12},{24,120},{28,20},{32... | collective-permute-start | bytes 2359304 | tf_op jit(solution)/shard_map/ppermute | solution.py:207

commit v7 on v6

--- a/solution.py
+++ b/solution.py
@@ -31,8 +31,9 @@
     ((0, 0), (3, 0), (1, 0), (0, 3), (0, 1)),
     ((2, 0), (1, 3)),
     ((3, 1), (1, 1), (3, 3)),
-    ((2, 1), (1, 2), (3, 2)),
-    ((0, 2), (2, 3), (2, 2)),
+    ((2, 1), (1, 2)),
+    ((3, 2), (0, 2), (2, 3)),
+    ((2, 2),),
 )
 
 
@@ -286,9 +287,11 @@
     store, kv = build(7, (left_up, right_up, left_down), store, kv)
     two_up, kv = lax.optimization_barrier((two_up, kv))
     both_two = go(two_up, False, -1)
-    store, kv = build(10, (two_up, right_two, left_two), store, kv)
-    second_two, two_down, both_two, kv = lax.optimization_barrier((second_two, two_down, both_two, kv))
-    store, kv = build(13, (second_two, two_down, both_two), store, kv)
+    store, kv = build(10, (two_up, right_two), store, kv)
+    left_two, second_two, two_down, kv = lax.optimization_barrier((left_two, second_two, two_down, kv))
+    store, kv = build(12, (left_two, second_two, two_down), store, kv)
+    both_two, kv = lax.optimization_barrier((both_two, kv))
+    store, kv = build(15, (both_two,), store, kv)
 
     def half(over_rows, parts, copies, store):
         last = copies == 0

time: 179 us -> 177 us (0.989); the launches traced: 179 us -> 175 us
  Pallas kernels: 40.9 us -> 51.3 us
  blocking collectives: 86.1 us -> 78.3 us
  waiting for transfers between devices: 17.4 us -> 11.2 us
    all_to_all x2, blocking collectives: 40.4 us -> 28.7 us  [on_device(): ktu_parts = lax.all_to_all(ktu, ('y', 'x'), 0, 0, tiled=True)]
    ppermute x15, waiting for transfers between devices: 13.7 us -> 7.56 us  [go(): return lax.ppermute(block, ('y', 'x', 'core'), moves(first, shift))]
    all_to_all x3, blocking collectives: 33.5 us -> 39.5 us  [on_device(): kv_parts = lax.all_to_all(kv, ('core', 'z'), 0, 0, tiled=True)]
    pallas_call x5 -> x6, Pallas kernels: 23.8 us -> 29 us  [build(): pl.pallas_call(lambda *refs: build_kernel(scale, first, blocks, last, *re...]
    pallas_call x5, Pallas kernels: 13.1 us -> 17.7 us  [half(): pl.pallas_call(lambda *refs: pass_kernel(over_rows, last, *refs), out_sha...]
    all_to_all x1, blocking collectives: 12.1 us -> 10.1 us  [on_device(): mine = lax.all_to_all(ktu, ('y', 'x'), 0, 0, tiled=True)]
  transfers between devices with their start and end apart: 17 -> 17, of which waited for: 7 -> 4; matrix products, arithmetic and copies ran while one was open for 1% -> 1% of each run, Pallas kernels for 13% -> 19%
where the time goes in v7:
time: 177 us; the launch traced here: 175 us
  blocking collectives  78.3 us (44%)
  Pallas kernels  51.3 us (29%)
  starting transfers between devices  29.7 us (17%)
  waiting for transfers between devices  11.2 us (6%)
  other arithmetic  2.26 us (1%)
    all_to_all x3, blocking collectives, on_device(): kv_parts = lax.all_to_all(kv, ('core', 'z'), 0, 0, tiled=True)  39.5 us
    ppermute x15, starting transfers between devices, go(): return lax.ppermute(block, ('y', 'x', 'core'), moves(first, shift))  29.6 us
    pallas_call x6, Pallas kernels, build(): pl.pallas_call(lambda *refs: build_kernel(scale, first, blocks, last, *re...  29 us
    all_to_all x2, blocking collectives, on_device(): ktu_parts = lax.all_to_all(ktu, ('y', 'x'), 0, 0, tiled=True)  28.7 us
    pallas_call x5, Pallas kernels, half(): pl.pallas_call(lambda *refs: pass_kernel(over_rows, last, *refs), out_sha...  17.7 us
    all_to_all x1, blocking collectives, on_device(): mine = lax.all_to_all(ktu, ('y', 'x'), 0, 0, tiled=True)  10.1 us
    ppermute x15, waiting for transfers between devices, go(): return lax.ppermute(block, ('y', 'x', 'core'), moves(first, shift))  7.56 us
    pallas_call x1, Pallas kernels, on_device(): pl.pallas_call(plan_kernel, out_shape=(jax.ShapeDtypeStruct((3, CAP), jnp...  3.99 us
  transfers between devices with their start and end apart: 17, of which 4 were waited for; matrix products, arithmetic and copies ran while one was open for 1% of the time, Pallas kernels for 19%

profile of v7, /device:TPU:0, one launch (start us, length us, event | category | flops | bytes accessed | tf_op | source)
XLA Modules:
  0.0 175.0 jit_solution(9541520492462608747)
XLA Ops:
  0.6 0.0 copy-start
  0.6 0.1 collective-permute-start.3
  0.7 1.6 collective-permute-start.1
  2.4 1.7 collective-permute-start.2
  4.7 0.8 pad_add_fusion
  5.5 0.0 collective-permute-start
  5.5 1.7 collective-permute-start.6
  7.2 3.6 %collective-permute-done = s32[1,128]{1,0:T(1,128)S(1)} collective-permute-done((s32[1,128]{1,0:T(1,128)S(1)}, s32[1,128]{1,0:T(1,128)S(1)}, u32[]{:S(2)}, u32[]{:S(2)}) %collective-permute-start) | collective-permute-done | bytes 544 | tf_op jit(solution)/shard_map/ppermute | solution.py:220
  10.8 3.1 %collective-permute-start.7 = (bf16[512,768]{1,0:T(8,128)(2,1)}, bf16[512,768]{1,0:T(8,128)(2,1)}, u32[]{:S(2)}, u32[]{:S(2)}) collective-permute-start(bf16[512,768]{1,0:T(8,128)(2,1)} %refs_5_.1), channel_id=1, source_target_pairs={{0,96},{4,28},{8,104},{12,4},{16,112},{20,12},{24,120},{28,20},{32... | collective-permute-start | bytes 2359304 | tf_op jit(solution)/shard_map/ppermute | solution.py:208
  13.9 0.1 pad_add_fusion.1.place.refs_2_
  14.0 0.8 add_select_fusion.lists
  14.8 0.7 copy-done.1
  15.5 4.0 %plan.1 = (s32[3,64]{1,0:T(4,128)S(1)}, s32[17]{0:T(128)S(1)}) custom-call(s32[2,128]{1,0:T(2,128)S(1)} %add_select_fusion.lists, s32[3]{0:T(128)S(1)} %pad_add_fusion.1.place.refs_2_, s32[16]{0:T(128)S(1)} %copy-done.1), custom_call_target="tpu_custom_call" | custom-call | tf_op jit(solution)/shard_map/plan/pallas_call | solution.py:229
  19.5 0.0 collective-permute-done.2.refs_7_
  19.5 4.4 %collective-permute-start.4 = (bf16[512,768]{1,0:T(8,128)(2,1)S(1)}, bf16[512,768]{1,0:T(8,128)(2,1)S(1)}, u32[]{:S(2)}, u32[]{:S(2)}) collective-permute-start(bf16[512,768]{1,0:T(8,128)(2,1)S(1)} %collective-permute-done.2.refs_7_), channel_id=1, source_target_pairs={{0,24},{4,100},{8,0},{12,108},{16,8},{20,116},{24,16},{28,124},{32... | collective-permute-start | bytes 2359304 | tf_op jit(solution)/shard_map/ppermute | solution.py:208
  23.9 0.6 room.1.refs_10_
  24.5 3.3 %collective-permute-start.10 = (bf16[512,768]{1,0:T(8,128)(2,1)S(1)}, bf16[512,768]{1,0:T(8,128)(2,1)S(1)}, u32[]{:S(2)}, u32[]{:S(2)}) collective-permute-start(bf16[512,768]{1,0:T(8,128)(2,1)S(1)} %collective-permute-done.2.refs_7_), channel_id=1, source_target_pairs={{0,96},{4,28},{8,104},{12,4},{16,112},{20,12},{24,120},{28,20},{32... | collective-permute-start | bytes 2359304 | tf_op jit(solution)/shard_map/ppermute | solution.py:208
  27.8 0.0 collective-permute-start.11
  27.8 0.0 collective-permute-done.3.refs_4_
  27.8 3.2 %collective-permute-start.9 = (bf16[512,768]{1,0:T(8,128)(2,1)S(1)}, bf16[512,768]{1,0:T(8,128)(2,1)S(1)}, u32[]{:S(2)}, u32[]{:S(2)}) collective-permute-start(bf16[512,768]{1,0:T(8,128)(2,1)S(1)} %collective-permute-done.1.refs_6_), channel_id=1, source_target_pairs={{0,96},{4,28},{8,104},{12,4},{16,112},{20,12},{24,120},{28,20},{32... | collective-permute-start | bytes 2359304 | tf_op jit(solution)/shard_map/ppermute | solution.py:208
  31.1 8.2 %build.6 = (bf16[64,512,512]{2,1,0:T(8,128)(2,1)S(1)}, f32[16,512]{1,0:T(8,128)S(1)}) custom-call(s32[3,64]{1,0:T(4,128)S(1)} %get-tuple-element.45.pairs.refs_0_, s32[17]{0:T(128)S(1)} %get-tuple-element.47.bounds.refs_1_, s32[3]{0:T(128)S(1)} %pad_add_fusion.1.place.refs_2_, bf16[4096,768]{1,0:T(8,128)(2,1)} %refs_3_.11, ...), custom_call_target="tpu_custom_call", output_to_operand_aliasing={{0}: (10, {})} | custom-call | flops 4026531840 | bytes 15728640 | tf_op jit(solution)/shard_map/build/pallas_call | solution.py:253
  39.3 1.6 collective-permute-done.4.refs_5_
  40.9 0.0 collective-permute-done.5.refs_6_
  40.9 0.0 collective-permute-start.8
  40.9 2.0 %collective-permute-start.16 = (bf16[512,768]{1,0:T(8,128)(2,1)S(1)}, bf16[512,768]{1,0:T(8,128)(2,1)S(1)}, u32[]{:S(2)}, u32[]{:S(2)}) collective-permute-start(bf16[512,768]{1,0:T(8,128)(2,1)S(1)} %collective-permute-done.5.refs_6_), channel_id=1, source_target_pairs={{0,32},{4,12},{8,40},{12,20},{16,48},{20,28},{24,56},{28,4},{32,64... | collective-permute-start | bytes 2359304 | tf_op jit(solution)/shard_map/ppermute | solution.py:208
  42.9 3.5 %build.7 = (bf16[64,512,512]{2,1,0:T(8,128)(2,1)S(1)}, f32[16,512]{1,0:T(8,128)S(1)}) custom-call(s32[3,64]{1,0:T(4,128)S(1)} %get-tuple-element.45.pairs.refs_0_, s32[17]{0:T(128)S(1)} %get-tuple-element.47.bounds.refs_1_, s32[3]{0:T(128)S(1)} %pad_add_fusion.1.place.refs_2_, bf16[4096,768]{1,0:T(8,128)(2,1)} %refs_3_.11, ...), custom_call_target="tpu_custom_call", output_to_operand_aliasing={{0}: (7, {})} | custom-call | flops 1610612736 | bytes 6291456 | tf_op jit(solution)/shard_map/build/pallas_call | solution.py:253
  46.5 0.1 collective-permute-start.15
  46.6 2.3 %collective-permute-done.9.refs_5_ = bf16[512,768]{1,0:T(8,128)(2,1)S(1)} collective-permute-done((bf16[512,768]{1,0:T(8,128)(2,1)S(1)}, bf16[512,768]{1,0:T(8,128)(2,1)S(1)}, u32[]{:S(2)}, u32[]{:S(2)}) %collective-permute-start.9) | collective-permute-done | bytes 786464 | tf_op jit(solution)/shard_map/ppermute | solution.py:208
  48.9 3.7 %collective-permute-start.13 = (bf16[512,768]{1,0:T(8,128)(2,1)S(1)}, bf16[512,768]{1,0:T(8,128)(2,1)S(1)}, u32[]{:S(2)}, u32[]{:S(2)}) collective-permute-start(bf16[512,768]{1,0:T(8,128)(2,1)S(1)} %collective-permute-done.9.refs_5_), channel_id=1, source_target_pairs={{0,96},{4,28},{8,104},{12,4},{16,112},{20,12},{24,120},{28,20},{32... | collective-permute-start | bytes 2359304 | tf_op jit(solution)/shard_map/ppermute | solution.py:208
  52.6 0.0 collective-permute-start.14
  52.6 5.0 %build.8 = (bf16[64,512,512]{2,1,0:T(8,128)(2,1)S(1)}, f32[16,512]{1,0:T(8,128)S(1)}) custom-call(s32[3,64]{1,0:T(4,128)S(1)} %get-tuple-element.45.pairs.refs_0_, s32[17]{0:T(128)S(1)} %get-tuple-element.47.bounds.refs_1_, s32[3]{0:T(128)S(1)} %pad_add_fusion.1.place.refs_2_, bf16[4096,768]{1,0:T(8,128)(2,1)} %refs_3_.11, ...), custom_call_target="tpu_custom_call", output_to_operand_aliasing={{0}: (8, {})} | custom-call | flops 2415919104 | bytes 9437184 | tf_op jit(solution)/shard_map/build/pallas_call | solution.py:253
  57.7 4.7 %collective-permute-start.12 = (bf16[512,768]{1,0:T(8,128)(2,1)S(1)}, bf16[512,768]{1,0:T(8,128)(2,1)S(1)}, u32[]{:S(2)}, u32[]{:S(2)}) collective-permute-start(bf16[512,768]{1,0:T(8,128)(2,1)S(1)} %collective-permute-done.8.refs_5_), channel_id=1, source_target_pairs={{0,96},{4,28},{8,104},{12,4},{16,112},{20,12},{24,120},{28,20},{32... | collective-permute-start | bytes 2359304 | tf_op jit(solution)/shard_map/ppermute | solution.py:208
  62.4 5.0 %build.9 = (bf16[64,512,512]{2,1,0:T(8,128)(2,1)S(1)}, f32[16,512]{1,0:T(8,128)S(1)}) custom-call(s32[3,64]{1,0:T(4,128)S(1)} %get-tuple-element.45.pairs.refs_0_, s32[17]{0:T(128)S(1)} %get-tuple-element.47.bounds.refs_1_, s32[3]{0:T(128)S(1)} %pad_add_fusion.1.place.refs_2_, bf16[4096,768]{1,0:T(8,128)(2,1)} %refs_3_.11, ...), custom_call_target="tpu_custom_call", output_to_operand_aliasing={{0}: (7, {})} | custom-call | flops 1610612736 | bytes 6291456 | tf_op jit(solution)/shard_map/build/pallas_call | solution.py:253
  67.4 3.5 %collective-permute-done.14.refs_6_ = bf16[512,768]{1,0:T(8,128)(2,1)S(1)} collective-permute-done((bf16[512,768]{1,0:T(8,128)(2,1)S(1)}, bf16[512,768]{1,0:T(8,128)(2,1)S(1)}, u32[]{:S(2)}, u32[]{:S(2)}) %collective-permute-start.14) | collective-permute-done | bytes 786464 | tf_op jit(solution)/shard_map/ppermute | solution.py:208
  71.0 6.5 %build.10 = (bf16[64,512,512]{2,1,0:T(8,128)(2,1)S(1)}, f32[16,512]{1,0:T(8,128)S(1)}) custom-call(s32[3,64]{1,0:T(4,128)S(1)} %get-tuple-element.45.pairs.refs_0_, s32[17]{0:T(128)S(1)} %get-tuple-element.47.bounds.refs_1_, s32[3]{0:T(128)S(1)} %pad_add_fusion.1.place.refs_2_, bf16[4096,768]{1,0:T(8,128)(2,1)} %refs_3_.11, ...), custom_call_target="tpu_custom_call", output_to_operand_aliasing={{0}: (8, {})} | custom-call | flops 2415919104 | bytes 9437184 | tf_op jit(solution)/shard_map/build/pallas_call | solution.py:253
  77.5 0.7 build.11
  78.2 16.3 %all_to_all.30.refs_3_ = f32[8,16,512]{2,1,0:T(8,128)S(1)} all-to-all(f32[8,16,512]{2,1,0:T(8,128)S(1)} %get-tuple-element.76), channel_id=1, replica_groups=mesh['y'=4,'x'=4,'core'=2,'z'=4] {'core','z'}, dimensions={0} | all-to-all | bytes 524288 | tf_op jit(solution)/shard_map/all_to_all | solution.py:314
  94.6 2.6 %columns.3 = (f32[16,16,512]{2,1,0:T(8,128)S(1)}, bf16[64,512,512]{2,1,0:T(8,128)(2,1)S(1)}) custom-call(s32[3,64]{1,0:T(4,128)S(1)} %get-tuple-element.45.pairs.refs_0_, s32[17]{0:T(128)S(1)} %get-tuple-element.47.bounds.refs_1_, s32[3]{0:T(128)S(1)} %pad_add_fusion.1.place.refs_2_, ...), custom_call_target="tpu_custom_call", output_to_operand_aliasing={{1}: (4, {})} | custom-call | tf_op jit(solution)/shard_map/columns/pallas_call | solution.py:300
  97.2 14.6 %all_to_all.31.refs_3_ = f32[16,16,512]{2,1,0:T(8,128)S(1)} all-to-all(f32[16,16,512]{2,1,0:T(8,128)S(1)} %get-tuple-element.78), channel_id=1, replica_groups=mesh['y'=4,'x'=4,'core'=2,'z'=4] {'y','x'}, dimensions={0} | all-to-all | bytes 1048576 | tf_op jit(solution)/shard_map/all_to_all | solution.py:317
  111.8 4.6 %rows.2 = (f32[8,16,512]{2,1,0:T(8,128)S(1)}, bf16[64,512,512]{2,1,0:T(8,128)(2,1)S(1)}) custom-call(s32[3,64]{1,0:T(4,128)S(1)} %get-tuple-element.45.pairs.refs_0_, s32[17]{0:T(128)S(1)} %get-tuple-element.47.bounds.refs_1_, s32[3]{0:T(128)S(1)} %pad_add_fusion.1.place.refs_2_, ...), custom_call_target="tpu_custom_call", output_to_operand_aliasing={{1}: (4, {})} | custom-call | tf_op jit(solution)/shard_map/rows/pallas_call | solution.py:300
  116.5 11.4 %all_to_all.32.refs_3_ = f32[8,16,512]{2,1,0:T(8,128)S(1)} all-to-all(f32[8,16,512]{2,1,0:T(8,128)S(1)} %get-tuple-element.80), channel_id=1, replica_groups=mesh['y'=4,'x'=4,'core'=2,'z'=4] {'core','z'}, dimensions={0} | all-to-all | bytes 524288 | tf_op jit(solution)/shard_map/all_to_all | solution.py:314
  127.9 2.6 %columns.4 = (f32[16,16,512]{2,1,0:T(8,128)S(1)}, bf16[64,512,512]{2,1,0:T(8,128)(2,1)S(1)}) custom-call(s32[3,64]{1,0:T(4,128)S(1)} %get-tuple-element.45.pairs.refs_0_, s32[17]{0:T(128)S(1)} %get-tuple-element.47.bounds.refs_1_, s32[3]{0:T(128)S(1)} %pad_add_fusion.1.place.refs_2_, ...), custom_call_target="tpu_custom_call", output_to_operand_aliasing={{1}: (4, {})} | custom-call | tf_op jit(solution)/shard_map/columns/pallas_call | solution.py:300
  130.5 14.1 %all_to_all.33.refs_3_ = f32[16,16,512]{2,1,0:T(8,128)S(1)} all-to-all(f32[16,16,512]{2,1,0:T(8,128)S(1)} %get-tuple-element.82), channel_id=1, replica_groups=mesh['y'=4,'x'=4,'core'=2,'z'=4] {'y','x'}, dimensions={0} | all-to-all | bytes 1048576 | tf_op jit(solution)/shard_map/all_to_all | solution.py:317
  144.6 4.6 %rows.3 = (f32[8,16,512]{2,1,0:T(8,128)S(1)}, bf16[64,512,512]{2,1,0:T(8,128)(2,1)S(1)}) custom-call(s32[3,64]{1,0:T(4,128)S(1)} %get-tuple-element.45.pairs.refs_0_, s32[17]{0:T(128)S(1)} %get-tuple-element.47.bounds.refs_1_, s32[3]{0:T(128)S(1)} %pad_add_fusion.1.place.refs_2_, ...), custom_call_target="tpu_custom_call", output_to_operand_aliasing={{1}: (4, {})} | custom-call | tf_op jit(solution)/shard_map/rows/pallas_call | solution.py:300
  149.2 11.8 %all_to_all.34.refs_3_ = f32[8,16,512]{2,1,0:T(8,128)S(1)} all-to-all(f32[8,16,512]{2,1,0:T(8,128)S(1)} %get-tuple-element.84), channel_id=1, replica_groups=mesh['y'=4,'x'=4,'core'=2,'z'=4] {'core','z'}, dimensions={0} | all-to-all | bytes 524288 | tf_op jit(solution)/shard_map/all_to_all | solution.py:314
  161.0 3.2 %columns.5 = (f32[16,4,128]{2,1,0:T(4,128)S(1)}, f32[32,128]{1,0:T(8,128)}) custom-call(s32[3,64]{1,0:T(4,128)S(1)} %get-tuple-element.45.pairs.refs_0_, s32[17]{0:T(128)S(1)} %get-tuple-element.47.bounds.refs_1_, s32[3]{0:T(128)S(1)} %pad_add_fusion.1.place.refs_2_, f32[8,16,512]{2,1,0:T(8,128)S(1)} %all_to_all.34.refs_3_, ...), custom_call_target="tpu_custom_call" | custom-call | tf_op jit(solution)/shard_map/columns/pallas_call | solution.py:300
  164.2 10.1 %all_to_all.35 = f32[16,4,128]{2,1,0:T(4,128)S(1)} all-to-all(f32[16,4,128]{2,1,0:T(4,128)S(1)} %get-tuple-element.87), channel_id=1, replica_groups=mesh['y'=4,'x'=4,'core'=2,'z'=4] {'y','x'}, dimensions={0} | all-to-all | bytes 65536 | tf_op jit(solution)/shard_map/all_to_all | solution.py:319
  174.4 0.6 log_bitcast_fusion
  (16 shorter events, 0.1 us)
Async XLA Ops:
  0.6 30.4 %copy-start = (bf16[512,768]{1,0:T(8,128)(2,1)S(1)}, bf16[512,768]{1,0:T(8,128)(2,1)}, u32[]{:S(2)}) copy-start(bf16[512,768]{1,0:T(8,128)(2,1)} %refs_5_.1) | copy-start | bytes 2359300
  0.6 27.2 %collective-permute-start.3 = (bf16[4096,768]{1,0:T(8,128)(2,1)}, bf16[4096,768]{1,0:T(8,128)(2,1)}, u32[]{:S(2)}, u32[]{:S(2)}) collective-permute-start(bf16[4096,768]{1,0:T(8,128)(2,1)} %refs_3_.11), channel_id=1, source_target_pairs={{0,4},{4,0},{1,5},{5,1},{2,6},{6,2},{3,7},{7,3},{8,12},{12,8},{9,1... | collective-permute-start | bytes 18874376 | tf_op jit(solution)/shard_map/ppermute | solution.py:219
  0.7 18.8 %collective-permute-start.1 = (bf16[512,768]{1,0:T(8,128)(2,1)}, bf16[512,768]{1,0:T(8,128)(2,1)S(1)}, u32[]{:S(2)}, u32[]{:S(2)}) collective-permute-start(bf16[512,768]{1,0:T(8,128)(2,1)} %refs_5_.1), channel_id=1, source_target_pairs={{0,8},{4,36},{8,16},{12,44},{16,24},{20,52},{24,0},{28,60},{32,40}... | collective-permute-start | bytes 2359304 | tf_op jit(solution)/shard_map/ppermute | solution.py:208
  2.4 17.1 %collective-permute-start.2 = (bf16[512,768]{1,0:T(8,128)(2,1)}, bf16[512,768]{1,0:T(8,128)(2,1)S(1)}, u32[]{:S(2)}, u32[]{:S(2)}) collective-permute-start(bf16[512,768]{1,0:T(8,128)(2,1)} %refs_5_.1), channel_id=1, source_target_pairs={{0,24},{4,100},{8,0},{12,108},{16,8},{20,116},{24,16},{28,124},{32... | collective-permute-start | bytes 2359304 | tf_op jit(solution)/shard_map/ppermute | solution.py:208
  5.5 5.4 %collective-permute-start = (s32[1,128]{1,0:T(1,128)S(1)}, s32[1,128]{1,0:T(1,128)S(1)}, u32[]{:S(2)}, u32[]{:S(2)}) collective-permute-start(s32[1,128]{1,0:T(1,128)S(1)} %pad_add_fusion), channel_id=1, source_target_pairs={{0,4},{4,0},{1,5},{5,1},{2,6},{6,2},{3,7},{7,3},{8,12},{12,8},{9,1... | collective-permute-start | bytes 1544 | tf_op jit(solution)/shard_map/ppermute | solution.py:220
  5.5 19.0 %collective-permute-start.6 = (bf16[512,768]{1,0:T(8,128)(2,1)}, bf16[512,768]{1,0:T(8,128)(2,1)S(1)}, u32[]{:S(2)}, u32[]{:S(2)}) collective-permute-start(bf16[512,768]{1,0:T(8,128)(2,1)} %refs_5_.1), channel_id=1, source_target_pairs={{0,32},{4,12},{8,40},{12,20},{16,48},{20,28},{24,56},{28,4},{32,64... | collective-permute-start | bytes 2359304 | tf_op jit(solution)/shard_map/ppermute | solution.py:208
  10.8 17.0 %collective-permute-start.7 = (bf16[512,768]{1,0:T(8,128)(2,1)}, bf16[512,768]{1,0:T(8,128)(2,1)}, u32[]{:S(2)}, u32[]{:S(2)}) collective-permute-start(bf16[512,768]{1,0:T(8,128)(2,1)} %refs_5_.1), channel_id=1, source_target_pairs={{0,96},{4,28},{8,104},{12,4},{16,112},{20,12},{24,120},{28,20},{32... | collective-permute-start | bytes 2359304 | tf_op jit(solution)/shard_map/ppermute | solution.py:208
  14.8 0.7 copy-start.1
  19.5 21.4 %collective-permute-start.4 = (bf16[512,768]{1,0:T(8,128)(2,1)S(1)}, bf16[512,768]{1,0:T(8,128)(2,1)S(1)}, u32[]{:S(2)}, u32[]{:S(2)}) collective-permute-start(bf16[512,768]{1,0:T(8,128)(2,1)S(1)} %collective-permute-done.2.refs_7_), channel_id=1, source_target_pairs={{0,24},{4,100},{8,0},{12,108},{16,8},{20,116},{24,16},{28,124},{32... | collective-permute-start | bytes 2359304 | tf_op jit(solution)/shard_map/ppermute | solution.py:208
  23.9 17.0 %collective-permute-start.5 = (bf16[512,768]{1,0:T(8,128)(2,1)S(1)}, bf16[512,768]{1,0:T(8,128)(2,1)S(1)}, u32[]{:S(2)}, u32[]{:S(2)}) collective-permute-start(bf16[512,768]{1,0:T(8,128)(2,1)S(1)} %collective-permute-done.2.refs_7_), channel_id=1, source_target_pairs={{0,32},{4,12},{8,40},{12,20},{16,48},{20,28},{24,56},{28,4},{32,64... | collective-permute-start | bytes 2359304 | tf_op jit(solution)/shard_map/ppermute | solution.py:208
  24.5 22.0 %collective-permute-start.10 = (bf16[512,768]{1,0:T(8,128)(2,1)S(1)}, bf16[512,768]{1,0:T(8,128)(2,1)S(1)}, u32[]{:S(2)}, u32[]{:S(2)}) collective-permute-start(bf16[512,768]{1,0:T(8,128)(2,1)S(1)} %collective-permute-done.2.refs_7_), channel_id=1, source_target_pairs={{0,96},{4,28},{8,104},{12,4},{16,112},{20,12},{24,120},{28,20},{32... | collective-permute-start | bytes 2359304 | tf_op jit(solution)/shard_map/ppermute | solution.py:208
  27.8 18.8 %collective-permute-start.11 = (bf16[512,768]{1,0:T(8,128)(2,1)S(1)}, bf16[512,768]{1,0:T(8,128)(2,1)S(1)}, u32[]{:S(2)}, u32[]{:S(2)}) collective-permute-start(bf16[512,768]{1,0:T(8,128)(2,1)S(1)} %collective-permute-done.1.refs_6_), channel_id=1, source_target_pairs={{0,32},{4,12},{8,40},{12,20},{16,48},{20,28},{24,56},{28,4},{32,64... | collective-permute-start | bytes 2359304 | tf_op jit(solution)/shard_map/ppermute | solution.py:208
  27.8 21.1 %collective-permute-start.9 = (bf16[512,768]{1,0:T(8,128)(2,1)S(1)}, bf16[512,768]{1,0:T(8,128)(2,1)S(1)}, u32[]{:S(2)}, u32[]{:S(2)}) collective-permute-start(bf16[512,768]{1,0:T(8,128)(2,1)S(1)} %collective-permute-done.1.refs_6_), channel_id=1, source_target_pairs={{0,96},{4,28},{8,104},{12,4},{16,112},{20,12},{24,120},{28,20},{32... | collective-permute-start | bytes 2359304 | tf_op jit(solution)/shard_map/ppermute | solution.py:208
  40.9 16.8 %collective-permute-start.8 = (bf16[512,768]{1,0:T(8,128)(2,1)S(1)}, bf16[512,768]{1,0:T(8,128)(2,1)S(1)}, u32[]{:S(2)}, u32[]{:S(2)}) collective-permute-start(bf16[512,768]{1,0:T(8,128)(2,1)S(1)} %collective-permute-done.4.refs_5_), channel_id=1, source_target_pairs={{0,96},{4,28},{8,104},{12,4},{16,112},{20,12},{24,120},{28,20},{32... | collective-permute-start | bytes 2359304 | tf_op jit(solution)/shard_map/ppermute | solution.py:208
  40.9 21.5 %collective-permute-start.16 = (bf16[512,768]{1,0:T(8,128)(2,1)S(1)}, bf16[512,768]{1,0:T(8,128)(2,1)S(1)}, u32[]{:S(2)}, u32[]{:S(2)}) collective-permute-start(bf16[512,768]{1,0:T(8,128)(2,1)S(1)} %collective-permute-done.5.refs_6_), channel_id=1, source_target_pairs={{0,32},{4,12},{8,40},{12,20},{16,48},{20,28},{24,56},{28,4},{32,64... | collective-permute-start | bytes 2359304 | tf_op jit(solution)/shard_map/ppermute | solution.py:208
  46.5 24.5 %collective-permute-start.15 = (bf16[512,768]{1,0:T(8,128)(2,1)S(1)}, bf16[512,768]{1,0:T(8,128)(2,1)S(1)}, u32[]{:S(2)}, u32[]{:S(2)}) collective-permute-start(bf16[512,768]{1,0:T(8,128)(2,1)S(1)} %collective-permute-done.4.refs_5_), channel_id=1, source_target_pairs={{0,32},{4,12},{8,40},{12,20},{16,48},{20,28},{24,56},{28,4},{32,64... | collective-permute-start | bytes 2359304 | tf_op jit(solution)/shard_map/ppermute | solution.py:208
  48.9 18.5 %collective-permute-start.13 = (bf16[512,768]{1,0:T(8,128)(2,1)S(1)}, bf16[512,768]{1,0:T(8,128)(2,1)S(1)}, u32[]{:S(2)}, u32[]{:S(2)}) collective-permute-start(bf16[512,768]{1,0:T(8,128)(2,1)S(1)} %collective-permute-done.9.refs_5_), channel_id=1, source_target_pairs={{0,96},{4,28},{8,104},{12,4},{16,112},{20,12},{24,120},{28,20},{32... | collective-permute-start | bytes 2359304 | tf_op jit(solution)/shard_map/ppermute | solution.py:208
  52.6 18.3 %collective-permute-start.14 = (bf16[512,768]{1,0:T(8,128)(2,1)S(1)}, bf16[512,768]{1,0:T(8,128)(2,1)S(1)}, u32[]{:S(2)}, u32[]{:S(2)}) collective-permute-start(bf16[512,768]{1,0:T(8,128)(2,1)S(1)} %collective-permute-done.6.refs_8_), channel_id=1, source_target_pairs={{0,32},{4,12},{8,40},{12,20},{16,48},{20,28},{24,56},{28,4},{32,64... | collective-permute-start | bytes 2359304 | tf_op jit(solution)/shard_map/ppermute | solution.py:208
  57.7 19.8 %collective-permute-start.12 = (bf16[512,768]{1,0:T(8,128)(2,1)S(1)}, bf16[512,768]{1,0:T(8,128)(2,1)S(1)}, u32[]{:S(2)}, u32[]{:S(2)}) collective-permute-start(bf16[512,768]{1,0:T(8,128)(2,1)S(1)} %collective-permute-done.8.refs_5_), channel_id=1, source_target_pairs={{0,96},{4,28},{8,104},{12,4},{16,112},{20,12},{24,120},{28,20},{32... | collective-permute-start | bytes 2359304 | tf_op jit(solution)/shard_map/ppermute | solution.py:208

commit v8 on v6

--- a/solution.py
+++ b/solution.py
@@ -215,7 +215,6 @@
     own = jnp.concatenate(
         [pair_a.reshape(1, -1), pair_b.reshape(1, -1), pair_count.reshape(1, 1), jnp.zeros((1, 63), jnp.int32)], axis=1
     )
-    a_other = lax.ppermute(table_a, "core", swap)
     other = lax.ppermute(own, "core", swap)
     lists = jnp.where(core == 0, jnp.concatenate([own, other]), jnp.concatenate([other, own]))
     place = jnp.stack([core, lax.axis_index("y"), lax.axis_index("x")]).astype(jnp.int32)
@@ -272,8 +271,9 @@
         )(pairs, bounds, place, table_a, a_other, *group, store, kv)
 
     kv = jnp.zeros((NC * ABLK, TILE), F32)
-    left, right, bounds = lax.optimization_barrier((left, right, bounds))
+    left, right, down, up, bounds, mine = lax.optimization_barrier((left, right, down, up, bounds, table_a))
     first_two = go(right, True, -1)
+    a_other = lax.ppermute(mine, "core", swap)
     left_down, right_down = go(left, False, 1), go(right, False, 1)
     left_up, right_up = go(left, False, -1), go(right, False, -1)
     store, kv = build(0, (table_b, left, right, down, up), store, kv)

time: 179 us -> 182 us (1.017)
  Pallas kernels: 40.9 us -> 45.1 us
  waiting for transfers between devices: 17.4 us -> 15.2 us
    pallas_call x5, Pallas kernels: 13.1 us -> 16.4 us  [half(): pl.pallas_call(lambda *refs: pass_kernel(over_rows, last, *refs), out_sha...]
    ppermute x1, waiting for transfers between devices: 3.62 us -> 1.02 us  [on_device(): other = lax.ppermute(own, 'core', swap)]
  transfers between devices with their start and end apart: 17 -> 17, of which waited for: 7 -> 9; matrix products, arithmetic and copies ran while one was open for 1% -> 1% of each run, Pallas kernels for 13% -> 15%
where the time goes in v8:
time: 182 us
  blocking collectives  87.3 us (48%)
  Pallas kernels  45.1 us (25%)
  starting transfers between devices  29.9 us (16%)
  waiting for transfers between devices  15.2 us (8%)
  other arithmetic  2.27 us (1%)
    all_to_all x2, blocking collectives, on_device(): ktu_parts = lax.all_to_all(ktu, ('y', 'x'), 0, 0, tiled=True)  39.7 us
    all_to_all x3, blocking collectives, on_device(): kv_parts = lax.all_to_all(kv, ('core', 'z'), 0, 0, tiled=True)  35.3 us
    ppermute x15, starting transfers between devices, go(): return lax.ppermute(block, ('y', 'x', 'core'), moves(first, shift))  28.7 us
    pallas_call x5, Pallas kernels, build(): pl.pallas_call(lambda *refs: build_kernel(scale, first, blocks, last, *re...  24.1 us
    pallas_call x5, Pallas kernels, half(): pl.pallas_call(lambda *refs: pass_kernel(over_rows, last, *refs), out_sha...  16.4 us
    ppermute x15, waiting for transfers between devices, go(): return lax.ppermute(block, ('y', 'x', 'core'), moves(first, shift))  12.9 us
    all_to_all x1, blocking collectives, on_device(): mine = lax.all_to_all(ktu, ('y', 'x'), 0, 0, tiled=True)  12.3 us
    pallas_call x1, Pallas kernels, on_device(): pl.pallas_call(plan_kernel, out_shape=(jax.ShapeDtypeStruct((3, CAP), jnp...  4.01 us
  transfers between devices with their start and end apart: 17, of which 9 were waited for; matrix products, arithmetic and copies ran while one was open for 1% of the time, Pallas kernels for 15%

profile of v8, /device:TPU:0, one launch (start us, length us, event | category | flops | bytes accessed | tf_op | source)
XLA Modules:
  0.0 182.5 jit_solution(6301591493424132796)
XLA Ops:
  0.6 1.6 collective-permute-start.1
  2.3 1.7 collective-permute-start.2
  3.9 1.7 collective-permute-start.3
  5.6 1.6 collective-permute-start.4
  7.8 0.8 pad_add_fusion
  8.6 0.1 pad_add_fusion.1.place.refs_2_
  8.7 1.0 collective-permute-done
  9.7 0.8 add_select_fusion.lists
  10.6 0.7 copy-done.1
  11.2 4.0 %plan.1 = (s32[3,64]{1,0:T(4,128)S(1)}, s32[17]{0:T(128)S(1)}) custom-call(s32[2,128]{1,0:T(2,128)S(1)} %add_select_fusion.lists, s32[3]{0:T(128)S(1)} %pad_add_fusion.1.place.refs_2_, s32[16]{0:T(128)S(1)} %copy-done.1), custom_call_target="tpu_custom_call" | custom-call | tf_op jit(solution)/shard_map/plan/pallas_call | solution.py:227
  15.2 5.5 %collective-permute-done.1.refs_6_ = bf16[512,768]{1,0:T(8,128)(2,1)S(1)} collective-permute-done((bf16[512,768]{1,0:T(8,128)(2,1)}, bf16[512,768]{1,0:T(8,128)(2,1)S(1)}, u32[]{:S(2)}, u32[]{:S(2)}) %collective-permute-start.1) | collective-permute-done | bytes 786464 | tf_op jit(solution)/shard_map/ppermute | solution.py:207
  20.7 0.7 collective-permute-done.2.refs_7_
  21.5 0.1 collective-permute-done.3.refs_8_
  21.6 0.1 collective-permute-done.4.refs_9_
  21.7 1.2 collective-permute-start.5
  22.8 2.9 %collective-permute-start.6 = (bf16[512,768]{1,0:T(8,128)(2,1)S(1)}, bf16[512,768]{1,0:T(8,128)(2,1)S(1)}, u32[]{:S(2)}, u32[]{:S(2)}) collective-permute-start(bf16[512,768]{1,0:T(8,128)(2,1)S(1)} %collective-permute-done.2.refs_7_), channel_id=1, source_target_pairs={{0,24},{4,100},{8,0},{12,108},{16,8},{20,116},{24,16},{28,124},{32... | collective-permute-start | bytes 2359304 | tf_op jit(solution)/shard_map/ppermute | solution.py:207
  25.7 1.8 collective-permute-start.7
  27.5 0.6 room.1.refs_10_
  28.1 1.5 collective-permute-start.12
  29.6 2.0 %collective-permute-start.11 = (bf16[512,768]{1,0:T(8,128)(2,1)S(1)}, bf16[512,768]{1,0:T(8,128)(2,1)S(1)}, u32[]{:S(2)}, u32[]{:S(2)}) collective-permute-start(bf16[512,768]{1,0:T(8,128)(2,1)S(1)} %collective-permute-done.1.refs_6_), channel_id=1, source_target_pairs={{0,96},{4,28},{8,104},{12,4},{16,112},{20,12},{24,120},{28,20},{32... | collective-permute-start | bytes 2359304 | tf_op jit(solution)/shard_map/ppermute | solution.py:207
  31.6 1.2 collective-permute-done.5.refs_4_
  32.8 2.0 %collective-permute-start.13 = (bf16[512,768]{1,0:T(8,128)(2,1)S(1)}, bf16[512,768]{1,0:T(8,128)(2,1)S(1)}, u32[]{:S(2)}, u32[]{:S(2)}) collective-permute-start(bf16[512,768]{1,0:T(8,128)(2,1)S(1)} %collective-permute-done.1.refs_6_), channel_id=1, source_target_pairs={{0,32},{4,12},{8,40},{12,20},{16,48},{20,28},{24,56},{28,4},{32,64... | collective-permute-start | bytes 2359304 | tf_op jit(solution)/shard_map/ppermute | solution.py:207
  34.8 0.7 copy-done.2
  35.5 8.2 %build.5 = (bf16[64,512,512]{2,1,0:T(8,128)(2,1)S(1)}, f32[16,512]{1,0:T(8,128)S(1)}) custom-call(s32[3,64]{1,0:T(4,128)S(1)} %get-tuple-element.44.pairs.refs_0_, s32[17]{0:T(128)S(1)} %get-tuple-element.46.bounds.refs_1_, s32[3]{0:T(128)S(1)} %pad_add_fusion.1.place.refs_2_, bf16[4096,768]{1,0:T(8,128)(2,1)} %refs_3_.9, ...), custom_call_target="tpu_custom_call", output_to_operand_aliasing={{0}: (10, {})} | custom-call | flops 4026531840 | bytes 15728640 | tf_op jit(solution)/shard_map/build/pallas_call | solution.py:251
  43.7 2.7 %collective-permute-start.10 = (bf16[512,768]{1,0:T(8,128)(2,1)S(1)}, bf16[512,768]{1,0:T(8,128)(2,1)S(1)}, u32[]{:S(2)}, u32[]{:S(2)}) collective-permute-start(bf16[512,768]{1,0:T(8,128)(2,1)S(1)} %collective-permute-done.6.refs_5_), channel_id=1, source_target_pairs={{0,96},{4,28},{8,104},{12,4},{16,112},{20,12},{24,120},{28,20},{32... | collective-permute-start | bytes 2359304 | tf_op jit(solution)/shard_map/ppermute | solution.py:207
  46.4 0.9 collective-permute-start.15
  47.3 5.0 %build.6 = (bf16[64,512,512]{2,1,0:T(8,128)(2,1)S(1)}, f32[16,512]{1,0:T(8,128)S(1)}) custom-call(s32[3,64]{1,0:T(4,128)S(1)} %get-tuple-element.44.pairs.refs_0_, s32[17]{0:T(128)S(1)} %get-tuple-element.46.bounds.refs_1_, s32[3]{0:T(128)S(1)} %pad_add_fusion.1.place.refs_2_, bf16[4096,768]{1,0:T(8,128)(2,1)} %refs_3_.9, ...), custom_call_target="tpu_custom_call", output_to_operand_aliasing={{0}: (7, {})} | custom-call | flops 1610612736 | bytes 6291456 | tf_op jit(solution)/shard_map/build/pallas_call | solution.py:251
  52.3 3.4 %collective-permute-start.9 = (bf16[512,768]{1,0:T(8,128)(2,1)S(1)}, bf16[512,768]{1,0:T(8,128)(2,1)S(1)}, u32[]{:S(2)}, u32[]{:S(2)}) collective-permute-start(bf16[512,768]{1,0:T(8,128)(2,1)S(1)} %collective-permute-done.6.refs_5_), channel_id=1, source_target_pairs={{0,32},{4,12},{8,40},{12,20},{16,48},{20,28},{24,56},{28,4},{32,64... | collective-permute-start | bytes 2359304 | tf_op jit(solution)/shard_map/ppermute | solution.py:207
  55.7 2.0 %collective-permute-start.8 = (bf16[512,768]{1,0:T(8,128)(2,1)S(1)}, bf16[512,768]{1,0:T(8,128)(2,1)S(1)}, u32[]{:S(2)}, u32[]{:S(2)}) collective-permute-start(bf16[512,768]{1,0:T(8,128)(2,1)S(1)} %collective-permute-done.3.refs_8_), channel_id=1, source_target_pairs={{0,32},{4,12},{8,40},{12,20},{16,48},{20,28},{24,56},{28,4},{32,64... | collective-permute-start | bytes 2359304 | tf_op jit(solution)/shard_map/ppermute | solution.py:207
  57.7 3.4 %build.7 = (bf16[64,512,512]{2,1,0:T(8,128)(2,1)S(1)}, f32[16,512]{1,0:T(8,128)S(1)}) custom-call(s32[3,64]{1,0:T(4,128)S(1)} %get-tuple-element.44.pairs.refs_0_, s32[17]{0:T(128)S(1)} %get-tuple-element.46.bounds.refs_1_, s32[3]{0:T(128)S(1)} %pad_add_fusion.1.place.refs_2_, bf16[4096,768]{1,0:T(8,128)(2,1)} %refs_3_.9, ...), custom_call_target="tpu_custom_call", output_to_operand_aliasing={{0}: (8, {})} | custom-call | flops 2415919104 | bytes 9437184 | tf_op jit(solution)/shard_map/build/pallas_call | solution.py:251
  61.1 3.0 %collective-permute-start.14 = (bf16[512,768]{1,0:T(8,128)(2,1)S(1)}, bf16[512,768]{1,0:T(8,128)(2,1)S(1)}, u32[]{:S(2)}, u32[]{:S(2)}) collective-permute-start(bf16[512,768]{1,0:T(8,128)(2,1)S(1)} %collective-permute-done.10.refs_5_), channel_id=1, source_target_pairs={{0,96},{4,28},{8,104},{12,4},{16,112},{20,12},{24,120},{28,20},{32... | collective-permute-start | bytes 2359304 | tf_op jit(solution)/shard_map/ppermute | solution.py:207
  64.1 4.5 %collective-permute-done.16.refs_7_ = bf16[512,768]{1,0:T(8,128)(2,1)S(1)} collective-permute-done((bf16[512,768]{1,0:T(8,128)(2,1)S(1)}, bf16[512,768]{1,0:T(8,128)(2,1)S(1)}, u32[]{:S(2)}, u32[]{:S(2)}) %collective-permute-start.16) | collective-permute-done | bytes 786464 | tf_op jit(solution)/shard_map/ppermute | solution.py:207
  68.6 6.5 %build.8 = (bf16[64,512,512]{2,1,0:T(8,128)(2,1)S(1)}, f32[16,512]{1,0:T(8,128)S(1)}) custom-call(s32[3,64]{1,0:T(4,128)S(1)} %get-tuple-element.44.pairs.refs_0_, s32[17]{0:T(128)S(1)} %get-tuple-element.46.bounds.refs_1_, s32[3]{0:T(128)S(1)} %pad_add_fusion.1.place.refs_2_, bf16[4096,768]{1,0:T(8,128)(2,1)} %refs_3_.9, ...), custom_call_target="tpu_custom_call", output_to_operand_aliasing={{0}: (8, {})} | custom-call | flops 2415919104 | bytes 9437184 | tf_op jit(solution)/shard_map/build/pallas_call | solution.py:251
  75.1 1.3 collective-permute-done.8.refs_5_
  76.5 0.6 collective-permute-done.14.refs_7_
  77.1 1.0 build.9
  78.1 16.2 %all_to_all.30.refs_3_ = f32[8,16,512]{2,1,0:T(8,128)S(1)} all-to-all(f32[8,16,512]{2,1,0:T(8,128)S(1)} %get-tuple-element.74), channel_id=1, replica_groups=mesh['y'=4,'x'=4,'core'=2,'z'=4] {'core','z'}, dimensions={0} | all-to-all | bytes 524288 | tf_op jit(solution)/shard_map/all_to_all | solution.py:311
  94.3 2.6 %columns.3 = (f32[16,16,512]{2,1,0:T(8,128)S(1)}, bf16[64,512,512]{2,1,0:T(8,128)(2,1)S(1)}) custom-call(s32[3,64]{1,0:T(4,128)S(1)} %get-tuple-element.44.pairs.refs_0_, s32[17]{0:T(128)S(1)} %get-tuple-element.46.bounds.refs_1_, s32[3]{0:T(128)S(1)} %pad_add_fusion.1.place.refs_2_, ...), custom_call_target="tpu_custom_call", output_to_operand_aliasing={{1}: (4, {})} | custom-call | tf_op jit(solution)/shard_map/columns/pallas_call | solution.py:297
  97.0 23.0 %all_to_all.31.refs_3_ = f32[16,16,512]{2,1,0:T(8,128)S(1)} all-to-all(f32[16,16,512]{2,1,0:T(8,128)S(1)} %get-tuple-element.76), channel_id=1, replica_groups=mesh['y'=4,'x'=4,'core'=2,'z'=4] {'y','x'}, dimensions={0} | all-to-all | bytes 1048576 | tf_op jit(solution)/shard_map/all_to_all | solution.py:314
  120.0 4.0 %rows.2 = (f32[8,16,512]{2,1,0:T(8,128)S(1)}, bf16[64,512,512]{2,1,0:T(8,128)(2,1)S(1)}) custom-call(s32[3,64]{1,0:T(4,128)S(1)} %get-tuple-element.44.pairs.refs_0_, s32[17]{0:T(128)S(1)} %get-tuple-element.46.bounds.refs_1_, s32[3]{0:T(128)S(1)} %pad_add_fusion.1.place.refs_2_, ...), custom_call_target="tpu_custom_call", output_to_operand_aliasing={{1}: (4, {})} | custom-call | tf_op jit(solution)/shard_map/rows/pallas_call | solution.py:297
  124.0 9.8 %all_to_all.32.refs_3_ = f32[8,16,512]{2,1,0:T(8,128)S(1)} all-to-all(f32[8,16,512]{2,1,0:T(8,128)S(1)} %get-tuple-element.78), channel_id=1, replica_groups=mesh['y'=4,'x'=4,'core'=2,'z'=4] {'core','z'}, dimensions={0} | all-to-all | bytes 524288 | tf_op jit(solution)/shard_map/all_to_all | solution.py:311
  133.7 2.6 %columns.4 = (f32[16,16,512]{2,1,0:T(8,128)S(1)}, bf16[64,512,512]{2,1,0:T(8,128)(2,1)S(1)}) custom-call(s32[3,64]{1,0:T(4,128)S(1)} %get-tuple-element.44.pairs.refs_0_, s32[17]{0:T(128)S(1)} %get-tuple-element.46.bounds.refs_1_, s32[3]{0:T(128)S(1)} %pad_add_fusion.1.place.refs_2_, ...), custom_call_target="tpu_custom_call", output_to_operand_aliasing={{1}: (4, {})} | custom-call | tf_op jit(solution)/shard_map/columns/pallas_call | solution.py:297
  136.4 16.7 %all_to_all.33.refs_3_ = f32[16,16,512]{2,1,0:T(8,128)S(1)} all-to-all(f32[16,16,512]{2,1,0:T(8,128)S(1)} %get-tuple-element.80), channel_id=1, replica_groups=mesh['y'=4,'x'=4,'core'=2,'z'=4] {'y','x'}, dimensions={0} | all-to-all | bytes 1048576 | tf_op jit(solution)/shard_map/all_to_all | solution.py:314
  153.0 4.0 %rows.3 = (f32[8,16,512]{2,1,0:T(8,128)S(1)}, bf16[64,512,512]{2,1,0:T(8,128)(2,1)S(1)}) custom-call(s32[3,64]{1,0:T(4,128)S(1)} %get-tuple-element.44.pairs.refs_0_, s32[17]{0:T(128)S(1)} %get-tuple-element.46.bounds.refs_1_, s32[3]{0:T(128)S(1)} %pad_add_fusion.1.place.refs_2_, ...), custom_call_target="tpu_custom_call", output_to_operand_aliasing={{1}: (4, {})} | custom-call | tf_op jit(solution)/shard_map/rows/pallas_call | solution.py:297
  157.0 9.3 %all_to_all.34.refs_3_ = f32[8,16,512]{2,1,0:T(8,128)S(1)} all-to-all(f32[8,16,512]{2,1,0:T(8,128)S(1)} %get-tuple-element.82), channel_id=1, replica_groups=mesh['y'=4,'x'=4,'core'=2,'z'=4] {'core','z'}, dimensions={0} | all-to-all | bytes 524288 | tf_op jit(solution)/shard_map/all_to_all | solution.py:311
  166.3 3.2 %columns.5 = (f32[16,4,128]{2,1,0:T(4,128)S(1)}, f32[32,128]{1,0:T(8,128)}) custom-call(s32[3,64]{1,0:T(4,128)S(1)} %get-tuple-element.44.pairs.refs_0_, s32[17]{0:T(128)S(1)} %get-tuple-element.46.bounds.refs_1_, s32[3]{0:T(128)S(1)} %pad_add_fusion.1.place.refs_2_, f32[8,16,512]{2,1,0:T(8,128)S(1)} %all_to_all.34.refs_3_, ...), custom_call_target="tpu_custom_call" | custom-call | tf_op jit(solution)/shard_map/columns/pallas_call | solution.py:297
  169.6 12.3 %all_to_all.35 = f32[16,4,128]{2,1,0:T(4,128)S(1)} all-to-all(f32[16,4,128]{2,1,0:T(4,128)S(1)} %get-tuple-element.85), channel_id=1, replica_groups=mesh['y'=4,'x'=4,'core'=2,'z'=4] {'y','x'}, dimensions={0} | all-to-all | bytes 65536 | tf_op jit(solution)/shard_map/all_to_all | solution.py:316
  181.9 0.6 log_bitcast_fusion
  (17 shorter events, 0.1 us)
Async XLA Ops:
  0.6 34.8 %copy-start = (bf16[512,768]{1,0:T(8,128)(2,1)S(1)}, bf16[512,768]{1,0:T(8,128)(2,1)}, u32[]{:S(2)}) copy-start(bf16[512,768]{1,0:T(8,128)(2,1)} %refs_5_.1) | copy-start | bytes 2359300
  0.6 20.1 %collective-permute-start.1 = (bf16[512,768]{1,0:T(8,128)(2,1)}, bf16[512,768]{1,0:T(8,128)(2,1)S(1)}, u32[]{:S(2)}, u32[]{:S(2)}) collective-permute-start(bf16[512,768]{1,0:T(8,128)(2,1)} %refs_5_.1), channel_id=1, source_target_pairs={{0,8},{4,36},{8,16},{12,44},{16,24},{20,52},{24,0},{28,60},{32,40}... | collective-permute-start | bytes 2359304 | tf_op jit(solution)/shard_map/ppermute | solution.py:207
  2.3 19.2 %collective-permute-start.2 = (bf16[512,768]{1,0:T(8,128)(2,1)}, bf16[512,768]{1,0:T(8,128)(2,1)S(1)}, u32[]{:S(2)}, u32[]{:S(2)}) collective-permute-start(bf16[512,768]{1,0:T(8,128)(2,1)} %refs_5_.1), channel_id=1, source_target_pairs={{0,24},{4,100},{8,0},{12,108},{16,8},{20,116},{24,16},{28,124},{32... | collective-permute-start | bytes 2359304 | tf_op jit(solution)/shard_map/ppermute | solution.py:207
  3.9 17.6 %collective-permute-start.3 = (bf16[512,768]{1,0:T(8,128)(2,1)}, bf16[512,768]{1,0:T(8,128)(2,1)S(1)}, u32[]{:S(2)}, u32[]{:S(2)}) collective-permute-start(bf16[512,768]{1,0:T(8,128)(2,1)} %refs_5_.1), channel_id=1, source_target_pairs={{0,32},{4,12},{8,40},{12,20},{16,48},{20,28},{24,56},{28,4},{32,64... | collective-permute-start | bytes 2359304 | tf_op jit(solution)/shard_map/ppermute | solution.py:207
  5.6 16.1 %collective-permute-start.4 = (bf16[512,768]{1,0:T(8,128)(2,1)}, bf16[512,768]{1,0:T(8,128)(2,1)}, u32[]{:S(2)}, u32[]{:S(2)}) collective-permute-start(bf16[512,768]{1,0:T(8,128)(2,1)} %refs_5_.1), channel_id=1, source_target_pairs={{0,96},{4,28},{8,104},{12,4},{16,112},{20,12},{24,120},{28,20},{32... | collective-permute-start | bytes 2359304 | tf_op jit(solution)/shard_map/ppermute | solution.py:207
  8.6 1.1 collective-permute-start
  10.5 0.7 copy-start.1
  21.7 11.1 %collective-permute-start.5 = (bf16[4096,768]{1,0:T(8,128)(2,1)}, bf16[4096,768]{1,0:T(8,128)(2,1)S(1)}, u32[]{:S(2)}, u32[]{:S(2)}) collective-permute-start(bf16[4096,768]{1,0:T(8,128)(2,1)} %refs_3_.9), channel_id=1, source_target_pairs={{0,4},{4,0},{1,5},{5,1},{2,6},{6,2},{3,7},{7,3},{8,12},{12,8},{9,1... | collective-permute-start | bytes 18874376 | tf_op jit(solution)/shard_map/ppermute | solution.py:276
  22.8 20.8 %collective-permute-start.6 = (bf16[512,768]{1,0:T(8,128)(2,1)S(1)}, bf16[512,768]{1,0:T(8,128)(2,1)S(1)}, u32[]{:S(2)}, u32[]{:S(2)}) collective-permute-start(bf16[512,768]{1,0:T(8,128)(2,1)S(1)} %collective-permute-done.2.refs_7_), channel_id=1, source_target_pairs={{0,24},{4,100},{8,0},{12,108},{16,8},{20,116},{24,16},{28,124},{32... | collective-permute-start | bytes 2359304 | tf_op jit(solution)/shard_map/ppermute | solution.py:207
  25.7 18.0 %collective-permute-start.7 = (bf16[512,768]{1,0:T(8,128)(2,1)S(1)}, bf16[512,768]{1,0:T(8,128)(2,1)S(1)}, u32[]{:S(2)}, u32[]{:S(2)}) collective-permute-start(bf16[512,768]{1,0:T(8,128)(2,1)S(1)} %collective-permute-done.2.refs_7_), channel_id=1, source_target_pairs={{0,32},{4,12},{8,40},{12,20},{16,48},{20,28},{24,56},{28,4},{32,64... | collective-permute-start | bytes 2359304 | tf_op jit(solution)/shard_map/ppermute | solution.py:207
  28.1 24.2 %collective-permute-start.12 = (bf16[512,768]{1,0:T(8,128)(2,1)S(1)}, bf16[512,768]{1,0:T(8,128)(2,1)S(1)}, u32[]{:S(2)}, u32[]{:S(2)}) collective-permute-start(bf16[512,768]{1,0:T(8,128)(2,1)S(1)} %collective-permute-done.2.refs_7_), channel_id=1, source_target_pairs={{0,96},{4,28},{8,104},{12,4},{16,112},{20,12},{24,120},{28,20},{32... | collective-permute-start | bytes 2359304 | tf_op jit(solution)/shard_map/ppermute | solution.py:207
  29.6 26.1 %collective-permute-start.11 = (bf16[512,768]{1,0:T(8,128)(2,1)S(1)}, bf16[512,768]{1,0:T(8,128)(2,1)S(1)}, u32[]{:S(2)}, u32[]{:S(2)}) collective-permute-start(bf16[512,768]{1,0:T(8,128)(2,1)S(1)} %collective-permute-done.1.refs_6_), channel_id=1, source_target_pairs={{0,96},{4,28},{8,104},{12,4},{16,112},{20,12},{24,120},{28,20},{32... | collective-permute-start | bytes 2359304 | tf_op jit(solution)/shard_map/ppermute | solution.py:207
  32.8 2.6 %copy-start.2 = (bf16[4096,768]{1,0:T(8,128)(2,1)}, bf16[4096,768]{1,0:T(8,128)(2,1)S(1)}, u32[]{:S(2)}) copy-start(bf16[4096,768]{1,0:T(8,128)(2,1)S(1)} %collective-permute-done.5.refs_4_) | copy-start | bytes 18874372
  32.8 22.9 %collective-permute-start.13 = (bf16[512,768]{1,0:T(8,128)(2,1)S(1)}, bf16[512,768]{1,0:T(8,128)(2,1)S(1)}, u32[]{:S(2)}, u32[]{:S(2)}) collective-permute-start(bf16[512,768]{1,0:T(8,128)(2,1)S(1)} %collective-permute-done.1.refs_6_), channel_id=1, source_target_pairs={{0,32},{4,12},{8,40},{12,20},{16,48},{20,28},{24,56},{28,4},{32,64... | collective-permute-start | bytes 2359304 | tf_op jit(solution)/shard_map/ppermute | solution.py:207
  43.7 17.4 %collective-permute-start.10 = (bf16[512,768]{1,0:T(8,128)(2,1)S(1)}, bf16[512,768]{1,0:T(8,128)(2,1)S(1)}, u32[]{:S(2)}, u32[]{:S(2)}) collective-permute-start(bf16[512,768]{1,0:T(8,128)(2,1)S(1)} %collective-permute-done.6.refs_5_), channel_id=1, source_target_pairs={{0,96},{4,28},{8,104},{12,4},{16,112},{20,12},{24,120},{28,20},{32... | collective-permute-start | bytes 2359304 | tf_op jit(solution)/shard_map/ppermute | solution.py:207
  46.4 22.2 %collective-permute-start.15 = (bf16[512,768]{1,0:T(8,128)(2,1)S(1)}, bf16[512,768]{1,0:T(8,128)(2,1)S(1)}, u32[]{:S(2)}, u32[]{:S(2)}) collective-permute-start(bf16[512,768]{1,0:T(8,128)(2,1)S(1)} %collective-permute-done.7.refs_6_), channel_id=1, source_target_pairs={{0,32},{4,12},{8,40},{12,20},{16,48},{20,28},{24,56},{28,4},{32,64... | collective-permute-start | bytes 2359304 | tf_op jit(solution)/shard_map/ppermute | solution.py:207
  52.3 24.1 %collective-permute-start.9 = (bf16[512,768]{1,0:T(8,128)(2,1)S(1)}, bf16[512,768]{1,0:T(8,128)(2,1)S(1)}, u32[]{:S(2)}, u32[]{:S(2)}) collective-permute-start(bf16[512,768]{1,0:T(8,128)(2,1)S(1)} %collective-permute-done.6.refs_5_), channel_id=1, source_target_pairs={{0,32},{4,12},{8,40},{12,20},{16,48},{20,28},{24,56},{28,4},{32,64... | collective-permute-start | bytes 2359304 | tf_op jit(solution)/shard_map/ppermute | solution.py:207
  55.7 12.9 %collective-permute-start.16 = (bf16[512,768]{1,0:T(8,128)(2,1)S(1)}, bf16[512,768]{1,0:T(8,128)(2,1)S(1)}, u32[]{:S(2)}, u32[]{:S(2)}) collective-permute-start(bf16[512,768]{1,0:T(8,128)(2,1)S(1)} %collective-permute-done.11.refs_5_), channel_id=1, source_target_pairs={{0,96},{4,28},{8,104},{12,4},{16,112},{20,12},{24,120},{28,20},{32... | collective-permute-start | bytes 2359304 | tf_op jit(solution)/shard_map/ppermute | solution.py:207
  55.7 20.7 %collective-permute-start.8 = (bf16[512,768]{1,0:T(8,128)(2,1)S(1)}, bf16[512,768]{1,0:T(8,128)(2,1)S(1)}, u32[]{:S(2)}, u32[]{:S(2)}) collective-permute-start(bf16[512,768]{1,0:T(8,128)(2,1)S(1)} %collective-permute-done.3.refs_8_), channel_id=1, source_target_pairs={{0,32},{4,12},{8,40},{12,20},{16,48},{20,28},{24,56},{28,4},{32,64... | collective-permute-start | bytes 2359304 | tf_op jit(solution)/shard_map/ppermute | solution.py:207
  61.1 15.9 %collective-permute-start.14 = (bf16[512,768]{1,0:T(8,128)(2,1)S(1)}, bf16[512,768]{1,0:T(8,128)(2,1)S(1)}, u32[]{:S(2)}, u32[]{:S(2)}) collective-permute-start(bf16[512,768]{1,0:T(8,128)(2,1)S(1)} %collective-permute-done.10.refs_5_), channel_id=1, source_target_pairs={{0,96},{4,28},{8,104},{12,4},{16,112},{20,12},{24,120},{28,20},{32... | collective-permute-start | bytes 2359304 | tf_op jit(solution)/shard_map/ppermute | solution.py:207

commit v9 on v7

--- a/solution.py
+++ b/solution.py
@@ -85,7 +85,8 @@
 
 
 def build_kernel(scale, first, blocks, last, pairs, bounds, place, a_mine, a_other, *refs):
-    b_refs, (_, kv_in, store, out), scratch = refs[:blocks], refs[blocks : blocks + 4], refs[blocks + 4 :]
+    pieces = len(refs) - 9
+    b_refs, (_, kv_in, store, out), scratch = refs[:pieces], refs[pieces : pieces + 4], refs[pieces + 4 :]
     kv, abuf, bbuf, a_sems, b_sems = scratch
     core = place[0]
     low, high = bounds[first], bounds[first + blocks]
@@ -106,13 +107,17 @@
             def _():
                 pltpu.make_async_copy(a_other.at[pl.ds(row, TILE)], abuf.at[slot], a_sems.at[slot]).start()
 
-    loads = [pltpu.make_async_copy(b_refs[k], bbuf.at[k], b_sems.at[k]) for k in range(blocks)]
+    loads, filled = [], 0
+    for k in range(pieces):
+        rows = b_refs[k].shape[0]
+        spot = bbuf.at[filled // TILE, pl.ds(filled % TILE, rows)]
+        loads.append(pltpu.make_async_copy(b_refs[k], spot, b_sems.at[k]))
+        filled += rows
     for load in loads:
         load.start()
     for k in range(ahead):
         fetch(low + k)
     kv[...] = kv_in[...]
-    ones = jnp.ones((16, TILE), BF16)
     for load in loads:
         load.wait()
 
@@ -134,8 +139,12 @@
             score = lax.dot_general(block_a, block_b, (((1,), (1,)), ((), ())), preferred_element_type=F32)
             tile = jnp.exp(score * scale).astype(BF16)
             store[t] = tile
-            part = lax.dot_general(ones, tile, (((1,), (1,)), ((), ())), preferred_element_type=F32)
-            sums.append((pairs[0, t], jnp.where(base + k < high, part[0:1], 0.0)))
+            wide = tile.astype(F32)
+            part = wide[:, :LANES]
+            for q in range(1, TILE // LANES):
+                part = part + wide[:, q * LANES : (q + 1) * LANES]
+            part = jnp.sum(part.T, axis=0, keepdims=True)
+            sums.append((pairs[0, t], jnp.where(base + k < high, part, 0.0)))
         for a, part in sums:
             kv[pl.ds(a, 1), :] += part
         return carry
@@ -175,10 +184,17 @@
             b = pairs[1, safe]
             source, target = (b, a) if over_rows else (a, b)
             row = jnp.where(t < number, weight[pl.ds(source, 1), :], 0.0)
+            if over_rows and k % 2 == 0:
+                part = store[safe, :, :LANES].astype(F32) * row[:, :LANES]
+                for q in range(1, TILE // LANES):
+                    lanes = slice(q * LANES, (q + 1) * LANES)
+                    part = part + store[safe, :, lanes].astype(F32) * row[:, lanes]
+                found.append((target, jnp.sum(part.T, axis=0, keepdims=True)))
+                continue
             row = jnp.broadcast_to(row, (16, TILE)).astype(BF16)
-            found.append((target, lax.dot_general(row, store[safe], dims, preferred_element_type=F32)))
+            found.append((target, lax.dot_general(row, store[safe], dims, preferred_element_type=F32)[0:1]))
         for target, part in found:
-            sums[pl.ds(target, 1), :] += part[0:1]
+            sums[pl.ds(target, 1), :] += part
         return carry
 
     lax.fori_loop(0, (number + size - 1) // size, step, 0)
@@ -246,23 +262,24 @@
     )(pairs, bounds, place)
 
     def build(first, group, store, kv):
-        blocks = len(group)
+        blocks = sum(piece.shape[0] for piece in group) // TILE
+        pieces = len(group)
         last = first + blocks == NCHIP
         shape = (NC * NZ, NC * ABLK, TILE) if last else (NC * ABLK, TILE)
         share = 2 * blocks
         return pl.pallas_call(
             lambda *refs: build_kernel(scale, first, blocks, last, *refs),
             out_shape=(pltpu.VMEM((CAP, TILE, TILE), BF16), jax.ShapeDtypeStruct(shape, F32)),
-            in_specs=[SM, SM, SM, HB, HB] + [ANY] * blocks + [VM, VM],
+            in_specs=[SM, SM, SM, HB, HB] + [ANY] * pieces + [VM, VM],
             out_specs=(VM, VM),
             scratch_shapes=[
                 pltpu.VMEM((NC * ABLK, TILE), F32),
                 pltpu.VMEM((BUFFERS, TILE, width), BF16),
                 pltpu.VMEM((blocks, TILE, width), BF16),
                 pltpu.SemaphoreType.DMA((BUFFERS,)),
-                pltpu.SemaphoreType.DMA((blocks,)),
+                pltpu.SemaphoreType.DMA((pieces,)),
             ],
-            input_output_aliases={5 + blocks: 0},
+            input_output_aliases={5 + pieces: 0},
             cost_estimate=pl.CostEstimate(
                 flops=share * 2 * TILE * TILE * width,
                 transcendentals=share * TILE * TILE,

time: 177 us -> 172 us (0.972); the launches traced: 175 us -> 172 us
  Pallas kernels: 51.3 us -> 47.6 us
  blocking collectives: 78.3 us -> 81 us
  starting transfers between devices: 29.7 us -> 27.9 us
    all_to_all x2, blocking collectives: 28.7 us -> 36.7 us  [on_device(): ktu_parts = lax.all_to_all(ktu, ('y', 'x'), 0, 0, tiled=True)]
    all_to_all x3, blocking collectives: 39.5 us -> 32.8 us  [on_device(): kv_parts = lax.all_to_all(kv, ('core', 'z'), 0, 0, tiled=True)]
    pallas_call x5, Pallas kernels: 17.7 us -> 14.6 us  [half(): pl.pallas_call(lambda *refs: pass_kernel(over_rows, last, *refs), out_sha...]
    ppermute x15, starting transfers between devices: 29.6 us -> 27.8 us  [go(): return lax.ppermute(block, ('y', 'x', 'core'), moves(first, shift))]
  transfers between devices with their start and end apart: 17 -> 17, of which waited for: 4 -> 5; matrix products, arithmetic and copies ran while one was open for 1% -> 1% of each run, Pallas kernels for 19% -> 19%
where the time goes in v9:
time: 172 us
  blocking collectives  81 us (47%)
  Pallas kernels  47.6 us (28%)
  starting transfers between devices  27.9 us (16%)
  waiting for transfers between devices  11.3 us (7%)
  other arithmetic  2.26 us (1%)
    all_to_all x2, blocking collectives, on_device(): ktu_parts = lax.all_to_all(ktu, ('y', 'x'), 0, 0, tiled=True)  36.7 us
    all_to_all x3, blocking collectives, on_device(): kv_parts = lax.all_to_all(kv, ('core', 'z'), 0, 0, tiled=True)  32.8 us
    pallas_call x6, Pallas kernels, build(): pl.pallas_call(lambda *refs: build_kernel(scale, first, blocks, last, *re...  27.8 us
    ppermute x15, starting transfers between devices, go(): return lax.ppermute(block, ('y', 'x', 'core'), moves(first, shift))  27.8 us
    pallas_call x5, Pallas kernels, half(): pl.pallas_call(lambda *refs: pass_kernel(over_rows, last, *refs), out_sha...  14.6 us
    all_to_all x1, blocking collectives, on_device(): mine = lax.all_to_all(ktu, ('y', 'x'), 0, 0, tiled=True)  11.5 us
    ppermute x15, waiting for transfers between devices, go(): return lax.ppermute(block, ('y', 'x', 'core'), moves(first, shift))  7.7 us
    pallas_call x1, Pallas kernels, on_device(): pl.pallas_call(plan_kernel, out_shape=(jax.ShapeDtypeStruct((3, CAP), jnp...  4.65 us
  transfers between devices with their start and end apart: 17, of which 5 were waited for; matrix products, arithmetic and copies ran while one was open for 1% of the time, Pallas kernels for 19%

profile of v9, /device:TPU:0, one launch (start us, length us, event | category | flops | bytes accessed | tf_op | source)
XLA Modules:
  0.0 172.2 jit_solution(16370297944960320334)
XLA Ops:
  0.6 0.0 copy-start
  0.6 0.1 collective-permute-start.3
  0.7 1.6 collective-permute-start.1
  2.4 1.7 collective-permute-start.2
  4.7 0.8 pad_add_fusion
  5.5 0.0 collective-permute-start
  5.5 1.7 %collective-permute-start.6 = (bf16[512,768]{1,0:T(8,128)(2,1)}, bf16[512,768]{1,0:T(8,128)(2,1)S(1)}, u32[]{:S(2)}, u32[]{:S(2)}) collective-permute-start(bf16[512,768]{1,0:T(8,128)(2,1)} %refs_5_.1), channel_id=1, source_target_pairs={{0,32},{4,12},{8,40},{12,20},{16,48},{20,28},{24,56},{28,4},{32,64... | collective-permute-start | bytes 2359304 | tf_op jit(solution)/shard_map/ppermute | solution.py:224
  7.2 3.6 %collective-permute-done = s32[1,128]{1,0:T(1,128)S(1)} collective-permute-done((s32[1,128]{1,0:T(1,128)S(1)}, s32[1,128]{1,0:T(1,128)S(1)}, u32[]{:S(2)}, u32[]{:S(2)}) %collective-permute-start) | collective-permute-done | bytes 544 | tf_op jit(solution)/shard_map/ppermute | solution.py:236
  10.8 3.1 %collective-permute-start.7 = (bf16[512,768]{1,0:T(8,128)(2,1)}, bf16[512,768]{1,0:T(8,128)(2,1)}, u32[]{:S(2)}, u32[]{:S(2)}) collective-permute-start(bf16[512,768]{1,0:T(8,128)(2,1)} %refs_5_.1), channel_id=1, source_target_pairs={{0,96},{4,28},{8,104},{12,4},{16,112},{20,12},{24,120},{28,20},{32... | collective-permute-start | bytes 2359304 | tf_op jit(solution)/shard_map/ppermute | solution.py:224
  13.9 0.1 pad_add_fusion.1.place.refs_2_
  14.0 0.8 add_select_fusion.lists
  14.8 0.7 copy-done.1
  15.5 4.7 %plan.1 = (s32[3,64]{1,0:T(4,128)S(1)}, s32[17]{0:T(128)S(1)}) custom-call(s32[2,128]{1,0:T(2,128)S(1)} %add_select_fusion.lists, s32[3]{0:T(128)S(1)} %pad_add_fusion.1.place.refs_2_, s32[16]{0:T(128)S(1)} %copy-done.1), custom_call_target="tpu_custom_call" | custom-call | tf_op jit(solution)/shard_map/plan/pallas_call | solution.py:245
  20.1 0.0 collective-permute-done.1.refs_6_
  20.2 0.0 collective-permute-done.2.refs_7_
  20.2 1.0 collective-permute-start.4
  21.1 1.7 collective-permute-start.5
  22.8 0.6 room.1.refs_10_
  23.4 0.0 collective-permute-done.6.refs_8_
  23.4 1.6 collective-permute-start.10
  25.0 2.0 %collective-permute-start.11 = (bf16[512,768]{1,0:T(8,128)(2,1)S(1)}, bf16[512,768]{1,0:T(8,128)(2,1)S(1)}, u32[]{:S(2)}, u32[]{:S(2)}) collective-permute-start(bf16[512,768]{1,0:T(8,128)(2,1)S(1)} %collective-permute-done.1.refs_6_), channel_id=1, source_target_pairs={{0,32},{4,12},{8,40},{12,20},{16,48},{20,28},{24,56},{28,4},{32,64... | collective-permute-start | bytes 2359304 | tf_op jit(solution)/shard_map/ppermute | solution.py:224
  27.0 1.3 collective-permute-start.9
  28.3 7.5 %build.6 = (bf16[64,512,512]{2,1,0:T(8,128)(2,1)S(1)}, f32[16,512]{1,0:T(8,128)S(1)}) custom-call(s32[3,64]{1,0:T(4,128)S(1)} %get-tuple-element.45.pairs.refs_0_, s32[17]{0:T(128)S(1)} %get-tuple-element.47.bounds.refs_1_, s32[3]{0:T(128)S(1)} %pad_add_fusion.1.place.refs_2_, bf16[4096,768]{1,0:T(8,128)(2,1)} %refs_3_.11, ...), custom_call_target="tpu_custom_call", output_to_operand_aliasing={{0}: (10, {})} | custom-call | flops 4026531840 | bytes 15728640 | tf_op jit(solution)/shard_map/build/pallas_call | solution.py:270
  35.7 2.1 %collective-permute-done.4.refs_5_ = bf16[512,768]{1,0:T(8,128)(2,1)S(1)} collective-permute-done((bf16[512,768]{1,0:T(8,128)(2,1)S(1)}, bf16[512,768]{1,0:T(8,128)(2,1)S(1)}, u32[]{:S(2)}, u32[]{:S(2)}) %collective-permute-start.4) | collective-permute-done | bytes 786464 | tf_op jit(solution)/shard_map/ppermute | solution.py:224
  37.8 2.6 %collective-permute-start.8 = (bf16[512,768]{1,0:T(8,128)(2,1)S(1)}, bf16[512,768]{1,0:T(8,128)(2,1)S(1)}, u32[]{:S(2)}, u32[]{:S(2)}) collective-permute-start(bf16[512,768]{1,0:T(8,128)(2,1)S(1)} %collective-permute-done.4.refs_5_), channel_id=1, source_target_pairs={{0,96},{4,28},{8,104},{12,4},{16,112},{20,12},{24,120},{28,20},{32... | collective-permute-start | bytes 2359304 | tf_op jit(solution)/shard_map/ppermute | solution.py:224
  40.4 5.7 %build.7 = (bf16[64,512,512]{2,1,0:T(8,128)(2,1)S(1)}, f32[16,512]{1,0:T(8,128)S(1)}) custom-call(s32[3,64]{1,0:T(4,128)S(1)} %get-tuple-element.45.pairs.refs_0_, s32[17]{0:T(128)S(1)} %get-tuple-element.47.bounds.refs_1_, s32[3]{0:T(128)S(1)} %pad_add_fusion.1.place.refs_2_, bf16[4096,768]{1,0:T(8,128)(2,1)} %refs_3_.11, ...), custom_call_target="tpu_custom_call", output_to_operand_aliasing={{0}: (7, {})} | custom-call | flops 1610612736 | bytes 6291456 | tf_op jit(solution)/shard_map/build/pallas_call | solution.py:270
  46.2 0.1 collective-permute-start.15
  46.3 2.7 %collective-permute-done.9.refs_5_ = bf16[512,768]{1,0:T(8,128)(2,1)S(1)} collective-permute-done((bf16[512,768]{1,0:T(8,128)(2,1)S(1)}, bf16[512,768]{1,0:T(8,128)(2,1)S(1)}, u32[]{:S(2)}, u32[]{:S(2)}) %collective-permute-start.9) | collective-permute-done | bytes 786464 | tf_op jit(solution)/shard_map/ppermute | solution.py:224
  49.0 3.7 %collective-permute-start.13 = (bf16[512,768]{1,0:T(8,128)(2,1)S(1)}, bf16[512,768]{1,0:T(8,128)(2,1)S(1)}, u32[]{:S(2)}, u32[]{:S(2)}) collective-permute-start(bf16[512,768]{1,0:T(8,128)(2,1)S(1)} %collective-permute-done.9.refs_5_), channel_id=1, source_target_pairs={{0,96},{4,28},{8,104},{12,4},{16,112},{20,12},{24,120},{28,20},{32... | collective-permute-start | bytes 2359304 | tf_op jit(solution)/shard_map/ppermute | solution.py:224
  52.7 4.6 %build.8 = (bf16[64,512,512]{2,1,0:T(8,128)(2,1)S(1)}, f32[16,512]{1,0:T(8,128)S(1)}) custom-call(s32[3,64]{1,0:T(4,128)S(1)} %get-tuple-element.45.pairs.refs_0_, s32[17]{0:T(128)S(1)} %get-tuple-element.47.bounds.refs_1_, s32[3]{0:T(128)S(1)} %pad_add_fusion.1.place.refs_2_, bf16[4096,768]{1,0:T(8,128)(2,1)} %refs_3_.11, ...), custom_call_target="tpu_custom_call", output_to_operand_aliasing={{0}: (8, {})} | custom-call | flops 2415919104 | bytes 9437184 | tf_op jit(solution)/shard_map/build/pallas_call | solution.py:270
  57.3 0.1 collective-permute-done.8.refs_5_
  57.4 5.8 %collective-permute-start.12 = (bf16[512,768]{1,0:T(8,128)(2,1)S(1)}, bf16[512,768]{1,0:T(8,128)(2,1)S(1)}, u32[]{:S(2)}, u32[]{:S(2)}) collective-permute-start(bf16[512,768]{1,0:T(8,128)(2,1)S(1)} %collective-permute-done.8.refs_5_), channel_id=1, source_target_pairs={{0,96},{4,28},{8,104},{12,4},{16,112},{20,12},{24,120},{28,20},{32... | collective-permute-start | bytes 2359304 | tf_op jit(solution)/shard_map/ppermute | solution.py:224
  63.2 4.5 %build.9 = (bf16[64,512,512]{2,1,0:T(8,128)(2,1)S(1)}, f32[16,512]{1,0:T(8,128)S(1)}) custom-call(s32[3,64]{1,0:T(4,128)S(1)} %get-tuple-element.45.pairs.refs_0_, s32[17]{0:T(128)S(1)} %get-tuple-element.47.bounds.refs_1_, s32[3]{0:T(128)S(1)} %pad_add_fusion.1.place.refs_2_, bf16[4096,768]{1,0:T(8,128)(2,1)} %refs_3_.11, ...), custom_call_target="tpu_custom_call", output_to_operand_aliasing={{0}: (7, {})} | custom-call | flops 1610612736 | bytes 6291456 | tf_op jit(solution)/shard_map/build/pallas_call | solution.py:270
  67.7 2.7 %collective-permute-done.14.refs_6_ = bf16[512,768]{1,0:T(8,128)(2,1)S(1)} collective-permute-done((bf16[512,768]{1,0:T(8,128)(2,1)S(1)}, bf16[512,768]{1,0:T(8,128)(2,1)S(1)}, u32[]{:S(2)}, u32[]{:S(2)}) %collective-permute-start.14) | collective-permute-done | bytes 786464 | tf_op jit(solution)/shard_map/ppermute | solution.py:224
  70.5 4.6 %build.10 = (bf16[64,512,512]{2,1,0:T(8,128)(2,1)S(1)}, f32[16,512]{1,0:T(8,128)S(1)}) custom-call(s32[3,64]{1,0:T(4,128)S(1)} %get-tuple-element.45.pairs.refs_0_, s32[17]{0:T(128)S(1)} %get-tuple-element.47.bounds.refs_1_, s32[3]{0:T(128)S(1)} %pad_add_fusion.1.place.refs_2_, bf16[4096,768]{1,0:T(8,128)(2,1)} %refs_3_.11, ...), custom_call_target="tpu_custom_call", output_to_operand_aliasing={{0}: (8, {})} | custom-call | flops 2415919104 | bytes 9437184 | tf_op jit(solution)/shard_map/build/pallas_call | solution.py:270
  75.1 0.9 build.11
  76.0 14.1 %all_to_all.30.refs_3_ = f32[8,16,512]{2,1,0:T(8,128)S(1)} all-to-all(f32[8,16,512]{2,1,0:T(8,128)S(1)} %get-tuple-element.76), channel_id=1, replica_groups=mesh['y'=4,'x'=4,'core'=2,'z'=4] {'core','z'}, dimensions={0} | all-to-all | bytes 524288 | tf_op jit(solution)/shard_map/all_to_all | solution.py:331
  90.1 2.6 %columns.3 = (f32[16,16,512]{2,1,0:T(8,128)S(1)}, bf16[64,512,512]{2,1,0:T(8,128)(2,1)S(1)}) custom-call(s32[3,64]{1,0:T(4,128)S(1)} %get-tuple-element.45.pairs.refs_0_, s32[17]{0:T(128)S(1)} %get-tuple-element.47.bounds.refs_1_, s32[3]{0:T(128)S(1)} %pad_add_fusion.1.place.refs_2_, ...), custom_call_target="tpu_custom_call", output_to_operand_aliasing={{1}: (4, {})} | custom-call | tf_op jit(solution)/shard_map/columns/pallas_call | solution.py:317
  92.8 20.6 %all_to_all.31.refs_3_ = f32[16,16,512]{2,1,0:T(8,128)S(1)} all-to-all(f32[16,16,512]{2,1,0:T(8,128)S(1)} %get-tuple-element.78), channel_id=1, replica_groups=mesh['y'=4,'x'=4,'core'=2,'z'=4] {'y','x'}, dimensions={0} | all-to-all | bytes 1048576 | tf_op jit(solution)/shard_map/all_to_all | solution.py:334
  113.4 3.0 %rows.2 = (f32[8,16,512]{2,1,0:T(8,128)S(1)}, bf16[64,512,512]{2,1,0:T(8,128)(2,1)S(1)}) custom-call(s32[3,64]{1,0:T(4,128)S(1)} %get-tuple-element.45.pairs.refs_0_, s32[17]{0:T(128)S(1)} %get-tuple-element.47.bounds.refs_1_, s32[3]{0:T(128)S(1)} %pad_add_fusion.1.place.refs_2_, ...), custom_call_target="tpu_custom_call", output_to_operand_aliasing={{1}: (4, {})} | custom-call | tf_op jit(solution)/shard_map/rows/pallas_call | solution.py:317
  116.4 9.4 %all_to_all.32.refs_3_ = f32[8,16,512]{2,1,0:T(8,128)S(1)} all-to-all(f32[8,16,512]{2,1,0:T(8,128)S(1)} %get-tuple-element.80), channel_id=1, replica_groups=mesh['y'=4,'x'=4,'core'=2,'z'=4] {'core','z'}, dimensions={0} | all-to-all | bytes 524288 | tf_op jit(solution)/shard_map/all_to_all | solution.py:331
  125.8 2.6 %columns.4 = (f32[16,16,512]{2,1,0:T(8,128)S(1)}, bf16[64,512,512]{2,1,0:T(8,128)(2,1)S(1)}) custom-call(s32[3,64]{1,0:T(4,128)S(1)} %get-tuple-element.45.pairs.refs_0_, s32[17]{0:T(128)S(1)} %get-tuple-element.47.bounds.refs_1_, s32[3]{0:T(128)S(1)} %pad_add_fusion.1.place.refs_2_, ...), custom_call_target="tpu_custom_call", output_to_operand_aliasing={{1}: (4, {})} | custom-call | tf_op jit(solution)/shard_map/columns/pallas_call | solution.py:317
  128.4 16.1 %all_to_all.33.refs_3_ = f32[16,16,512]{2,1,0:T(8,128)S(1)} all-to-all(f32[16,16,512]{2,1,0:T(8,128)S(1)} %get-tuple-element.82), channel_id=1, replica_groups=mesh['y'=4,'x'=4,'core'=2,'z'=4] {'y','x'}, dimensions={0} | all-to-all | bytes 1048576 | tf_op jit(solution)/shard_map/all_to_all | solution.py:334
  144.5 3.0 %rows.3 = (f32[8,16,512]{2,1,0:T(8,128)S(1)}, bf16[64,512,512]{2,1,0:T(8,128)(2,1)S(1)}) custom-call(s32[3,64]{1,0:T(4,128)S(1)} %get-tuple-element.45.pairs.refs_0_, s32[17]{0:T(128)S(1)} %get-tuple-element.47.bounds.refs_1_, s32[3]{0:T(128)S(1)} %pad_add_fusion.1.place.refs_2_, ...), custom_call_target="tpu_custom_call", output_to_operand_aliasing={{1}: (4, {})} | custom-call | tf_op jit(solution)/shard_map/rows/pallas_call | solution.py:317
  147.6 9.3 %all_to_all.34.refs_3_ = f32[8,16,512]{2,1,0:T(8,128)S(1)} all-to-all(f32[8,16,512]{2,1,0:T(8,128)S(1)} %get-tuple-element.84), channel_id=1, replica_groups=mesh['y'=4,'x'=4,'core'=2,'z'=4] {'core','z'}, dimensions={0} | all-to-all | bytes 524288 | tf_op jit(solution)/shard_map/all_to_all | solution.py:331
  156.9 3.2 %columns.5 = (f32[16,4,128]{2,1,0:T(4,128)S(1)}, f32[32,128]{1,0:T(8,128)}) custom-call(s32[3,64]{1,0:T(4,128)S(1)} %get-tuple-element.45.pairs.refs_0_, s32[17]{0:T(128)S(1)} %get-tuple-element.47.bounds.refs_1_, s32[3]{0:T(128)S(1)} %pad_add_fusion.1.place.refs_2_, f32[8,16,512]{2,1,0:T(8,128)S(1)} %all_to_all.34.refs_3_, ...), custom_call_target="tpu_custom_call" | custom-call | tf_op jit(solution)/shard_map/columns/pallas_call | solution.py:317
  160.1 11.5 %all_to_all.35 = f32[16,4,128]{2,1,0:T(4,128)S(1)} all-to-all(f32[16,4,128]{2,1,0:T(4,128)S(1)} %get-tuple-element.87), channel_id=1, replica_groups=mesh['y'=4,'x'=4,'core'=2,'z'=4] {'y','x'}, dimensions={0} | all-to-all | bytes 65536 | tf_op jit(solution)/shard_map/all_to_all | solution.py:336
  171.7 0.6 log_bitcast_fusion
  (16 shorter events, 0.1 us)
Async XLA Ops:
  0.6 27.6 %copy-start = (bf16[512,768]{1,0:T(8,128)(2,1)S(1)}, bf16[512,768]{1,0:T(8,128)(2,1)}, u32[]{:S(2)}) copy-start(bf16[512,768]{1,0:T(8,128)(2,1)} %refs_5_.1) | copy-start | bytes 2359300
  0.6 26.3 %collective-permute-start.3 = (bf16[4096,768]{1,0:T(8,128)(2,1)}, bf16[4096,768]{1,0:T(8,128)(2,1)}, u32[]{:S(2)}, u32[]{:S(2)}) collective-permute-start(bf16[4096,768]{1,0:T(8,128)(2,1)} %refs_3_.11), channel_id=1, source_target_pairs={{0,4},{4,0},{1,5},{5,1},{2,6},{6,2},{3,7},{7,3},{8,12},{12,8},{9,1... | collective-permute-start | bytes 18874376 | tf_op jit(solution)/shard_map/ppermute | solution.py:235
  0.7 19.4 %collective-permute-start.1 = (bf16[512,768]{1,0:T(8,128)(2,1)}, bf16[512,768]{1,0:T(8,128)(2,1)S(1)}, u32[]{:S(2)}, u32[]{:S(2)}) collective-permute-start(bf16[512,768]{1,0:T(8,128)(2,1)} %refs_5_.1), channel_id=1, source_target_pairs={{0,8},{4,36},{8,16},{12,44},{16,24},{20,52},{24,0},{28,60},{32,40}... | collective-permute-start | bytes 2359304 | tf_op jit(solution)/shard_map/ppermute | solution.py:224
  2.4 17.8 %collective-permute-start.2 = (bf16[512,768]{1,0:T(8,128)(2,1)}, bf16[512,768]{1,0:T(8,128)(2,1)S(1)}, u32[]{:S(2)}, u32[]{:S(2)}) collective-permute-start(bf16[512,768]{1,0:T(8,128)(2,1)} %refs_5_.1), channel_id=1, source_target_pairs={{0,24},{4,100},{8,0},{12,108},{16,8},{20,116},{24,16},{28,124},{32... | collective-permute-start | bytes 2359304 | tf_op jit(solution)/shard_map/ppermute | solution.py:224
  5.5 5.4 %collective-permute-start = (s32[1,128]{1,0:T(1,128)S(1)}, s32[1,128]{1,0:T(1,128)S(1)}, u32[]{:S(2)}, u32[]{:S(2)}) collective-permute-start(s32[1,128]{1,0:T(1,128)S(1)} %pad_add_fusion), channel_id=1, source_target_pairs={{0,4},{4,0},{1,5},{5,1},{2,6},{6,2},{3,7},{7,3},{8,12},{12,8},{9,1... | collective-permute-start | bytes 1544 | tf_op jit(solution)/shard_map/ppermute | solution.py:236
  5.5 17.9 %collective-permute-start.6 = (bf16[512,768]{1,0:T(8,128)(2,1)}, bf16[512,768]{1,0:T(8,128)(2,1)S(1)}, u32[]{:S(2)}, u32[]{:S(2)}) collective-permute-start(bf16[512,768]{1,0:T(8,128)(2,1)} %refs_5_.1), channel_id=1, source_target_pairs={{0,32},{4,12},{8,40},{12,20},{16,48},{20,28},{24,56},{28,4},{32,64... | collective-permute-start | bytes 2359304 | tf_op jit(solution)/shard_map/ppermute | solution.py:224
  10.8 14.2 %collective-permute-start.7 = (bf16[512,768]{1,0:T(8,128)(2,1)}, bf16[512,768]{1,0:T(8,128)(2,1)}, u32[]{:S(2)}, u32[]{:S(2)}) collective-permute-start(bf16[512,768]{1,0:T(8,128)(2,1)} %refs_5_.1), channel_id=1, source_target_pairs={{0,96},{4,28},{8,104},{12,4},{16,112},{20,12},{24,120},{28,20},{32... | collective-permute-start | bytes 2359304 | tf_op jit(solution)/shard_map/ppermute | solution.py:224
  14.8 0.7 copy-start.1
  20.2 17.6 %collective-permute-start.4 = (bf16[512,768]{1,0:T(8,128)(2,1)S(1)}, bf16[512,768]{1,0:T(8,128)(2,1)S(1)}, u32[]{:S(2)}, u32[]{:S(2)}) collective-permute-start(bf16[512,768]{1,0:T(8,128)(2,1)S(1)} %collective-permute-done.2.refs_7_), channel_id=1, source_target_pairs={{0,24},{4,100},{8,0},{12,108},{16,8},{20,116},{24,16},{28,124},{32... | collective-permute-start | bytes 2359304 | tf_op jit(solution)/shard_map/ppermute | solution.py:224
  21.1 16.7 %collective-permute-start.5 = (bf16[512,768]{1,0:T(8,128)(2,1)S(1)}, bf16[512,768]{1,0:T(8,128)(2,1)S(1)}, u32[]{:S(2)}, u32[]{:S(2)}) collective-permute-start(bf16[512,768]{1,0:T(8,128)(2,1)S(1)} %collective-permute-done.2.refs_7_), channel_id=1, source_target_pairs={{0,32},{4,12},{8,40},{12,20},{16,48},{20,28},{24,56},{28,4},{32,64... | collective-permute-start | bytes 2359304 | tf_op jit(solution)/shard_map/ppermute | solution.py:224
  23.4 22.8 %collective-permute-start.10 = (bf16[512,768]{1,0:T(8,128)(2,1)S(1)}, bf16[512,768]{1,0:T(8,128)(2,1)S(1)}, u32[]{:S(2)}, u32[]{:S(2)}) collective-permute-start(bf16[512,768]{1,0:T(8,128)(2,1)S(1)} %collective-permute-done.2.refs_7_), channel_id=1, source_target_pairs={{0,96},{4,28},{8,104},{12,4},{16,112},{20,12},{24,120},{28,20},{32... | collective-permute-start | bytes 2359304 | tf_op jit(solution)/shard_map/ppermute | solution.py:224
  25.0 21.2 %collective-permute-start.11 = (bf16[512,768]{1,0:T(8,128)(2,1)S(1)}, bf16[512,768]{1,0:T(8,128)(2,1)S(1)}, u32[]{:S(2)}, u32[]{:S(2)}) collective-permute-start(bf16[512,768]{1,0:T(8,128)(2,1)S(1)} %collective-permute-done.1.refs_6_), channel_id=1, source_target_pairs={{0,32},{4,12},{8,40},{12,20},{16,48},{20,28},{24,56},{28,4},{32,64... | collective-permute-start | bytes 2359304 | tf_op jit(solution)/shard_map/ppermute | solution.py:224
  27.0 22.0 %collective-permute-start.9 = (bf16[512,768]{1,0:T(8,128)(2,1)S(1)}, bf16[512,768]{1,0:T(8,128)(2,1)S(1)}, u32[]{:S(2)}, u32[]{:S(2)}) collective-permute-start(bf16[512,768]{1,0:T(8,128)(2,1)S(1)} %collective-permute-done.1.refs_6_), channel_id=1, source_target_pairs={{0,96},{4,28},{8,104},{12,4},{16,112},{20,12},{24,120},{28,20},{32... | collective-permute-start | bytes 2359304 | tf_op jit(solution)/shard_map/ppermute | solution.py:224
  37.8 19.6 %collective-permute-start.8 = (bf16[512,768]{1,0:T(8,128)(2,1)S(1)}, bf16[512,768]{1,0:T(8,128)(2,1)S(1)}, u32[]{:S(2)}, u32[]{:S(2)}) collective-permute-start(bf16[512,768]{1,0:T(8,128)(2,1)S(1)} %collective-permute-done.4.refs_5_), channel_id=1, source_target_pairs={{0,96},{4,28},{8,104},{12,4},{16,112},{20,12},{24,120},{28,20},{32... | collective-permute-start | bytes 2359304 | tf_op jit(solution)/shard_map/ppermute | solution.py:224
  40.4 22.8 %collective-permute-start.16 = (bf16[512,768]{1,0:T(8,128)(2,1)S(1)}, bf16[512,768]{1,0:T(8,128)(2,1)S(1)}, u32[]{:S(2)}, u32[]{:S(2)}) collective-permute-start(bf16[512,768]{1,0:T(8,128)(2,1)S(1)} %collective-permute-done.5.refs_6_), channel_id=1, source_target_pairs={{0,32},{4,12},{8,40},{12,20},{16,48},{20,28},{24,56},{28,4},{32,64... | collective-permute-start | bytes 2359304 | tf_op jit(solution)/shard_map/ppermute | solution.py:224
  46.2 24.3 %collective-permute-start.15 = (bf16[512,768]{1,0:T(8,128)(2,1)S(1)}, bf16[512,768]{1,0:T(8,128)(2,1)S(1)}, u32[]{:S(2)}, u32[]{:S(2)}) collective-permute-start(bf16[512,768]{1,0:T(8,128)(2,1)S(1)} %collective-permute-done.4.refs_5_), channel_id=1, source_target_pairs={{0,32},{4,12},{8,40},{12,20},{16,48},{20,28},{24,56},{28,4},{32,64... | collective-permute-start | bytes 2359304 | tf_op jit(solution)/shard_map/ppermute | solution.py:224
  49.0 18.7 %collective-permute-start.13 = (bf16[512,768]{1,0:T(8,128)(2,1)S(1)}, bf16[512,768]{1,0:T(8,128)(2,1)S(1)}, u32[]{:S(2)}, u32[]{:S(2)}) collective-permute-start(bf16[512,768]{1,0:T(8,128)(2,1)S(1)} %collective-permute-done.9.refs_5_), channel_id=1, source_target_pairs={{0,96},{4,28},{8,104},{12,4},{16,112},{20,12},{24,120},{28,20},{32... | collective-permute-start | bytes 2359304 | tf_op jit(solution)/shard_map/ppermute | solution.py:224
  52.7 17.8 %collective-permute-start.14 = (bf16[512,768]{1,0:T(8,128)(2,1)S(1)}, bf16[512,768]{1,0:T(8,128)(2,1)S(1)}, u32[]{:S(2)}, u32[]{:S(2)}) collective-permute-start(bf16[512,768]{1,0:T(8,128)(2,1)S(1)} %collective-permute-done.6.refs_8_), channel_id=1, source_target_pairs={{0,32},{4,12},{8,40},{12,20},{16,48},{20,28},{24,56},{28,4},{32,64... | collective-permute-start | bytes 2359304 | tf_op jit(solution)/shard_map/ppermute | solution.py:224
  57.4 17.7 %collective-permute-start.12 = (bf16[512,768]{1,0:T(8,128)(2,1)S(1)}, bf16[512,768]{1,0:T(8,128)(2,1)S(1)}, u32[]{:S(2)}, u32[]{:S(2)}) collective-permute-start(bf16[512,768]{1,0:T(8,128)(2,1)S(1)} %collective-permute-done.8.refs_5_), channel_id=1, source_target_pairs={{0,96},{4,28},{8,104},{12,4},{16,112},{20,12},{24,120},{28,20},{32... | collective-permute-start | bytes 2359304 | tf_op jit(solution)/shard_map/ppermute | solution.py:224

commit v10 on v9

--- a/solution.py
+++ b/solution.py
@@ -13,7 +13,7 @@
 LANES = 128
 BUILD_STEP = 2
 BUFFERS = 4
-ROW_STEP = 4
+ROW_STEP = 8
 COLUMN_STEP = 8
 NY, NX, NC, NZ = 4, 4, 2, 4
 NCHIP = NY * NX
@@ -190,6 +190,14 @@
                     lanes = slice(q * LANES, (q + 1) * LANES)
                     part = part + store[safe, :, lanes].astype(F32) * row[:, lanes]
                 found.append((target, jnp.sum(part.T, axis=0, keepdims=True)))
+                continue
+            if not over_rows and k % 4 == 0:
+                tall = jnp.broadcast_to(row, (LANES, TILE)).T
+                cut = []
+                for q in range(TILE // LANES):
+                    lanes = slice(q * LANES, (q + 1) * LANES)
+                    cut.append(jnp.sum(store[safe, :, lanes].astype(F32) * tall, axis=0, keepdims=True))
+                found.append((target, jnp.concatenate(cut, axis=1)))
                 continue
             row = jnp.broadcast_to(row, (16, TILE)).astype(BF16)
             found.append((target, lax.dot_general(row, store[safe], dims, preferred_element_type=F32)[0:1]))

time: 172 us -> 169 us (0.983)
  Pallas kernels: 47.6 us -> 36.2 us
  waiting for transfers between devices: 11.3 us -> 18.5 us
    ppermute x15, waiting for transfers between devices: 7.7 us -> 14.9 us  [go(): return lax.ppermute(block, ('y', 'x', 'core'), moves(first, shift))]
    pallas_call x6, Pallas kernels: 27.8 us -> 22.4 us  [build(): pl.pallas_call(lambda *refs: build_kernel(scale, first, blocks, last, *re...]
    pallas_call x5, Pallas kernels: 14.6 us -> 9.82 us  [half(): pl.pallas_call(lambda *refs: pass_kernel(over_rows, last, *refs), out_sha...]
    all_to_all x3, blocking collectives: 32.8 us -> 35 us  [on_device(): kv_parts = lax.all_to_all(kv, ('core', 'z'), 0, 0, tiled=True)]
    all_to_all x2, blocking collectives: 36.7 us -> 34.8 us  [on_device(): ktu_parts = lax.all_to_all(ktu, ('y', 'x'), 0, 0, tiled=True)]
  transfers between devices with their start and end apart: 17 -> 17, of which waited for: 5 -> 7; matrix products, arithmetic and copies ran while one was open for 1% -> 1% of each run, Pallas kernels for 19% -> 14%
where the time goes in v10:
time: 169 us
  blocking collectives  80.9 us (48%)
  Pallas kernels  36.2 us (21%)
  starting transfers between devices  28.6 us (17%)
  waiting for transfers between devices  18.5 us (11%)
  other arithmetic  2.26 us (1%)
    all_to_all x3, blocking collectives, on_device(): kv_parts = lax.all_to_all(kv, ('core', 'z'), 0, 0, tiled=True)  35 us
    all_to_all x2, blocking collectives, on_device(): ktu_parts = lax.all_to_all(ktu, ('y', 'x'), 0, 0, tiled=True)  34.8 us
    ppermute x15, starting transfers between devices, go(): return lax.ppermute(block, ('y', 'x', 'core'), moves(first, shift))  28.5 us
    pallas_call x6, Pallas kernels, build(): pl.pallas_call(lambda *refs: build_kernel(scale, first, blocks, last, *re...  22.4 us
    ppermute x15, waiting for transfers between devices, go(): return lax.ppermute(block, ('y', 'x', 'core'), moves(first, shift))  14.9 us
    all_to_all x1, blocking collectives, on_device(): mine = lax.all_to_all(ktu, ('y', 'x'), 0, 0, tiled=True)  11.1 us
    pallas_call x5, Pallas kernels, half(): pl.pallas_call(lambda *refs: pass_kernel(over_rows, last, *refs), out_sha...  9.82 us
    ppermute x1, waiting for transfers between devices, on_device(): other = lax.ppermute(own, 'core', swap)  3.62 us
  transfers between devices with their start and end apart: 17, of which 7 were waited for; matrix products, arithmetic and copies ran while one was open for 1% of the time, Pallas kernels for 14%

profile of v10, /device:TPU:0, one launch (start us, length us, event | category | flops | bytes accessed | tf_op | source)
XLA Modules:
  0.0 168.6 jit_solution(3508233414383330983)
XLA Ops:
  0.6 0.0 copy-start
  0.6 0.1 collective-permute-start.3
  0.7 1.6 collective-permute-start.1
  2.4 1.7 collective-permute-start.2
  4.7 0.8 pad_add_fusion
  5.5 0.0 collective-permute-start
  5.5 1.7 %collective-permute-start.6 = (bf16[512,768]{1,0:T(8,128)(2,1)}, bf16[512,768]{1,0:T(8,128)(2,1)S(1)}, u32[]{:S(2)}, u32[]{:S(2)}) collective-permute-start(bf16[512,768]{1,0:T(8,128)(2,1)} %refs_5_.1), channel_id=1, source_target_pairs={{0,32},{4,12},{8,40},{12,20},{16,48},{20,28},{24,56},{28,4},{32,64... | collective-permute-start | bytes 2359304 | tf_op jit(solution)/shard_map/ppermute | solution.py:232
  7.2 3.6 %collective-permute-done = s32[1,128]{1,0:T(1,128)S(1)} collective-permute-done((s32[1,128]{1,0:T(1,128)S(1)}, s32[1,128]{1,0:T(1,128)S(1)}, u32[]{:S(2)}, u32[]{:S(2)}) %collective-permute-start) | collective-permute-done | bytes 544 | tf_op jit(solution)/shard_map/ppermute | solution.py:244
  10.8 3.1 %collective-permute-start.7 = (bf16[512,768]{1,0:T(8,128)(2,1)}, bf16[512,768]{1,0:T(8,128)(2,1)}, u32[]{:S(2)}, u32[]{:S(2)}) collective-permute-start(bf16[512,768]{1,0:T(8,128)(2,1)} %refs_5_.1), channel_id=1, source_target_pairs={{0,96},{4,28},{8,104},{12,4},{16,112},{20,12},{24,120},{28,20},{32... | collective-permute-start | bytes 2359304 | tf_op jit(solution)/shard_map/ppermute | solution.py:232
  13.9 0.1 pad_add_fusion.1.place.refs_2_
  14.0 0.8 add_select_fusion.lists
  14.8 0.7 copy-done.1
  15.5 3.4 %plan.1 = (s32[3,64]{1,0:T(4,128)S(1)}, s32[17]{0:T(128)S(1)}) custom-call(s32[2,128]{1,0:T(2,128)S(1)} %add_select_fusion.lists, s32[3]{0:T(128)S(1)} %pad_add_fusion.1.place.refs_2_, s32[16]{0:T(128)S(1)} %copy-done.1), custom_call_target="tpu_custom_call" | custom-call | tf_op jit(solution)/shard_map/plan/pallas_call | solution.py:253
  18.9 0.0 collective-permute-done.2.refs_7_
  18.9 4.0 %collective-permute-start.4 = (bf16[512,768]{1,0:T(8,128)(2,1)S(1)}, bf16[512,768]{1,0:T(8,128)(2,1)S(1)}, u32[]{:S(2)}, u32[]{:S(2)}) collective-permute-start(bf16[512,768]{1,0:T(8,128)(2,1)S(1)} %collective-permute-done.2.refs_7_), channel_id=1, source_target_pairs={{0,24},{4,100},{8,0},{12,108},{16,8},{20,116},{24,16},{28,124},{32... | collective-permute-start | bytes 2359304 | tf_op jit(solution)/shard_map/ppermute | solution.py:232
  22.9 0.1 collective-permute-start.5
  23.1 0.6 room.1.refs_10_
  23.6 0.0 collective-permute-done.6.refs_8_
  23.7 3.2 %collective-permute-start.10 = (bf16[512,768]{1,0:T(8,128)(2,1)S(1)}, bf16[512,768]{1,0:T(8,128)(2,1)S(1)}, u32[]{:S(2)}, u32[]{:S(2)}) collective-permute-start(bf16[512,768]{1,0:T(8,128)(2,1)S(1)} %collective-permute-done.2.refs_7_), channel_id=1, source_target_pairs={{0,96},{4,28},{8,104},{12,4},{16,112},{20,12},{24,120},{28,20},{32... | collective-permute-start | bytes 2359304 | tf_op jit(solution)/shard_map/ppermute | solution.py:232
  26.9 3.2 %collective-permute-start.9 = (bf16[512,768]{1,0:T(8,128)(2,1)S(1)}, bf16[512,768]{1,0:T(8,128)(2,1)S(1)}, u32[]{:S(2)}, u32[]{:S(2)}) collective-permute-start(bf16[512,768]{1,0:T(8,128)(2,1)S(1)} %collective-permute-done.1.refs_6_), channel_id=1, source_target_pairs={{0,96},{4,28},{8,104},{12,4},{16,112},{20,12},{24,120},{28,20},{32... | collective-permute-start | bytes 2359304 | tf_op jit(solution)/shard_map/ppermute | solution.py:232
  30.1 6.1 %build.6 = (bf16[64,512,512]{2,1,0:T(8,128)(2,1)S(1)}, f32[16,512]{1,0:T(8,128)S(1)}) custom-call(s32[3,64]{1,0:T(4,128)S(1)} %get-tuple-element.45.pairs.refs_0_, s32[17]{0:T(128)S(1)} %get-tuple-element.47.bounds.refs_1_, s32[3]{0:T(128)S(1)} %pad_add_fusion.1.place.refs_2_, bf16[4096,768]{1,0:T(8,128)(2,1)} %refs_3_.11, ...), custom_call_target="tpu_custom_call", output_to_operand_aliasing={{0}: (10, {})} | custom-call | flops 4026531840 | bytes 15728640 | tf_op jit(solution)/shard_map/build/pallas_call | solution.py:278
  36.2 1.9 %collective-permute-done.4.refs_5_ = bf16[512,768]{1,0:T(8,128)(2,1)S(1)} collective-permute-done((bf16[512,768]{1,0:T(8,128)(2,1)S(1)}, bf16[512,768]{1,0:T(8,128)(2,1)S(1)}, u32[]{:S(2)}, u32[]{:S(2)}) %collective-permute-start.4) | collective-permute-done | bytes 786464 | tf_op jit(solution)/shard_map/ppermute | solution.py:232
  38.1 2.3 %collective-permute-start.8 = (bf16[512,768]{1,0:T(8,128)(2,1)S(1)}, bf16[512,768]{1,0:T(8,128)(2,1)S(1)}, u32[]{:S(2)}, u32[]{:S(2)}) collective-permute-start(bf16[512,768]{1,0:T(8,128)(2,1)S(1)} %collective-permute-done.4.refs_5_), channel_id=1, source_target_pairs={{0,96},{4,28},{8,104},{12,4},{16,112},{20,12},{24,120},{28,20},{32... | collective-permute-start | bytes 2359304 | tf_op jit(solution)/shard_map/ppermute | solution.py:232
  40.4 5.7 %build.7 = (bf16[64,512,512]{2,1,0:T(8,128)(2,1)S(1)}, f32[16,512]{1,0:T(8,128)S(1)}) custom-call(s32[3,64]{1,0:T(4,128)S(1)} %get-tuple-element.45.pairs.refs_0_, s32[17]{0:T(128)S(1)} %get-tuple-element.47.bounds.refs_1_, s32[3]{0:T(128)S(1)} %pad_add_fusion.1.place.refs_2_, bf16[4096,768]{1,0:T(8,128)(2,1)} %refs_3_.11, ...), custom_call_target="tpu_custom_call", output_to_operand_aliasing={{0}: (7, {})} | custom-call | flops 1610612736 | bytes 6291456 | tf_op jit(solution)/shard_map/build/pallas_call | solution.py:278
  46.2 0.1 collective-permute-start.15
  46.3 2.7 %collective-permute-done.9.refs_5_ = bf16[512,768]{1,0:T(8,128)(2,1)S(1)} collective-permute-done((bf16[512,768]{1,0:T(8,128)(2,1)S(1)}, bf16[512,768]{1,0:T(8,128)(2,1)S(1)}, u32[]{:S(2)}, u32[]{:S(2)}) %collective-permute-start.9) | collective-permute-done | bytes 786464 | tf_op jit(solution)/shard_map/ppermute | solution.py:232
  48.9 3.7 %collective-permute-start.13 = (bf16[512,768]{1,0:T(8,128)(2,1)S(1)}, bf16[512,768]{1,0:T(8,128)(2,1)S(1)}, u32[]{:S(2)}, u32[]{:S(2)}) collective-permute-start(bf16[512,768]{1,0:T(8,128)(2,1)S(1)} %collective-permute-done.9.refs_5_), channel_id=1, source_target_pairs={{0,96},{4,28},{8,104},{12,4},{16,112},{20,12},{24,120},{28,20},{32... | collective-permute-start | bytes 2359304 | tf_op jit(solution)/shard_map/ppermute | solution.py:232
  52.6 3.4 %build.8 = (bf16[64,512,512]{2,1,0:T(8,128)(2,1)S(1)}, f32[16,512]{1,0:T(8,128)S(1)}) custom-call(s32[3,64]{1,0:T(4,128)S(1)} %get-tuple-element.45.pairs.refs_0_, s32[17]{0:T(128)S(1)} %get-tuple-element.47.bounds.refs_1_, s32[3]{0:T(128)S(1)} %pad_add_fusion.1.place.refs_2_, bf16[4096,768]{1,0:T(8,128)(2,1)} %refs_3_.11, ...), custom_call_target="tpu_custom_call", output_to_operand_aliasing={{0}: (8, {})} | custom-call | flops 2415919104 | bytes 9437184 | tf_op jit(solution)/shard_map/build/pallas_call | solution.py:278
  56.0 1.4 collective-permute-done.8.refs_5_
  57.4 3.7 %collective-permute-start.12 = (bf16[512,768]{1,0:T(8,128)(2,1)S(1)}, bf16[512,768]{1,0:T(8,128)(2,1)S(1)}, u32[]{:S(2)}, u32[]{:S(2)}) collective-permute-start(bf16[512,768]{1,0:T(8,128)(2,1)S(1)} %collective-permute-done.8.refs_5_), channel_id=1, source_target_pairs={{0,96},{4,28},{8,104},{12,4},{16,112},{20,12},{24,120},{28,20},{32... | collective-permute-start | bytes 2359304 | tf_op jit(solution)/shard_map/ppermute | solution.py:232
  61.1 0.8 build.9
  61.8 3.9 %collective-permute-done.13.refs_5_ = bf16[512,768]{1,0:T(8,128)(2,1)S(1)} collective-permute-done((bf16[512,768]{1,0:T(8,128)(2,1)S(1)}, bf16[512,768]{1,0:T(8,128)(2,1)S(1)}, u32[]{:S(2)}, u32[]{:S(2)}) %collective-permute-start.13) | collective-permute-done | bytes 786464 | tf_op jit(solution)/shard_map/ppermute | solution.py:232
  65.8 4.7 %collective-permute-done.14.refs_6_ = bf16[512,768]{1,0:T(8,128)(2,1)S(1)} collective-permute-done((bf16[512,768]{1,0:T(8,128)(2,1)S(1)}, bf16[512,768]{1,0:T(8,128)(2,1)S(1)}, u32[]{:S(2)}, u32[]{:S(2)}) %collective-permute-start.14) | collective-permute-done | bytes 786464 | tf_op jit(solution)/shard_map/ppermute | solution.py:232
  70.5 3.4 %build.10 = (bf16[64,512,512]{2,1,0:T(8,128)(2,1)S(1)}, f32[16,512]{1,0:T(8,128)S(1)}) custom-call(s32[3,64]{1,0:T(4,128)S(1)} %get-tuple-element.45.pairs.refs_0_, s32[17]{0:T(128)S(1)} %get-tuple-element.47.bounds.refs_1_, s32[3]{0:T(128)S(1)} %pad_add_fusion.1.place.refs_2_, bf16[4096,768]{1,0:T(8,128)(2,1)} %refs_3_.11, ...), custom_call_target="tpu_custom_call", output_to_operand_aliasing={{0}: (8, {})} | custom-call | flops 2415919104 | bytes 9437184 | tf_op jit(solution)/shard_map/build/pallas_call | solution.py:278
  73.8 0.4 collective-permute-done.12.refs_5_
  74.2 3.0 %build.11 = (bf16[64,512,512]{2,1,0:T(8,128)(2,1)S(1)}, f32[8,16,512]{2,1,0:T(8,128)S(1)}) custom-call(s32[3,64]{1,0:T(4,128)S(1)} %get-tuple-element.45.pairs.refs_0_, s32[17]{0:T(128)S(1)} %get-tuple-element.47.bounds.refs_1_, s32[3]{0:T(128)S(1)} %pad_add_fusion.1.place.refs_2_, bf16[4096,768]{1,0:T(8,128)(2,1)} %refs_3_.11, ...), custom_call_target="tpu_custom_call", output_to_operand_aliasing={{0}: (6, {})} | custom-call | flops 805306368 | bytes 3145728 | tf_op jit(solution)/shard_map/build/pallas_call | solution.py:278
  77.2 13.0 %all_to_all.30.refs_3_ = f32[8,16,512]{2,1,0:T(8,128)S(1)} all-to-all(f32[8,16,512]{2,1,0:T(8,128)S(1)} %get-tuple-element.76), channel_id=1, replica_groups=mesh['y'=4,'x'=4,'core'=2,'z'=4] {'core','z'}, dimensions={0} | all-to-all | bytes 524288 | tf_op jit(solution)/shard_map/all_to_all | solution.py:339
  90.2 1.8 %columns.3 = (f32[16,16,512]{2,1,0:T(8,128)S(1)}, bf16[64,512,512]{2,1,0:T(8,128)(2,1)S(1)}) custom-call(s32[3,64]{1,0:T(4,128)S(1)} %get-tuple-element.45.pairs.refs_0_, s32[17]{0:T(128)S(1)} %get-tuple-element.47.bounds.refs_1_, s32[3]{0:T(128)S(1)} %pad_add_fusion.1.place.refs_2_, ...), custom_call_target="tpu_custom_call", output_to_operand_aliasing={{1}: (4, {})} | custom-call | tf_op jit(solution)/shard_map/columns/pallas_call | solution.py:325
  92.0 19.5 %all_to_all.31.refs_3_ = f32[16,16,512]{2,1,0:T(8,128)S(1)} all-to-all(f32[16,16,512]{2,1,0:T(8,128)S(1)} %get-tuple-element.78), channel_id=1, replica_groups=mesh['y'=4,'x'=4,'core'=2,'z'=4] {'y','x'}, dimensions={0} | all-to-all | bytes 1048576 | tf_op jit(solution)/shard_map/all_to_all | solution.py:342
  111.5 2.0 %rows.2 = (f32[8,16,512]{2,1,0:T(8,128)S(1)}, bf16[64,512,512]{2,1,0:T(8,128)(2,1)S(1)}) custom-call(s32[3,64]{1,0:T(4,128)S(1)} %get-tuple-element.45.pairs.refs_0_, s32[17]{0:T(128)S(1)} %get-tuple-element.47.bounds.refs_1_, s32[3]{0:T(128)S(1)} %pad_add_fusion.1.place.refs_2_, ...), custom_call_target="tpu_custom_call", output_to_operand_aliasing={{1}: (4, {})} | custom-call | tf_op jit(solution)/shard_map/rows/pallas_call | solution.py:325
  113.5 11.2 %all_to_all.32.refs_3_ = f32[8,16,512]{2,1,0:T(8,128)S(1)} all-to-all(f32[8,16,512]{2,1,0:T(8,128)S(1)} %get-tuple-element.80), channel_id=1, replica_groups=mesh['y'=4,'x'=4,'core'=2,'z'=4] {'core','z'}, dimensions={0} | all-to-all | bytes 524288 | tf_op jit(solution)/shard_map/all_to_all | solution.py:339
  124.7 1.8 %columns.4 = (f32[16,16,512]{2,1,0:T(8,128)S(1)}, bf16[64,512,512]{2,1,0:T(8,128)(2,1)S(1)}) custom-call(s32[3,64]{1,0:T(4,128)S(1)} %get-tuple-element.45.pairs.refs_0_, s32[17]{0:T(128)S(1)} %get-tuple-element.47.bounds.refs_1_, s32[3]{0:T(128)S(1)} %pad_add_fusion.1.place.refs_2_, ...), custom_call_target="tpu_custom_call", output_to_operand_aliasing={{1}: (4, {})} | custom-call | tf_op jit(solution)/shard_map/columns/pallas_call | solution.py:325
  126.5 15.3 %all_to_all.33.refs_3_ = f32[16,16,512]{2,1,0:T(8,128)S(1)} all-to-all(f32[16,16,512]{2,1,0:T(8,128)S(1)} %get-tuple-element.82), channel_id=1, replica_groups=mesh['y'=4,'x'=4,'core'=2,'z'=4] {'y','x'}, dimensions={0} | all-to-all | bytes 1048576 | tf_op jit(solution)/shard_map/all_to_all | solution.py:342
  141.8 2.0 %rows.3 = (f32[8,16,512]{2,1,0:T(8,128)S(1)}, bf16[64,512,512]{2,1,0:T(8,128)(2,1)S(1)}) custom-call(s32[3,64]{1,0:T(4,128)S(1)} %get-tuple-element.45.pairs.refs_0_, s32[17]{0:T(128)S(1)} %get-tuple-element.47.bounds.refs_1_, s32[3]{0:T(128)S(1)} %pad_add_fusion.1.place.refs_2_, ...), custom_call_target="tpu_custom_call", output_to_operand_aliasing={{1}: (4, {})} | custom-call | tf_op jit(solution)/shard_map/rows/pallas_call | solution.py:325
  143.7 10.8 %all_to_all.34.refs_3_ = f32[8,16,512]{2,1,0:T(8,128)S(1)} all-to-all(f32[8,16,512]{2,1,0:T(8,128)S(1)} %get-tuple-element.84), channel_id=1, replica_groups=mesh['y'=4,'x'=4,'core'=2,'z'=4] {'core','z'}, dimensions={0} | all-to-all | bytes 524288 | tf_op jit(solution)/shard_map/all_to_all | solution.py:339
  154.5 2.3 %columns.5 = (f32[16,4,128]{2,1,0:T(4,128)S(1)}, f32[32,128]{1,0:T(8,128)}) custom-call(s32[3,64]{1,0:T(4,128)S(1)} %get-tuple-element.45.pairs.refs_0_, s32[17]{0:T(128)S(1)} %get-tuple-element.47.bounds.refs_1_, s32[3]{0:T(128)S(1)} %pad_add_fusion.1.place.refs_2_, f32[8,16,512]{2,1,0:T(8,128)S(1)} %all_to_all.34.refs_3_, ...), custom_call_target="tpu_custom_call" | custom-call | tf_op jit(solution)/shard_map/columns/pallas_call | solution.py:325
  156.9 11.1 %all_to_all.35 = f32[16,4,128]{2,1,0:T(4,128)S(1)} all-to-all(f32[16,4,128]{2,1,0:T(4,128)S(1)} %get-tuple-element.87), channel_id=1, replica_groups=mesh['y'=4,'x'=4,'core'=2,'z'=4] {'y','x'}, dimensions={0} | all-to-all | bytes 65536 | tf_op jit(solution)/shard_map/all_to_all | solution.py:344
  168.0 0.6 log_bitcast_fusion
  (16 shorter events, 0.1 us)
Async XLA Ops:
  0.6 29.5 %copy-start = (bf16[512,768]{1,0:T(8,128)(2,1)S(1)}, bf16[512,768]{1,0:T(8,128)(2,1)}, u32[]{:S(2)}) copy-start(bf16[512,768]{1,0:T(8,128)(2,1)} %refs_5_.1) | copy-start | bytes 2359300
  0.6 26.2 %collective-permute-start.3 = (bf16[4096,768]{1,0:T(8,128)(2,1)}, bf16[4096,768]{1,0:T(8,128)(2,1)}, u32[]{:S(2)}, u32[]{:S(2)}) collective-permute-start(bf16[4096,768]{1,0:T(8,128)(2,1)} %refs_3_.11), channel_id=1, source_target_pairs={{0,4},{4,0},{1,5},{5,1},{2,6},{6,2},{3,7},{7,3},{8,12},{12,8},{9,1... | collective-permute-start | bytes 18874376 | tf_op jit(solution)/shard_map/ppermute | solution.py:243
  0.7 18.2 %collective-permute-start.1 = (bf16[512,768]{1,0:T(8,128)(2,1)}, bf16[512,768]{1,0:T(8,128)(2,1)S(1)}, u32[]{:S(2)}, u32[]{:S(2)}) collective-permute-start(bf16[512,768]{1,0:T(8,128)(2,1)} %refs_5_.1), channel_id=1, source_target_pairs={{0,8},{4,36},{8,16},{12,44},{16,24},{20,52},{24,0},{28,60},{32,40}... | collective-permute-start | bytes 2359304 | tf_op jit(solution)/shard_map/ppermute | solution.py:232
  2.4 16.5 %collective-permute-start.2 = (bf16[512,768]{1,0:T(8,128)(2,1)}, bf16[512,768]{1,0:T(8,128)(2,1)S(1)}, u32[]{:S(2)}, u32[]{:S(2)}) collective-permute-start(bf16[512,768]{1,0:T(8,128)(2,1)} %refs_5_.1), channel_id=1, source_target_pairs={{0,24},{4,100},{8,0},{12,108},{16,8},{20,116},{24,16},{28,124},{32... | collective-permute-start | bytes 2359304 | tf_op jit(solution)/shard_map/ppermute | solution.py:232
  5.5 5.4 %collective-permute-start = (s32[1,128]{1,0:T(1,128)S(1)}, s32[1,128]{1,0:T(1,128)S(1)}, u32[]{:S(2)}, u32[]{:S(2)}) collective-permute-start(s32[1,128]{1,0:T(1,128)S(1)} %pad_add_fusion), channel_id=1, source_target_pairs={{0,4},{4,0},{1,5},{5,1},{2,6},{6,2},{3,7},{7,3},{8,12},{12,8},{9,1... | collective-permute-start | bytes 1544 | tf_op jit(solution)/shard_map/ppermute | solution.py:244
  5.5 18.2 %collective-permute-start.6 = (bf16[512,768]{1,0:T(8,128)(2,1)}, bf16[512,768]{1,0:T(8,128)(2,1)S(1)}, u32[]{:S(2)}, u32[]{:S(2)}) collective-permute-start(bf16[512,768]{1,0:T(8,128)(2,1)} %refs_5_.1), channel_id=1, source_target_pairs={{0,32},{4,12},{8,40},{12,20},{16,48},{20,28},{24,56},{28,4},{32,64... | collective-permute-start | bytes 2359304 | tf_op jit(solution)/shard_map/ppermute | solution.py:232
  10.8 16.0 %collective-permute-start.7 = (bf16[512,768]{1,0:T(8,128)(2,1)}, bf16[512,768]{1,0:T(8,128)(2,1)}, u32[]{:S(2)}, u32[]{:S(2)}) collective-permute-start(bf16[512,768]{1,0:T(8,128)(2,1)} %refs_5_.1), channel_id=1, source_target_pairs={{0,96},{4,28},{8,104},{12,4},{16,112},{20,12},{24,120},{28,20},{32... | collective-permute-start | bytes 2359304 | tf_op jit(solution)/shard_map/ppermute | solution.py:232
  14.8 0.7 copy-start.1
  18.9 19.2 %collective-permute-start.4 = (bf16[512,768]{1,0:T(8,128)(2,1)S(1)}, bf16[512,768]{1,0:T(8,128)(2,1)S(1)}, u32[]{:S(2)}, u32[]{:S(2)}) collective-permute-start(bf16[512,768]{1,0:T(8,128)(2,1)S(1)} %collective-permute-done.2.refs_7_), channel_id=1, source_target_pairs={{0,24},{4,100},{8,0},{12,108},{16,8},{20,116},{24,16},{28,124},{32... | collective-permute-start | bytes 2359304 | tf_op jit(solution)/shard_map/ppermute | solution.py:232
  22.9 15.1 %collective-permute-start.5 = (bf16[512,768]{1,0:T(8,128)(2,1)S(1)}, bf16[512,768]{1,0:T(8,128)(2,1)S(1)}, u32[]{:S(2)}, u32[]{:S(2)}) collective-permute-start(bf16[512,768]{1,0:T(8,128)(2,1)S(1)} %collective-permute-done.2.refs_7_), channel_id=1, source_target_pairs={{0,32},{4,12},{8,40},{12,20},{16,48},{20,28},{24,56},{28,4},{32,64... | collective-permute-start | bytes 2359304 | tf_op jit(solution)/shard_map/ppermute | solution.py:232
  23.7 22.5 %collective-permute-start.10 = (bf16[512,768]{1,0:T(8,128)(2,1)S(1)}, bf16[512,768]{1,0:T(8,128)(2,1)S(1)}, u32[]{:S(2)}, u32[]{:S(2)}) collective-permute-start(bf16[512,768]{1,0:T(8,128)(2,1)S(1)} %collective-permute-done.2.refs_7_), channel_id=1, source_target_pairs={{0,96},{4,28},{8,104},{12,4},{16,112},{20,12},{24,120},{28,20},{32... | collective-permute-start | bytes 2359304 | tf_op jit(solution)/shard_map/ppermute | solution.py:232
  26.9 19.4 %collective-permute-start.11 = (bf16[512,768]{1,0:T(8,128)(2,1)S(1)}, bf16[512,768]{1,0:T(8,128)(2,1)S(1)}, u32[]{:S(2)}, u32[]{:S(2)}) collective-permute-start(bf16[512,768]{1,0:T(8,128)(2,1)S(1)} %collective-permute-done.1.refs_6_), channel_id=1, source_target_pairs={{0,32},{4,12},{8,40},{12,20},{16,48},{20,28},{24,56},{28,4},{32,64... | collective-permute-start | bytes 2359304 | tf_op jit(solution)/shard_map/ppermute | solution.py:232
  26.9 22.1 %collective-permute-start.9 = (bf16[512,768]{1,0:T(8,128)(2,1)S(1)}, bf16[512,768]{1,0:T(8,128)(2,1)S(1)}, u32[]{:S(2)}, u32[]{:S(2)}) collective-permute-start(bf16[512,768]{1,0:T(8,128)(2,1)S(1)} %collective-permute-done.1.refs_6_), channel_id=1, source_target_pairs={{0,96},{4,28},{8,104},{12,4},{16,112},{20,12},{24,120},{28,20},{32... | collective-permute-start | bytes 2359304 | tf_op jit(solution)/shard_map/ppermute | solution.py:232
  38.1 19.3 %collective-permute-start.8 = (bf16[512,768]{1,0:T(8,128)(2,1)S(1)}, bf16[512,768]{1,0:T(8,128)(2,1)S(1)}, u32[]{:S(2)}, u32[]{:S(2)}) collective-permute-start(bf16[512,768]{1,0:T(8,128)(2,1)S(1)} %collective-permute-done.4.refs_5_), channel_id=1, source_target_pairs={{0,96},{4,28},{8,104},{12,4},{16,112},{20,12},{24,120},{28,20},{32... | collective-permute-start | bytes 2359304 | tf_op jit(solution)/shard_map/ppermute | solution.py:232
  40.4 20.6 %collective-permute-start.16 = (bf16[512,768]{1,0:T(8,128)(2,1)S(1)}, bf16[512,768]{1,0:T(8,128)(2,1)S(1)}, u32[]{:S(2)}, u32[]{:S(2)}) collective-permute-start(bf16[512,768]{1,0:T(8,128)(2,1)S(1)} %collective-permute-done.5.refs_6_), channel_id=1, source_target_pairs={{0,32},{4,12},{8,40},{12,20},{16,48},{20,28},{24,56},{28,4},{32,64... | collective-permute-start | bytes 2359304 | tf_op jit(solution)/shard_map/ppermute | solution.py:232
  46.2 24.3 %collective-permute-start.15 = (bf16[512,768]{1,0:T(8,128)(2,1)S(1)}, bf16[512,768]{1,0:T(8,128)(2,1)S(1)}, u32[]{:S(2)}, u32[]{:S(2)}) collective-permute-start(bf16[512,768]{1,0:T(8,128)(2,1)S(1)} %collective-permute-done.4.refs_5_), channel_id=1, source_target_pairs={{0,32},{4,12},{8,40},{12,20},{16,48},{20,28},{24,56},{28,4},{32,64... | collective-permute-start | bytes 2359304 | tf_op jit(solution)/shard_map/ppermute | solution.py:232
  48.9 16.9 %collective-permute-start.13 = (bf16[512,768]{1,0:T(8,128)(2,1)S(1)}, bf16[512,768]{1,0:T(8,128)(2,1)S(1)}, u32[]{:S(2)}, u32[]{:S(2)}) collective-permute-start(bf16[512,768]{1,0:T(8,128)(2,1)S(1)} %collective-permute-done.9.refs_5_), channel_id=1, source_target_pairs={{0,96},{4,28},{8,104},{12,4},{16,112},{20,12},{24,120},{28,20},{32... | collective-permute-start | bytes 2359304 | tf_op jit(solution)/shard_map/ppermute | solution.py:232
  52.6 17.8 %collective-permute-start.14 = (bf16[512,768]{1,0:T(8,128)(2,1)S(1)}, bf16[512,768]{1,0:T(8,128)(2,1)S(1)}, u32[]{:S(2)}, u32[]{:S(2)}) collective-permute-start(bf16[512,768]{1,0:T(8,128)(2,1)S(1)} %collective-permute-done.6.refs_8_), channel_id=1, source_target_pairs={{0,32},{4,12},{8,40},{12,20},{16,48},{20,28},{24,56},{28,4},{32,64... | collective-permute-start | bytes 2359304 | tf_op jit(solution)/shard_map/ppermute | solution.py:232
  57.4 16.9 %collective-permute-start.12 = (bf16[512,768]{1,0:T(8,128)(2,1)S(1)}, bf16[512,768]{1,0:T(8,128)(2,1)S(1)}, u32[]{:S(2)}, u32[]{:S(2)}) collective-permute-start(bf16[512,768]{1,0:T(8,128)(2,1)S(1)} %collective-permute-done.8.refs_5_), channel_id=1, source_target_pairs={{0,96},{4,28},{8,104},{12,4},{16,112},{20,12},{24,120},{28,20},{32... | collective-permute-start | bytes 2359304 | tf_op jit(solution)/shard_map/ppermute | solution.py:232

commit v11 on v10

--- a/solution.py
+++ b/solution.py
@@ -191,7 +191,7 @@
                     part = part + store[safe, :, lanes].astype(F32) * row[:, lanes]
                 found.append((target, jnp.sum(part.T, axis=0, keepdims=True)))
                 continue
-            if not over_rows and k % 4 == 0:
+            if not over_rows and k % 3 == 0:
                 tall = jnp.broadcast_to(row, (LANES, TILE)).T
                 cut = []
                 for q in range(TILE // LANES):

time: 169 us -> 170 us (level)
  Pallas kernels: 36.2 us -> 55.2 us
  waiting for transfers between devices: 18.5 us -> 9.69 us
  blocking collectives: 80.9 us -> 75.9 us
  starting transfers between devices: 28.6 us -> 24 us
    pallas_call x6, Pallas kernels: 22.4 us -> 33.7 us  [build(): pl.pallas_call(lambda *refs: build_kernel(scale, first, blocks, last, *re...]
    ppermute x15, waiting for transfers between devices: 14.9 us -> 6.06 us  [go(): return lax.ppermute(block, ('y', 'x', 'core'), moves(first, shift))]
    pallas_call x5, Pallas kernels: 9.82 us -> 15.4 us  [half(): pl.pallas_call(lambda *refs: pass_kernel(over_rows, last, *refs), out_sha...]
    ppermute x15, starting transfers between devices: 28.5 us -> 23.9 us  [go(): return lax.ppermute(block, ('y', 'x', 'core'), moves(first, shift))]
    all_to_all x3, blocking collectives: 35 us -> 30.7 us  [on_device(): kv_parts = lax.all_to_all(kv, ('core', 'z'), 0, 0, tiled=True)]
    pallas_call x1, Pallas kernels: 3.4 us -> 5.49 us  [on_device(): pl.pallas_call(plan_kernel, out_shape=(jax.ShapeDtypeStruct((3, CAP), jnp...]
  transfers between devices with their start and end apart: 17 -> 17, of which waited for: 7 -> 3; matrix products, arithmetic and copies ran while one was open for 1% -> 1% of each run, Pallas kernels for 14% -> 22%
where the time goes in v11:
time: 170 us; the launch traced here: 169 us
  blocking collectives  75.9 us (45%)
  Pallas kernels  55.2 us (32%)
  starting transfers between devices  24 us (14%)
  waiting for transfers between devices  9.69 us (6%)
  other arithmetic  2.26 us (1%)
    all_to_all x2, blocking collectives, on_device(): ktu_parts = lax.all_to_all(ktu, ('y', 'x'), 0, 0, tiled=True)  35.1 us
    pallas_call x6, Pallas kernels, build(): pl.pallas_call(lambda *refs: build_kernel(scale, first, blocks, last, *re...  33.7 us
    all_to_all x3, blocking collectives, on_device(): kv_parts = lax.all_to_all(kv, ('core', 'z'), 0, 0, tiled=True)  30.7 us
    ppermute x15, starting transfers between devices, go(): return lax.ppermute(block, ('y', 'x', 'core'), moves(first, shift))  23.9 us
    pallas_call x5, Pallas kernels, half(): pl.pallas_call(lambda *refs: pass_kernel(over_rows, last, *refs), out_sha...  15.4 us
    all_to_all x1, blocking collectives, on_device(): mine = lax.all_to_all(ktu, ('y', 'x'), 0, 0, tiled=True)  10.1 us
    ppermute x15, waiting for transfers between devices, go(): return lax.ppermute(block, ('y', 'x', 'core'), moves(first, shift))  6.06 us
    pallas_call x1, Pallas kernels, on_device(): pl.pallas_call(plan_kernel, out_shape=(jax.ShapeDtypeStruct((3, CAP), jnp...  5.49 us
  transfers between devices with their start and end apart: 17, of which 3 were waited for; matrix products, arithmetic and copies ran while one was open for 1% of the time, Pallas kernels for 22%

profile of v11, /device:TPU:0, one launch (start us, length us, event | category | flops | bytes accessed | tf_op | source)
XLA Modules:
  0.0 169.2 jit_solution(9113957712489287746)
XLA Ops:
  0.6 0.0 copy-start
  0.6 0.1 collective-permute-start.3
  0.7 1.6 collective-permute-start.1
  2.4 1.7 collective-permute-start.2
  4.7 0.8 pad_add_fusion
  5.5 0.0 collective-permute-start
  5.5 1.7 %collective-permute-start.6 = (bf16[512,768]{1,0:T(8,128)(2,1)}, bf16[512,768]{1,0:T(8,128)(2,1)S(1)}, u32[]{:S(2)}, u32[]{:S(2)}) collective-permute-start(bf16[512,768]{1,0:T(8,128)(2,1)} %refs_5_.1), channel_id=1, source_target_pairs={{0,32},{4,12},{8,40},{12,20},{16,48},{20,28},{24,56},{28,4},{32,64... | collective-permute-start | bytes 2359304 | tf_op jit(solution)/shard_map/ppermute | solution.py:232
  7.2 3.6 %collective-permute-done = s32[1,128]{1,0:T(1,128)S(1)} collective-permute-done((s32[1,128]{1,0:T(1,128)S(1)}, s32[1,128]{1,0:T(1,128)S(1)}, u32[]{:S(2)}, u32[]{:S(2)}) %collective-permute-start) | collective-permute-done | bytes 544 | tf_op jit(solution)/shard_map/ppermute | solution.py:244
  10.8 3.1 %collective-permute-start.7 = (bf16[512,768]{1,0:T(8,128)(2,1)}, bf16[512,768]{1,0:T(8,128)(2,1)}, u32[]{:S(2)}, u32[]{:S(2)}) collective-permute-start(bf16[512,768]{1,0:T(8,128)(2,1)} %refs_5_.1), channel_id=1, source_target_pairs={{0,96},{4,28},{8,104},{12,4},{16,112},{20,12},{24,120},{28,20},{32... | collective-permute-start | bytes 2359304 | tf_op jit(solution)/shard_map/ppermute | solution.py:232
  13.9 0.1 pad_add_fusion.1.place.refs_2_
  14.0 0.8 add_select_fusion.lists
  14.8 0.7 copy-done.1
  15.5 5.5 %plan.1 = (s32[3,64]{1,0:T(4,128)S(1)}, s32[17]{0:T(128)S(1)}) custom-call(s32[2,128]{1,0:T(2,128)S(1)} %add_select_fusion.lists, s32[3]{0:T(128)S(1)} %pad_add_fusion.1.place.refs_2_, s32[16]{0:T(128)S(1)} %copy-done.1), custom_call_target="tpu_custom_call" | custom-call | tf_op jit(solution)/shard_map/plan/pallas_call | solution.py:253
  21.0 0.0 collective-permute-done.2.refs_7_
  21.0 2.3 %collective-permute-start.4 = (bf16[512,768]{1,0:T(8,128)(2,1)S(1)}, bf16[512,768]{1,0:T(8,128)(2,1)S(1)}, u32[]{:S(2)}, u32[]{:S(2)}) collective-permute-start(bf16[512,768]{1,0:T(8,128)(2,1)S(1)} %collective-permute-done.2.refs_7_), channel_id=1, source_target_pairs={{0,24},{4,100},{8,0},{12,108},{16,8},{20,116},{24,16},{28,124},{32... | collective-permute-start | bytes 2359304 | tf_op jit(solution)/shard_map/ppermute | solution.py:232
  23.3 0.0 collective-permute-start.5
  23.3 0.6 room.1.refs_10_
  23.9 0.0 collective-permute-done.6.refs_8_
  23.9 3.3 %collective-permute-start.10 = (bf16[512,768]{1,0:T(8,128)(2,1)S(1)}, bf16[512,768]{1,0:T(8,128)(2,1)S(1)}, u32[]{:S(2)}, u32[]{:S(2)}) collective-permute-start(bf16[512,768]{1,0:T(8,128)(2,1)S(1)} %collective-permute-done.2.refs_7_), channel_id=1, source_target_pairs={{0,96},{4,28},{8,104},{12,4},{16,112},{20,12},{24,120},{28,20},{32... | collective-permute-start | bytes 2359304 | tf_op jit(solution)/shard_map/ppermute | solution.py:232
  27.2 0.0 collective-permute-done.7.refs_9_
  27.2 3.2 %collective-permute-start.9 = (bf16[512,768]{1,0:T(8,128)(2,1)S(1)}, bf16[512,768]{1,0:T(8,128)(2,1)S(1)}, u32[]{:S(2)}, u32[]{:S(2)}) collective-permute-start(bf16[512,768]{1,0:T(8,128)(2,1)S(1)} %collective-permute-done.1.refs_6_), channel_id=1, source_target_pairs={{0,96},{4,28},{8,104},{12,4},{16,112},{20,12},{24,120},{28,20},{32... | collective-permute-start | bytes 2359304 | tf_op jit(solution)/shard_map/ppermute | solution.py:232
  30.4 7.5 %build.6 = (bf16[64,512,512]{2,1,0:T(8,128)(2,1)S(1)}, f32[16,512]{1,0:T(8,128)S(1)}) custom-call(s32[3,64]{1,0:T(4,128)S(1)} %get-tuple-element.45.pairs.refs_0_, s32[17]{0:T(128)S(1)} %get-tuple-element.47.bounds.refs_1_, s32[3]{0:T(128)S(1)} %pad_add_fusion.1.place.refs_2_, bf16[4096,768]{1,0:T(8,128)(2,1)} %refs_3_.11, ...), custom_call_target="tpu_custom_call", output_to_operand_aliasing={{0}: (10, {})} | custom-call | flops 4026531840 | bytes 15728640 | tf_op jit(solution)/shard_map/build/pallas_call | solution.py:278
  37.9 3.1 %collective-permute-done.4.refs_5_ = bf16[512,768]{1,0:T(8,128)(2,1)S(1)} collective-permute-done((bf16[512,768]{1,0:T(8,128)(2,1)S(1)}, bf16[512,768]{1,0:T(8,128)(2,1)S(1)}, u32[]{:S(2)}, u32[]{:S(2)}) %collective-permute-start.4) | collective-permute-done | bytes 786464 | tf_op jit(solution)/shard_map/ppermute | solution.py:232
  41.0 0.0 collective-permute-done.5.refs_6_
  41.0 2.0 %collective-permute-start.16 = (bf16[512,768]{1,0:T(8,128)(2,1)S(1)}, bf16[512,768]{1,0:T(8,128)(2,1)S(1)}, u32[]{:S(2)}, u32[]{:S(2)}) collective-permute-start(bf16[512,768]{1,0:T(8,128)(2,1)S(1)} %collective-permute-done.5.refs_6_), channel_id=1, source_target_pairs={{0,32},{4,12},{8,40},{12,20},{16,48},{20,28},{24,56},{28,4},{32,64... | collective-permute-start | bytes 2359304 | tf_op jit(solution)/shard_map/ppermute | solution.py:232
  43.1 5.9 %build.7 = (bf16[64,512,512]{2,1,0:T(8,128)(2,1)S(1)}, f32[16,512]{1,0:T(8,128)S(1)}) custom-call(s32[3,64]{1,0:T(4,128)S(1)} %get-tuple-element.45.pairs.refs_0_, s32[17]{0:T(128)S(1)} %get-tuple-element.47.bounds.refs_1_, s32[3]{0:T(128)S(1)} %pad_add_fusion.1.place.refs_2_, bf16[4096,768]{1,0:T(8,128)(2,1)} %refs_3_.11, ...), custom_call_target="tpu_custom_call", output_to_operand_aliasing={{0}: (7, {})} | custom-call | flops 1610612736 | bytes 6291456 | tf_op jit(solution)/shard_map/build/pallas_call | solution.py:278
  48.9 0.0 collective-permute-done.10.refs_6_
  48.9 0.1 collective-permute-start.15
  49.0 0.0 collective-permute-done.9.refs_5_
  49.0 3.6 %collective-permute-start.13 = (bf16[512,768]{1,0:T(8,128)(2,1)S(1)}, bf16[512,768]{1,0:T(8,128)(2,1)S(1)}, u32[]{:S(2)}, u32[]{:S(2)}) collective-permute-start(bf16[512,768]{1,0:T(8,128)(2,1)S(1)} %collective-permute-done.9.refs_5_), channel_id=1, source_target_pairs={{0,96},{4,28},{8,104},{12,4},{16,112},{20,12},{24,120},{28,20},{32... | collective-permute-start | bytes 2359304 | tf_op jit(solution)/shard_map/ppermute | solution.py:232
  52.6 7.1 %build.8 = (bf16[64,512,512]{2,1,0:T(8,128)(2,1)S(1)}, f32[16,512]{1,0:T(8,128)S(1)}) custom-call(s32[3,64]{1,0:T(4,128)S(1)} %get-tuple-element.45.pairs.refs_0_, s32[17]{0:T(128)S(1)} %get-tuple-element.47.bounds.refs_1_, s32[3]{0:T(128)S(1)} %pad_add_fusion.1.place.refs_2_, bf16[4096,768]{1,0:T(8,128)(2,1)} %refs_3_.11, ...), custom_call_target="tpu_custom_call", output_to_operand_aliasing={{0}: (8, {})} | custom-call | flops 2415919104 | bytes 9437184 | tf_op jit(solution)/shard_map/build/pallas_call | solution.py:278
  59.8 1.3 collective-permute-start.12
  61.1 7.1 %build.9 = (bf16[64,512,512]{2,1,0:T(8,128)(2,1)S(1)}, f32[16,512]{1,0:T(8,128)S(1)}) custom-call(s32[3,64]{1,0:T(4,128)S(1)} %get-tuple-element.45.pairs.refs_0_, s32[17]{0:T(128)S(1)} %get-tuple-element.47.bounds.refs_1_, s32[3]{0:T(128)S(1)} %pad_add_fusion.1.place.refs_2_, bf16[4096,768]{1,0:T(8,128)(2,1)} %refs_3_.11, ...), custom_call_target="tpu_custom_call", output_to_operand_aliasing={{0}: (7, {})} | custom-call | flops 1610612736 | bytes 6291456 | tf_op jit(solution)/shard_map/build/pallas_call | solution.py:278
  68.2 2.9 %collective-permute-done.14.refs_6_ = bf16[512,768]{1,0:T(8,128)(2,1)S(1)} collective-permute-done((bf16[512,768]{1,0:T(8,128)(2,1)S(1)}, bf16[512,768]{1,0:T(8,128)(2,1)S(1)}, u32[]{:S(2)}, u32[]{:S(2)}) %collective-permute-start.14) | collective-permute-done | bytes 786464 | tf_op jit(solution)/shard_map/ppermute | solution.py:232
  71.1 3.1 %build.10 = (bf16[64,512,512]{2,1,0:T(8,128)(2,1)S(1)}, f32[16,512]{1,0:T(8,128)S(1)}) custom-call(s32[3,64]{1,0:T(4,128)S(1)} %get-tuple-element.45.pairs.refs_0_, s32[17]{0:T(128)S(1)} %get-tuple-element.47.bounds.refs_1_, s32[3]{0:T(128)S(1)} %pad_add_fusion.1.place.refs_2_, bf16[4096,768]{1,0:T(8,128)(2,1)} %refs_3_.11, ...), custom_call_target="tpu_custom_call", output_to_operand_aliasing={{0}: (8, {})} | custom-call | flops 2415919104 | bytes 9437184 | tf_op jit(solution)/shard_map/build/pallas_call | solution.py:278
  74.2 3.0 %build.11 = (bf16[64,512,512]{2,1,0:T(8,128)(2,1)S(1)}, f32[8,16,512]{2,1,0:T(8,128)S(1)}) custom-call(s32[3,64]{1,0:T(4,128)S(1)} %get-tuple-element.45.pairs.refs_0_, s32[17]{0:T(128)S(1)} %get-tuple-element.47.bounds.refs_1_, s32[3]{0:T(128)S(1)} %pad_add_fusion.1.place.refs_2_, bf16[4096,768]{1,0:T(8,128)(2,1)} %refs_3_.11, ...), custom_call_target="tpu_custom_call", output_to_operand_aliasing={{0}: (6, {})} | custom-call | flops 805306368 | bytes 3145728 | tf_op jit(solution)/shard_map/build/pallas_call | solution.py:278
  77.3 12.0 %all_to_all.30.refs_3_ = f32[8,16,512]{2,1,0:T(8,128)S(1)} all-to-all(f32[8,16,512]{2,1,0:T(8,128)S(1)} %get-tuple-element.76), channel_id=1, replica_groups=mesh['y'=4,'x'=4,'core'=2,'z'=4] {'core','z'}, dimensions={0} | all-to-all | bytes 524288 | tf_op jit(solution)/shard_map/all_to_all | solution.py:339
  89.3 2.7 %columns.3 = (f32[16,16,512]{2,1,0:T(8,128)S(1)}, bf16[64,512,512]{2,1,0:T(8,128)(2,1)S(1)}) custom-call(s32[3,64]{1,0:T(4,128)S(1)} %get-tuple-element.45.pairs.refs_0_, s32[17]{0:T(128)S(1)} %get-tuple-element.47.bounds.refs_1_, s32[3]{0:T(128)S(1)} %pad_add_fusion.1.place.refs_2_, ...), custom_call_target="tpu_custom_call", output_to_operand_aliasing={{1}: (4, {})} | custom-call | tf_op jit(solution)/shard_map/columns/pallas_call | solution.py:325
  92.0 20.4 %all_to_all.31.refs_3_ = f32[16,16,512]{2,1,0:T(8,128)S(1)} all-to-all(f32[16,16,512]{2,1,0:T(8,128)S(1)} %get-tuple-element.78), channel_id=1, replica_groups=mesh['y'=4,'x'=4,'core'=2,'z'=4] {'y','x'}, dimensions={0} | all-to-all | bytes 1048576 | tf_op jit(solution)/shard_map/all_to_all | solution.py:342
  112.4 3.3 %rows.2 = (f32[8,16,512]{2,1,0:T(8,128)S(1)}, bf16[64,512,512]{2,1,0:T(8,128)(2,1)S(1)}) custom-call(s32[3,64]{1,0:T(4,128)S(1)} %get-tuple-element.45.pairs.refs_0_, s32[17]{0:T(128)S(1)} %get-tuple-element.47.bounds.refs_1_, s32[3]{0:T(128)S(1)} %pad_add_fusion.1.place.refs_2_, ...), custom_call_target="tpu_custom_call", output_to_operand_aliasing={{1}: (4, {})} | custom-call | tf_op jit(solution)/shard_map/rows/pallas_call | solution.py:325
  115.7 9.3 %all_to_all.32.refs_3_ = f32[8,16,512]{2,1,0:T(8,128)S(1)} all-to-all(f32[8,16,512]{2,1,0:T(8,128)S(1)} %get-tuple-element.80), channel_id=1, replica_groups=mesh['y'=4,'x'=4,'core'=2,'z'=4] {'core','z'}, dimensions={0} | all-to-all | bytes 524288 | tf_op jit(solution)/shard_map/all_to_all | solution.py:339
  125.1 2.7 %columns.4 = (f32[16,16,512]{2,1,0:T(8,128)S(1)}, bf16[64,512,512]{2,1,0:T(8,128)(2,1)S(1)}) custom-call(s32[3,64]{1,0:T(4,128)S(1)} %get-tuple-element.45.pairs.refs_0_, s32[17]{0:T(128)S(1)} %get-tuple-element.47.bounds.refs_1_, s32[3]{0:T(128)S(1)} %pad_add_fusion.1.place.refs_2_, ...), custom_call_target="tpu_custom_call", output_to_operand_aliasing={{1}: (4, {})} | custom-call | tf_op jit(solution)/shard_map/columns/pallas_call | solution.py:325
  127.8 14.7 %all_to_all.33.refs_3_ = f32[16,16,512]{2,1,0:T(8,128)S(1)} all-to-all(f32[16,16,512]{2,1,0:T(8,128)S(1)} %get-tuple-element.82), channel_id=1, replica_groups=mesh['y'=4,'x'=4,'core'=2,'z'=4] {'y','x'}, dimensions={0} | all-to-all | bytes 1048576 | tf_op jit(solution)/shard_map/all_to_all | solution.py:342
  142.5 3.3 %rows.3 = (f32[8,16,512]{2,1,0:T(8,128)S(1)}, bf16[64,512,512]{2,1,0:T(8,128)(2,1)S(1)}) custom-call(s32[3,64]{1,0:T(4,128)S(1)} %get-tuple-element.45.pairs.refs_0_, s32[17]{0:T(128)S(1)} %get-tuple-element.47.bounds.refs_1_, s32[3]{0:T(128)S(1)} %pad_add_fusion.1.place.refs_2_, ...), custom_call_target="tpu_custom_call", output_to_operand_aliasing={{1}: (4, {})} | custom-call | tf_op jit(solution)/shard_map/rows/pallas_call | solution.py:325
  145.9 9.3 %all_to_all.34.refs_3_ = f32[8,16,512]{2,1,0:T(8,128)S(1)} all-to-all(f32[8,16,512]{2,1,0:T(8,128)S(1)} %get-tuple-element.84), channel_id=1, replica_groups=mesh['y'=4,'x'=4,'core'=2,'z'=4] {'core','z'}, dimensions={0} | all-to-all | bytes 524288 | tf_op jit(solution)/shard_map/all_to_all | solution.py:339
  155.2 3.3 %columns.5 = (f32[16,4,128]{2,1,0:T(4,128)S(1)}, f32[32,128]{1,0:T(8,128)}) custom-call(s32[3,64]{1,0:T(4,128)S(1)} %get-tuple-element.45.pairs.refs_0_, s32[17]{0:T(128)S(1)} %get-tuple-element.47.bounds.refs_1_, s32[3]{0:T(128)S(1)} %pad_add_fusion.1.place.refs_2_, f32[8,16,512]{2,1,0:T(8,128)S(1)} %all_to_all.34.refs_3_, ...), custom_call_target="tpu_custom_call" | custom-call | tf_op jit(solution)/shard_map/columns/pallas_call | solution.py:325
  158.5 10.1 %all_to_all.35 = f32[16,4,128]{2,1,0:T(4,128)S(1)} all-to-all(f32[16,4,128]{2,1,0:T(4,128)S(1)} %get-tuple-element.87), channel_id=1, replica_groups=mesh['y'=4,'x'=4,'core'=2,'z'=4] {'y','x'}, dimensions={0} | all-to-all | bytes 65536 | tf_op jit(solution)/shard_map/all_to_all | solution.py:344
  168.6 0.6 log_bitcast_fusion
  (16 shorter events, 0.1 us)
Async XLA Ops:
  0.6 29.8 %copy-start = (bf16[512,768]{1,0:T(8,128)(2,1)S(1)}, bf16[512,768]{1,0:T(8,128)(2,1)}, u32[]{:S(2)}) copy-start(bf16[512,768]{1,0:T(8,128)(2,1)} %refs_5_.1) | copy-start | bytes 2359300
  0.6 26.5 %collective-permute-start.3 = (bf16[4096,768]{1,0:T(8,128)(2,1)}, bf16[4096,768]{1,0:T(8,128)(2,1)}, u32[]{:S(2)}, u32[]{:S(2)}) collective-permute-start(bf16[4096,768]{1,0:T(8,128)(2,1)} %refs_3_.11), channel_id=1, source_target_pairs={{0,4},{4,0},{1,5},{5,1},{2,6},{6,2},{3,7},{7,3},{8,12},{12,8},{9,1... | collective-permute-start | bytes 18874376 | tf_op jit(solution)/shard_map/ppermute | solution.py:243
  0.7 20.3 %collective-permute-start.1 = (bf16[512,768]{1,0:T(8,128)(2,1)}, bf16[512,768]{1,0:T(8,128)(2,1)S(1)}, u32[]{:S(2)}, u32[]{:S(2)}) collective-permute-start(bf16[512,768]{1,0:T(8,128)(2,1)} %refs_5_.1), channel_id=1, source_target_pairs={{0,8},{4,36},{8,16},{12,44},{16,24},{20,52},{24,0},{28,60},{32,40}... | collective-permute-start | bytes 2359304 | tf_op jit(solution)/shard_map/ppermute | solution.py:232
  2.4 18.6 %collective-permute-start.2 = (bf16[512,768]{1,0:T(8,128)(2,1)}, bf16[512,768]{1,0:T(8,128)(2,1)S(1)}, u32[]{:S(2)}, u32[]{:S(2)}) collective-permute-start(bf16[512,768]{1,0:T(8,128)(2,1)} %refs_5_.1), channel_id=1, source_target_pairs={{0,24},{4,100},{8,0},{12,108},{16,8},{20,116},{24,16},{28,124},{32... | collective-permute-start | bytes 2359304 | tf_op jit(solution)/shard_map/ppermute | solution.py:232
  5.5 5.4 %collective-permute-start = (s32[1,128]{1,0:T(1,128)S(1)}, s32[1,128]{1,0:T(1,128)S(1)}, u32[]{:S(2)}, u32[]{:S(2)}) collective-permute-start(s32[1,128]{1,0:T(1,128)S(1)} %pad_add_fusion), channel_id=1, source_target_pairs={{0,4},{4,0},{1,5},{5,1},{2,6},{6,2},{3,7},{7,3},{8,12},{12,8},{9,1... | collective-permute-start | bytes 1544 | tf_op jit(solution)/shard_map/ppermute | solution.py:244
  5.5 18.4 %collective-permute-start.6 = (bf16[512,768]{1,0:T(8,128)(2,1)}, bf16[512,768]{1,0:T(8,128)(2,1)S(1)}, u32[]{:S(2)}, u32[]{:S(2)}) collective-permute-start(bf16[512,768]{1,0:T(8,128)(2,1)} %refs_5_.1), channel_id=1, source_target_pairs={{0,32},{4,12},{8,40},{12,20},{16,48},{20,28},{24,56},{28,4},{32,64... | collective-permute-start | bytes 2359304 | tf_op jit(solution)/shard_map/ppermute | solution.py:232
  10.8 16.3 %collective-permute-start.7 = (bf16[512,768]{1,0:T(8,128)(2,1)}, bf16[512,768]{1,0:T(8,128)(2,1)}, u32[]{:S(2)}, u32[]{:S(2)}) collective-permute-start(bf16[512,768]{1,0:T(8,128)(2,1)} %refs_5_.1), channel_id=1, source_target_pairs={{0,96},{4,28},{8,104},{12,4},{16,112},{20,12},{24,120},{28,20},{32... | collective-permute-start | bytes 2359304 | tf_op jit(solution)/shard_map/ppermute | solution.py:232
  14.8 0.7 copy-start.1
  21.0 20.0 %collective-permute-start.4 = (bf16[512,768]{1,0:T(8,128)(2,1)S(1)}, bf16[512,768]{1,0:T(8,128)(2,1)S(1)}, u32[]{:S(2)}, u32[]{:S(2)}) collective-permute-start(bf16[512,768]{1,0:T(8,128)(2,1)S(1)} %collective-permute-done.2.refs_7_), channel_id=1, source_target_pairs={{0,24},{4,100},{8,0},{12,108},{16,8},{20,116},{24,16},{28,124},{32... | collective-permute-start | bytes 2359304 | tf_op jit(solution)/shard_map/ppermute | solution.py:232
  23.3 17.8 %collective-permute-start.5 = (bf16[512,768]{1,0:T(8,128)(2,1)S(1)}, bf16[512,768]{1,0:T(8,128)(2,1)S(1)}, u32[]{:S(2)}, u32[]{:S(2)}) collective-permute-start(bf16[512,768]{1,0:T(8,128)(2,1)S(1)} %collective-permute-done.2.refs_7_), channel_id=1, source_target_pairs={{0,32},{4,12},{8,40},{12,20},{16,48},{20,28},{24,56},{28,4},{32,64... | collective-permute-start | bytes 2359304 | tf_op jit(solution)/shard_map/ppermute | solution.py:232
  23.9 25.1 %collective-permute-start.10 = (bf16[512,768]{1,0:T(8,128)(2,1)S(1)}, bf16[512,768]{1,0:T(8,128)(2,1)S(1)}, u32[]{:S(2)}, u32[]{:S(2)}) collective-permute-start(bf16[512,768]{1,0:T(8,128)(2,1)S(1)} %collective-permute-done.2.refs_7_), channel_id=1, source_target_pairs={{0,96},{4,28},{8,104},{12,4},{16,112},{20,12},{24,120},{28,20},{32... | collective-permute-start | bytes 2359304 | tf_op jit(solution)/shard_map/ppermute | solution.py:232
  27.2 21.9 %collective-permute-start.11 = (bf16[512,768]{1,0:T(8,128)(2,1)S(1)}, bf16[512,768]{1,0:T(8,128)(2,1)S(1)}, u32[]{:S(2)}, u32[]{:S(2)}) collective-permute-start(bf16[512,768]{1,0:T(8,128)(2,1)S(1)} %collective-permute-done.1.refs_6_), channel_id=1, source_target_pairs={{0,32},{4,12},{8,40},{12,20},{16,48},{20,28},{24,56},{28,4},{32,64... | collective-permute-start | bytes 2359304 | tf_op jit(solution)/shard_map/ppermute | solution.py:232
  27.2 21.9 %collective-permute-start.9 = (bf16[512,768]{1,0:T(8,128)(2,1)S(1)}, bf16[512,768]{1,0:T(8,128)(2,1)S(1)}, u32[]{:S(2)}, u32[]{:S(2)}) collective-permute-start(bf16[512,768]{1,0:T(8,128)(2,1)S(1)} %collective-permute-done.1.refs_6_), channel_id=1, source_target_pairs={{0,96},{4,28},{8,104},{12,4},{16,112},{20,12},{24,120},{28,20},{32... | collective-permute-start | bytes 2359304 | tf_op jit(solution)/shard_map/ppermute | solution.py:232
  41.0 18.8 %collective-permute-start.8 = (bf16[512,768]{1,0:T(8,128)(2,1)S(1)}, bf16[512,768]{1,0:T(8,128)(2,1)S(1)}, u32[]{:S(2)}, u32[]{:S(2)}) collective-permute-start(bf16[512,768]{1,0:T(8,128)(2,1)S(1)} %collective-permute-done.4.refs_5_), channel_id=1, source_target_pairs={{0,96},{4,28},{8,104},{12,4},{16,112},{20,12},{24,120},{28,20},{32... | collective-permute-start | bytes 2359304 | tf_op jit(solution)/shard_map/ppermute | solution.py:232
  41.0 20.0 %collective-permute-start.16 = (bf16[512,768]{1,0:T(8,128)(2,1)S(1)}, bf16[512,768]{1,0:T(8,128)(2,1)S(1)}, u32[]{:S(2)}, u32[]{:S(2)}) collective-permute-start(bf16[512,768]{1,0:T(8,128)(2,1)S(1)} %collective-permute-done.5.refs_6_), channel_id=1, source_target_pairs={{0,32},{4,12},{8,40},{12,20},{16,48},{20,28},{24,56},{28,4},{32,64... | collective-permute-start | bytes 2359304 | tf_op jit(solution)/shard_map/ppermute | solution.py:232
  48.9 22.2 %collective-permute-start.15 = (bf16[512,768]{1,0:T(8,128)(2,1)S(1)}, bf16[512,768]{1,0:T(8,128)(2,1)S(1)}, u32[]{:S(2)}, u32[]{:S(2)}) collective-permute-start(bf16[512,768]{1,0:T(8,128)(2,1)S(1)} %collective-permute-done.4.refs_5_), channel_id=1, source_target_pairs={{0,32},{4,12},{8,40},{12,20},{16,48},{20,28},{24,56},{28,4},{32,64... | collective-permute-start | bytes 2359304 | tf_op jit(solution)/shard_map/ppermute | solution.py:232
  49.0 19.1 %collective-permute-start.13 = (bf16[512,768]{1,0:T(8,128)(2,1)S(1)}, bf16[512,768]{1,0:T(8,128)(2,1)S(1)}, u32[]{:S(2)}, u32[]{:S(2)}) collective-permute-start(bf16[512,768]{1,0:T(8,128)(2,1)S(1)} %collective-permute-done.9.refs_5_), channel_id=1, source_target_pairs={{0,96},{4,28},{8,104},{12,4},{16,112},{20,12},{24,120},{28,20},{32... | collective-permute-start | bytes 2359304 | tf_op jit(solution)/shard_map/ppermute | solution.py:232
  52.6 18.5 %collective-permute-start.14 = (bf16[512,768]{1,0:T(8,128)(2,1)S(1)}, bf16[512,768]{1,0:T(8,128)(2,1)S(1)}, u32[]{:S(2)}, u32[]{:S(2)}) collective-permute-start(bf16[512,768]{1,0:T(8,128)(2,1)S(1)} %collective-permute-done.6.refs_8_), channel_id=1, source_target_pairs={{0,32},{4,12},{8,40},{12,20},{16,48},{20,28},{24,56},{28,4},{32,64... | collective-permute-start | bytes 2359304 | tf_op jit(solution)/shard_map/ppermute | solution.py:232
  59.8 14.4 %collective-permute-start.12 = (bf16[512,768]{1,0:T(8,128)(2,1)S(1)}, bf16[512,768]{1,0:T(8,128)(2,1)S(1)}, u32[]{:S(2)}, u32[]{:S(2)}) collective-permute-start(bf16[512,768]{1,0:T(8,128)(2,1)S(1)} %collective-permute-done.8.refs_5_), channel_id=1, source_target_pairs={{0,96},{4,28},{8,104},{12,4},{16,112},{20,12},{24,120},{28,20},{32... | collective-permute-start | bytes 2359304 | tf_op jit(solution)/shard_map/ppermute | solution.py:232

commit v12 on v11

--- a/solution.py
+++ b/solution.py
@@ -191,7 +191,7 @@
                     part = part + store[safe, :, lanes].astype(F32) * row[:, lanes]
                 found.append((target, jnp.sum(part.T, axis=0, keepdims=True)))
                 continue
-            if not over_rows and k % 3 == 0:
+            if not over_rows and k % 2 == 0:
                 tall = jnp.broadcast_to(row, (LANES, TILE)).T
                 cut = []
                 for q in range(TILE // LANES):

time: 170 us -> 171 us (level)
  transfers between devices with their start and end apart: 17 -> 17, of which waited for: 3 -> 4; matrix products, arithmetic and copies ran while one was open for 1% -> 1% of each run, Pallas kernels for 22% -> 21%
where the time goes in v12:
time: 171 us; the launch traced here: 169 us
  blocking collectives  74.5 us (44%)
  Pallas kernels  54.1 us (32%)
  starting transfers between devices  25.3 us (15%)
  waiting for transfers between devices  11.1 us (6%)
  other arithmetic  2.26 us (1%)
    all_to_all x2, blocking collectives, on_device(): ktu_parts = lax.all_to_all(ktu, ('y', 'x'), 0, 0, tiled=True)  33.5 us
    pallas_call x6, Pallas kernels, build(): pl.pallas_call(lambda *refs: build_kernel(scale, first, blocks, last, *re...  32.9 us
    all_to_all x3, blocking collectives, on_device(): kv_parts = lax.all_to_all(kv, ('core', 'z'), 0, 0, tiled=True)  30.7 us
    ppermute x15, starting transfers between devices, go(): return lax.ppermute(block, ('y', 'x', 'core'), moves(first, shift))  25.2 us
    pallas_call x5, Pallas kernels, half(): pl.pallas_call(lambda *refs: pass_kernel(over_rows, last, *refs), out_sha...  15.9 us
    all_to_all x1, blocking collectives, on_device(): mine = lax.all_to_all(ktu, ('y', 'x'), 0, 0, tiled=True)  10.2 us
    ppermute x15, waiting for transfers between devices, go(): return lax.ppermute(block, ('y', 'x', 'core'), moves(first, shift))  7.46 us
    pallas_call x1, Pallas kernels, on_device(): pl.pallas_call(plan_kernel, out_shape=(jax.ShapeDtypeStruct((3, CAP), jnp...  4.78 us
  transfers between devices with their start and end apart: 17, of which 4 were waited for; matrix products, arithmetic and copies ran while one was open for 1% of the time, Pallas kernels for 21%

profile of v12, /device:TPU:0, one launch (start us, length us, event | category | flops | bytes accessed | tf_op | source)
XLA Modules:
  0.0 169.4 jit_solution(4154675553981032662)
XLA Ops:
  0.6 0.0 copy-start
  0.6 0.1 collective-permute-start.3
  0.7 1.6 collective-permute-start.1
  2.4 1.7 collective-permute-start.2
  4.7 0.8 pad_add_fusion
  5.5 0.0 collective-permute-start
  5.5 1.7 %collective-permute-start.6 = (bf16[512,768]{1,0:T(8,128)(2,1)}, bf16[512,768]{1,0:T(8,128)(2,1)S(1)}, u32[]{:S(2)}, u32[]{:S(2)}) collective-permute-start(bf16[512,768]{1,0:T(8,128)(2,1)} %refs_5_.1), channel_id=1, source_target_pairs={{0,32},{4,12},{8,40},{12,20},{16,48},{20,28},{24,56},{28,4},{32,64... | collective-permute-start | bytes 2359304 | tf_op jit(solution)/shard_map/ppermute | solution.py:232
  7.2 3.6 %collective-permute-done = s32[1,128]{1,0:T(1,128)S(1)} collective-permute-done((s32[1,128]{1,0:T(1,128)S(1)}, s32[1,128]{1,0:T(1,128)S(1)}, u32[]{:S(2)}, u32[]{:S(2)}) %collective-permute-start) | collective-permute-done | bytes 544 | tf_op jit(solution)/shard_map/ppermute | solution.py:244
  10.8 3.1 %collective-permute-start.7 = (bf16[512,768]{1,0:T(8,128)(2,1)}, bf16[512,768]{1,0:T(8,128)(2,1)}, u32[]{:S(2)}, u32[]{:S(2)}) collective-permute-start(bf16[512,768]{1,0:T(8,128)(2,1)} %refs_5_.1), channel_id=1, source_target_pairs={{0,96},{4,28},{8,104},{12,4},{16,112},{20,12},{24,120},{28,20},{32... | collective-permute-start | bytes 2359304 | tf_op jit(solution)/shard_map/ppermute | solution.py:232
  13.9 0.1 pad_add_fusion.1.place.refs_2_
  14.0 0.8 add_select_fusion.lists
  14.8 0.7 copy-done.1
  15.5 4.8 %plan.1 = (s32[3,64]{1,0:T(4,128)S(1)}, s32[17]{0:T(128)S(1)}) custom-call(s32[2,128]{1,0:T(2,128)S(1)} %add_select_fusion.lists, s32[3]{0:T(128)S(1)} %pad_add_fusion.1.place.refs_2_, s32[16]{0:T(128)S(1)} %copy-done.1), custom_call_target="tpu_custom_call" | custom-call | tf_op jit(solution)/shard_map/plan/pallas_call | solution.py:253
  20.3 0.0 collective-permute-done.2.refs_7_
  20.3 2.0 %collective-permute-start.4 = (bf16[512,768]{1,0:T(8,128)(2,1)S(1)}, bf16[512,768]{1,0:T(8,128)(2,1)S(1)}, u32[]{:S(2)}, u32[]{:S(2)}) collective-permute-start(bf16[512,768]{1,0:T(8,128)(2,1)S(1)} %collective-permute-done.2.refs_7_), channel_id=1, source_target_pairs={{0,24},{4,100},{8,0},{12,108},{16,8},{20,116},{24,16},{28,124},{32... | collective-permute-start | bytes 2359304 | tf_op jit(solution)/shard_map/ppermute | solution.py:232
  22.3 0.5 collective-permute-start.5
  22.8 0.6 room.1.refs_10_
  23.4 0.0 collective-permute-done.6.refs_8_
  23.4 2.8 %collective-permute-start.10 = (bf16[512,768]{1,0:T(8,128)(2,1)S(1)}, bf16[512,768]{1,0:T(8,128)(2,1)S(1)}, u32[]{:S(2)}, u32[]{:S(2)}) collective-permute-start(bf16[512,768]{1,0:T(8,128)(2,1)S(1)} %collective-permute-done.2.refs_7_), channel_id=1, source_target_pairs={{0,96},{4,28},{8,104},{12,4},{16,112},{20,12},{24,120},{28,20},{32... | collective-permute-start | bytes 2359304 | tf_op jit(solution)/shard_map/ppermute | solution.py:232
  26.2 0.0 collective-permute-done.7.refs_9_
  26.2 0.8 collective-permute-start.11
  27.0 2.6 %collective-permute-start.9 = (bf16[512,768]{1,0:T(8,128)(2,1)S(1)}, bf16[512,768]{1,0:T(8,128)(2,1)S(1)}, u32[]{:S(2)}, u32[]{:S(2)}) collective-permute-start(bf16[512,768]{1,0:T(8,128)(2,1)S(1)} %collective-permute-done.1.refs_6_), channel_id=1, source_target_pairs={{0,96},{4,28},{8,104},{12,4},{16,112},{20,12},{24,120},{28,20},{32... | collective-permute-start | bytes 2359304 | tf_op jit(solution)/shard_map/ppermute | solution.py:232
  29.7 7.5 %build.6 = (bf16[64,512,512]{2,1,0:T(8,128)(2,1)S(1)}, f32[16,512]{1,0:T(8,128)S(1)}) custom-call(s32[3,64]{1,0:T(4,128)S(1)} %get-tuple-element.45.pairs.refs_0_, s32[17]{0:T(128)S(1)} %get-tuple-element.47.bounds.refs_1_, s32[3]{0:T(128)S(1)} %pad_add_fusion.1.place.refs_2_, bf16[4096,768]{1,0:T(8,128)(2,1)} %refs_3_.11, ...), custom_call_target="tpu_custom_call", output_to_operand_aliasing={{0}: (10, {})} | custom-call | flops 4026531840 | bytes 15728640 | tf_op jit(solution)/shard_map/build/pallas_call | solution.py:278
  37.1 2.4 %collective-permute-done.4.refs_5_ = bf16[512,768]{1,0:T(8,128)(2,1)S(1)} collective-permute-done((bf16[512,768]{1,0:T(8,128)(2,1)S(1)}, bf16[512,768]{1,0:T(8,128)(2,1)S(1)}, u32[]{:S(2)}, u32[]{:S(2)}) %collective-permute-start.4) | collective-permute-done | bytes 786464 | tf_op jit(solution)/shard_map/ppermute | solution.py:232
  39.5 0.9 collective-permute-start.8
  40.4 1.1 collective-permute-start.16
  41.5 5.9 %build.7 = (bf16[64,512,512]{2,1,0:T(8,128)(2,1)S(1)}, f32[16,512]{1,0:T(8,128)S(1)}) custom-call(s32[3,64]{1,0:T(4,128)S(1)} %get-tuple-element.45.pairs.refs_0_, s32[17]{0:T(128)S(1)} %get-tuple-element.47.bounds.refs_1_, s32[3]{0:T(128)S(1)} %pad_add_fusion.1.place.refs_2_, bf16[4096,768]{1,0:T(8,128)(2,1)} %refs_3_.11, ...), custom_call_target="tpu_custom_call", output_to_operand_aliasing={{0}: (7, {})} | custom-call | flops 1610612736 | bytes 6291456 | tf_op jit(solution)/shard_map/build/pallas_call | solution.py:278
  47.4 0.1 collective-permute-start.15
  47.5 1.4 collective-permute-done.9.refs_5_
  48.9 3.7 %collective-permute-start.13 = (bf16[512,768]{1,0:T(8,128)(2,1)S(1)}, bf16[512,768]{1,0:T(8,128)(2,1)S(1)}, u32[]{:S(2)}, u32[]{:S(2)}) collective-permute-start(bf16[512,768]{1,0:T(8,128)(2,1)S(1)} %collective-permute-done.9.refs_5_), channel_id=1, source_target_pairs={{0,96},{4,28},{8,104},{12,4},{16,112},{20,12},{24,120},{28,20},{32... | collective-permute-start | bytes 2359304 | tf_op jit(solution)/shard_map/ppermute | solution.py:232
  52.6 5.9 %build.8 = (bf16[64,512,512]{2,1,0:T(8,128)(2,1)S(1)}, f32[16,512]{1,0:T(8,128)S(1)}) custom-call(s32[3,64]{1,0:T(4,128)S(1)} %get-tuple-element.45.pairs.refs_0_, s32[17]{0:T(128)S(1)} %get-tuple-element.47.bounds.refs_1_, s32[3]{0:T(128)S(1)} %pad_add_fusion.1.place.refs_2_, bf16[4096,768]{1,0:T(8,128)(2,1)} %refs_3_.11, ...), custom_call_target="tpu_custom_call", output_to_operand_aliasing={{0}: (8, {})} | custom-call | flops 2415919104 | bytes 9437184 | tf_op jit(solution)/shard_map/build/pallas_call | solution.py:278
  58.6 2.5 %collective-permute-start.12 = (bf16[512,768]{1,0:T(8,128)(2,1)S(1)}, bf16[512,768]{1,0:T(8,128)(2,1)S(1)}, u32[]{:S(2)}, u32[]{:S(2)}) collective-permute-start(bf16[512,768]{1,0:T(8,128)(2,1)S(1)} %collective-permute-done.8.refs_5_), channel_id=1, source_target_pairs={{0,96},{4,28},{8,104},{12,4},{16,112},{20,12},{24,120},{28,20},{32... | collective-permute-start | bytes 2359304 | tf_op jit(solution)/shard_map/ppermute | solution.py:232
  61.1 5.7 %build.9 = (bf16[64,512,512]{2,1,0:T(8,128)(2,1)S(1)}, f32[16,512]{1,0:T(8,128)S(1)}) custom-call(s32[3,64]{1,0:T(4,128)S(1)} %get-tuple-element.45.pairs.refs_0_, s32[17]{0:T(128)S(1)} %get-tuple-element.47.bounds.refs_1_, s32[3]{0:T(128)S(1)} %pad_add_fusion.1.place.refs_2_, bf16[4096,768]{1,0:T(8,128)(2,1)} %refs_3_.11, ...), custom_call_target="tpu_custom_call", output_to_operand_aliasing={{0}: (7, {})} | custom-call | flops 1610612736 | bytes 6291456 | tf_op jit(solution)/shard_map/build/pallas_call | solution.py:278
  66.8 3.6 %collective-permute-done.14.refs_6_ = bf16[512,768]{1,0:T(8,128)(2,1)S(1)} collective-permute-done((bf16[512,768]{1,0:T(8,128)(2,1)S(1)}, bf16[512,768]{1,0:T(8,128)(2,1)S(1)}, u32[]{:S(2)}, u32[]{:S(2)}) %collective-permute-start.14) | collective-permute-done | bytes 786464 | tf_op jit(solution)/shard_map/ppermute | solution.py:232
  70.5 4.6 %build.10 = (bf16[64,512,512]{2,1,0:T(8,128)(2,1)S(1)}, f32[16,512]{1,0:T(8,128)S(1)}) custom-call(s32[3,64]{1,0:T(4,128)S(1)} %get-tuple-element.45.pairs.refs_0_, s32[17]{0:T(128)S(1)} %get-tuple-element.47.bounds.refs_1_, s32[3]{0:T(128)S(1)} %pad_add_fusion.1.place.refs_2_, bf16[4096,768]{1,0:T(8,128)(2,1)} %refs_3_.11, ...), custom_call_target="tpu_custom_call", output_to_operand_aliasing={{0}: (8, {})} | custom-call | flops 2415919104 | bytes 9437184 | tf_op jit(solution)/shard_map/build/pallas_call | solution.py:278
  75.1 3.3 %build.11 = (bf16[64,512,512]{2,1,0:T(8,128)(2,1)S(1)}, f32[8,16,512]{2,1,0:T(8,128)S(1)}) custom-call(s32[3,64]{1,0:T(4,128)S(1)} %get-tuple-element.45.pairs.refs_0_, s32[17]{0:T(128)S(1)} %get-tuple-element.47.bounds.refs_1_, s32[3]{0:T(128)S(1)} %pad_add_fusion.1.place.refs_2_, bf16[4096,768]{1,0:T(8,128)(2,1)} %refs_3_.11, ...), custom_call_target="tpu_custom_call", output_to_operand_aliasing={{0}: (6, {})} | custom-call | flops 805306368 | bytes 3145728 | tf_op jit(solution)/shard_map/build/pallas_call | solution.py:278
  78.3 12.1 %all_to_all.30.refs_3_ = f32[8,16,512]{2,1,0:T(8,128)S(1)} all-to-all(f32[8,16,512]{2,1,0:T(8,128)S(1)} %get-tuple-element.76), channel_id=1, replica_groups=mesh['y'=4,'x'=4,'core'=2,'z'=4] {'core','z'}, dimensions={0} | all-to-all | bytes 524288 | tf_op jit(solution)/shard_map/all_to_all | solution.py:339
  90.4 2.9 %columns.3 = (f32[16,16,512]{2,1,0:T(8,128)S(1)}, bf16[64,512,512]{2,1,0:T(8,128)(2,1)S(1)}) custom-call(s32[3,64]{1,0:T(4,128)S(1)} %get-tuple-element.45.pairs.refs_0_, s32[17]{0:T(128)S(1)} %get-tuple-element.47.bounds.refs_1_, s32[3]{0:T(128)S(1)} %pad_add_fusion.1.place.refs_2_, ...), custom_call_target="tpu_custom_call", output_to_operand_aliasing={{1}: (4, {})} | custom-call | tf_op jit(solution)/shard_map/columns/pallas_call | solution.py:325
  93.3 19.0 %all_to_all.31.refs_3_ = f32[16,16,512]{2,1,0:T(8,128)S(1)} all-to-all(f32[16,16,512]{2,1,0:T(8,128)S(1)} %get-tuple-element.78), channel_id=1, replica_groups=mesh['y'=4,'x'=4,'core'=2,'z'=4] {'y','x'}, dimensions={0} | all-to-all | bytes 1048576 | tf_op jit(solution)/shard_map/all_to_all | solution.py:342
  112.4 3.3 %rows.2 = (f32[8,16,512]{2,1,0:T(8,128)S(1)}, bf16[64,512,512]{2,1,0:T(8,128)(2,1)S(1)}) custom-call(s32[3,64]{1,0:T(4,128)S(1)} %get-tuple-element.45.pairs.refs_0_, s32[17]{0:T(128)S(1)} %get-tuple-element.47.bounds.refs_1_, s32[3]{0:T(128)S(1)} %pad_add_fusion.1.place.refs_2_, ...), custom_call_target="tpu_custom_call", output_to_operand_aliasing={{1}: (4, {})} | custom-call | tf_op jit(solution)/shard_map/rows/pallas_call | solution.py:325
  115.7 9.3 %all_to_all.32.refs_3_ = f32[8,16,512]{2,1,0:T(8,128)S(1)} all-to-all(f32[8,16,512]{2,1,0:T(8,128)S(1)} %get-tuple-element.80), channel_id=1, replica_groups=mesh['y'=4,'x'=4,'core'=2,'z'=4] {'core','z'}, dimensions={0} | all-to-all | bytes 524288 | tf_op jit(solution)/shard_map/all_to_all | solution.py:339
  125.0 2.9 %columns.4 = (f32[16,16,512]{2,1,0:T(8,128)S(1)}, bf16[64,512,512]{2,1,0:T(8,128)(2,1)S(1)}) custom-call(s32[3,64]{1,0:T(4,128)S(1)} %get-tuple-element.45.pairs.refs_0_, s32[17]{0:T(128)S(1)} %get-tuple-element.47.bounds.refs_1_, s32[3]{0:T(128)S(1)} %pad_add_fusion.1.place.refs_2_, ...), custom_call_target="tpu_custom_call", output_to_operand_aliasing={{1}: (4, {})} | custom-call | tf_op jit(solution)/shard_map/columns/pallas_call | solution.py:325
  127.9 14.5 %all_to_all.33.refs_3_ = f32[16,16,512]{2,1,0:T(8,128)S(1)} all-to-all(f32[16,16,512]{2,1,0:T(8,128)S(1)} %get-tuple-element.82), channel_id=1, replica_groups=mesh['y'=4,'x'=4,'core'=2,'z'=4] {'y','x'}, dimensions={0} | all-to-all | bytes 1048576 | tf_op jit(solution)/shard_map/all_to_all | solution.py:342
  142.4 3.3 %rows.3 = (f32[8,16,512]{2,1,0:T(8,128)S(1)}, bf16[64,512,512]{2,1,0:T(8,128)(2,1)S(1)}) custom-call(s32[3,64]{1,0:T(4,128)S(1)} %get-tuple-element.45.pairs.refs_0_, s32[17]{0:T(128)S(1)} %get-tuple-element.47.bounds.refs_1_, s32[3]{0:T(128)S(1)} %pad_add_fusion.1.place.refs_2_, ...), custom_call_target="tpu_custom_call", output_to_operand_aliasing={{1}: (4, {})} | custom-call | tf_op jit(solution)/shard_map/rows/pallas_call | solution.py:325
  145.8 9.3 %all_to_all.34.refs_3_ = f32[8,16,512]{2,1,0:T(8,128)S(1)} all-to-all(f32[8,16,512]{2,1,0:T(8,128)S(1)} %get-tuple-element.84), channel_id=1, replica_groups=mesh['y'=4,'x'=4,'core'=2,'z'=4] {'core','z'}, dimensions={0} | all-to-all | bytes 524288 | tf_op jit(solution)/shard_map/all_to_all | solution.py:339
  155.1 3.5 %columns.5 = (f32[16,4,128]{2,1,0:T(4,128)S(1)}, f32[32,128]{1,0:T(8,128)}) custom-call(s32[3,64]{1,0:T(4,128)S(1)} %get-tuple-element.45.pairs.refs_0_, s32[17]{0:T(128)S(1)} %get-tuple-element.47.bounds.refs_1_, s32[3]{0:T(128)S(1)} %pad_add_fusion.1.place.refs_2_, f32[8,16,512]{2,1,0:T(8,128)S(1)} %all_to_all.34.refs_3_, ...), custom_call_target="tpu_custom_call" | custom-call | tf_op jit(solution)/shard_map/columns/pallas_call | solution.py:325
  158.6 10.2 %all_to_all.35 = f32[16,4,128]{2,1,0:T(4,128)S(1)} all-to-all(f32[16,4,128]{2,1,0:T(4,128)S(1)} %get-tuple-element.87), channel_id=1, replica_groups=mesh['y'=4,'x'=4,'core'=2,'z'=4] {'y','x'}, dimensions={0} | all-to-all | bytes 65536 | tf_op jit(solution)/shard_map/all_to_all | solution.py:344
  168.8 0.6 log_bitcast_fusion
  (16 shorter events, 0.1 us)
Async XLA Ops:
  0.6 29.0 %copy-start = (bf16[512,768]{1,0:T(8,128)(2,1)S(1)}, bf16[512,768]{1,0:T(8,128)(2,1)}, u32[]{:S(2)}) copy-start(bf16[512,768]{1,0:T(8,128)(2,1)} %refs_5_.1) | copy-start | bytes 2359300
  0.6 26.4 %collective-permute-start.3 = (bf16[4096,768]{1,0:T(8,128)(2,1)}, bf16[4096,768]{1,0:T(8,128)(2,1)}, u32[]{:S(2)}, u32[]{:S(2)}) collective-permute-start(bf16[4096,768]{1,0:T(8,128)(2,1)} %refs_3_.11), channel_id=1, source_target_pairs={{0,4},{4,0},{1,5},{5,1},{2,6},{6,2},{3,7},{7,3},{8,12},{12,8},{9,1... | collective-permute-start | bytes 18874376 | tf_op jit(solution)/shard_map/ppermute | solution.py:243
  0.7 19.5 %collective-permute-start.1 = (bf16[512,768]{1,0:T(8,128)(2,1)}, bf16[512,768]{1,0:T(8,128)(2,1)S(1)}, u32[]{:S(2)}, u32[]{:S(2)}) collective-permute-start(bf16[512,768]{1,0:T(8,128)(2,1)} %refs_5_.1), channel_id=1, source_target_pairs={{0,8},{4,36},{8,16},{12,44},{16,24},{20,52},{24,0},{28,60},{32,40}... | collective-permute-start | bytes 2359304 | tf_op jit(solution)/shard_map/ppermute | solution.py:232
  2.4 17.9 %collective-permute-start.2 = (bf16[512,768]{1,0:T(8,128)(2,1)}, bf16[512,768]{1,0:T(8,128)(2,1)S(1)}, u32[]{:S(2)}, u32[]{:S(2)}) collective-permute-start(bf16[512,768]{1,0:T(8,128)(2,1)} %refs_5_.1), channel_id=1, source_target_pairs={{0,24},{4,100},{8,0},{12,108},{16,8},{20,116},{24,16},{28,124},{32... | collective-permute-start | bytes 2359304 | tf_op jit(solution)/shard_map/ppermute | solution.py:232
  5.5 5.4 %collective-permute-start = (s32[1,128]{1,0:T(1,128)S(1)}, s32[1,128]{1,0:T(1,128)S(1)}, u32[]{:S(2)}, u32[]{:S(2)}) collective-permute-start(s32[1,128]{1,0:T(1,128)S(1)} %pad_add_fusion), channel_id=1, source_target_pairs={{0,4},{4,0},{1,5},{5,1},{2,6},{6,2},{3,7},{7,3},{8,12},{12,8},{9,1... | collective-permute-start | bytes 1544 | tf_op jit(solution)/shard_map/ppermute | solution.py:244
  5.5 17.9 %collective-permute-start.6 = (bf16[512,768]{1,0:T(8,128)(2,1)}, bf16[512,768]{1,0:T(8,128)(2,1)S(1)}, u32[]{:S(2)}, u32[]{:S(2)}) collective-permute-start(bf16[512,768]{1,0:T(8,128)(2,1)} %refs_5_.1), channel_id=1, source_target_pairs={{0,32},{4,12},{8,40},{12,20},{16,48},{20,28},{24,56},{28,4},{32,64... | collective-permute-start | bytes 2359304 | tf_op jit(solution)/shard_map/ppermute | solution.py:232
  10.8 15.4 %collective-permute-start.7 = (bf16[512,768]{1,0:T(8,128)(2,1)}, bf16[512,768]{1,0:T(8,128)(2,1)}, u32[]{:S(2)}, u32[]{:S(2)}) collective-permute-start(bf16[512,768]{1,0:T(8,128)(2,1)} %refs_5_.1), channel_id=1, source_target_pairs={{0,96},{4,28},{8,104},{12,4},{16,112},{20,12},{24,120},{28,20},{32... | collective-permute-start | bytes 2359304 | tf_op jit(solution)/shard_map/ppermute | solution.py:232
  14.8 0.7 copy-start.1
  20.3 19.2 %collective-permute-start.4 = (bf16[512,768]{1,0:T(8,128)(2,1)S(1)}, bf16[512,768]{1,0:T(8,128)(2,1)S(1)}, u32[]{:S(2)}, u32[]{:S(2)}) collective-permute-start(bf16[512,768]{1,0:T(8,128)(2,1)S(1)} %collective-permute-done.2.refs_7_), channel_id=1, source_target_pairs={{0,24},{4,100},{8,0},{12,108},{16,8},{20,116},{24,16},{28,124},{32... | collective-permute-start | bytes 2359304 | tf_op jit(solution)/shard_map/ppermute | solution.py:232
  22.3 17.2 %collective-permute-start.5 = (bf16[512,768]{1,0:T(8,128)(2,1)S(1)}, bf16[512,768]{1,0:T(8,128)(2,1)S(1)}, u32[]{:S(2)}, u32[]{:S(2)}) collective-permute-start(bf16[512,768]{1,0:T(8,128)(2,1)S(1)} %collective-permute-done.2.refs_7_), channel_id=1, source_target_pairs={{0,32},{4,12},{8,40},{12,20},{16,48},{20,28},{24,56},{28,4},{32,64... | collective-permute-start | bytes 2359304 | tf_op jit(solution)/shard_map/ppermute | solution.py:232
  23.4 24.0 %collective-permute-start.10 = (bf16[512,768]{1,0:T(8,128)(2,1)S(1)}, bf16[512,768]{1,0:T(8,128)(2,1)S(1)}, u32[]{:S(2)}, u32[]{:S(2)}) collective-permute-start(bf16[512,768]{1,0:T(8,128)(2,1)S(1)} %collective-permute-done.2.refs_7_), channel_id=1, source_target_pairs={{0,96},{4,28},{8,104},{12,4},{16,112},{20,12},{24,120},{28,20},{32... | collective-permute-start | bytes 2359304 | tf_op jit(solution)/shard_map/ppermute | solution.py:232
  26.2 21.3 %collective-permute-start.11 = (bf16[512,768]{1,0:T(8,128)(2,1)S(1)}, bf16[512,768]{1,0:T(8,128)(2,1)S(1)}, u32[]{:S(2)}, u32[]{:S(2)}) collective-permute-start(bf16[512,768]{1,0:T(8,128)(2,1)S(1)} %collective-permute-done.1.refs_6_), channel_id=1, source_target_pairs={{0,32},{4,12},{8,40},{12,20},{16,48},{20,28},{24,56},{28,4},{32,64... | collective-permute-start | bytes 2359304 | tf_op jit(solution)/shard_map/ppermute | solution.py:232
  27.0 21.9 %collective-permute-start.9 = (bf16[512,768]{1,0:T(8,128)(2,1)S(1)}, bf16[512,768]{1,0:T(8,128)(2,1)S(1)}, u32[]{:S(2)}, u32[]{:S(2)}) collective-permute-start(bf16[512,768]{1,0:T(8,128)(2,1)S(1)} %collective-permute-done.1.refs_6_), channel_id=1, source_target_pairs={{0,96},{4,28},{8,104},{12,4},{16,112},{20,12},{24,120},{28,20},{32... | collective-permute-start | bytes 2359304 | tf_op jit(solution)/shard_map/ppermute | solution.py:232
  39.5 19.1 %collective-permute-start.8 = (bf16[512,768]{1,0:T(8,128)(2,1)S(1)}, bf16[512,768]{1,0:T(8,128)(2,1)S(1)}, u32[]{:S(2)}, u32[]{:S(2)}) collective-permute-start(bf16[512,768]{1,0:T(8,128)(2,1)S(1)} %collective-permute-done.4.refs_5_), channel_id=1, source_target_pairs={{0,96},{4,28},{8,104},{12,4},{16,112},{20,12},{24,120},{28,20},{32... | collective-permute-start | bytes 2359304 | tf_op jit(solution)/shard_map/ppermute | solution.py:232
  40.4 20.6 %collective-permute-start.16 = (bf16[512,768]{1,0:T(8,128)(2,1)S(1)}, bf16[512,768]{1,0:T(8,128)(2,1)S(1)}, u32[]{:S(2)}, u32[]{:S(2)}) collective-permute-start(bf16[512,768]{1,0:T(8,128)(2,1)S(1)} %collective-permute-done.5.refs_6_), channel_id=1, source_target_pairs={{0,32},{4,12},{8,40},{12,20},{16,48},{20,28},{24,56},{28,4},{32,64... | collective-permute-start | bytes 2359304 | tf_op jit(solution)/shard_map/ppermute | solution.py:232
  47.4 23.1 %collective-permute-start.15 = (bf16[512,768]{1,0:T(8,128)(2,1)S(1)}, bf16[512,768]{1,0:T(8,128)(2,1)S(1)}, u32[]{:S(2)}, u32[]{:S(2)}) collective-permute-start(bf16[512,768]{1,0:T(8,128)(2,1)S(1)} %collective-permute-done.4.refs_5_), channel_id=1, source_target_pairs={{0,32},{4,12},{8,40},{12,20},{16,48},{20,28},{24,56},{28,4},{32,64... | collective-permute-start | bytes 2359304 | tf_op jit(solution)/shard_map/ppermute | solution.py:232
  48.9 17.9 %collective-permute-start.13 = (bf16[512,768]{1,0:T(8,128)(2,1)S(1)}, bf16[512,768]{1,0:T(8,128)(2,1)S(1)}, u32[]{:S(2)}, u32[]{:S(2)}) collective-permute-start(bf16[512,768]{1,0:T(8,128)(2,1)S(1)} %collective-permute-done.9.refs_5_), channel_id=1, source_target_pairs={{0,96},{4,28},{8,104},{12,4},{16,112},{20,12},{24,120},{28,20},{32... | collective-permute-start | bytes 2359304 | tf_op jit(solution)/shard_map/ppermute | solution.py:232
  52.6 17.8 %collective-permute-start.14 = (bf16[512,768]{1,0:T(8,128)(2,1)S(1)}, bf16[512,768]{1,0:T(8,128)(2,1)S(1)}, u32[]{:S(2)}, u32[]{:S(2)}) collective-permute-start(bf16[512,768]{1,0:T(8,128)(2,1)S(1)} %collective-permute-done.6.refs_8_), channel_id=1, source_target_pairs={{0,32},{4,12},{8,40},{12,20},{16,48},{20,28},{24,56},{28,4},{32,64... | collective-permute-start | bytes 2359304 | tf_op jit(solution)/shard_map/ppermute | solution.py:232
  58.6 16.5 %collective-permute-start.12 = (bf16[512,768]{1,0:T(8,128)(2,1)S(1)}, bf16[512,768]{1,0:T(8,128)(2,1)S(1)}, u32[]{:S(2)}, u32[]{:S(2)}) collective-permute-start(bf16[512,768]{1,0:T(8,128)(2,1)S(1)} %collective-permute-done.8.refs_5_), channel_id=1, source_target_pairs={{0,96},{4,28},{8,104},{12,4},{16,112},{20,12},{24,120},{28,20},{32... | collective-permute-start | bytes 2359304 | tf_op jit(solution)/shard_map/ppermute | solution.py:232
